TPU v7x, 32 devices: a whole 2x2x4 slice. The times are simulated.
32 devices in a mesh: shard: 4 (over y, x), context: 2 (over core), tensor: 4 (over z).
Axes of the slice: x: 2, y: 2, z: 4, core: 2. Of those that a mesh axis runs over, the one named last changes fastest.
Arguments:
- hidden: bfloat16 [4, 2048, 2048], P('shard', 'context'), may hold values from -6 to 6
- segment_ids: int32 [4, 2048], P('shard', 'context'), may hold values from 0 to 3, as said below
- norm1_gain: float32 [2048], replicated, may hold values from 0.25 to 1.75
- w_query: bfloat16 [2048, 2048], P(('shard', 'context'), 'tensor'), may hold values from -0.125 to 0.125
- w_forget: bfloat16 [2048, 2048], P(('shard', 'context'), 'tensor'), may hold values from -0.125 to 0.125
- w_input: bfloat16 [2048, 2048], P(('shard', 'context'), 'tensor'), may hold values from -0.125 to 0.125
- w_gate_out: bfloat16 [2048, 2048], P(('shard', 'context'), 'tensor'), may hold values from -0.125 to 0.125
- forget_floor: float32 [16, 128], P('tensor'), may hold values from 0.9 to 0.99975
- head_gain: float32 [128], replicated, may hold values from 0.25 to 1.75
- w_out: bfloat16 [2048, 2048], P('tensor', ('shard', 'context')), may hold values from -0.1875 to 0.1875
- norm2_gain: float32 [2048], replicated, may hold values from 0.25 to 1.75
- w_ffn_gate: bfloat16 [2048, 5632], P(('shard', 'context'), 'tensor'), may hold values from -0.125 to 0.125
- w_ffn_up: bfloat16 [2048, 5632], P(('shard', 'context'), 'tensor'), may hold values from -0.125 to 0.125
- w_ffn_down: bfloat16 [5632, 2048], P('tensor', ('shard', 'context')), may hold values from -0.15625 to 0.15625
- out_grad: bfloat16 [4, 2048, 2048], P('shard', 'context'), may hold values from -6 to 6
Outputs:
- block_out: bfloat16 [4, 2048, 2048], P('shard', 'context')
- input_grad: bfloat16 [4, 2048, 2048], P('shard', 'context')
- grad_norm1: float32 [2048], P(('shard', 'context'))
- grad_query: float32 [2048, 2048], P(('shard', 'context'), 'tensor')
- grad_forget: float32 [2048, 2048], P(('shard', 'context'), 'tensor')
- grad_input: float32 [2048, 2048], P(('shard', 'context'), 'tensor')
- grad_gate_out: float32 [2048, 2048], P(('shard', 'context'), 'tensor')
- grad_floor: float32 [16, 128], P('tensor', ('shard', 'context'))
- grad_head_gain: float32 [128], P(('shard', 'context'))
- grad_out_proj: float32 [2048, 2048], P('tensor', ('shard', 'context'))
- grad_norm2: float32 [2048], P(('shard', 'context'))
- grad_ffn_gate: float32 [2048, 5632], P(('shard', 'context'), 'tensor')
- grad_ffn_up: float32 [2048, 5632], P(('shard', 'context'), 'tensor')
- grad_ffn_down: float32 [5632, 2048], P('tensor', ('shard', 'context'))
Inputs may be any that keep to these rules, and one draw needn't show every extreme that they name: `segment_ids`: in each sequence a document's tokens are consecutive and share one positive id that differs from the ids of the neighbouring documents; every sequence holds three or more documents and ends with one or more pad slots (id 0), and pads stand nowhere else.
All inputs are finite; a program needn't handle non-finite values.
Results may differ from a plain program's by a relative error of at most 0.018.
Values may be sent and summed in bfloat16 or wider, within the bound.
A program may use at most 256 MiB of HBM per device.

v0:
```python
from functools import partial

import jax
import jax.numpy as jnp
from jax import lax
from jax.sharding import PartitionSpec as P

STRETCH = 64


EPSILON = 1e-05
HIGHEST = lax.Precision.HIGHEST


def prefix(part, axis, combine, identity):
    place = lax.axis_index(axis)
    gathered = jax.tree.map(lambda a: lax.all_gather(a, axis), part)
    state = jax.tree.map(lambda a, e: jnp.zeros_like(a) + jnp.asarray(e, a.dtype), part, identity)

    def one(step, state):
        return combine(
            state, jax.tree.map(lambda a: lax.dynamic_index_in_dim(a, step, 0, False), gathered)
        )

    return lax.fori_loop(0, place, one, state)


def prefix_2(x, axis, join, neutral):
    count = lax.axis_size(axis)
    place = lax.axis_index(axis)
    ahead = count - 1 - place
    gathered = jax.tree.map(
        lambda a, kind: lax.all_gather(a.astype(kind), axis),
        x,
        jax.tree.map(lambda a: jnp.bfloat16 if a.dtype == jnp.float32 else a.dtype, x),
    )
    state = jax.tree.map(lambda a, e: jnp.zeros_like(a) + jnp.asarray(e, a.dtype), x, neutral)

    def one(step, state):
        source = count - 1 - step
        return join(
            state,
            jax.tree.map(
                lambda a, own: lax.dynamic_index_in_dim(a, source, 0, False).astype(own.dtype),
                gathered,
                x,
            ),
        )

    return lax.fori_loop(0, ahead, one, state)


def rms_parts(values):
    inverse = lax.rsqrt(jnp.mean(values * values, axis=-1, keepdims=True) + EPSILON)
    return (values * inverse, inverse)


def head_gated(results, weights, gating):
    unit_rows, _ = rms_parts(results)
    return unit_rows * weights * jax.nn.silu(gating)


def block_step(key_scale, carried, block_in):
    queries, inputs_in, values, log_decay, starts, keep_flags = block_in
    counter = jnp.cumsum(starts, axis=-1)
    cumulated = jnp.cumsum(log_decay, axis=2)
    keep_col = keep_flags[:, None, :, None]
    length = starts.shape[-1]
    positions = jnp.arange(length)
    causal = positions[:, None] >= positions[None, :]
    linked = jnp.logical_and(counter[:, :, None] == counter[:, None, :], causal[None]).astype(
        jnp.float32
    )
    lifted = queries * jnp.exp(cumulated)
    lowered = inputs_in * jnp.exp(-cumulated) * keep_col
    scores = jnp.einsum("ghtk,ghsk->ghts", lifted, lowered, precision=HIGHEST) * linked[:, None]
    fresh_mask = (counter == 0).astype(jnp.float32)[:, None, :, None]
    results = jnp.einsum("ghts,ghsv->ghtv", scores, values, precision=HIGHEST)
    results = results + jnp.einsum(
        "ghtk,ghkv->ghtv", lifted * fresh_mask, carried, precision=HIGHEST
    )
    results = results * key_scale * keep_col
    ending = cumulated[:, :, -1:, :]
    tail_mask = (counter == counter[:, -1:]).astype(jnp.float32)[:, None, :, None]
    moved_in = inputs_in * jnp.exp(ending - cumulated) * keep_col * tail_mask
    closing = (counter[:, -1] == 0).astype(jnp.float32)[:, None, None, None]
    updated = jnp.exp(ending[:, :, 0, :])[..., None] * closing * carried
    updated = updated + jnp.einsum("ghsk,ghsv->ghkv", moved_in, values, precision=HIGHEST)
    return (updated, results)


def recurrence(
    key_scale, block_len, starts, keep_flags, queries, inputs_in, values, log_decay, carried
):
    groups, length, head_count, key_dim = queries.shape
    value_dim = values.shape[-1]
    blocks = length // block_len

    def split_heads(matrix):
        return matrix.reshape(groups, blocks, block_len, head_count, matrix.shape[-1]).transpose(
            1, 0, 3, 2, 4
        )

    def split_flags(matrix):
        return matrix.reshape(groups, blocks, block_len).transpose(1, 0, 2)

    stepper = jax.checkpoint(partial(block_step, key_scale))
    ending, results = lax.scan(
        stepper,
        carried,
        (
            split_heads(queries),
            split_heads(inputs_in),
            split_heads(values),
            split_heads(log_decay),
            split_flags(starts),
            split_flags(keep_flags),
        ),
    )
    return (results.transpose(1, 0, 3, 2, 4).reshape(groups, length, head_count, value_dim), ending)


def choose_side(take_two, take_one, joined, option_one, option_two):
    shaping = (-1,) + (1,) * (joined.ndim - 1)
    return jnp.where(
        take_two.reshape(shaping),
        option_two,
        jnp.where(take_one.reshape(shaping), option_one, joined),
    )


def join_states(earlier, follower):
    decay_one, state_one, first_one, last_one, valid_one = earlier
    decay_two, state_two, first_two, last_two, valid_two = follower
    linked = (last_one == first_two).astype(jnp.float32)
    decay_join = decay_one * decay_two * linked[:, None, None]
    state_join = decay_two[..., None] * linked[:, None, None, None] * state_one + state_two
    take_two = valid_one == 0
    take_one = valid_two == 0
    return (
        choose_side(take_two, take_one, decay_join, decay_one, decay_two),
        choose_side(take_two, take_one, state_join, state_one, state_two),
        choose_side(take_two, take_one, first_one, first_one, first_two),
        choose_side(take_two, take_one, last_two, last_one, last_two),
        jnp.maximum(valid_one, valid_two),
    )


def join_grads(earlier, follower):
    decay_one, state_one = earlier
    decay_two, state_two = follower
    return (decay_one * decay_two, state_two + decay_two[..., None] * state_one)


def head_sums(values):
    return lax.psum(values, "tensor")


def local(
    hidden,
    segment_ids,
    norm1_gain,
    w_query,
    w_forget,
    w_input,
    w_gate_out,
    forget_floor,
    head_gain,
    w_out,
    norm2_gain,
    w_ffn_gate,
    w_ffn_up,
    w_ffn_down,
    out_grad,
):
    sequences, span_len, model_width = hidden.shape
    tokens = sequences * span_len
    head_count, key_dim = forget_floor.shape
    value_dim = head_gain.shape[0]
    key_scale = key_dim ** (-0.5)
    mixer_shards = (w_query, w_forget, w_input, w_gate_out, w_out)
    feed_shards = (w_ffn_gate, w_ffn_up, w_ffn_down)
    query_full, forget_full, input_full, gate_out_full, out_full = (
        lax.all_gather(mixer_shards[0], ("shard", "context"), axis=0, tiled=True),
        lax.all_gather(mixer_shards[1], ("shard", "context"), axis=0, tiled=True),
        lax.all_gather(mixer_shards[2], ("shard", "context"), axis=0, tiled=True),
        lax.all_gather(mixer_shards[3], ("shard", "context"), axis=0, tiled=True),
        lax.all_gather(mixer_shards[4], ("shard", "context"), axis=1, tiled=True),
    )
    gate_full, up_full, down_full = (
        lax.all_gather(feed_shards[0], ("shard", "context"), axis=0, tiled=True),
        lax.all_gather(feed_shards[1], ("shard", "context"), axis=0, tiled=True),
        lax.all_gather(feed_shards[2], ("shard", "context"), axis=1, tiled=True),
    )
    inputs = hidden.reshape(tokens, model_width).astype(jnp.float32)
    unit_one, inverse_one = rms_parts(inputs)
    normed_one = (unit_one * norm1_gain).astype(jnp.bfloat16)
    query_pre = jnp.dot(normed_one, query_full, preferred_element_type=jnp.float32)
    forget_pre = jnp.dot(normed_one, forget_full, preferred_element_type=jnp.float32)
    input_pre = jnp.dot(normed_one, input_full, preferred_element_type=jnp.float32)
    gate_pre = jnp.dot(normed_one, gate_out_full, preferred_element_type=jnp.float32)
    queries = jax.nn.silu(query_pre).reshape(sequences, span_len, head_count, key_dim)
    open_part = (1.0 - forget_floor).reshape(1, head_count * key_dim)
    closed = jax.nn.sigmoid(-forget_pre)
    inputs_in = open_part * closed
    log_decay = jnp.log1p(-inputs_in)
    key_blocks = inputs_in.reshape(sequences, span_len, head_count, key_dim)
    decay_blocks = log_decay.reshape(sequences, span_len, head_count, key_dim)
    value_blocks = input_pre.reshape(sequences, span_len, head_count, value_dim)
    boundary = (segment_ids[:, 1:] != segment_ids[:, :-1]).astype(jnp.float32)
    starts = jnp.concatenate([jnp.zeros((sequences, 1), jnp.float32), boundary], axis=1)
    keep_flags = (segment_ids > 0).astype(jnp.float32)
    mixer_fn = partial(recurrence, key_scale, STRETCH, starts, keep_flags)
    empty_state = jnp.zeros((sequences, head_count, key_dim, value_dim), jnp.float32)
    local_out, local_state = mixer_fn(queries, key_blocks, value_blocks, decay_blocks, empty_state)
    reach_mask = (jnp.cumsum(starts, axis=1) == 0).astype(jnp.float32)
    rising = jnp.cumsum(decay_blocks, axis=1)
    lead_rows = queries * jnp.exp(rising) * (reach_mask * keep_flags * key_scale)[:, :, None, None]
    kept_all = (jnp.sum(starts, axis=1) == 0).astype(jnp.float32)
    decay_all = jnp.exp(rising[:, -1]) * kept_all[:, None, None]
    first_ids = segment_ids[:, 0].astype(jnp.float32)
    last_ids = segment_ids[:, -1].astype(jnp.float32)
    ones_seq = jnp.ones((sequences,), jnp.float32)
    identity = (
        jnp.ones_like(decay_all),
        jnp.zeros_like(local_state),
        jnp.zeros_like(first_ids),
        jnp.zeros_like(first_ids),
        jnp.zeros_like(first_ids),
    )
    prefix_in = prefix(
        (decay_all, local_state, first_ids, last_ids, ones_seq), "context", join_states, identity
    )
    link_in = (prefix_in[3] == first_ids).astype(jnp.float32) * prefix_in[4]
    carry_in = prefix_in[1] * link_in[:, None, None, None]
    mixed_out = local_out + jnp.einsum("sthk,shkv->sthv", lead_rows, carry_in, precision=HIGHEST)
    gate_heads = gate_pre.reshape(tokens, head_count, value_dim)
    mixed_rows = mixed_out.reshape(tokens, head_count, value_dim)
    gated_rows = head_gated(mixed_rows, head_gain, gate_heads)
    gated_low = gated_rows.reshape(tokens, head_count * value_dim).astype(jnp.bfloat16)
    mix_part = jnp.dot(gated_low, out_full, preferred_element_type=jnp.float32)
    residual = inputs + head_sums(mix_part)
    unit_two, inverse_two = rms_parts(residual)
    normed_two = (unit_two * norm2_gain).astype(jnp.bfloat16)
    gate_ffn = jnp.dot(normed_two, gate_full, preferred_element_type=jnp.float32)
    up_ffn = jnp.dot(normed_two, up_full, preferred_element_type=jnp.float32)
    sigma_gate = jax.nn.sigmoid(gate_ffn)
    active = gate_ffn * sigma_gate
    hidden_low = (active * up_ffn).astype(jnp.bfloat16)
    feed_part = jnp.dot(hidden_low, down_full, preferred_element_type=jnp.float32)
    output_rows = (residual + head_sums(feed_part)).astype(jnp.bfloat16)
    gate_full, up_full, down_full = (
        lax.all_gather(feed_shards[0], ("shard", "context"), axis=0, tiled=True),
        lax.all_gather(feed_shards[1], ("shard", "context"), axis=0, tiled=True),
        lax.all_gather(feed_shards[2], ("shard", "context"), axis=1, tiled=True),
    )
    query_full, forget_full, input_full, gate_out_full, out_full = (
        lax.all_gather(mixer_shards[0], ("shard", "context"), axis=0, tiled=True),
        lax.all_gather(mixer_shards[1], ("shard", "context"), axis=0, tiled=True),
        lax.all_gather(mixer_shards[2], ("shard", "context"), axis=0, tiled=True),
        lax.all_gather(mixer_shards[3], ("shard", "context"), axis=0, tiled=True),
        lax.all_gather(mixer_shards[4], ("shard", "context"), axis=1, tiled=True),
    )
    grad_rows = out_grad.reshape(tokens, model_width)
    grad_down = jnp.einsum("tf,td->fd", hidden_low, grad_rows, preferred_element_type=jnp.float32)
    grad_hidden = jnp.einsum("td,fd->tf", grad_rows, down_full, preferred_element_type=jnp.float32)
    grad_gate_low = (
        grad_hidden * up_ffn * sigma_gate * (1.0 + gate_ffn * (1.0 - sigma_gate))
    ).astype(jnp.bfloat16)
    grad_up_low = (grad_hidden * active).astype(jnp.bfloat16)
    grad_gate = jnp.einsum(
        "td,tf->df", normed_two, grad_gate_low, preferred_element_type=jnp.float32
    )
    grad_up = jnp.einsum("td,tf->df", normed_two, grad_up_low, preferred_element_type=jnp.float32)
    back_two = jnp.einsum("tf,df->td", grad_gate_low, gate_full, preferred_element_type=jnp.float32)
    back_two = back_two + jnp.einsum(
        "tf,df->td", grad_up_low, up_full, preferred_element_type=jnp.float32
    )
    grad_normed_two = head_sums(back_two)
    cotangent_rows = grad_rows.astype(jnp.float32)
    grad_norm_two = jnp.sum(grad_normed_two * unit_two, axis=0)
    lifted_two = grad_normed_two * norm2_gain
    grad_residual = cotangent_rows + inverse_two * (
        lifted_two - unit_two * jnp.mean(lifted_two * unit_two, axis=-1, keepdims=True)
    )
    grad_mix_low = grad_residual.astype(jnp.bfloat16)
    grad_out = jnp.einsum("tv,td->vd", gated_low, grad_mix_low, preferred_element_type=jnp.float32)
    grad_gated = jnp.einsum(
        "td,vd->tv", grad_mix_low, out_full, preferred_element_type=jnp.float32
    ).reshape(tokens, head_count, value_dim)
    _, pull_gate = jax.vjp(head_gated, mixed_rows, head_gain, gate_heads)
    grad_mixed, grad_head_part, grad_gate_heads = pull_gate(grad_gated)
    grad_mixed_blocks = grad_mixed.reshape(sequences, span_len, head_count, value_dim)
    carry_back = (
        jnp.einsum("sthk,sthv->shkv", lead_rows, grad_mixed_blocks, precision=HIGHEST)
        * link_in[:, None, None, None]
    )
    decay_back = decay_all * link_in[:, None, None]
    after_back = prefix_2(
        (decay_back, carry_back),
        "context",
        join_grads,
        (jnp.ones_like(decay_back), jnp.zeros_like(carry_back)),
    )
    _, pull_mixer = jax.vjp(mixer_fn, queries, key_blocks, value_blocks, decay_blocks, carry_in)
    grad_queries, grad_keys, grad_values, grad_decay, _ = pull_mixer(
        (grad_mixed_blocks, after_back[1])
    )
    sigma_query = jax.nn.sigmoid(query_pre)
    grad_query_low = (
        grad_queries.reshape(tokens, head_count * key_dim)
        * sigma_query
        * (1.0 + query_pre * (1.0 - sigma_query))
    ).astype(jnp.bfloat16)
    key_total = grad_keys.reshape(tokens, head_count * key_dim) - grad_decay.reshape(
        tokens, head_count * key_dim
    ) / (1.0 - inputs_in)
    grad_floor_part = -jnp.sum(key_total * closed, axis=0).reshape(head_count, key_dim)
    grad_forget_low = (-key_total * open_part * closed * (1.0 - closed)).astype(jnp.bfloat16)
    grad_input_low = grad_values.reshape(tokens, head_count * value_dim).astype(jnp.bfloat16)
    grad_gatepre_low = grad_gate_heads.reshape(tokens, head_count * value_dim).astype(jnp.bfloat16)
    grad_query_w = jnp.einsum(
        "td,tk->dk", normed_one, grad_query_low, preferred_element_type=jnp.float32
    )
    grad_forget_w = jnp.einsum(
        "td,tk->dk", normed_one, grad_forget_low, preferred_element_type=jnp.float32
    )
    grad_input_w = jnp.einsum(
        "td,tk->dk", normed_one, grad_input_low, preferred_element_type=jnp.float32
    )
    grad_gate_w = jnp.einsum(
        "td,tk->dk", normed_one, grad_gatepre_low, preferred_element_type=jnp.float32
    )
    back_one = jnp.einsum(
        "tk,dk->td", grad_query_low, query_full, preferred_element_type=jnp.float32
    )
    back_one = back_one + jnp.einsum(
        "tk,dk->td", grad_forget_low, forget_full, preferred_element_type=jnp.float32
    )
    back_one = back_one + jnp.einsum(
        "tk,dk->td", grad_input_low, input_full, preferred_element_type=jnp.float32
    )
    back_one = back_one + jnp.einsum(
        "tk,dk->td", grad_gatepre_low, gate_out_full, preferred_element_type=jnp.float32
    )
    grad_normed_one, head_total = head_sums((back_one, grad_head_part))
    grad_norm_one = jnp.sum(grad_normed_one * unit_one, axis=0)
    lifted_one = grad_normed_one * norm1_gain
    grad_inputs = grad_residual + inverse_one * (
        lifted_one - unit_one * jnp.mean(lifted_one * unit_one, axis=-1, keepdims=True)
    )
    input_rows = grad_inputs.astype(jnp.bfloat16)
    block_out = output_rows.reshape(sequences, span_len, model_width)
    input_grad = input_rows.reshape(sequences, span_len, model_width)
    shares = (
        lax.psum_scatter(
            grad_query_w.astype(jnp.bfloat16), ("shard", "context"), scatter_dimension=0, tiled=True
        ).astype(jnp.float32),
        lax.psum_scatter(
            grad_forget_w.astype(jnp.bfloat16),
            ("shard", "context"),
            scatter_dimension=0,
            tiled=True,
        ).astype(jnp.float32),
        lax.psum_scatter(
            grad_input_w.astype(jnp.bfloat16), ("shard", "context"), scatter_dimension=0, tiled=True
        ).astype(jnp.float32),
        lax.psum_scatter(
            grad_gate_w.astype(jnp.bfloat16), ("shard", "context"), scatter_dimension=0, tiled=True
        ).astype(jnp.float32),
        lax.psum_scatter(
            grad_floor_part.astype(jnp.bfloat16),
            ("shard", "context"),
            scatter_dimension=1,
            tiled=True,
        ).astype(jnp.float32),
        lax.psum_scatter(
            head_total.astype(jnp.bfloat16), ("shard", "context"), scatter_dimension=0, tiled=True
        ).astype(jnp.float32),
        lax.psum_scatter(
            grad_out.astype(jnp.bfloat16), ("shard", "context"), scatter_dimension=1, tiled=True
        ).astype(jnp.float32),
        lax.psum_scatter(
            grad_norm_one.astype(jnp.bfloat16),
            ("shard", "context"),
            scatter_dimension=0,
            tiled=True,
        ).astype(jnp.float32),
        lax.psum_scatter(
            grad_gate.astype(jnp.bfloat16), ("shard", "context"), scatter_dimension=0, tiled=True
        ).astype(jnp.float32),
        lax.psum_scatter(
            grad_up.astype(jnp.bfloat16), ("shard", "context"), scatter_dimension=0, tiled=True
        ).astype(jnp.float32),
        lax.psum_scatter(
            grad_down.astype(jnp.bfloat16), ("shard", "context"), scatter_dimension=1, tiled=True
        ).astype(jnp.float32),
        lax.psum_scatter(
            grad_norm_two.astype(jnp.bfloat16),
            ("shard", "context"),
            scatter_dimension=0,
            tiled=True,
        ).astype(jnp.float32),
    )
    (
        share_query,
        share_forget,
        share_input,
        share_gate,
        share_floor,
        share_head,
        share_out,
        share_one,
        share_ffn_gate,
        share_ffn_up,
        share_ffn_down,
        share_two,
    ) = shares
    return (
        block_out,
        input_grad,
        share_one,
        share_query,
        share_forget,
        share_input,
        share_gate,
        share_floor,
        share_head,
        share_out,
        share_two,
        share_ffn_gate,
        share_ffn_up,
        share_ffn_down,
    )


def solution(mesh):
    in_specs = (
        P("shard", "context", None),
        P("shard", "context"),
        P(),
        P(("shard", "context"), "tensor"),
        P(("shard", "context"), "tensor"),
        P(("shard", "context"), "tensor"),
        P(("shard", "context"), "tensor"),
        P("tensor", None),
        P(),
        P("tensor", ("shard", "context")),
        P(),
        P(("shard", "context"), "tensor"),
        P(("shard", "context"), "tensor"),
        P("tensor", ("shard", "context")),
        P("shard", "context", None),
    )
    out_specs = (
        P("shard", "context", None),
        P("shard", "context", None),
        P(("shard", "context")),
        P(("shard", "context"), "tensor"),
        P(("shard", "context"), "tensor"),
        P(("shard", "context"), "tensor"),
        P(("shard", "context"), "tensor"),
        P("tensor", ("shard", "context")),
        P(("shard", "context")),
        P("tensor", ("shard", "context")),
        P(("shard", "context")),
        P(("shard", "context"), "tensor"),
        P(("shard", "context"), "tensor"),
        P("tensor", ("shard", "context")),
    )
    return jax.shard_map(local, mesh=mesh, in_specs=in_specs, out_specs=out_specs, check_vma=False)
```

profile of v0, /device:TPU:0, one launch (start us, length us, event | category | flops | bytes accessed | tf_op | source)
XLA Modules:
  0.0 2451.3 jit_solution(10695409598800309038)
XLA Ops:
  21.2 5.2 fusion.130
  31.8 8.8 all-gather.11.cloned.1.call-done
  40.6 8.1 broadcast_multiply_fusion.2
  62.6 7.9 all-gather.13.cloned.1.call-done
  74.4 25.9 %all-gather.15.cloned.1.call-done = bf16[2048,512]{1,0:T(8,128)(2,1)} async-done(((bf16[256,512]{1,0:T(8,128)(2,1)}), bf16[2048,512]{1,0:T(8,128)(2,1)}) %all-gather.15.cloned.1.call-update) | async-done | bytes 2097168 | tf_op jit(solution)/shard_map/all_gather | solution.py:184
  100.3 7.5 fusion.159
  117.0 5.3 convolution_bitcast_fusion.4
  122.3 161.4 %while.82 = (s32[]{:T(128)}, f32[1,4,128,128]{3,2,1,0:T(8,128)S(1)}, f32[16,1,4,64,128]{4,3,0,2,1:T(8,128)}, f32[16,1,4,64,128]{4,3,2,1,0:T(8,128)}, f32[16,1,64...) while((s32[]{:T(128)}, ...), condition=%wide.region_4.5_spmd.clone, body=%wide.region_1.4_spmd.clone.sunk | while | flops 153752320 | bytes 3215802 | solution.py:108
  298.1 10.4 multiply_bitcast_fusion.1
  329.1 7.5 fusion.183
  340.2 292.1 %all-reduce.14.cloned.1.call-done = f32[1024,2048]{1,0:T(8,128)} async-done(((f32[1024,2048]{1,0:T(8,128)}), f32[1024,2048]{1,0:T(8,128)}) %all-reduce.14.cloned.1.call-update) | async-done | bytes 8388624 | tf_op jit(solution)/shard_map/psum | solution.py:156
  632.3 5.7 multiply_reduce_fusion.3
  644.1 32.4 %all-gather.21.cloned.1.call-done = bf16[2048,1408]{1,0:T(8,128)(2,1)} async-done(((bf16[256,1408]{1,0:T(8,128)(2,1)}), bf16[2048,1408]{1,0:T(8,128)(2,1)}) %all-gather.21.cloned.1.call-update) | async-done | bytes 5767184 | tf_op jit(solution)/shard_map/all_gather | solution.py:191
  676.5 11.9 fusion.184
  688.5 33.3 %all-gather.23.cloned.1.call-done = bf16[2048,1408]{1,0:T(8,128)(2,1)} async-done(((bf16[256,1408]{1,0:T(8,128)(2,1)}), bf16[2048,1408]{1,0:T(8,128)(2,1)}) %all-gather.23.cloned.1.call-update) | async-done | bytes 5767184 | tf_op jit(solution)/shard_map/all_gather | solution.py:192
  721.8 11.7 fusion.185
  733.5 34.6 %all-gather.25.cloned.1.call-done = bf16[1408,2048]{1,0:T(8,128)(2,1)} async-done(((bf16[1408,256]{1,0:T(8,128)(2,1)}), bf16[1408,2048]{1,0:T(8,128)(2,1)}) %all-gather.25.cloned.1.call-update) | async-done | bytes 5767184 | tf_op jit(solution)/shard_map/all_gather | solution.py:193
  768.1 15.6 multiply_convert_fusion.1
  783.6 10.9 fusion.187
  794.5 9.0 convolution_add_fusion.2
  803.6 101.7 %while.80 = (s32[]{:T(128)}, f32[1,4,128,128]{3,2,1,0:T(8,128)S(1)}, f32[16,1,4,128,128]{4,3,2,1,0:T(8,128)}, f32[16,1,4,64,128]{4,3,2,1,0:T(8,128)}, f32[16,1,6...) while((s32[]{:T(128)}, ...), condition=%wide.region_24.25_spmd, body=%wide.region_21.24_spmd.sunk | while | flops 52662852 | bytes 1982623 | solution.py:108
  907.8 186.7 %all-reduce.16.cloned.1.call-done = f32[1024,2048]{1,0:T(8,128)} async-done(((f32[1024,2048]{1,0:T(8,128)}), f32[1024,2048]{1,0:T(8,128)}) %all-reduce.16.cloned.1.call-update) | async-done | bytes 8388624 | tf_op jit(solution)/shard_map/psum | solution.py:156
  1094.5 7.6 multiply_reduce_fusion.1
  1108.5 5.7 fusion.156
  1132.5 242.7 %while.81 = (s32[]{:T(128)}, f32[1,4,128,128]{2,3,1,0:T(8,128)S(1)}, f32[16,1,4,64,128]{4,3,2,1,0:T(8,128)S(1)}, f32[16,1,4,64,128]{4,3,2,1,0:T(8,128)}, bf16[16...) while((s32[]{:T(128)}, ...), condition=%wide.region_31.32_spmd, body=%wide.region_25.31_spmd.sunk | while | flops 333272256 | bytes 10709303 | solution.py:108
  1397.1 11.1 convolution_convert_fusion.2
  1408.3 11.0 convolution_convert_fusion.1
  1419.3 10.5 convolution_convert_fusion
  1430.5 6.6 convolution_convert_fusion.4
  1437.2 8.0 convolution_convert_fusion.3
  1462.5 6.3 fusion.146
  1468.8 6.0 fusion.143
  1475.1 11.7 fusion.186
  1489.4 5.6 fusion.188
  1495.0 5.9 fusion.162
  1500.9 14.1 add_add_fusion
  1517.6 8.6 psum.39
  1529.8 23.0 reduce-scatter.24.cloned.1.call-done
  1555.1 60.5 %reduce-scatter.26.cloned.1.call-done = bf16[1408,256]{1,0:T(8,128)(2,1)} async-done(((bf16[1408,2048]{1,0:T(8,128)(2,1)}), bf16[1408,256]{1,0:T(8,128)(2,1)}) %reduce-scatter.26.cloned.1.call-update) | async-done | bytes 720912 | tf_op jit(solution)/shard_map/reduce_scatter | solution.py:395
  1617.9 42.1 %reduce-scatter.14.cloned.1.call-done = bf16[256,512]{1,0:T(8,128)(2,1)} async-done(((bf16[2048,512]{1,0:T(8,128)(2,1)}), bf16[256,512]{1,0:T(8,128)(2,1)}) %reduce-scatter.14.cloned.1.call-update) | async-done | bytes 262160 | tf_op jit(solution)/shard_map/reduce_scatter | solution.py:359
  1661.7 42.9 %reduce-scatter.20.cloned.1.call-done = bf16[512,256]{1,0:T(8,128)(2,1)} async-done(((bf16[512,2048]{1,0:T(8,128)(2,1)}), bf16[512,256]{1,0:T(8,128)(2,1)}) %reduce-scatter.20.cloned.1.call-update) | async-done | bytes 262160 | tf_op jit(solution)/shard_map/reduce_scatter | solution.py:380
  1706.5 43.1 %reduce-scatter.12.cloned.1.call-done = bf16[256,512]{1,0:T(8,128)(2,1)} async-done(((bf16[2048,512]{1,0:T(8,128)(2,1)}), bf16[256,512]{1,0:T(8,128)(2,1)}) %reduce-scatter.12.cloned.1.call-update) | async-done | bytes 262160 | tf_op jit(solution)/shard_map/reduce_scatter | solution.py:356
  1751.4 42.9 %reduce-scatter.16.cloned.1.call-done = bf16[256,512]{1,0:T(8,128)(2,1)} async-done(((bf16[2048,512]{1,0:T(8,128)(2,1)}), bf16[256,512]{1,0:T(8,128)(2,1)}) %reduce-scatter.16.cloned.1.call-update) | async-done | bytes 262160 | tf_op jit(solution)/shard_map/reduce_scatter | solution.py:365
  1796.2 42.7 %reduce-scatter.18.cloned.1.call-done = bf16[256,512]{1,0:T(8,128)(2,1)} async-done(((bf16[2048,512]{1,0:T(8,128)(2,1)}), bf16[256,512]{1,0:T(8,128)(2,1)}) %reduce-scatter.18.cloned.1.call-update) | async-done | bytes 262160 | tf_op jit(solution)/shard_map/reduce_scatter | solution.py:368
  1840.7 564.2 %all-reduce.18.cloned.1.call-done = (f32[1024,2048]{1,0:T(8,128)}, f32[1024,2048]{1,0:T(8,128)}) async-done(((f32[1024,2048]{1,0:T(8,128)}, f32[1024,2048]{1,0:T(8,128)}), (f32[1024,2048]{1,0:T(8,128)}, f32[1024,2048]{1,0:T(8,128)})) %all-reduce.18.cloned.1.call-update) | async-done | bytes 16777232 | tf_op jit(solution)/shard_map/psum | solution.py:156
  2404.8 5.8 fusion.127
  2410.7 14.2 all-reduce.9
  2425.4 18.2 fusion.132
  (1150 shorter events, 648.4 us)
Async XLA Ops:
  7.2 11.3 copy-start.32
  7.2 9.3 copy-start.37
  7.2 14.0 copy-start.28
  7.2 33.4 %all-gather.11.cloned.1.call-start = ((), (), s32[]{:S(2)}) async-start(), calls=%async_computation.9 | async-start | bytes 2359296 | tf_op jit(solution)/shard_map/all_gather | solution.py:185
  7.9 62.5 %all-gather.13.cloned.1.call-start = ((), (), s32[]{:S(2)}) async-start(), calls=%async_computation.10 | async-start | bytes 2359296 | tf_op jit(solution)/shard_map/all_gather | solution.py:186
  8.7 91.6 %all-gather.15.cloned.1.call-start = ((), (), s32[]{:S(2)}) async-start(), calls=%async_computation.11 | async-start | bytes 2359296 | tf_op jit(solution)/shard_map/all_gather | solution.py:184
  9.4 301.0 %all-gather.17.cloned.1.call-start = ((), (), s32[]{:S(2)}) async-start(), calls=%async_computation.12 | async-start | bytes 2359296 | tf_op jit(solution)/shard_map/all_gather | solution.py:187
  10.0 319.1 %all-gather.19.cloned.1.call-start = ((), (), s32[]{:S(2)}) async-start(), calls=%async_computation.13 | async-start | bytes 2359296 | tf_op jit(solution)/shard_map/all_gather | solution.py:188
  10.6 621.7 %all-reduce.14.cloned.1.call-start = ((), (), s32[]{:S(2)}) async-start(), calls=%async_computation.14 | async-start | bytes 16777216 | tf_op jit(solution)/shard_map/psum | solution.py:156
  16.5 83.8 %copy-start.30 = (f32[1024]{0:T(1024)}, f32[1024]{0:T(1024)S(1)}, u32[]{:S(2)}) copy-start(f32[1024]{0:T(1024)S(1)} %add_rsqrt_fusion.1) | copy-start | bytes 12292
  16.5 24.1 copy-start.34
  283.7 6.7 copy-start.6
  336.7 339.9 %all-gather.21.cloned.1.call-start = ((), (), s32[]{:S(2)}) async-start(), calls=%async_computation.15 | async-start | bytes 6488064 | tf_op jit(solution)/shard_map/all_gather | solution.py:191
  337.4 384.3 %all-gather.23.cloned.1.call-start = ((), (), s32[]{:S(2)}) async-start(), calls=%async_computation.16 | async-start | bytes 6488064 | tf_op jit(solution)/shard_map/all_gather | solution.py:192
  338.2 429.9 %all-gather.25.cloned.1.call-start = ((), (), s32[]{:S(2)}) async-start(), calls=%async_computation.17 | async-start | bytes 6488064 | tf_op jit(solution)/shard_map/all_gather | solution.py:193
  338.9 755.6 %all-reduce.16.cloned.1.call-start = ((), (), s32[]{:S(2)}) async-start(), calls=%async_computation.18 | async-start | bytes 16777216 | tf_op jit(solution)/shard_map/psum | solution.py:156
  340.2 301.2 %copy-start.27 = (f32[2048]{0:T(1024)S(1)}, f32[2048]{0:T(1024)}, u32[]{:S(2)}) copy-start(f32[2048]{0:T(1024)} %param.35) | copy-start | bytes 24580
  783.6 10.9 copy-start.46
  783.6 10.9 copy-start.45
  783.6 10.9 copy-start.39
  803.5 722.6 %reduce-scatter.28.cloned.1.call-start = ((), (), s32[]{:S(2)}) async-start(), calls=%async_computation.27 | async-start | bytes 36864
  1094.5 8.2 copy-start.2
  1094.5 9.4 copy-start.16
  1139.0 6.1 copy-start.15
  1154.2 6.1 copy-start.15
  1169.3 6.1 copy-start.15
  1184.5 6.1 copy-start.15
  1199.7 6.1 copy-start.15
  1245.1 6.1 copy-start.15
  1260.2 6.1 copy-start.15
  1275.4 6.1 copy-start.15
  1290.5 6.1 copy-start.15
  1305.6 6.1 copy-start.15
  1320.8 6.1 copy-start.15
  1335.9 6.1 copy-start.15
  1397.0 130.5 %reduce-scatter.22.cloned.1.call-start = ((), (), s32[]{:S(2)}) async-start(), calls=%async_computation.24 | async-start | bytes 6488064 | tf_op jit(solution)/shard_map/reduce_scatter | solution.py:389
  1408.2 144.6 %reduce-scatter.24.cloned.1.call-start = ((), (), s32[]{:S(2)}) async-start(), calls=%async_computation.25 | async-start | bytes 6488064 | tf_op jit(solution)/shard_map/reduce_scatter | solution.py:392
  1419.3 196.3 %reduce-scatter.26.cloned.1.call-start = ((), (), s32[]{:S(2)}) async-start(), calls=%async_computation.26 | async-start | bytes 6488064 | tf_op jit(solution)/shard_map/reduce_scatter | solution.py:395
  1429.9 230.1 %reduce-scatter.14.cloned.1.call-start = ((), (), s32[]{:S(2)}) async-start(), calls=%async_computation.20 | async-start | bytes 2359296 | tf_op jit(solution)/shard_map/reduce_scatter | solution.py:359
  1430.5 6.6 copy-start.42
  1437.1 267.5 %reduce-scatter.20.cloned.1.call-start = ((), (), s32[]{:S(2)}) async-start(), calls=%async_computation.23 | async-start | bytes 2359296 | tf_op jit(solution)/shard_map/reduce_scatter | solution.py:380
  1445.2 304.4 %reduce-scatter.12.cloned.1.call-start = ((), (), s32[]{:S(2)}) async-start(), calls=%async_computation.19 | async-start | bytes 2359296 | tf_op jit(solution)/shard_map/reduce_scatter | solution.py:356
  1461.5 332.9 %reduce-scatter.16.cloned.1.call-start = ((), (), s32[]{:S(2)}) async-start(), calls=%async_computation.21 | async-start | bytes 2359296 | tf_op jit(solution)/shard_map/reduce_scatter | solution.py:365
  1462.5 6.3 copy-start.25
  1462.5 6.4 copy-start.17
  1468.8 370.1 %reduce-scatter.18.cloned.1.call-start = ((), (), s32[]{:S(2)}) async-start(), calls=%async_computation.22 | async-start | bytes 2359296 | tf_op jit(solution)/shard_map/reduce_scatter | solution.py:368
  1474.9 929.9 %all-reduce.18.cloned.1.call-start = ((), (), s32[]{:S(2)}) async-start(), calls=%async_computation.28 | async-start | bytes 33554432 | tf_op jit(solution)/shard_map/psum | solution.py:156
  1475.1 11.8 copy-start.40
  (49 other events, 140.6 us)
Sparse Core Ops, SparseCore 0:
  9.9 30.6 all-gather.10
  42.5 27.9 all-gather.12
  72.4 27.8 all-gather.14
  102.0 27.8 all-gather.16
  131.7 28.2 all-gather.18
  336.8 295.4 all-reduce.13
  634.2 42.3 all-gather.20
  678.4 43.3 all-gather.22
  723.7 44.3 all-gather.24
  803.6 290.8 all-reduce.15
  1397.1 30.3 reduce-scatter.27
  1431.2 59.0 reduce-scatter.21
  1493.7 59.0 reduce-scatter.23
  1556.5 59.0 reduce-scatter.25
  1618.7 41.1 reduce-scatter.13
  1663.4 41.2 reduce-scatter.19
  1708.4 41.1 reduce-scatter.11
  1753.1 41.2 reduce-scatter.15
  1797.6 41.1 reduce-scatter.17
  1841.5 563.2 all-reduce.17
where the time goes:
time: 2460 us; the launch traced here: 2450 us
  waiting for transfers between devices  1490 us (61%)
  matrix products  420 us (17%)
  local copies, waits for them, and re-layouts  279 us (11%)
  other arithmetic  175 us (7%)
  loops' own time  36.2 us (1%)
  blocking collectives  33 us (1%)
    psum x3, waiting for transfers between devices, head_sums(): return lax.psum(values, 'tensor')  1040 us
    squeeze x128, local copies, waits for them, and re-layouts, recurrence(): lax.scan(stepper, carried, (split_heads(queries), split_heads(inputs_in),...  108 us
    dot_general x64, matrix products, block_step(): jnp.einsum('ghsk,ghsv->ghkv', moved_in, values, precision=HIGHEST)  79.7 us
    reduce_scatter x1, waiting for transfers between devices, local(): lax.psum_scatter(grad_down.astype(jnp.bfloat16), ('shard', 'context'), sc...  60.5 us
    dot_general x64, matrix products, block_step(): jnp.einsum('ghtk,ghsk->ghts', lifted, lowered, precision=HIGHEST)  49.8 us
    dot_general x48, matrix products, block_step(): jnp.einsum('ghtk,ghkv->ghtv', lifted * fresh_mask, carried, precision=HIG...  49.8 us
  transfers between devices with their start and end apart: 20, of which 16 were waited for; matrix products, arithmetic and copies ran while one was open for 21% of the time, Pallas kernels for 0%

commit v1 on v0

--- a/solution.py
+++ b/solution.py
@@ -152,8 +152,14 @@
     return (decay_one * decay_two, state_two + decay_two[..., None] * state_one)
 
 
-def head_sums(values):
-    return lax.psum(values, "tensor")
+def scatter_sum(values):
+    return lax.psum_scatter(
+        values.astype(jnp.bfloat16), "tensor", scatter_dimension=0, tiled=True
+    ).astype(jnp.float32)
+
+
+def gather_rows(values):
+    return lax.all_gather(values, "tensor", axis=0, tiled=True)
 
 
 def local(
@@ -239,16 +245,23 @@
     gated_rows = head_gated(mixed_rows, head_gain, gate_heads)
     gated_low = gated_rows.reshape(tokens, head_count * value_dim).astype(jnp.bfloat16)
     mix_part = jnp.dot(gated_low, out_full, preferred_element_type=jnp.float32)
-    residual = inputs + head_sums(mix_part)
+    part_rows = tokens // lax.axis_size("tensor")
+    place = lax.axis_index("tensor") * part_rows
+
+    def own_rows(values):
+        return lax.dynamic_slice_in_dim(values, place, part_rows, 0)
+
+    inputs_own = own_rows(hidden.reshape(tokens, model_width)).astype(jnp.float32)
+    residual = inputs_own + scatter_sum(mix_part)
     unit_two, inverse_two = rms_parts(residual)
-    normed_two = (unit_two * norm2_gain).astype(jnp.bfloat16)
+    normed_two = gather_rows((unit_two * norm2_gain).astype(jnp.bfloat16))
     gate_ffn = jnp.dot(normed_two, gate_full, preferred_element_type=jnp.float32)
     up_ffn = jnp.dot(normed_two, up_full, preferred_element_type=jnp.float32)
     sigma_gate = jax.nn.sigmoid(gate_ffn)
     active = gate_ffn * sigma_gate
     hidden_low = (active * up_ffn).astype(jnp.bfloat16)
     feed_part = jnp.dot(hidden_low, down_full, preferred_element_type=jnp.float32)
-    output_rows = (residual + head_sums(feed_part)).astype(jnp.bfloat16)
+    output_rows = gather_rows((residual + scatter_sum(feed_part)).astype(jnp.bfloat16))
     gate_full, up_full, down_full = (
         lax.all_gather(feed_shards[0], ("shard", "context"), axis=0, tiled=True),
         lax.all_gather(feed_shards[1], ("shard", "context"), axis=0, tiled=True),
@@ -276,14 +289,14 @@
     back_two = back_two + jnp.einsum(
         "tf,df->td", grad_up_low, up_full, preferred_element_type=jnp.float32
     )
-    grad_normed_two = head_sums(back_two)
-    cotangent_rows = grad_rows.astype(jnp.float32)
+    grad_normed_two = scatter_sum(back_two)
+    cotangent_rows = own_rows(grad_rows).astype(jnp.float32)
     grad_norm_two = jnp.sum(grad_normed_two * unit_two, axis=0)
     lifted_two = grad_normed_two * norm2_gain
     grad_residual = cotangent_rows + inverse_two * (
         lifted_two - unit_two * jnp.mean(lifted_two * unit_two, axis=-1, keepdims=True)
     )
-    grad_mix_low = grad_residual.astype(jnp.bfloat16)
+    grad_mix_low = gather_rows(grad_residual.astype(jnp.bfloat16))
     grad_out = jnp.einsum("tv,td->vd", gated_low, grad_mix_low, preferred_element_type=jnp.float32)
     grad_gated = jnp.einsum(
         "td,vd->tv", grad_mix_low, out_full, preferred_element_type=jnp.float32
@@ -343,13 +356,17 @@
     back_one = back_one + jnp.einsum(
         "tk,dk->td", grad_gatepre_low, gate_out_full, preferred_element_type=jnp.float32
     )
-    grad_normed_one, head_total = head_sums((back_one, grad_head_part))
+    grad_normed_one = scatter_sum(back_one)
+    unit_one, inverse_one = rms_parts(inputs_own)
     grad_norm_one = jnp.sum(grad_normed_one * unit_one, axis=0)
+    grad_norm_one, grad_norm_two, head_total = lax.psum(
+        (grad_norm_one, grad_norm_two, grad_head_part), "tensor"
+    )
     lifted_one = grad_normed_one * norm1_gain
     grad_inputs = grad_residual + inverse_one * (
         lifted_one - unit_one * jnp.mean(lifted_one * unit_one, axis=-1, keepdims=True)
     )
-    input_rows = grad_inputs.astype(jnp.bfloat16)
+    input_rows = gather_rows(grad_inputs.astype(jnp.bfloat16))
     block_out = output_rows.reshape(sequences, span_len, model_width)
     input_grad = input_rows.reshape(sequences, span_len, model_width)
     shares = (

time: 2460 us -> 2020 us (0.82)
  waiting for transfers between devices: 1490 us -> 1020 us
    psum x3 -> x0, waiting for transfers between devices: 1040 us -> none  [head_sums(): return lax.psum(values, 'tensor')]
    reduce_scatter x0 -> x4, waiting for transfers between devices: none -> 230 us  [scatter_sum(): lax.psum_scatter(values.astype(jnp.bfloat16), 'tensor', scatter_dimension...]
    all_gather x0 -> x4, waiting for transfers between devices: none -> 212 us  [gather_rows(): return lax.all_gather(values, 'tensor', axis=0, tiled=True)]
    reduce_scatter x1, waiting for transfers between devices: 0.01 us -> 55.3 us  [local(): lax.psum_scatter(grad_gate.astype(jnp.bfloat16), ('shard', 'context'), sc...]
    reduce_scatter x1, waiting for transfers between devices: 23 us -> 60.5 us  [local(): lax.psum_scatter(grad_up.astype(jnp.bfloat16), ('shard', 'context'), scat...]
    unnamed x21 -> x26, waiting for transfers between devices: 5.38 us -> 38.7 us
  transfers between devices with their start and end apart: 20 -> 25, of which waited for: 16 -> 21; matrix products, arithmetic and copies ran while one was open for 21% -> 26% of each run, Pallas kernels for 0% -> 0%
where the time goes in v1:
time: 2020 us; the launch traced here: 2010 us
  waiting for transfers between devices  1020 us (50%)
  matrix products  418 us (21%)
  local copies, waits for them, and re-layouts  298 us (15%)
  other arithmetic  171 us (8%)
  blocking collectives  43 us (2%)
  loops' own time  35.4 us (2%)
    reduce_scatter x4, waiting for transfers between devices, scatter_sum(): lax.psum_scatter(values.astype(jnp.bfloat16), 'tensor', scatter_dimension...  230 us
    all_gather x4, waiting for transfers between devices, gather_rows(): return lax.all_gather(values, 'tensor', axis=0, tiled=True)  212 us
    squeeze x128, local copies, waits for them, and re-layouts, recurrence(): lax.scan(stepper, carried, (split_heads(queries), split_heads(inputs_in),...  118 us
    dot_general x64, matrix products, block_step(): jnp.einsum('ghsk,ghsv->ghkv', moved_in, values, precision=HIGHEST)  79.7 us
    reduce_scatter x1, waiting for transfers between devices, local(): lax.psum_scatter(grad_up.astype(jnp.bfloat16), ('shard', 'context'), scat...  60.5 us
    reduce_scatter x1, waiting for transfers between devices, local(): lax.psum_scatter(grad_down.astype(jnp.bfloat16), ('shard', 'context'), sc...  60.1 us
    reduce_scatter x1, waiting for transfers between devices, local(): lax.psum_scatter(grad_gate.astype(jnp.bfloat16), ('shard', 'context'), sc...  55.3 us
    dot_general x48, matrix products, block_step(): jnp.einsum('ghtk,ghkv->ghtv', lifted * fresh_mask, carried, precision=HIG...  50 us
  transfers between devices with their start and end apart: 25, of which 21 were waited for; matrix products, arithmetic and copies ran while one was open for 26% of the time, Pallas kernels for 0%

profile of v1, /device:TPU:0, one launch (start us, length us, event | category | flops | bytes accessed | tf_op | source)
XLA Modules:
  0.0 2006.0 jit_solution(5281937722514718664)
XLA Ops:
  31.8 8.8 all-gather.15.cloned.1.call-done
  40.5 8.1 broadcast_multiply_fusion.2
  62.7 7.7 all-gather.17.cloned.1.call-done
  74.4 25.9 %all-gather.19.cloned.1.call-done = bf16[2048,512]{1,0:T(8,128)(2,1)} async-done(((bf16[256,512]{1,0:T(8,128)(2,1)}), bf16[2048,512]{1,0:T(8,128)(2,1)}) %all-gather.19.cloned.1.call-update) | async-done | bytes 2097168 | tf_op jit(solution)/shard_map/all_gather | solution.py:190
  100.2 7.6 fusion.160
  122.5 161.6 %while.82 = (s32[]{:T(128)}, f32[1,4,128,128]{3,2,1,0:T(8,128)S(1)}, f32[16,1,4,64,128]{4,3,0,2,1:T(8,128)}, f32[16,1,4,64,128]{4,3,2,1,0:T(8,128)}, f32[16,1,64...) while((s32[]{:T(128)}, ...), condition=%wide.region_4.5_spmd.clone, body=%wide.region_1.4_spmd.clone.sunk | while | flops 153752320 | bytes 3215802 | solution.py:108
  298.3 10.4 multiply_bitcast_fusion.1
  328.8 6.4 convolution_convert_fusion.4
  336.0 80.7 %reduce-scatter.16.cloned.1.call-done = bf16[256,2048]{1,0:T(8,128)(2,1)} async-done(((bf16[1024,2048]{1,0:T(8,128)(2,1)}), bf16[256,2048]{1,0:T(8,128)(2,1)}) %reduce-scatter.16.cloned.1.call-update) | async-done | bytes 1048592 | tf_op jit(solution)/shard_map/reduce_scatter | solution.py:156
  423.2 39.4 %all-gather.27.cloned.1.call-done = bf16[2048,1408]{1,0:T(8,128)(2,1)} async-done(((bf16[256,1408]{1,0:T(8,128)(2,1)}), bf16[2048,1408]{1,0:T(8,128)(2,1)}) %all-gather.27.cloned.1.call-update) | async-done | bytes 5767184 | tf_op jit(solution)/shard_map/all_gather | solution.py:197
  462.6 83.0 %all-gather.25.cloned.1.call-done = bf16[1024,2048]{1,0:T(8,128)(2,1)} async-done(((bf16[256,2048]{1,0:T(8,128)(2,1)}), bf16[1024,2048]{1,0:T(8,128)(2,1)}) %all-gather.25.cloned.1.call-update) | async-done | bytes 4194320 | tf_op jit(solution)/shard_map/all_gather | solution.py:162
  545.6 11.7 fusion.185
  557.4 32.2 %all-gather.29.cloned.1.call-done = bf16[2048,1408]{1,0:T(8,128)(2,1)} async-done(((bf16[256,1408]{1,0:T(8,128)(2,1)}), bf16[2048,1408]{1,0:T(8,128)(2,1)}) %all-gather.29.cloned.1.call-update) | async-done | bytes 5767184 | tf_op jit(solution)/shard_map/all_gather | solution.py:198
  589.6 11.7 fusion.186
  601.3 34.6 %all-gather.31.cloned.1.call-done = bf16[1408,2048]{1,0:T(8,128)(2,1)} async-done(((bf16[1408,256]{1,0:T(8,128)(2,1)}), bf16[1408,2048]{1,0:T(8,128)(2,1)}) %all-gather.31.cloned.1.call-update) | async-done | bytes 5767184 | tf_op jit(solution)/shard_map/all_gather | solution.py:199
  635.8 15.6 multiply_convert_fusion
  651.4 10.9 fusion.187
  662.3 8.2 add_convert_fusion.1
  672.0 75.5 %reduce-scatter.20.cloned.1.call-done = bf16[256,2048]{1,0:T(8,128)(2,1)} async-done(((bf16[1024,2048]{1,0:T(8,128)(2,1)}), bf16[256,2048]{1,0:T(8,128)(2,1)}) %reduce-scatter.20.cloned.1.call-update) | async-done | bytes 1048592 | tf_op jit(solution)/shard_map/reduce_scatter | solution.py:156
  754.5 147.3 %while.80 = (s32[]{:T(128)}, f32[1,4,128,128]{3,2,1,0:T(8,128)S(1)}, f32[16,1,4,128,128]{4,3,2,1,0:T(8,128)}, f32[16,1,4,64,128]{4,3,2,1,0:T(8,128)}, f32[16,1,6...) while((s32[]{:T(128)}, ...), condition=%wide.region_25.26_spmd, body=%wide.region_22.25_spmd.sunk | while | flops 52662852 | bytes 1983675 | solution.py:108
  929.1 232.7 %while.81 = (s32[]{:T(128)}, f32[1,4,128,128]{2,3,1,0:T(8,128)S(1)}, f32[16,1,4,64,128]{4,3,2,1,0:T(8,128)}, f32[16,1,4,64,128]{4,3,2,1,0:T(8,128)}, bf16[16,1,4...) while((s32[]{:T(128)}, ...), condition=%wide.region_32.33_spmd, body=%wide.region_26.32_spmd.sunk | while | flops 333272256 | bytes 10578175 | solution.py:108
  1194.6 5.7 fusion.190
  1200.4 5.8 fusion.189
  1206.2 5.6 fusion.164
  1211.8 12.8 add_convert_fusion
  1224.6 11.1 convolution_convert_fusion.3
  1235.8 11.1 convolution_convert_fusion.2
  1246.9 11.0 convolution_convert_fusion.1
  1258.0 10.5 convolution_convert_fusion
  1269.7 6.4 convolution_convert_fusion.6
  1277.4 5.9 convolution_convert_fusion.5
  1284.5 6.6 convolution_convert_fusion.7
  1292.3 5.9 fusion.134
  1298.5 5.9 fusion.131
  1307.6 74.0 %reduce-scatter.18.cloned.1.call-done = bf16[256,2048]{1,0:T(8,128)(2,1)} async-done(((bf16[1024,2048]{1,0:T(8,128)(2,1)}), bf16[256,2048]{1,0:T(8,128)(2,1)}) %reduce-scatter.18.cloned.1.call-update) | async-done | bytes 1048592 | tf_op jit(solution)/shard_map/reduce_scatter | solution.py:156
  1389.1 55.3 %reduce-scatter.34.cloned.1.call-done = bf16[256,1408]{1,0:T(8,128)(2,1)} async-done(((bf16[2048,1408]{1,0:T(8,128)(2,1)}), bf16[256,1408]{1,0:T(8,128)(2,1)}) %reduce-scatter.34.cloned.1.call-update) | async-done | bytes 720912 | tf_op jit(solution)/shard_map/reduce_scatter | solution.py:406
  1446.7 60.5 %reduce-scatter.36.cloned.1.call-done = bf16[256,1408]{1,0:T(8,128)(2,1)} async-done(((bf16[2048,1408]{1,0:T(8,128)(2,1)}), bf16[256,1408]{1,0:T(8,128)(2,1)}) %reduce-scatter.36.cloned.1.call-update) | async-done | bytes 720912 | tf_op jit(solution)/shard_map/reduce_scatter | solution.py:409
  1509.5 60.1 %reduce-scatter.38.cloned.1.call-done = bf16[1408,256]{1,0:T(8,128)(2,1)} async-done(((bf16[1408,2048]{1,0:T(8,128)(2,1)}), bf16[1408,256]{1,0:T(8,128)(2,1)}) %reduce-scatter.38.cloned.1.call-update) | async-done | bytes 720912 | tf_op jit(solution)/shard_map/reduce_scatter | solution.py:412
  1571.8 32.7 %reduce-scatter.40.cloned.1.call-done = bf16[16,4]{1,0:T(8,128)(2,1)} async-done(((bf16[128,4]{1,0:T(8,128)(2,1)}), bf16[16,4]{1,0:T(8,128)(2,1)}) %reduce-scatter.40.cloned.1.call-update) | async-done | bytes 144
  1605.8 43.2 %reduce-scatter.26.cloned.1.call-done = bf16[256,512]{1,0:T(8,128)(2,1)} async-done(((bf16[2048,512]{1,0:T(8,128)(2,1)}), bf16[256,512]{1,0:T(8,128)(2,1)}) %reduce-scatter.26.cloned.1.call-update) | async-done | bytes 262160 | tf_op jit(solution)/shard_map/reduce_scatter | solution.py:376
  1650.8 42.9 %reduce-scatter.32.cloned.1.call-done = bf16[512,256]{1,0:T(8,128)(2,1)} async-done(((bf16[512,2048]{1,0:T(8,128)(2,1)}), bf16[512,256]{1,0:T(8,128)(2,1)}) %reduce-scatter.32.cloned.1.call-update) | async-done | bytes 262160 | tf_op jit(solution)/shard_map/reduce_scatter | solution.py:397
  1695.5 42.8 %reduce-scatter.24.cloned.1.call-done = bf16[256,512]{1,0:T(8,128)(2,1)} async-done(((bf16[2048,512]{1,0:T(8,128)(2,1)}), bf16[256,512]{1,0:T(8,128)(2,1)}) %reduce-scatter.24.cloned.1.call-update) | async-done | bytes 262160 | tf_op jit(solution)/shard_map/reduce_scatter | solution.py:373
  1740.1 43.1 %reduce-scatter.28.cloned.1.call-done = bf16[256,512]{1,0:T(8,128)(2,1)} async-done(((bf16[2048,512]{1,0:T(8,128)(2,1)}), bf16[256,512]{1,0:T(8,128)(2,1)}) %reduce-scatter.28.cloned.1.call-update) | async-done | bytes 262160 | tf_op jit(solution)/shard_map/reduce_scatter | solution.py:382
  1785.0 42.7 %reduce-scatter.30.cloned.1.call-done = bf16[256,512]{1,0:T(8,128)(2,1)} async-done(((bf16[2048,512]{1,0:T(8,128)(2,1)}), bf16[256,512]{1,0:T(8,128)(2,1)}) %reduce-scatter.30.cloned.1.call-update) | async-done | bytes 262160 | tf_op jit(solution)/shard_map/reduce_scatter | solution.py:385
  1829.5 19.6 all-reduce.7
  1849.1 13.2 all-reduce.9
  1863.5 47.4 %all-gather.33.cloned.1.call-done = bf16[1024,2048]{1,0:T(8,128)(2,1)} async-done(((bf16[256,2048]{1,0:T(8,128)(2,1)}), bf16[1024,2048]{1,0:T(8,128)(2,1)}) %all-gather.33.cloned.1.call-update) | async-done | bytes 4194320 | tf_op jit(solution)/shard_map/all_gather | solution.py:162
  1910.9 81.3 %all-gather.37.cloned.1.call-done = bf16[1024,2048]{1,0:T(8,128)(2,1)} async-done(((bf16[256,2048]{1,0:T(8,128)(2,1)}), bf16[1024,2048]{1,0:T(8,128)(2,1)}) %all-gather.37.cloned.1.call-update) | async-done | bytes 4194320 | tf_op jit(solution)/shard_map/all_gather | solution.py:162
  (1160 shorter events, 711.8 us)
Async XLA Ops:
  7.2 33.4 %all-gather.15.cloned.1.call-start = ((), (), s32[]{:S(2)}) async-start(), calls=%async_computation.13 | async-start | bytes 2359296 | tf_op jit(solution)/shard_map/all_gather | solution.py:191
  7.9 62.5 %all-gather.17.cloned.1.call-start = ((), (), s32[]{:S(2)}) async-start(), calls=%async_computation.14 | async-start | bytes 2359296 | tf_op jit(solution)/shard_map/all_gather | solution.py:192
  8.7 91.6 %all-gather.19.cloned.1.call-start = ((), (), s32[]{:S(2)}) async-start(), calls=%async_computation.15 | async-start | bytes 2359296 | tf_op jit(solution)/shard_map/all_gather | solution.py:190
  9.4 301.3 %all-gather.21.cloned.1.call-start = ((), (), s32[]{:S(2)}) async-start(), calls=%async_computation.16 | async-start | bytes 2359296 | tf_op jit(solution)/shard_map/all_gather | solution.py:193
  10.0 318.8 %all-gather.23.cloned.1.call-start = ((), (), s32[]{:S(2)}) async-start(), calls=%async_computation.17 | async-start | bytes 2359296 | tf_op jit(solution)/shard_map/all_gather | solution.py:194
  10.6 406.1 %reduce-scatter.16.cloned.1.call-start = ((), (), s32[]{:S(2)}) async-start(), calls=%async_computation.18 | async-start | bytes 5242880 | tf_op jit(solution)/shard_map/reduce_scatter | solution.py:156
  13.3 7.9 copy-start.31
  16.5 83.7 %copy-start.38 = (f32[1024]{0:T(1024)}, f32[1024]{0:T(1024)S(1)}, u32[]{:S(2)}) copy-start(f32[1024]{0:T(1024)S(1)} %add_rsqrt_fusion) | copy-start | bytes 12292
  16.5 24.0 %copy-start.42 = (f32[512]{0:T(512)}, f32[512]{0:T(512)S(1)}, u32[]{:S(2)}) copy-start(f32[512]{0:T(512)S(1)} %subtract_bitcast_fusion) | copy-start | bytes 6148
  328.8 6.4 copy-start.51
  335.2 83.6 %copy-start.29 = (f32[2048]{0:T(1024)S(1)}, f32[2048]{0:T(1024)}, u32[]{:S(2)}) copy-start(f32[2048]{0:T(1024)} %param.35) | copy-start | bytes 24580
  335.2 127.4 %all-gather.27.cloned.1.call-start = ((), (), s32[]{:S(2)}) async-start(), calls=%async_computation.20 | async-start | bytes 6488064 | tf_op jit(solution)/shard_map/all_gather | solution.py:197
  335.9 209.7 %all-gather.25.cloned.1.call-start = ((), (), s32[]{:S(2)}) async-start(), calls=%async_computation.19 | async-start | bytes 5242880 | tf_op jit(solution)/shard_map/all_gather | solution.py:162
  418.8 332.0 %copy-start.35 = (f32[256]{0:T(256)}, f32[256]{0:T(256)S(1)}, u32[]{:S(2)}) copy-start(f32[256]{0:T(256)S(1)} %add_rsqrt_fusion.2) | copy-start | bytes 3076
  421.4 168.2 %all-gather.29.cloned.1.call-start = ((), (), s32[]{:S(2)}) async-start(), calls=%async_computation.21 | async-start | bytes 6488064 | tf_op jit(solution)/shard_map/all_gather | solution.py:198
  422.1 213.7 %all-gather.31.cloned.1.call-start = ((), (), s32[]{:S(2)}) async-start(), calls=%async_computation.22 | async-start | bytes 6488064 | tf_op jit(solution)/shard_map/all_gather | solution.py:199
  422.7 324.8 %reduce-scatter.20.cloned.1.call-start = ((), (), s32[]{:S(2)}) async-start(), calls=%async_computation.25 | async-start | bytes 5242880 | tf_op jit(solution)/shard_map/reduce_scatter | solution.py:156
  651.4 10.9 copy-start.56
  651.4 10.9 copy-start.57
  651.4 10.9 copy-start.48
  670.6 233.7 %all-gather.35.cloned.1.call-start = ((), (), s32[]{:S(2)}) async-start(), calls=%async_computation.26 | async-start | bytes 5242880 | tf_op jit(solution)/shard_map/all_gather | solution.py:162
  754.4 550.6 %reduce-scatter.22.cloned.1.call-start = ((), (), s32[]{:S(2)}) async-start(), calls=%async_computation.27 | async-start | bytes 5242880 | tf_op jit(solution)/shard_map/reduce_scatter | solution.py:156
  904.3 5.4 copy-start.9
  1189.8 16.4 copy-start.25
  1192.6 7.8 copy-start.21
  1194.0 6.3 copy-start.23
  1194.6 5.8 copy-start.50
  1200.4 5.8 copy-start.19
  1206.1 5.6 copy-start.7
  1206.1 5.6 copy-start.13
  1224.6 157.0 %reduce-scatter.18.cloned.1.call-start = ((), (), s32[]{:S(2)}) async-start(), calls=%async_computation.23 | async-start | bytes 5242880 | tf_op jit(solution)/shard_map/reduce_scatter | solution.py:156
  1235.7 208.7 %reduce-scatter.34.cloned.1.call-start = ((), (), s32[]{:S(2)}) async-start(), calls=%async_computation.34 | async-start | bytes 6488064 | tf_op jit(solution)/shard_map/reduce_scatter | solution.py:406
  1246.8 260.3 %reduce-scatter.36.cloned.1.call-start = ((), (), s32[]{:S(2)}) async-start(), calls=%async_computation.35 | async-start | bytes 6488064 | tf_op jit(solution)/shard_map/reduce_scatter | solution.py:409
  1257.9 311.6 %reduce-scatter.38.cloned.1.call-start = ((), (), s32[]{:S(2)}) async-start(), calls=%async_computation.36 | async-start | bytes 6488064 | tf_op jit(solution)/shard_map/reduce_scatter | solution.py:412
  1268.5 336.0 %reduce-scatter.40.cloned.1.call-start = ((), (), s32[]{:S(2)}) async-start(), calls=%async_computation.37 | async-start | bytes 36864
  1269.3 379.7 %reduce-scatter.26.cloned.1.call-start = ((), (), s32[]{:S(2)}) async-start(), calls=%async_computation.30 | async-start | bytes 2359296 | tf_op jit(solution)/shard_map/reduce_scatter | solution.py:376
  1276.2 417.6 %reduce-scatter.32.cloned.1.call-start = ((), (), s32[]{:S(2)}) async-start(), calls=%async_computation.33 | async-start | bytes 2359296 | tf_op jit(solution)/shard_map/reduce_scatter | solution.py:397
  1283.3 455.0 %reduce-scatter.24.cloned.1.call-start = ((), (), s32[]{:S(2)}) async-start(), calls=%async_computation.29 | async-start | bytes 2359296 | tf_op jit(solution)/shard_map/reduce_scatter | solution.py:373
  1291.1 492.1 %reduce-scatter.28.cloned.1.call-start = ((), (), s32[]{:S(2)}) async-start(), calls=%async_computation.31 | async-start | bytes 2359296 | tf_op jit(solution)/shard_map/reduce_scatter | solution.py:382
  1298.2 529.5 %reduce-scatter.30.cloned.1.call-start = ((), (), s32[]{:S(2)}) async-start(), calls=%async_computation.32 | async-start | bytes 2359296 | tf_op jit(solution)/shard_map/reduce_scatter | solution.py:385
  1304.4 77.1 %copy-start.5 = (bf16[256,2048]{1,0:T(8,128)(2,1)S(1)}, bf16[256,2048]{1,0:T(8,128)(2,1)}, u32[]{:S(2)}) copy-start(bf16[256,2048]{1,0:T(8,128)(2,1)} %reduce-scatter.20.cloned.1.call-done) | copy-start | bytes 3145732
  1304.4 77.1 %copy-start.30 = (f32[2048]{0:T(1024)S(1)}, f32[2048]{0:T(1024)}, u32[]{:S(2)}) copy-start(f32[2048]{0:T(1024)} %param.35) | copy-start | bytes 24580
  1304.4 77.1 %copy-start.36 = (f32[256]{0:T(256)S(1)}, f32[256]{0:T(256)}, u32[]{:S(2)}) copy-start(f32[256]{0:T(256)} %copy-done.35) | copy-start | bytes 3076
  1304.4 77.1 %copy-start.41 = (f32[256]{0:T(256)S(1)}, f32[256]{0:T(256)}, u32[]{:S(2)}) copy-start(f32[256]{0:T(256)} %copy-done.40) | copy-start | bytes 3076
  1304.4 606.5 %all-gather.33.cloned.1.call-start = ((), (), s32[]{:S(2)}) async-start(), calls=%async_computation.24 | async-start | bytes 5242880 | tf_op jit(solution)/shard_map/all_gather | solution.py:162
  1305.1 76.5 %copy-start.17 = (bf16[256,2048]{1,0:T(8,128)(2,1)S(1)}, bf16[256,2048]{1,0:T(8,128)(2,1)}, u32[]{:S(2)}) copy-start(bf16[256,2048]{1,0:T(8,128)(2,1)} %reduce-scatter.22.cloned.1.call-done) | copy-start | bytes 3145732
  1386.5 605.8 %all-gather.37.cloned.1.call-start = ((), (), s32[]{:S(2)}) async-start(), calls=%async_computation.28 | async-start | bytes 5242880 | tf_op jit(solution)/shard_map/all_gather | solution.py:162
  1571.8 257.7 %copy-start.34 = (f32[2048]{0:T(1024)S(1)}, f32[2048]{0:T(1024)}, u32[]{:S(2)}) copy-start(f32[2048]{0:T(1024)} %get-tuple-element.784) | copy-start | bytes 24580
  (50 other events, 124.6 us)
Sparse Core Ops, SparseCore 0:
  9.9 30.5 all-gather.14
  42.4 27.9 all-gather.16
  72.3 27.8 all-gather.18
  102.0 27.8 all-gather.20
  131.6 28.2 all-gather.22
  335.3 81.3 reduce-scatter.15
  418.7 43.8 all-gather.26
  464.8 80.7 all-gather.24
  547.7 41.8 all-gather.28
  591.4 44.3 all-gather.30
  670.7 76.7 reduce-scatter.19
  754.6 81.2 all-gather.34
  1224.7 77.2 reduce-scatter.21
  1304.2 77.2 reduce-scatter.17
  1384.8 59.5 reduce-scatter.33
  1448.1 59.0 reduce-scatter.35
  1510.4 59.0 reduce-scatter.37
  1573.2 31.2 reduce-scatter.39
  1607.8 41.1 reduce-scatter.25
  1652.5 41.2 reduce-scatter.31
  1697.0 41.1 reduce-scatter.23
  1741.9 41.2 reduce-scatter.27
  1786.5 41.1 reduce-scatter.29
  1829.8 81.0 all-gather.32
  1913.1 79.0 all-gather.36

commit v2 on v1

v2 whole, which is shorter than its diff:
```python
from functools import partial

import jax
import jax.numpy as jnp
from jax import lax
from jax.experimental import pallas as pl
from jax.experimental.pallas import tpu as pltpu
from jax.sharding import PartitionSpec as P

EPSILON = 1e-05


BLOCK = 128
F32 = jnp.float32
BF16 = jnp.bfloat16


def mm(a, b, dims):
    return lax.dot_general(a, b, (dims, ((), ())), preferred_element_type=F32)


def mm_nn(a, b):
    return mm(a, b, ((1,), (0,)))


def mm_nt(a, b):
    return mm(a, b, ((1,), (1,)))


def mm_tn(a, b):
    return mm(a, b, ((0,), (0,)))


def split_sum(tri, values):
    high = values.astype(BF16)
    low = (values - high.astype(F32)).astype(BF16)
    return mm_nn(tri, high) + mm_nn(tri, low)


def block_masks(counts, flags_row):
    rows = counts.shape[0]
    row_ids = lax.broadcasted_iota(jnp.int32, (rows, rows), 0)
    col_ids = lax.broadcasted_iota(jnp.int32, (rows, rows), 1)
    linked = jnp.logical_and(counts == flags_row[0:1], row_ids >= col_ids)
    fresh = (counts == flags_row[1:2, 0:1]).astype(F32)
    tail = (counts == flags_row[2:3, 0:1]).astype(F32)
    closing = (flags_row[1:2, 0:1] == flags_row[2:3, 0:1]).astype(F32)
    return row_ids, col_ids, linked, fresh, tail, closing


def mixer_forward_kernel(
    head_count,
    key_scale,
    pre_ref,
    open_ref,
    count_ref,
    keep_ref,
    flags_ref,
    mixed_ref,
    lead_ref,
    start_ref,
    run_ref,
    end_ref,
    total_ref,
    state_scr,
    run_scr,
):
    step = pl.program_id(0)
    width = open_ref.shape[1]
    lanes = width // head_count

    @pl.when(step == 0)
    def _():
        state_scr[...] = jnp.zeros_like(state_scr)
        run_scr[...] = jnp.zeros_like(run_scr)

    counts, keep = count_ref[...], keep_ref[...]
    row_ids, col_ids, linked, fresh, tail, closing = block_masks(counts, flags_ref[0])
    tri = (row_ids >= col_ids).astype(BF16)
    query_pre = pre_ref[:, :width]
    values = pre_ref[:, 2 * width : 3 * width].astype(BF16)
    keys = open_ref[...] * jax.nn.sigmoid(-pre_ref[:, width : 2 * width])
    cum = split_sum(tri, jnp.log1p(-keys))
    rows = cum.shape[0]
    ending = cum[rows - 1 : rows, :]
    lifted = query_pre * jax.nn.sigmoid(query_pre) * jnp.exp(cum)
    lowered = (keys * jnp.exp(-cum) * keep).astype(BF16)
    moved = (keys * jnp.exp(ending - cum) * (keep * tail)).astype(BF16)
    run = run_scr[...]
    lead_ref[...] = (lifted * jnp.exp(run) * (counts == 0).astype(F32)).astype(BF16)
    run_ref[0] = run
    run_scr[...] = run + ending
    total_ref[...] = run + ending
    fresh_lifted = (lifted * fresh).astype(BF16)
    lifted = lifted.astype(BF16)
    end_decay = jnp.exp(ending) * closing
    for head in range(head_count):
        part = slice(head * lanes, (head + 1) * lanes)
        state = state_scr[head]
        start_ref[0, head] = state
        scores = jnp.where(linked, mm_nt(lifted[:, part], lowered[:, part]), 0.0)
        results = mm_nn(scores.astype(BF16), values[:, part])
        results = results + mm_nt(fresh_lifted[:, part], state.astype(BF16))
        mixed_ref[:, part] = results * (key_scale * keep)
        state = state * end_decay[:, part] + mm_tn(values[:, part], moved[:, part])
        state_scr[head] = state
        end_ref[head] = state


def mixer_forward(pre, open_part, counts, keep, flags, head_count, key_scale):
    tokens, all_width = pre.shape
    width = open_part.shape[1]
    lanes = width // head_count
    blocks = tokens // BLOCK
    return pl.pallas_call(
        partial(mixer_forward_kernel, head_count, key_scale),
        grid=(blocks,),
        in_specs=[
            pl.BlockSpec((BLOCK, all_width), lambda i: (i, 0)),
            pl.BlockSpec((1, width), lambda i: (0, 0)),
            pl.BlockSpec((BLOCK, 1), lambda i: (i, 0)),
            pl.BlockSpec((BLOCK, 1), lambda i: (i, 0)),
            pl.BlockSpec((1, 8, BLOCK), lambda i: (i, 0, 0)),
        ],
        out_specs=[
            pl.BlockSpec((BLOCK, width), lambda i: (i, 0)),
            pl.BlockSpec((BLOCK, width), lambda i: (i, 0)),
            pl.BlockSpec((1, head_count, lanes, lanes), lambda i: (i, 0, 0, 0)),
            pl.BlockSpec((1, 1, width), lambda i: (i, 0, 0)),
            pl.BlockSpec((head_count, lanes, lanes), lambda i: (0, 0, 0)),
            pl.BlockSpec((1, width), lambda i: (0, 0)),
        ],
        out_shape=[
            jax.ShapeDtypeStruct((tokens, width), F32),
            jax.ShapeDtypeStruct((tokens, width), BF16),
            jax.ShapeDtypeStruct((blocks, head_count, lanes, lanes), F32),
            jax.ShapeDtypeStruct((blocks, 1, width), F32),
            jax.ShapeDtypeStruct((head_count, lanes, lanes), F32),
            jax.ShapeDtypeStruct((1, width), F32),
        ],
        scratch_shapes=[
            pltpu.VMEM((head_count, lanes, lanes), F32),
            pltpu.VMEM((1, width), F32),
        ],
        compiler_params=pltpu.CompilerParams(
            dimension_semantics=("arbitrary",), vmem_limit_bytes=40 << 20
        ),
        cost_estimate=pl.CostEstimate(
            flops=tokens * width * BLOCK * 12,
            bytes_accessed=tokens * width * 30,
            transcendentals=tokens * width * 7,
        ),
        name="mixer_forward",
    )(pre, open_part, counts, keep, flags)


def gate_forward_kernel(
    head_count,
    key_scale,
    local_ref,
    lead_ref,
    carry_ref,
    gate_ref,
    gain_ref,
    keep_ref,
    mixed_ref,
    gated_ref,
):
    lanes = gain_ref.shape[1]
    for head in range(head_count):
        part = slice(head * lanes, (head + 1) * lanes)
        carried = mm_nt(lead_ref[:, part], carry_ref[head])
        mixed = local_ref[:, part] + carried * (key_scale * keep_ref[...])
        mixed_ref[:, part] = mixed
        inverse = lax.rsqrt(jnp.mean(mixed * mixed, axis=-1, keepdims=True) + EPSILON)
        gate = gate_ref[:, part]
        gated = mixed * inverse * gain_ref[...] * (gate * jax.nn.sigmoid(gate))
        gated_ref[:, part] = gated.astype(BF16)


def gate_forward(local, lead, carry, pre, gain, keep, key_scale):
    tokens, width = local.shape
    head_count, lanes = carry.shape[0], carry.shape[2]
    rows = 2 * BLOCK
    return pl.pallas_call(
        partial(gate_forward_kernel, head_count, key_scale),
        grid=(tokens // rows,),
        in_specs=[
            pl.BlockSpec((rows, width), lambda i: (i, 0)),
            pl.BlockSpec((rows, width), lambda i: (i, 0)),
            pl.BlockSpec((head_count, lanes, lanes), lambda i: (0, 0, 0)),
            pl.BlockSpec((rows, width), lambda i: (i, 3)),
            pl.BlockSpec((1, lanes), lambda i: (0, 0)),
            pl.BlockSpec((rows, 1), lambda i: (i, 0)),
        ],
        out_specs=[
            pl.BlockSpec((rows, width), lambda i: (i, 0)),
            pl.BlockSpec((rows, width), lambda i: (i, 0)),
        ],
        out_shape=[
            jax.ShapeDtypeStruct((tokens, width), F32),
            jax.ShapeDtypeStruct((tokens, width), BF16),
        ],
        compiler_params=pltpu.CompilerParams(
            dimension_semantics=("arbitrary",), vmem_limit_bytes=40 << 20
        ),
        cost_estimate=pl.CostEstimate(
            flops=tokens * width * 300,
            bytes_accessed=tokens * width * 16,
            transcendentals=tokens * width,
        ),
        name="gate_forward",
    )(local, lead, carry, pre, gain, keep)


def gate_backward_kernel(
    head_count,
    key_scale,
    grad_ref,
    mixed_ref,
    lead_ref,
    gate_ref,
    gain_ref,
    keep_ref,
    grad_mixed_ref,
    grad_gate_ref,
    grad_gain_ref,
    back_ref,
):
    lanes = gain_ref.shape[1]

    @pl.when(pl.program_id(0) == 0)
    def _():
        grad_gain_ref[...] = jnp.zeros_like(grad_gain_ref)
        back_ref[...] = jnp.zeros_like(back_ref)

    gain = gain_ref[...]
    total = jnp.zeros_like(gain)
    for head in range(head_count):
        part = slice(head * lanes, (head + 1) * lanes)
        mixed, gate, grad = mixed_ref[:, part], gate_ref[:, part], grad_ref[:, part]
        inverse = lax.rsqrt(jnp.mean(mixed * mixed, axis=-1, keepdims=True) + EPSILON)
        unit = mixed * inverse
        sigma = jax.nn.sigmoid(gate)
        scaled = grad * unit
        total = total + jnp.sum(scaled * (gate * sigma), axis=0, keepdims=True)
        grad_gate = scaled * gain * sigma * (1.0 + gate * (1.0 - sigma))
        grad_gate_ref[:, part] = grad_gate.astype(BF16)
        lifted = grad * gain * (gate * sigma)
        mean = jnp.mean(lifted * unit, axis=-1, keepdims=True)
        grad_mixed = inverse * (lifted - unit * mean) * (key_scale * keep_ref[...])
        grad_mixed = grad_mixed.astype(BF16)
        grad_mixed_ref[:, part] = grad_mixed
        back_ref[head] += mm_tn(grad_mixed, lead_ref[:, part])
    grad_gain_ref[...] += total


def gate_backward(grad, mixed, lead, pre, gain, keep, head_count, key_scale):
    tokens, width = mixed.shape
    lanes = gain.shape[1]
    rows = 2 * BLOCK
    return pl.pallas_call(
        partial(gate_backward_kernel, head_count, key_scale),
        grid=(tokens // rows,),
        in_specs=[
            pl.BlockSpec((rows, width), lambda i: (i, 0)),
            pl.BlockSpec((rows, width), lambda i: (i, 0)),
            pl.BlockSpec((rows, width), lambda i: (i, 0)),
            pl.BlockSpec((rows, width), lambda i: (i, 3)),
            pl.BlockSpec((1, lanes), lambda i: (0, 0)),
            pl.BlockSpec((rows, 1), lambda i: (i, 0)),
        ],
        out_specs=[
            pl.BlockSpec((rows, width), lambda i: (i, 0)),
            pl.BlockSpec((rows, width), lambda i: (i, 0)),
            pl.BlockSpec((1, lanes), lambda i: (0, 0)),
            pl.BlockSpec((head_count, lanes, lanes), lambda i: (0, 0, 0)),
        ],
        out_shape=[
            jax.ShapeDtypeStruct((tokens, width), BF16),
            jax.ShapeDtypeStruct((tokens, width), BF16),
            jax.ShapeDtypeStruct((1, lanes), F32),
            jax.ShapeDtypeStruct((head_count, lanes, lanes), F32),
        ],
        compiler_params=pltpu.CompilerParams(
            dimension_semantics=("arbitrary",), vmem_limit_bytes=40 << 20
        ),
        cost_estimate=pl.CostEstimate(
            flops=tokens * width * 300,
            bytes_accessed=tokens * width * 18,
            transcendentals=tokens * width,
        ),
        name="gate_backward",
    )(grad, mixed, lead, pre, gain, keep)


def mixer_backward_kernel(
    head_count,
    pre_ref,
    grad_mixed_ref,
    grad_gate_ref,
    start_ref,
    run_ref,
    carry_ref,
    after_ref,
    open_ref,
    count_ref,
    keep_ref,
    flags_ref,
    grads_ref,
    floor_ref,
    grad_scr,
    lifted_scr,
    lowered_scr,
    moved_scr,
    value_scr,
):
    width = open_ref.shape[1]
    lanes = width // head_count

    @pl.when(pl.program_id(0) == 0)
    def _():
        grad_scr[...] = after_ref[...]
        floor_ref[...] = jnp.zeros_like(floor_ref)

    counts, keep = count_ref[...], keep_ref[...]
    flags = flags_ref[0]
    row_ids, col_ids, linked, fresh, tail, closing = block_masks(counts, flags)
    tri = (row_ids >= col_ids).astype(BF16)
    tri_back = (row_ids <= col_ids).astype(BF16)
    query_pre = pre_ref[:, :width]
    values = pre_ref[:, 2 * width : 3 * width].astype(BF16)
    opened = open_ref[...]
    closed = jax.nn.sigmoid(-pre_ref[:, width : 2 * width])
    keys = opened * closed
    cum = split_sum(tri, jnp.log1p(-keys))
    rows = cum.shape[0]
    ending = cum[rows - 1 : rows, :]
    rise, fall = jnp.exp(cum), jnp.exp(-cum) * keep
    shift = jnp.exp(ending - cum) * (keep * tail)
    sigma_query = jax.nn.sigmoid(query_pre)
    lifted = (query_pre * sigma_query * rise).astype(BF16)
    lowered = (keys * fall).astype(BF16)
    moved = (keys * shift).astype(BF16)
    fresh_lifted = (lifted.astype(F32) * fresh).astype(BF16)
    end_decay = jnp.exp(ending) * closing
    lead_in = jnp.exp(run_ref[0]) * (flags[1:2, 0:1] == 0).astype(F32)
    for head in range(head_count):
        part = slice(head * lanes, (head + 1) * lanes)
        grad_out, value = grad_mixed_ref[:, part], values[:, part]
        lift, lower, move = lifted[:, part], lowered[:, part], moved[:, part]
        scores = jnp.where(linked, mm_nt(lift, lower), 0.0).astype(BF16)
        pulls = jnp.where(linked, mm_nt(grad_out, value), 0.0).astype(BF16)
        state = start_ref[0, head] + lead_in[:, part] * carry_ref[head]
        grad_state = grad_scr[head]
        grad_low = grad_state.astype(BF16)
        lifted_scr[:, part] = mm_nn(pulls, lower) + fresh * mm_nn(grad_out, state.astype(BF16))
        lowered_scr[:, part] = mm_tn(pulls, lift)
        grad_moved = mm_nn(value, grad_low)
        moved_scr[:, part] = grad_moved
        grads_ref[:, 2 * width + head * lanes : 2 * width + (head + 1) * lanes] = (
            mm_tn(scores, grad_out) + mm_nt(move, grad_low)
        ).astype(BF16)
        value_scr[:, part] = jnp.sum(
            grad_moved * move.astype(F32), axis=0, keepdims=True
        ) + end_decay[:, part] * jnp.sum(state * grad_state, axis=0, keepdims=True)
        grad_scr[head] = grad_state * end_decay[:, part] + mm_tn(grad_out, fresh_lifted[:, part])
    grad_lifted, grad_lowered, grad_moved = lifted_scr[...], lowered_scr[...], moved_scr[...]
    grad_cum = (
        grad_lifted * lifted.astype(F32)
        - grad_lowered * lowered.astype(F32)
        - grad_moved * moved.astype(F32)
    )
    grad_decay = split_sum(tri_back, grad_cum) + value_scr[...]
    key_total = grad_lowered * fall + grad_moved * shift - grad_decay / (1.0 - keys)
    floor_ref[...] -= jnp.sum(key_total * closed, axis=0, keepdims=True)
    grads_ref[:, :width] = (
        grad_lifted * rise * sigma_query * (1.0 + query_pre * (1.0 - sigma_query))
    ).astype(BF16)
    grads_ref[:, width : 2 * width] = (-key_total * opened * closed * (1.0 - closed)).astype(BF16)
    grads_ref[:, 3 * width :] = grad_gate_ref[...]


def mixer_backward(
    pre, grad_mixed, grad_gate, starts, runs, carry, after, open_part, counts, keep, flags
):
    tokens, all_width = pre.shape
    width = open_part.shape[1]
    head_count, lanes = carry.shape[0], carry.shape[2]
    blocks = tokens // BLOCK
    last = blocks - 1
    return pl.pallas_call(
        partial(mixer_backward_kernel, head_count),
        grid=(blocks,),
        in_specs=[
            pl.BlockSpec((BLOCK, all_width), lambda i: (last - i, 0)),
            pl.BlockSpec((BLOCK, width), lambda i: (last - i, 0)),
            pl.BlockSpec((BLOCK, width), lambda i: (last - i, 0)),
            pl.BlockSpec((1, head_count, lanes, lanes), lambda i: (last - i, 0, 0, 0)),
            pl.BlockSpec((1, 1, width), lambda i: (last - i, 0, 0)),
            pl.BlockSpec((head_count, lanes, lanes), lambda i: (0, 0, 0)),
            pl.BlockSpec((head_count, lanes, lanes), lambda i: (0, 0, 0)),
            pl.BlockSpec((1, width), lambda i: (0, 0)),
            pl.BlockSpec((BLOCK, 1), lambda i: (last - i, 0)),
            pl.BlockSpec((BLOCK, 1), lambda i: (last - i, 0)),
            pl.BlockSpec((1, 8, BLOCK), lambda i: (last - i, 0, 0)),
        ],
        out_specs=[
            pl.BlockSpec((BLOCK, all_width), lambda i: (last - i, 0)),
            pl.BlockSpec((1, width), lambda i: (0, 0)),
        ],
        out_shape=[
            jax.ShapeDtypeStruct((tokens, all_width), BF16),
            jax.ShapeDtypeStruct((1, width), F32),
        ],
        scratch_shapes=[
            pltpu.VMEM((head_count, lanes, lanes), F32),
            pltpu.VMEM((BLOCK, width), F32),
            pltpu.VMEM((BLOCK, width), F32),
            pltpu.VMEM((BLOCK, width), F32),
            pltpu.VMEM((1, width), F32),
        ],
        compiler_params=pltpu.CompilerParams(
            dimension_semantics=("arbitrary",), vmem_limit_bytes=40 << 20
        ),
        cost_estimate=pl.CostEstimate(
            flops=tokens * width * BLOCK * 30,
            bytes_accessed=tokens * width * 36,
            transcendentals=tokens * width * 9,
        ),
        name="mixer_backward",
    )(pre, grad_mixed, grad_gate, starts, runs, carry, after, open_part, counts, keep, flags)


def row_flags(segment_ids):
    ids = segment_ids.reshape(-1)
    tokens = ids.shape[0]
    starts = jnp.concatenate([jnp.zeros((1,), F32), (ids[1:] != ids[:-1]).astype(F32)])
    positions = jnp.arange(tokens)
    counts = jnp.sum(
        jnp.where(positions[None, :] <= positions[:, None], starts[None, :], 0.0), axis=1
    )
    keep = (ids > 0).astype(F32)
    blocks = tokens // BLOCK
    by_block = counts.reshape(blocks, BLOCK)
    lasts = by_block[:, -1]
    before = jnp.concatenate([jnp.zeros((1,), F32), lasts[:-1]])
    wide = (blocks, BLOCK)
    flags = jnp.stack(
        [by_block, jnp.broadcast_to(before[:, None], wide), jnp.broadcast_to(lasts[:, None], wide)]
        + [jnp.zeros(wide, F32)] * 5,
        axis=1,
    )
    return counts[:, None], keep[:, None], flags, lasts[-1]


def from_earlier(values, axis, shift):
    count = lax.axis_size(axis)
    return lax.ppermute(values, axis, [(i, i + shift) for i in range(count - shift)])


def from_later(values, axis, shift):
    count = lax.axis_size(axis)
    return lax.ppermute(values, axis, [(i + shift, i) for i in range(count - shift)])


def state_before(state, decay, first_id, last_id, axis):
    head_count, lanes, _ = state.shape
    ids = jnp.stack([first_id, last_id, jnp.float32(1.0)] + [jnp.float32(0.0)] * 5)
    message = jnp.concatenate(
        [
            state.reshape(head_count * lanes, lanes),
            decay.reshape(head_count, lanes),
            jnp.broadcast_to(ids[:, None], (8, lanes)),
        ]
    )
    rows = head_count * lanes
    total = jnp.zeros_like(state)
    factor = jnp.ones((head_count, 1, lanes), F32)
    follower = first_id
    link_in = jnp.float32(0.0)
    for shift in range(1, lax.axis_size(axis)):
        got = from_earlier(message, axis, shift)
        got_ids = got[rows + head_count :, 0]
        linked = (got_ids[1] == follower).astype(F32) * got_ids[2]
        if shift == 1:
            link_in = linked
        factor = factor * linked
        total = total + factor * got[:rows].reshape(state.shape)
        factor = factor * got[rows : rows + head_count].reshape(head_count, 1, lanes)
        follower = got_ids[0]
    return total, link_in


def grad_after(back, decay, link_in, axis):
    head_count, lanes, _ = back.shape
    rows = head_count * lanes
    message = (
        jnp.concatenate([back.reshape(rows, lanes), decay.reshape(head_count, lanes)]) * link_in
    )
    message = jnp.pad(message, ((0, 8 - head_count % 8 if head_count % 8 else 0), (0, 0)))
    total = jnp.zeros_like(back)
    factor = jnp.ones((head_count, 1, lanes), F32)
    for shift in range(1, lax.axis_size(axis)):
        got = from_later(message, axis, shift)
        total = total + factor * got[:rows].reshape(back.shape)
        factor = factor * got[rows : rows + head_count].reshape(head_count, 1, lanes)
    return total


def scatter_sum(values):
    return lax.psum_scatter(
        values.astype(jnp.bfloat16), "tensor", scatter_dimension=0, tiled=True
    ).astype(jnp.float32)


def gather_rows(values):
    return lax.all_gather(values, "tensor", axis=0, tiled=True)


def rms_parts(values):
    inverse = lax.rsqrt(jnp.mean(values * values, axis=-1, keepdims=True) + EPSILON)
    return (values * inverse, inverse)


def local(
    hidden,
    segment_ids,
    norm1_gain,
    w_query,
    w_forget,
    w_input,
    w_gate_out,
    forget_floor,
    head_gain,
    w_out,
    norm2_gain,
    w_ffn_gate,
    w_ffn_up,
    w_ffn_down,
    out_grad,
):
    sequences, span_len, model_width = hidden.shape
    tokens = sequences * span_len
    head_count, key_dim = forget_floor.shape
    width = head_count * key_dim
    key_scale = key_dim ** (-0.5)
    both = ("shard", "context")
    mixer_full = lax.all_gather(
        jnp.concatenate([w_query, w_forget, w_input, w_gate_out], axis=1), both, axis=0, tiled=True
    )
    out_full = lax.all_gather(w_out, both, axis=1, tiled=True)
    gate_full = lax.all_gather(w_ffn_gate, both, axis=0, tiled=True)
    up_full = lax.all_gather(w_ffn_up, both, axis=0, tiled=True)
    down_full = lax.all_gather(w_ffn_down, both, axis=1, tiled=True)
    part_rows = tokens // lax.axis_size("tensor")
    place = lax.axis_index("tensor") * part_rows

    def own_rows(values):
        return lax.dynamic_slice_in_dim(values, place, part_rows, 0)

    hidden_rows = hidden.reshape(tokens, model_width)
    unit_rows, _ = rms_parts(hidden_rows.astype(F32))
    normed_one = (unit_rows * norm1_gain).astype(BF16)
    pre = jnp.dot(normed_one, mixer_full, preferred_element_type=F32)
    open_part = (1.0 - forget_floor).reshape(1, width)
    counts, keep, flags, last_count = row_flags(segment_ids)
    mixed_local, lead, starts, runs, state_end, run_end = mixer_forward(
        pre, open_part, counts, keep, flags, head_count, key_scale
    )
    decay = (jnp.exp(run_end) * (last_count == 0).astype(F32)).reshape(head_count, 1, key_dim)
    ids = segment_ids.reshape(-1).astype(F32)
    carry, link_in = state_before(state_end, decay, ids[0], ids[-1], "context")
    gain_row = head_gain.reshape(1, -1)
    mixed, gated_low = gate_forward(
        mixed_local, lead, carry.astype(BF16), pre, gain_row, keep, key_scale
    )
    mix_part = jnp.dot(gated_low, out_full, preferred_element_type=F32)
    inputs_own = own_rows(hidden_rows).astype(F32)
    residual = inputs_own + scatter_sum(mix_part)
    unit_two, inverse_two = rms_parts(residual)
    normed_two = gather_rows((unit_two * norm2_gain).astype(BF16))
    gate_ffn = jnp.dot(normed_two, gate_full, preferred_element_type=F32)
    up_ffn = jnp.dot(normed_two, up_full, preferred_element_type=F32)
    sigma_gate = jax.nn.sigmoid(gate_ffn)
    active = gate_ffn * sigma_gate
    hidden_low = (active * up_ffn).astype(BF16)
    feed_part = jnp.dot(hidden_low, down_full, preferred_element_type=F32)
    output_rows = gather_rows((residual + scatter_sum(feed_part)).astype(BF16))
    grad_rows = out_grad.reshape(tokens, model_width)
    grad_down = jnp.einsum("tf,td->fd", hidden_low, grad_rows, preferred_element_type=F32)
    grad_hidden = jnp.einsum("td,fd->tf", grad_rows, down_full, preferred_element_type=F32)
    grad_gate_low = (
        grad_hidden * up_ffn * sigma_gate * (1.0 + gate_ffn * (1.0 - sigma_gate))
    ).astype(BF16)
    grad_up_low = (grad_hidden * active).astype(BF16)
    grad_gate = jnp.einsum("td,tf->df", normed_two, grad_gate_low, preferred_element_type=F32)
    grad_up = jnp.einsum("td,tf->df", normed_two, grad_up_low, preferred_element_type=F32)
    back_two = jnp.einsum("tf,df->td", grad_gate_low, gate_full, preferred_element_type=F32)
    back_two = back_two + jnp.einsum(
        "tf,df->td", grad_up_low, up_full, preferred_element_type=F32
    )
    grad_normed_two = scatter_sum(back_two)
    cotangent_rows = own_rows(grad_rows).astype(F32)
    grad_norm_two = jnp.sum(grad_normed_two * unit_two, axis=0)
    lifted_two = grad_normed_two * norm2_gain
    grad_residual = cotangent_rows + inverse_two * (
        lifted_two - unit_two * jnp.mean(lifted_two * unit_two, axis=-1, keepdims=True)
    )
    grad_mix_low = gather_rows(grad_residual.astype(BF16))
    grad_out = jnp.einsum("tv,td->vd", gated_low, grad_mix_low, preferred_element_type=F32)
    grad_gated = jnp.einsum("td,vd->tv", grad_mix_low, out_full, preferred_element_type=F32)
    grad_mixed, grad_gate_pre, grad_head_part, back = gate_backward(
        grad_gated, mixed, lead, pre, gain_row, keep, head_count, key_scale
    )
    after = grad_after(back, decay, link_in, "context")
    grad_pre, grad_floor_part = mixer_backward(
        pre,
        grad_mixed,
        grad_gate_pre,
        starts,
        runs,
        carry,
        after,
        open_part,
        counts,
        keep,
        flags,
    )
    grad_mixer = jnp.einsum("td,tk->dk", normed_one, grad_pre, preferred_element_type=F32)
    back_one = jnp.einsum("tk,dk->td", grad_pre, mixer_full, preferred_element_type=F32)
    grad_normed_one = scatter_sum(back_one)
    unit_one, inverse_one = rms_parts(inputs_own)
    grad_norm_one = jnp.sum(grad_normed_one * unit_one, axis=0)
    grad_norm_one, grad_norm_two, head_total = lax.psum(
        (grad_norm_one, grad_norm_two, grad_head_part.reshape(-1)), "tensor"
    )
    lifted_one = grad_normed_one * norm1_gain
    grad_inputs = grad_residual + inverse_one * (
        lifted_one - unit_one * jnp.mean(lifted_one * unit_one, axis=-1, keepdims=True)
    )
    input_rows = gather_rows(grad_inputs.astype(BF16))

    def share(values, dim):
        return lax.psum_scatter(
            values.astype(BF16), both, scatter_dimension=dim, tiled=True
        ).astype(F32)

    share_mixer = share(grad_mixer, 0)
    return (
        output_rows.reshape(hidden.shape),
        input_rows.reshape(hidden.shape),
        share(grad_norm_one, 0),
        share_mixer[:, :width],
        share_mixer[:, width : 2 * width],
        share_mixer[:, 2 * width : 3 * width],
        share_mixer[:, 3 * width :],
        share(grad_floor_part.reshape(head_count, key_dim), 1),
        share(head_total, 0),
        share(grad_out, 1),
        share(grad_norm_two, 0),
        share(grad_gate, 0),
        share(grad_up, 0),
        share(grad_down, 1),
    )


def solution(mesh):
    in_specs = (
        P("shard", "context", None),
        P("shard", "context"),
        P(),
        P(("shard", "context"), "tensor"),
        P(("shard", "context"), "tensor"),
        P(("shard", "context"), "tensor"),
        P(("shard", "context"), "tensor"),
        P("tensor", None),
        P(),
        P("tensor", ("shard", "context")),
        P(),
        P(("shard", "context"), "tensor"),
        P(("shard", "context"), "tensor"),
        P("tensor", ("shard", "context")),
        P("shard", "context", None),
    )
    out_specs = (
        P("shard", "context", None),
        P("shard", "context", None),
        P(("shard", "context")),
        P(("shard", "context"), "tensor"),
        P(("shard", "context"), "tensor"),
        P(("shard", "context"), "tensor"),
        P(("shard", "context"), "tensor"),
        P("tensor", ("shard", "context")),
        P(("shard", "context")),
        P("tensor", ("shard", "context")),
        P(("shard", "context")),
        P(("shard", "context"), "tensor"),
        P(("shard", "context"), "tensor"),
        P("tensor", ("shard", "context")),
    )
    return jax.shard_map(local, mesh=mesh, in_specs=in_specs, out_specs=out_specs, check_vma=False)
```

time: 2020 us -> 1330 us (0.66)
  local copies, waits for them, and re-layouts: 298 us -> 20.5 us
  matrix products: 418 us -> 158 us
  other arithmetic: 171 us -> 38.7 us
  loops' own time: 35.4 us -> 0 us
  Pallas kernels: 0 us -> 34.4 us
    dot_general x248 -> x13, matrix products: 396 us -> 136 us  [the longest x1 15.6 us: local(): jnp.einsum('td,fd->tf', grad_rows, down_full, preferred_element_type=F32)]
    reduce_scatter x8 -> x5, waiting for transfers between devices: 390 us -> 259 us  [share(): lax.psum_scatter(values.astype(BF16), both, scatter_dimension=dim, tiled=...]
    squeeze x128 -> x0, local copies, waits for them, and re-layouts: 118 us -> none  [recurrence(): lax.scan(stepper, carried, (split_heads(queries), split_heads(inputs_in),...]
    all_gather x4, waiting for transfers between devices: 212 us -> 326 us  [gather_rows(): return lax.all_gather(values, 'tensor', axis=0, tiled=True)]
    another operation x134 -> x0, other arithmetic: 66.7 us -> none  [the longest x80 41.3 us: block_step(): cumulated = jnp.cumsum(log_decay, axis=2)]
    convert_element_type x99 -> x14, other arithmetic: 81.6 us -> 24 us  [the longest x7 10.5 us: share(): return lax.psum_scatter(values.astype(BF16), both, scatter_dimension=dim,...]
    another operation x5 -> x0, loops' own time: 35.4 us -> none  [the longest x3 34.9 us: recurrence(): lax.scan(stepper, carried, (split_heads(queries), split_heads(inputs_in),...]
    pallas_call x0 -> x4, Pallas kernels: none -> 34.4 us  [the longest x1 14.5 us: mixer_backward(): pl.pallas_call(partial(mixer_backward_kernel, head_count), grid=(blocks,)...]
  transfers between devices with their start and end apart: 25 -> 21, of which waited for: 21 -> 20; matrix products, arithmetic and copies ran while one was open for 26% -> 11% of each run, Pallas kernels for 0% -> 1%
where the time goes in v2:
time: 1330 us; the launch traced here: 1320 us
  waiting for transfers between devices  1020 us (77%)
  matrix products  158 us (12%)
  other arithmetic  38.7 us (3%)
  Pallas kernels  34.4 us (3%)
  blocking collectives  31.4 us (2%)
  local copies, waits for them, and re-layouts  20.5 us (2%)
  between operations  18.8 us (1%)
    all_gather x4, waiting for transfers between devices, gather_rows(): return lax.all_gather(values, 'tensor', axis=0, tiled=True)  326 us
    reduce_scatter x5, waiting for transfers between devices, share(): lax.psum_scatter(values.astype(BF16), both, scatter_dimension=dim, tiled=...  259 us
    reduce_scatter x4, waiting for transfers between devices, scatter_sum(): lax.psum_scatter(values.astype(jnp.bfloat16), 'tensor', scatter_dimension...  241 us
    all_gather x1, waiting for transfers between devices, local(): lax.all_gather(jnp.concatenate([w_query, w_forget, w_input, w_gate_out],...  46.4 us
    all_gather x1, waiting for transfers between devices, local(): gate_full = lax.all_gather(w_ffn_gate, both, axis=0, tiled=True)  39 us
    unnamed x20, waiting for transfers between devices  36 us
    all_gather x1, waiting for transfers between devices, local(): down_full = lax.all_gather(w_ffn_down, both, axis=1, tiled=True)  34.8 us
    all_gather x1, waiting for transfers between devices, local(): up_full = lax.all_gather(w_ffn_up, both, axis=0, tiled=True)  32.1 us
  transfers between devices with their start and end apart: 21, of which 20 were waited for; matrix products, arithmetic and copies ran while one was open for 11% of the time, Pallas kernels for 1%

profile of v2, /device:TPU:0, one launch (start us, length us, event | category | flops | bytes accessed | tf_op | source)
XLA Modules:
  0.0 1324.9 jit_solution(2683944143770669988)
XLA Ops:
  18.0 3.3 fusion
  21.3 46.4 %all-gather.10.cloned.1.call-done = bf16[2048,2048]{1,0:T(8,128)(2,1)} async-done(((bf16[256,2048]{1,0:T(8,128)(2,1)}), bf16[2048,2048]{1,0:T(8,128)(2,1)}) %all-gather.10.cloned.1.call-update) | async-done | bytes 8388624 | tf_op jit(solution)/shard_map/all_gather | solution.py:549
  67.7 14.5 %fusion.25.pre_ref.gate_ref = f32[1024,2048]{1,0:T(8,128)} fusion(bf16[2048,2048]{1,0:T(8,128)(2,1)} %all-gather.10.cloned.1.call-done, bf16[1,1024,2048]{2,1,0:T(8,128)(2,1)} %param.15, f32[2048]{0:T(1024)S(1)} %copy-done.12, f32[1024]{0:T(1024)S(1)} %add_rsqrt_fusion), kind=kOutput, calls=%fused_computation.50 | convolution fusion | flops 8598323200 | bytes 20983808 | tf_op jit(solution)/shard_map/dot_general | solution.py:565
  82.1 9.7 mixer_forward.1
  99.2 4.1 gate_forward.1
  104.6 6.3 convolution_convert_fusion.6
  111.5 76.2 %reduce-scatter.13.cloned.1.call-done = bf16[256,2048]{1,0:T(8,128)(2,1)} async-done(((bf16[1024,2048]{1,0:T(8,128)(2,1)}), bf16[256,2048]{1,0:T(8,128)(2,1)}) %reduce-scatter.13.cloned.1.call-update) | async-done | bytes 1048592 | tf_op jit(solution)/shard_map/reduce_scatter | solution.py:512
  189.7 2.9 multiply_convert_fusion.3
  194.5 39.0 %all-gather.16.cloned.1.call-done = bf16[2048,1408]{1,0:T(8,128)(2,1)} async-done(((bf16[256,1408]{1,0:T(8,128)(2,1)}), bf16[2048,1408]{1,0:T(8,128)(2,1)}) %all-gather.16.cloned.1.call-update) | async-done | bytes 5767184 | tf_op jit(solution)/shard_map/all_gather | solution.py:553
  233.5 82.9 %all-gather.14.cloned.1.call-done = bf16[1024,2048]{1,0:T(8,128)(2,1)} async-done(((bf16[256,2048]{1,0:T(8,128)(2,1)}), bf16[1024,2048]{1,0:T(8,128)(2,1)}) %all-gather.14.cloned.1.call-update) | async-done | bytes 4194320 | tf_op jit(solution)/shard_map/all_gather | solution.py:518
  316.4 11.7 fusion.32
  328.0 32.1 %all-gather.18.cloned.1.call-done = bf16[2048,1408]{1,0:T(8,128)(2,1)} async-done(((bf16[256,1408]{1,0:T(8,128)(2,1)}), bf16[2048,1408]{1,0:T(8,128)(2,1)}) %all-gather.18.cloned.1.call-update) | async-done | bytes 5767184 | tf_op jit(solution)/shard_map/all_gather | solution.py:554
  360.1 11.6 fusion.33
  371.8 34.8 %all-gather.20.cloned.1.call-done = bf16[1408,2048]{1,0:T(8,128)(2,1)} async-done(((bf16[1408,256]{1,0:T(8,128)(2,1)}), bf16[1408,2048]{1,0:T(8,128)(2,1)}) %all-gather.20.cloned.1.call-update) | async-done | bytes 5767184 | tf_op jit(solution)/shard_map/all_gather | solution.py:555
  406.6 15.6 %multiply_convert_fusion = (bf16[1024,1408]{1,0:T(8,128)(2,1)S(1)}, bf16[1024,1408]{1,0:T(8,128)(2,1)S(1)}, bf16[1024,1408]{1,0:T(8,128)(2,1)}) fusion(f32[1024,1408]{1,0:T(8,128)} %fusion.32, f32[1024,1408]{1,0:T(8,128)} %fusion.33, bf16[1408,2048]{1,0:T(8,128)(2,1)} %all-gather.20.cloned.1.call-done, bf16[1,1024,2048]{2,1,0:T(8,128)(2,1)} %param.29), kind=kOutput, calls=%fused_computation.10 | convolution fusion | flops 5927206912 | bytes 30146560 | tf_op jit(solution)/shard_map/td,fd->tf/dot_general | solution.py:592
  422.2 10.9 fusion.34
  433.1 8.2 add_convert_fusion
  441.6 76.7 %reduce-scatter.17.cloned.1.call-done = bf16[256,2048]{1,0:T(8,128)(2,1)} async-done(((bf16[1024,2048]{1,0:T(8,128)(2,1)}), bf16[256,2048]{1,0:T(8,128)(2,1)}) %reduce-scatter.17.cloned.1.call-update) | async-done | bytes 1048592 | tf_op jit(solution)/shard_map/reduce_scatter | solution.py:512
  518.3 2.7 fusion.19
  521.0 3.9 fusion.28
  524.9 81.4 %all-gather.24.cloned.1.call-done = bf16[1024,2048]{1,0:T(8,128)(2,1)} async-done(((bf16[256,2048]{1,0:T(8,128)(2,1)}), bf16[1024,2048]{1,0:T(8,128)(2,1)}) %all-gather.24.cloned.1.call-update) | async-done | bytes 4194320 | tf_op jit(solution)/shard_map/all_gather | solution.py:518
  606.3 5.4 fusion.35.grad_ref
  611.7 6.1 gate_backward.1
  621.6 14.5 %mixer_backward.1 = (bf16[1024,2048]{1,0:T(8,128)(2,1)S(1)}, f32[1,512]{1,0:T(1,128)S(1)}) custom-call(f32[1024,2048]{1,0:T(8,128)} %fusion.25.pre_ref.gate_ref, bf16[1024,512]{1,0:T(8,128)(2,1)S(1)} %get-tuple-element.34.grad_mixed_ref, bf16[1024,512]{1,0:T(8,128)(2,1)S(1)} %get-tuple-element.35.grad_gate_ref, f32[8,4,128,128]{3,2,1,0:T(8,128)S(1)} %copy-done.1, ...), custom_call_target="tpu_custom_call" | custom-call | flops 2013265920 | bytes 18874368 | tf_op jit(solution)/shard_map/mixer_backward/pallas_call | solution.py:392
  638.1 10.4 convolution_convert_fusion.4
  648.8 10.9 convolution_convert_fusion.5
  659.7 11.1 convolution_convert_fusion.2
  670.9 11.0 convolution_convert_fusion.1
  681.9 10.6 convolution_convert_fusion
  693.7 5.9 convolution_convert_fusion.7
  699.7 14.4 %convolution_convert_fusion.3 = bf16[2048,2048]{1,0:T(8,128)(2,1)} fusion(bf16[1024,2048]{1,0:T(8,128)(2,1)} %copy-done.5, bf16[1,1024,2048]{2,1,0:T(8,128)(2,1)} %param.15, f32[2048]{0:T(1024)S(1)} %copy-done.13, f32[1024]{0:T(1024)S(1)} %copy-done.15), kind=kOutput, calls=%fused_computation.9 | convolution fusion | flops 8602517504 | bytes 16789504 | tf_op jit(solution)/shard_map/td,tk->dk/dot_general | solution.py:630
  714.2 9.7 reduce-scatter.19.cloned.1.call-done
  723.9 2.4 fusion.21
  726.3 77.9 %reduce-scatter.15.cloned.1.call-done = bf16[256,2048]{1,0:T(8,128)(2,1)} async-done(((bf16[1024,2048]{1,0:T(8,128)(2,1)}), bf16[256,2048]{1,0:T(8,128)(2,1)}) %reduce-scatter.15.cloned.1.call-update) | async-done | bytes 1048592 | tf_op jit(solution)/shard_map/reduce_scatter | solution.py:512
  804.3 5.2 fusion.15
  812.2 55.0 %reduce-scatter.25.cloned.1.call-done = bf16[256,1408]{1,0:T(8,128)(2,1)} async-done(((bf16[2048,1408]{1,0:T(8,128)(2,1)}), bf16[256,1408]{1,0:T(8,128)(2,1)}) %reduce-scatter.25.cloned.1.call-update) | async-done | bytes 720912 | tf_op jit(solution)/shard_map/reduce_scatter | solution.py:645
  869.4 60.6 %reduce-scatter.27.cloned.1.call-done = bf16[256,1408]{1,0:T(8,128)(2,1)} async-done(((bf16[2048,1408]{1,0:T(8,128)(2,1)}), bf16[256,1408]{1,0:T(8,128)(2,1)}) %reduce-scatter.27.cloned.1.call-update) | async-done | bytes 720912 | tf_op jit(solution)/shard_map/reduce_scatter | solution.py:645
  932.4 60.0 %reduce-scatter.29.cloned.1.call-done = bf16[1408,256]{1,0:T(8,128)(2,1)} async-done(((bf16[1408,2048]{1,0:T(8,128)(2,1)}), bf16[1408,256]{1,0:T(8,128)(2,1)}) %reduce-scatter.29.cloned.1.call-update) | async-done | bytes 720912 | tf_op jit(solution)/shard_map/reduce_scatter | solution.py:645
  992.4 2.3 convert_element_type.203
  994.7 32.6 %reduce-scatter.31.cloned.1.call-done = bf16[16,4]{1,0:T(8,128)(2,1)} async-done(((bf16[128,4]{1,0:T(8,128)(2,1)}), bf16[16,4]{1,0:T(8,128)(2,1)}) %reduce-scatter.31.cloned.1.call-update) | async-done | bytes 144
  1028.7 43.0 %reduce-scatter.23.cloned.1.call-done = bf16[512,256]{1,0:T(8,128)(2,1)} async-done(((bf16[512,2048]{1,0:T(8,128)(2,1)}), bf16[512,256]{1,0:T(8,128)(2,1)}) %reduce-scatter.23.cloned.1.call-update) | async-done | bytes 262160 | tf_op jit(solution)/shard_map/reduce_scatter | solution.py:645
  1073.5 18.9 %all-reduce.4 = (bf16[2048]{0:T(1024)(128)(2,1)S(1)}, bf16[128]{0:T(256)(128)(2,1)S(1)}, bf16[2048]{0:T(1024)(128)(2,1)S(1)}) all-reduce(f32[2048]{0:T(1024)S(1)} %get-tuple-element.44, f32[128]{0:T(128)S(1)} %bitcast.94, f32[2048]{0:T(1024)S(1)} %get-tuple-element.42), channel_id=1, replica_groups=mesh['shard'=4,'context'=2,'tensor'=4] {'tensor'}, use_global_device_ids=true, to_apply=%region_11.12 | all-reduce | flops 4224 | bytes 25344 | tf_op jit(solution)/shard_map/psum | solution.py:635
  1092.4 12.5 all-reduce.5
  1106.1 40.6 %reduce-scatter.21.cloned.1.call-done = bf16[256,2048]{1,0:T(8,128)(2,1)} async-done(((bf16[2048,2048]{1,0:T(8,128)(2,1)}), bf16[256,2048]{1,0:T(8,128)(2,1)}) %reduce-scatter.21.cloned.1.call-update) | async-done | bytes 1048592 | tf_op jit(solution)/shard_map/reduce_scatter | solution.py:645
  1146.7 2.6 fusion.29
  1149.3 80.2 %all-gather.22.cloned.1.call-done = bf16[1024,2048]{1,0:T(8,128)(2,1)} async-done(((bf16[256,2048]{1,0:T(8,128)(2,1)}), bf16[1024,2048]{1,0:T(8,128)(2,1)}) %all-gather.22.cloned.1.call-update) | async-done | bytes 4194320 | tf_op jit(solution)/shard_map/all_gather | solution.py:518
  1229.5 81.5 %all-gather.26.cloned.1.call-done = bf16[1024,2048]{1,0:T(8,128)(2,1)} async-done(((bf16[256,2048]{1,0:T(8,128)(2,1)}), bf16[1024,2048]{1,0:T(8,128)(2,1)}) %all-gather.26.cloned.1.call-update) | async-done | bytes 4194320 | tf_op jit(solution)/shard_map/all_gather | solution.py:518
  1311.0 4.9 copy.51
  (135 shorter events, 41.2 us)
Async XLA Ops:
  7.2 60.5 %copy-start.12 = (f32[2048]{0:T(1024)S(1)}, f32[2048]{0:T(1024)}, u32[]{:S(2)}) copy-start(f32[2048]{0:T(1024)} %param.17) | copy-start | bytes 24580
  7.2 60.5 %all-gather.10.cloned.1.call-start = ((), (), s32[]{:S(2)}) async-start(), calls=%async_computation.10 | async-start | bytes 9437184 | tf_op jit(solution)/shard_map/all_gather | solution.py:549
  9.5 95.0 %all-gather.12.cloned.1.call-start = ((), (), s32[]{:S(2)}) async-start(), calls=%async_computation.11 | async-start | bytes 2359296 | tf_op jit(solution)/shard_map/all_gather | solution.py:552
  10.3 177.5 %reduce-scatter.13.cloned.1.call-start = ((), (), s32[]{:S(2)}) async-start(), calls=%async_computation.12 | async-start | bytes 5242880 | tf_op jit(solution)/shard_map/reduce_scatter | solution.py:512
  21.3 60.9 %copy-start.14 = (f32[1024]{0:T(1024)}, f32[1024]{0:T(1024)S(1)}, u32[]{:S(2)}) copy-start(f32[1024]{0:T(1024)S(1)} %add_rsqrt_fusion) | copy-start | bytes 12292
  82.1 17.0 %copy-start.4 = (f32[128]{0:T(128)S(1)}, f32[128]{0:T(128)}, u32[]{:S(2)}) copy-start(f32[128]{0:T(128)} %param.23) | copy-start | bytes 1540
  91.8 1.3 copy-start
  93.3 3.3 collective-permute-start
  103.2 1.3 copy-start.2
  104.6 6.3 copy-start.6
  110.9 78.8 %copy-start.11 = (f32[2048]{0:T(1024)S(1)}, f32[2048]{0:T(1024)}, u32[]{:S(2)}) copy-start(f32[2048]{0:T(1024)} %param.25) | copy-start | bytes 24580
  110.9 122.6 %all-gather.16.cloned.1.call-start = ((), (), s32[]{:S(2)}) async-start(), calls=%async_computation.14 | async-start | bytes 6488064 | tf_op jit(solution)/shard_map/all_gather | solution.py:553
  111.5 204.9 %all-gather.14.cloned.1.call-start = ((), (), s32[]{:S(2)}) async-start(), calls=%async_computation.13 | async-start | bytes 5242880 | tf_op jit(solution)/shard_map/all_gather | solution.py:518
  192.7 167.5 %all-gather.18.cloned.1.call-start = ((), (), s32[]{:S(2)}) async-start(), calls=%async_computation.15 | async-start | bytes 6488064 | tf_op jit(solution)/shard_map/all_gather | solution.py:554
  193.2 213.3 %all-gather.20.cloned.1.call-start = ((), (), s32[]{:S(2)}) async-start(), calls=%async_computation.16 | async-start | bytes 6488064 | tf_op jit(solution)/shard_map/all_gather | solution.py:555
  194.0 324.3 %reduce-scatter.17.cloned.1.call-start = ((), (), s32[]{:S(2)}) async-start(), calls=%async_computation.19 | async-start | bytes 5242880 | tf_op jit(solution)/shard_map/reduce_scatter | solution.py:512
  422.2 10.9 copy-start.18
  422.2 10.9 copy-start.19
  422.2 10.9 copy-start.16
  441.3 76.9 %copy-start.8 = (bf16[256,2048]{1,0:T(8,128)(2,1)S(1)}, bf16[256,2048]{1,0:T(8,128)(2,1)}, u32[]{:S(2)}) copy-start(bf16[256,2048]{1,0:T(8,128)(2,1)} %reduce-scatter.13.cloned.1.call-done) | copy-start | bytes 3145732
  441.3 165.0 %all-gather.24.cloned.1.call-start = ((), (), s32[]{:S(2)}) async-start(), calls=%async_computation.20 | async-start | bytes 5242880 | tf_op jit(solution)/shard_map/all_gather | solution.py:518
  524.9 199.1 %reduce-scatter.19.cloned.1.call-start = ((), (), s32[]{:S(2)}) async-start(), calls=%async_computation.21 | async-start | bytes 5242880 | tf_op jit(solution)/shard_map/reduce_scatter | solution.py:512
  606.3 5.4 copy-start.3
  611.7 9.9 copy-start.1
  611.7 26.4 %slice-start = ((s8[8388608]{0:T(1024)(128)(4,1)}), s8[4194304]{0:T(1024)(128)(4,1)S(1)}, s32[]{:S(2)}) async-start(s8[8388608]{0:T(1024)(128)(4,1)} %bitcast.107), calls=%async_computation.29 | async-start | bytes 8388608
  617.8 20.3 %slice-start.1 = ((s8[8388608]{0:T(1024)(128)(4,1)}), s8[4194304]{0:T(1024)(128)(4,1)S(1)}, s32[]{:S(2)}) async-start(s8[8388608]{0:T(1024)(128)(4,1)} %bitcast.107), calls=%async_computation.30 | async-start | bytes 8388608
  617.9 3.7 collective-permute-start.1
  636.2 1.9 copy-start.5
  648.5 155.7 %reduce-scatter.15.cloned.1.call-start = ((), (), s32[]{:S(2)}) async-start(), calls=%async_computation.17 | async-start | bytes 5242880 | tf_op jit(solution)/shard_map/reduce_scatter | solution.py:512
  659.7 207.5 %reduce-scatter.25.cloned.1.call-start = ((), (), s32[]{:S(2)}) async-start(), calls=%async_computation.25 | async-start | bytes 6488064 | tf_op jit(solution)/shard_map/reduce_scatter | solution.py:645
  670.8 259.2 %reduce-scatter.27.cloned.1.call-start = ((), (), s32[]{:S(2)}) async-start(), calls=%async_computation.26 | async-start | bytes 6488064 | tf_op jit(solution)/shard_map/reduce_scatter | solution.py:645
  681.8 310.5 %reduce-scatter.29.cloned.1.call-start = ((), (), s32[]{:S(2)}) async-start(), calls=%async_computation.27 | async-start | bytes 6488064 | tf_op jit(solution)/shard_map/reduce_scatter | solution.py:645
  692.5 1.2 copy-start.7
  692.5 334.9 %reduce-scatter.31.cloned.1.call-start = ((), (), s32[]{:S(2)}) async-start(), calls=%async_computation.28 | async-start | bytes 36864
  693.3 6.4 copy-start.13
  693.3 6.4 copy-start.15
  693.3 378.4 %reduce-scatter.23.cloned.1.call-start = ((), (), s32[]{:S(2)}) async-start(), calls=%async_computation.24 | async-start | bytes 2359296 | tf_op jit(solution)/shard_map/reduce_scatter | solution.py:645
  699.6 447.1 %reduce-scatter.21.cloned.1.call-start = ((), (), s32[]{:S(2)}) async-start(), calls=%async_computation.23 | async-start | bytes 9437184 | tf_op jit(solution)/shard_map/reduce_scatter | solution.py:645
  714.2 90.1 %copy-start.9 = (bf16[256,2048]{1,0:T(8,128)(2,1)S(1)}, bf16[256,2048]{1,0:T(8,128)(2,1)}, u32[]{:S(2)}) copy-start(bf16[256,2048]{1,0:T(8,128)(2,1)} %reduce-scatter.17.cloned.1.call-done) | copy-start | bytes 3145732
  714.2 515.3 %all-gather.22.cloned.1.call-start = ((), (), s32[]{:S(2)}) async-start(), calls=%async_computation.18 | async-start | bytes 5242880 | tf_op jit(solution)/shard_map/all_gather | solution.py:518
  726.3 83.9 %copy-start.17 = (u32[32]{0:T(128)S(1)}, u32[32]{0:T(128)}, u32[]{:S(2)}) copy-start(u32[32]{0:T(128)} %constant.50) | copy-start | bytes 388
  809.5 501.5 %all-gather.26.cloned.1.call-start = ((), (), s32[]{:S(2)}) async-start(), calls=%async_computation.22 | async-start | bytes 5242880 | tf_op jit(solution)/shard_map/all_gather | solution.py:518
  1311.0 4.9 copy-start.10
Sparse Core Ops, SparseCore 0:
  10.5 57.1 all-gather.9
  69.5 28.1 all-gather.11
  111.0 76.6 reduce-scatter.12
  189.7 43.8 all-gather.15
  235.6 80.7 all-gather.13
  318.3 41.8 all-gather.17
  362.2 44.3 all-gather.19
  441.5 76.7 reduce-scatter.16
  525.0 81.2 all-gather.23
  648.6 75.2 reduce-scatter.18
  726.9 77.2 reduce-scatter.14
  807.6 59.5 reduce-scatter.24
  871.0 59.0 reduce-scatter.26
  933.4 58.9 reduce-scatter.28
  996.1 31.2 reduce-scatter.30
  1030.5 41.2 reduce-scatter.22
  1075.4 71.2 reduce-scatter.20
  1148.7 80.7 all-gather.21
  1231.7 79.2 all-gather.25

commit v3 on v2

--- a/solution.py
+++ b/solution.py
@@ -508,14 +508,215 @@
     return total
 
 
-def scatter_sum(values):
-    return lax.psum_scatter(
-        values.astype(jnp.bfloat16), "tensor", scatter_dimension=0, tiled=True
-    ).astype(jnp.float32)
-
-
-def gather_rows(values):
-    return lax.all_gather(values, "tensor", axis=0, tiled=True)
+CHUNK = 32
+LAG = 2
+
+
+def line_exchange_kernel(transform, mesh_axes, n_in, n_out, *refs):
+    part, extra_in = refs[0], refs[1 : 1 + n_in]
+    out, extra_out = refs[1 + n_in], refs[2 + n_in : 2 + n_in + n_out]
+    arrived, passed, sum_send, sum_recv, back_send, back_recv = refs[2 + n_in + n_out :]
+    half = part.shape[0] // 2
+    chunks = half // CHUNK
+    size = lax.axis_size("tensor")
+    place = lax.axis_index("tensor")
+    others = {axis: lax.axis_index(axis) for axis in mesh_axes}
+
+    def device(position):
+        return tuple(
+            jnp.clip(position, 0, size - 1) if axis == "tensor" else others[axis]
+            for axis in mesh_axes
+        )
+
+    barrier = pltpu.get_barrier_semaphore()
+    for step in (-1, 1):
+        inside = jnp.logical_and(place + step >= 0, place + step < size)
+
+        @pl.when(inside)
+        def _(step=step):
+            pl.semaphore_signal(
+                barrier, inc=1, device_id=device(place + step), device_id_type=pl.DeviceIdType.MESH
+            )
+
+    at_end = jnp.logical_or(place == 0, place == size - 1)
+    pl.semaphore_wait(barrier, jnp.where(at_end, 1, 2))
+
+    transform(None, None, None, extra_in, out, extra_out)
+
+    lines = ((size - 1 - place, -1), (place, 1))
+
+    def rows_of(side, index):
+        return pl.ds(pl.multiple_of(side * half + index * CHUNK, CHUNK), CHUNK)
+
+    def sum_copy(side, index, source):
+        rows = rows_of(side, index)
+        return pltpu.make_async_remote_copy(
+            source.at[rows],
+            arrived.at[rows],
+            sum_send.at[side, index],
+            sum_recv.at[side, index],
+            device_id=device(place + lines[side][1]),
+            device_id_type=pl.DeviceIdType.MESH,
+        )
+
+    def back_copy(side, index):
+        rows = rows_of(side, index)
+        return pltpu.make_async_remote_copy(
+            out.at[rows],
+            out.at[rows],
+            back_send.at[side, index],
+            back_recv.at[side, index],
+            device_id=device(place - lines[side][1]),
+            device_id_type=pl.DeviceIdType.MESH,
+        )
+
+    def step(time, _):
+        for side in (0, 1):
+            hops = lines[side][0]
+            index = time - LAG * hops
+            valid = jnp.logical_and(index >= 0, index < chunks)
+            at_source, at_owner = hops == 0, hops == size - 1
+            index = jnp.clip(index, 0, chunks - 1)
+
+            @pl.when(jnp.logical_and(valid, at_source))
+            def _(side=side, index=index):
+                sum_copy(side, index, part).start()
+
+            @pl.when(jnp.logical_and(valid, jnp.logical_not(at_source)))
+            def _(side=side, index=index):
+                sum_copy(side, index, passed).wait_recv()
+
+            @pl.when(
+                jnp.logical_and(
+                    valid, jnp.logical_and(jnp.logical_not(at_source), jnp.logical_not(at_owner))
+                )
+            )
+            def _(side=side, index=index):
+                rows = rows_of(side, index)
+                passed[rows] = (part[rows].astype(F32) + arrived[rows].astype(F32)).astype(BF16)
+                sum_copy(side, index, passed).start()
+
+            @pl.when(jnp.logical_and(valid, at_owner))
+            def _(side=side, index=index):
+                rows = rows_of(side, index)
+                total = part[rows].astype(F32) + arrived[rows].astype(F32)
+                own = pl.ds(pl.multiple_of(index * CHUNK, CHUNK), CHUNK)
+                transform(total, rows, own, extra_in, out, extra_out)
+                back_copy(side, index).start()
+
+            away = size - 1 - hops
+            index = time - LAG * (size - 1 + away)
+            valid = jnp.logical_and(jnp.logical_and(index >= 0, index < chunks), away > 0)
+            index = jnp.clip(index, 0, chunks - 1)
+
+            @pl.when(valid)
+            def _(side=side, index=index):
+                back_copy(side, index).wait_recv()
+
+            @pl.when(jnp.logical_and(valid, away < size - 1))
+            def _(side=side, index=index):
+                back_copy(side, index).start()
+
+        return 0
+
+    lax.fori_loop(0, chunks + 2 * LAG * (size - 1), step, 0)
+
+    def finish(index, _):
+        for side in (0, 1):
+            hops = lines[side][0]
+
+            @pl.when(hops < size - 1)
+            def _(side=side):
+                sum_copy(side, index, passed).wait_send()
+
+            @pl.when(hops > 0)
+            def _(side=side):
+                back_copy(side, index).wait_send()
+
+        return 0
+
+    lax.fori_loop(0, chunks, finish, 0)
+
+
+def line_exchange(transform, mesh_axes, collective, part, extras, extra_shapes, name):
+    tokens, width = part.shape
+    chunks = tokens // 2 // CHUNK
+    whole = pl.BlockSpec(memory_space=pltpu.VMEM)
+    return pl.pallas_call(
+        partial(
+            line_exchange_kernel, transform, mesh_axes, len(extras), len(extra_shapes)
+        ),
+        in_specs=[whole] * (1 + len(extras)),
+        out_specs=[whole] * (1 + len(extra_shapes)),
+        out_shape=[jax.ShapeDtypeStruct((tokens, width), BF16)] + list(extra_shapes),
+        scratch_shapes=[
+            pltpu.VMEM((tokens, width), BF16),
+            pltpu.VMEM((tokens, width), BF16),
+            pltpu.SemaphoreType.DMA((2, chunks)),
+            pltpu.SemaphoreType.DMA((2, chunks)),
+            pltpu.SemaphoreType.DMA((2, chunks)),
+            pltpu.SemaphoreType.DMA((2, chunks)),
+        ],
+        compiler_params=pltpu.CompilerParams(
+            collective_id=collective, has_side_effects=True, vmem_limit_bytes=52 << 20
+        ),
+        cost_estimate=pl.CostEstimate(
+            flops=tokens * width * 8, bytes_accessed=360_000_000, transcendentals=0
+        ),
+        name=name,
+    )(part, *extras)
+
+
+def inverse_rms(values):
+    return lax.rsqrt(jnp.mean(values * values, axis=-1, keepdims=True) + EPSILON)
+
+
+def residual_norm(total, rows, own, extra_in, out, extra_out):
+    hidden, gain = extra_in
+    if total is None:
+        return
+    residual = hidden[rows].astype(F32) + total
+    extra_out[0][own] = residual
+    out[rows] = (residual * inverse_rms(residual) * gain[...]).astype(BF16)
+
+
+def residual_out(total, rows, own, extra_in, out, extra_out):
+    if total is None:
+        return
+    out[rows] = (extra_in[0][own] + total).astype(BF16)
+
+
+def norm_two_back(total, rows, own, extra_in, out, extra_out):
+    residual_ref, cotangent_ref, gain = extra_in
+    grad_ref, gain_grad = extra_out
+    if total is None:
+        gain_grad[...] = jnp.zeros_like(gain_grad)
+        return
+    residual = residual_ref[own]
+    inverse = inverse_rms(residual)
+    unit = residual * inverse
+    gain_grad[...] += jnp.sum(total * unit, axis=0, keepdims=True)
+    lifted = total * gain[...]
+    mean = jnp.mean(lifted * unit, axis=-1, keepdims=True)
+    grad = cotangent_ref[rows].astype(F32) + inverse * (lifted - unit * mean)
+    grad_ref[own] = grad
+    out[rows] = grad.astype(BF16)
+
+
+def norm_one_back(total, rows, own, extra_in, out, extra_out):
+    hidden, residual_grad, gain = extra_in
+    gain_grad = extra_out[0]
+    if total is None:
+        gain_grad[...] = jnp.zeros_like(gain_grad)
+        return
+    values = hidden[rows].astype(F32)
+    inverse = inverse_rms(values)
+    unit = values * inverse
+    gain_grad[...] += jnp.sum(total * unit, axis=0, keepdims=True)
+    lifted = total * gain[...]
+    mean = jnp.mean(lifted * unit, axis=-1, keepdims=True)
+    grad = residual_grad[own] + inverse * (lifted - unit * mean)
+    out[rows] = grad.astype(BF16)
 
 
 def rms_parts(values):
@@ -524,6 +725,7 @@
 
 
 def local(
+    mesh_axes,
     hidden,
     segment_ids,
     norm1_gain,
@@ -553,12 +755,9 @@
     gate_full = lax.all_gather(w_ffn_gate, both, axis=0, tiled=True)
     up_full = lax.all_gather(w_ffn_up, both, axis=0, tiled=True)
     down_full = lax.all_gather(w_ffn_down, both, axis=1, tiled=True)
-    part_rows = tokens // lax.axis_size("tensor")
-    place = lax.axis_index("tensor") * part_rows
-
-    def own_rows(values):
-        return lax.dynamic_slice_in_dim(values, place, part_rows, 0)
-
+    gain_one, gain_two = norm1_gain.reshape(1, -1), norm2_gain.reshape(1, -1)
+    half_wide = jax.ShapeDtypeStruct((tokens // 2, model_width), F32)
+    one_row = jax.ShapeDtypeStruct((1, model_width), F32)
     hidden_rows = hidden.reshape(tokens, model_width)
     unit_rows, _ = rms_parts(hidden_rows.astype(F32))
     normed_one = (unit_rows * norm1_gain).astype(BF16)
@@ -575,18 +774,19 @@
     mixed, gated_low = gate_forward(
         mixed_local, lead, carry.astype(BF16), pre, gain_row, keep, key_scale
     )
-    mix_part = jnp.dot(gated_low, out_full, preferred_element_type=F32)
-    inputs_own = own_rows(hidden_rows).astype(F32)
-    residual = inputs_own + scatter_sum(mix_part)
-    unit_two, inverse_two = rms_parts(residual)
-    normed_two = gather_rows((unit_two * norm2_gain).astype(BF16))
+    mix_part = jnp.dot(gated_low, out_full, preferred_element_type=F32).astype(BF16)
+    normed_two, residual = line_exchange(
+        residual_norm, mesh_axes, 0, mix_part, (hidden_rows, gain_two), [half_wide], "mix_line"
+    )
     gate_ffn = jnp.dot(normed_two, gate_full, preferred_element_type=F32)
     up_ffn = jnp.dot(normed_two, up_full, preferred_element_type=F32)
     sigma_gate = jax.nn.sigmoid(gate_ffn)
     active = gate_ffn * sigma_gate
     hidden_low = (active * up_ffn).astype(BF16)
-    feed_part = jnp.dot(hidden_low, down_full, preferred_element_type=F32)
-    output_rows = gather_rows((residual + scatter_sum(feed_part)).astype(BF16))
+    feed_part = jnp.dot(hidden_low, down_full, preferred_element_type=F32).astype(BF16)
+    (output_rows,) = line_exchange(
+        residual_out, mesh_axes, 1, feed_part, (residual,), [], "feed_line"
+    )
     grad_rows = out_grad.reshape(tokens, model_width)
     grad_down = jnp.einsum("tf,td->fd", hidden_low, grad_rows, preferred_element_type=F32)
     grad_hidden = jnp.einsum("td,fd->tf", grad_rows, down_full, preferred_element_type=F32)
@@ -600,14 +800,15 @@
     back_two = back_two + jnp.einsum(
         "tf,df->td", grad_up_low, up_full, preferred_element_type=F32
     )
-    grad_normed_two = scatter_sum(back_two)
-    cotangent_rows = own_rows(grad_rows).astype(F32)
-    grad_norm_two = jnp.sum(grad_normed_two * unit_two, axis=0)
-    lifted_two = grad_normed_two * norm2_gain
-    grad_residual = cotangent_rows + inverse_two * (
-        lifted_two - unit_two * jnp.mean(lifted_two * unit_two, axis=-1, keepdims=True)
-    )
-    grad_mix_low = gather_rows(grad_residual.astype(BF16))
+    grad_mix_low, grad_residual, grad_norm_two = line_exchange(
+        norm_two_back,
+        mesh_axes,
+        2,
+        back_two.astype(BF16),
+        (residual, grad_rows, gain_two),
+        [half_wide, one_row],
+        "norm_two_line",
+    )
     grad_out = jnp.einsum("tv,td->vd", gated_low, grad_mix_low, preferred_element_type=F32)
     grad_gated = jnp.einsum("td,vd->tv", grad_mix_low, out_full, preferred_element_type=F32)
     grad_mixed, grad_gate_pre, grad_head_part, back = gate_backward(
@@ -629,17 +830,19 @@
     )
     grad_mixer = jnp.einsum("td,tk->dk", normed_one, grad_pre, preferred_element_type=F32)
     back_one = jnp.einsum("tk,dk->td", grad_pre, mixer_full, preferred_element_type=F32)
-    grad_normed_one = scatter_sum(back_one)
-    unit_one, inverse_one = rms_parts(inputs_own)
-    grad_norm_one = jnp.sum(grad_normed_one * unit_one, axis=0)
+    input_rows, grad_norm_one = line_exchange(
+        norm_one_back,
+        mesh_axes,
+        3,
+        back_one.astype(BF16),
+        (hidden_rows, grad_residual, gain_one),
+        [one_row],
+        "norm_one_line",
+    )
     grad_norm_one, grad_norm_two, head_total = lax.psum(
-        (grad_norm_one, grad_norm_two, grad_head_part.reshape(-1)), "tensor"
-    )
-    lifted_one = grad_normed_one * norm1_gain
-    grad_inputs = grad_residual + inverse_one * (
-        lifted_one - unit_one * jnp.mean(lifted_one * unit_one, axis=-1, keepdims=True)
-    )
-    input_rows = gather_rows(grad_inputs.astype(BF16))
+        (grad_norm_one.reshape(-1), grad_norm_two.reshape(-1), grad_head_part.reshape(-1)),
+        "tensor",
+    )
 
     def share(values, dim):
         return lax.psum_scatter(
@@ -699,4 +902,5 @@
         P(("shard", "context"), "tensor"),
         P("tensor", ("shard", "context")),
     )
-    return jax.shard_map(local, mesh=mesh, in_specs=in_specs, out_specs=out_specs, check_vma=False)
+    return jax.shard_map(
+        partial(local, mesh.axis_names), mesh=mesh, in_specs=in_specs, out_specs=out_specs, check_vma=False)

time: 1330 us -> 811 us (0.61)
  waiting for transfers between devices: 1020 us -> 53.3 us
  Pallas kernels: 34.4 us -> 496 us
  other arithmetic: 38.7 us -> 16.6 us
    pallas_call x0 -> x4, Pallas kernels: none -> 461 us  [line_exchange(): pl.pallas_call(partial(line_exchange_kernel, transform, mesh_axes, len(ex...]
    all_gather x4 -> x0, waiting for transfers between devices: 326 us -> none  [gather_rows(): return lax.all_gather(values, 'tensor', axis=0, tiled=True)]
    reduce_scatter x5, waiting for transfers between devices: 259 us -> 0.01 us  [share(): lax.psum_scatter(values.astype(BF16), both, scatter_dimension=dim, tiled=...]
    reduce_scatter x4 -> x0, waiting for transfers between devices: 241 us -> none  [scatter_sum(): lax.psum_scatter(values.astype(jnp.bfloat16), 'tensor', scatter_dimension...]
    all_gather x1, waiting for transfers between devices: 39 us -> 0.02 us  [local(): gate_full = lax.all_gather(w_ffn_gate, both, axis=0, tiled=True)]
    all_gather x1, waiting for transfers between devices: 34.8 us -> 0.01 us  [local(): down_full = lax.all_gather(w_ffn_down, both, axis=1, tiled=True)]
    unnamed x20 -> x12, waiting for transfers between devices: 36 us -> 2.55 us
    all_gather x1, waiting for transfers between devices: 32.1 us -> 0.01 us  [local(): up_full = lax.all_gather(w_ffn_up, both, axis=0, tiled=True)]
  transfers between devices with their start and end apart: 21 -> 13, of which waited for: 20 -> 3; matrix products, arithmetic and copies ran while one was open for 11% -> 18% of each run, Pallas kernels for 1% -> 45%
where the time goes in v3:
time: 811 us; the launch traced here: 804 us
  Pallas kernels  496 us (61%)
  matrix products  161 us (20%)
  waiting for transfers between devices  53.3 us (7%)
  blocking collectives  31.2 us (4%)
  local copies, waits for them, and re-layouts  23.8 us (3%)
  between operations  18.6 us (2%)
  other arithmetic  16.6 us (2%)
    pallas_call x4, Pallas kernels, line_exchange(): pl.pallas_call(partial(line_exchange_kernel, transform, mesh_axes, len(ex...  461 us
    all_gather x1, waiting for transfers between devices, local(): lax.all_gather(jnp.concatenate([w_query, w_forget, w_input, w_gate_out],...  47.4 us
    psum x1, blocking collectives, local(): lax.psum((grad_norm_one.reshape(-1), grad_norm_two.reshape(-1), grad_head...  18.4 us
    unnamed x45, local copies, waits for them, and re-layouts  16.8 us
  transfers between devices with their start and end apart: 13, of which 3 were waited for; matrix products, arithmetic and copies ran while one was open for 18% of the time, Pallas kernels for 45%

profile of v3, /device:TPU:0, one launch (start us, length us, event | category | flops | bytes accessed | tf_op | source)
XLA Modules:
  0.0 803.8 jit_solution(15388053923145640087)
XLA Ops:
  7.2 2.3 pad_maximum_fusion
  15.0 1.4 stack.11
  17.1 3.1 fusion
  20.2 47.4 %all-gather.6.cloned.1.call-done = bf16[2048,2048]{1,0:T(8,128)(2,1)} async-done(((bf16[256,2048]{1,0:T(8,128)(2,1)}), bf16[2048,2048]{1,0:T(8,128)(2,1)}) %all-gather.6.cloned.1.call-update) | async-done | bytes 8388624 | tf_op jit(solution)/shard_map/all_gather | solution.py:751
  67.6 14.5 %fusion.5.pre_ref.gate_ref = f32[1024,2048]{1,0:T(8,128)} fusion(bf16[2048,2048]{1,0:T(8,128)(2,1)} %all-gather.6.cloned.1.call-done, f32[2048]{0:T(1024)S(1)} %copy-done.5, f32[1024]{0:T(1024)S(1)} %add_rsqrt_fusion, bf16[1,1024,2048]{2,1,0:T(8,128)(2,1)} %param.15), kind=kOutput, calls=%fused_computation.21 | convolution fusion | flops 8598323200 | bytes 20983808 | tf_op jit(solution)/shard_map/dot_general | solution.py:764
  82.2 9.7 %mixer_forward.1 = (f32[1024,512]{1,0:T(8,128)S(1)}, bf16[1024,512]{1,0:T(8,128)(2,1)S(1)}, f32[8,4,128,128]{3,2,1,0:T(8,128)S(1)}, f32[8,1,512]{2,1,0:T(1,128)S...) custom-call(f32[1024,2048]{1,0:T(8,128)} %fusion.5.pre_ref.gate_ref, f32[1,512]{1,0:T(1,128)S(1)} %bitcast.77, ...), custom_call_target="tpu_custom_call" | custom-call | flops 805306368 | bytes 15728640 | tf_op jit(solution)/shard_map/mixer_forward/pallas_call | solution.py:115
  91.8 1.4 copy-done
  93.3 2.2 collective-permute-start
  95.6 1.1 collective-permute-done
  99.2 4.1 gate_forward.1
  103.4 1.3 copy-done.2
  104.7 6.0 convolution_convert_fusion.6.refs_0_
  110.7 116.8 %mix_line.1 = (bf16[1024,2048]{1,0:T(8,128)(2,1)}, f32[512,2048]{1,0:T(8,128)}) custom-call(bf16[1024,2048]{1,0:T(8,128)(2,1)} %convolution_convert_fusion.6.refs_0_, bf16[1024,2048]{1,0:T(8,128)(2,1)} %bitcast.85, f32[1,2048]{1,0:T(1,128)S(1)} %bitcast.75), custom_call_target="tpu_custom_call" | custom-call | flops 16777216 | bytes 360000000 | tf_op jit(solution)/shard_map/mix_line/pallas_call | solution.py:645
  227.5 11.7 %fusion.16 = f32[1024,1408]{1,0:T(8,128)} fusion(bf16[1024,2048]{1,0:T(8,128)(2,1)} %get-tuple-element.40, bf16[2048,1408]{1,0:T(8,128)(2,1)} %all-gather.10.cloned.1.call-done), kind=kOutput, calls=%fused_computation.48 | convolution fusion | flops 5905580032 | bytes 15728640 | tf_op jit(solution)/shard_map/dot_general | solution.py:781
  239.2 11.6 %fusion.17 = f32[1024,1408]{1,0:T(8,128)} fusion(bf16[1024,2048]{1,0:T(8,128)(2,1)} %get-tuple-element.40, bf16[2048,1408]{1,0:T(8,128)(2,1)} %all-gather.12.cloned.1.call-done), kind=kOutput, calls=%fused_computation.49 | convolution fusion | flops 5905580032 | bytes 15728640 | tf_op jit(solution)/shard_map/dot_general | solution.py:782
  250.8 15.6 %multiply_convert_fusion = (bf16[1024,1408]{1,0:T(8,128)(2,1)S(1)}, bf16[1024,1408]{1,0:T(8,128)(2,1)S(1)}, bf16[1024,1408]{1,0:T(8,128)(2,1)}) fusion(f32[1024,1408]{1,0:T(8,128)} %fusion.16, f32[1024,1408]{1,0:T(8,128)} %fusion.17, bf16[1408,2048]{1,0:T(8,128)(2,1)} %all-gather.14.cloned.1.call-done, bf16[1,1024,2048]{2,1,0:T(8,128)(2,1)} %param.29), kind=kOutput, calls=%fused_computation.10 | convolution fusion | flops 5927206912 | bytes 30146560 | tf_op jit(solution)/shard_map/td,fd->tf/dot_general | solution.py:792
  266.4 10.9 %fusion.18 = f32[1024,2048]{1,0:T(8,128)S(1)} fusion(bf16[1024,1408]{1,0:T(8,128)(2,1)S(1)} %get-tuple-element.63, bf16[2048,1408]{1,0:T(8,128)(2,1)} %all-gather.10.cloned.1.call-done), kind=kOutput, calls=%fused_computation.50 | convolution fusion | flops 5905580032 | bytes 17039360 | tf_op jit(solution)/shard_map/tf,df->td/dot_general | solution.py:799
  277.3 8.4 %add_convert_fusion.refs_0_ = bf16[1024,2048]{1,0:T(8,128)(2,1)} fusion(f32[1024,2048]{1,0:T(8,128)S(1)} %fusion.18, bf16[1024,1408]{1,0:T(8,128)(2,1)S(1)} %get-tuple-element.62, bf16[2048,1408]{1,0:T(8,128)(2,1)S(1)} %copy-done.13), kind=kOutput, calls=%fused_computation.5 | convolution fusion | flops 5909774336 | bytes 21233664 | tf_op jit(solution)/shard_map/tf,df->td/dot_general | solution.py:800
  285.7 115.6 %norm_two_line.1 = (bf16[1024,2048]{1,0:T(8,128)(2,1)}, f32[512,2048]{1,0:T(8,128)}, f32[1,2048]{1,0:T(1,128)S(1)}) custom-call(bf16[1024,2048]{1,0:T(8,128)(2,1)} %add_convert_fusion.refs_0_, f32[512,2048]{1,0:T(8,128)} %get-tuple-element.41.refs_1_, bf16[1024,2048]{1,0:T(8,128)(2,1)} %bitcast.89, f32[1,2048]{1,0:T(1,128)S(1)} %bitcast.76), custom_call_target="tpu_custom_call" | custom-call | flops 16777216 | bytes 360000000 | tf_op jit(solution)/shard_map/norm_two_line/pallas_call | solution.py:645
  401.4 4.7 fusion.19.grad_ref
  406.1 6.2 gate_backward.1
  412.4 1.3 collective-permute-start.1
  413.7 2.1 collective-permute-done.1
  415.8 14.6 %mixer_backward.1 = (bf16[1024,2048]{1,0:T(8,128)(2,1)S(1)}, f32[1,512]{1,0:T(1,128)S(1)}) custom-call(f32[1024,2048]{1,0:T(8,128)} %fusion.5.pre_ref.gate_ref, bf16[1024,512]{1,0:T(8,128)(2,1)S(1)} %get-tuple-element.44.grad_mixed_ref, bf16[1024,512]{1,0:T(8,128)(2,1)S(1)} %get-tuple-element.45.grad_gate_ref, f32[8,4,128,128]{3,2,1,0:T(8,128)S(1)} %copy-done.1, ...), custom_call_target="tpu_custom_call" | custom-call | flops 2013265920 | bytes 18874368 | tf_op jit(solution)/shard_map/mixer_backward/pallas_call | solution.py:392
  430.4 2.0 copy-done.7
  432.5 0.7 copy.47
  433.3 5.9 convolution_convert_fusion.7
  439.3 11.2 %convolution_convert_fusion.2 = bf16[2048,1408]{1,0:T(8,128)(2,1)} fusion(bf16[1024,2048]{1,0:T(8,128)(2,1)} %get-tuple-element.40, bf16[1024,1408]{1,0:T(8,128)(2,1)} %copy-done.17), kind=kOutput, calls=%fused_computation.8 | convolution fusion | flops 5908463616 | bytes 12845056 | tf_op jit(solution)/shard_map/td,tf->df/dot_general | solution.py:797
  450.6 1.8 copy-done.19
  452.3 10.9 %convolution_convert_fusion.1 = bf16[2048,1408]{1,0:T(8,128)(2,1)} fusion(bf16[1024,2048]{1,0:T(8,128)(2,1)} %get-tuple-element.40, bf16[1024,1408]{1,0:T(8,128)(2,1)S(1)} %copy-done.19), kind=kOutput, calls=%fused_computation.7 | convolution fusion | flops 5908463616 | bytes 12845056 | tf_op jit(solution)/shard_map/td,tf->df/dot_general | solution.py:798
  463.3 1.8 copy-done.16
  465.0 10.7 %convolution_convert_fusion = bf16[1408,2048]{1,0:T(8,128)(2,1)} fusion(bf16[1024,1408]{1,0:T(8,128)(2,1)S(1)} %copy-done.16, bf16[1,1024,2048]{2,1,0:T(8,128)(2,1)} %param.29), kind=kOutput, calls=%fused_computation.6 | convolution fusion | flops 5908463616 | bytes 12845056 | tf_op jit(solution)/shard_map/tf,td->fd/dot_general | solution.py:791
  475.8 14.9 %convolution_convert_fusion.3 = bf16[2048,2048]{1,0:T(8,128)(2,1)} fusion(bf16[1024,2048]{1,0:T(8,128)(2,1)} %copy-done.7, f32[2048]{0:T(1024)S(1)} %copy-done.5, f32[1024]{0:T(1024)S(1)} %add_rsqrt_fusion, bf16[1,1024,2048]{2,1,0:T(8,128)(2,1)} %param.15), kind=kOutput, calls=%fused_computation.9 | convolution fusion | flops 8602517504 | bytes 16789504 | tf_op jit(solution)/shard_map/td,tk->dk/dot_general | solution.py:831
  493.2 11.1 %convolution_convert_fusion.5.refs_0_ = bf16[1024,2048]{1,0:T(8,128)(2,1)} fusion(bf16[1024,1408]{1,0:T(8,128)(2,1)S(1)} %copy-done.16, bf16[1408,2048]{1,0:T(8,128)(2,1)} %all-gather.14.cloned.1.call-done), kind=kOutput, calls=%fused_computation.18 | convolution fusion | flops 5907677184 | bytes 12845056 | tf_op jit(solution)/shard_map/dot_general | solution.py:786
  504.3 114.4 %feed_line.1 = bf16[1024,2048]{1,0:T(8,128)(2,1)} custom-call(bf16[1024,2048]{1,0:T(8,128)(2,1)} %convolution_convert_fusion.5.refs_0_, f32[512,2048]{1,0:T(8,128)} %get-tuple-element.41.refs_1_), custom_call_target="tpu_custom_call" | custom-call | flops 16777216 | bytes 360000000 | tf_op jit(solution)/shard_map/feed_line/pallas_call | solution.py:645
  618.7 12.6 %convolution_convert_fusion.4.refs_0_ = bf16[1024,2048]{1,0:T(8,128)(2,1)} fusion(bf16[1024,2048]{1,0:T(8,128)(2,1)S(1)} %copy-done.8, bf16[2048,2048]{1,0:T(8,128)(2,1)} %all-gather.6.cloned.1.call-done), kind=kOutput, calls=%fused_computation.17 | convolution fusion | flops 8592031744 | bytes 16777216 | tf_op jit(solution)/shard_map/tk,dk->td/dot_general | solution.py:832
  631.3 114.3 %norm_one_line.1 = (bf16[1024,2048]{1,0:T(8,128)(2,1)}, f32[1,2048]{1,0:T(1,128)S(1)}) custom-call(bf16[1024,2048]{1,0:T(8,128)(2,1)} %convolution_convert_fusion.4.refs_0_, bf16[1024,2048]{1,0:T(8,128)(2,1)} %bitcast.86, f32[512,2048]{1,0:T(8,128)} %get-tuple-element.50.refs_2_, f32[1,2048]{1,0:T(1,128)S(1)} %bitcast.81), custom_call_target="tpu_custom_call" | custom-call | flops 16777216 | bytes 360000000 | tf_op jit(solution)/shard_map/norm_one_line/pallas_call | solution.py:645
  745.6 18.4 %all-reduce.4 = (bf16[2048]{0:T(1024)(128)(2,1)S(1)}, bf16[128]{0:T(256)(128)(2,1)S(1)}, bf16[2048]{0:T(1024)(128)(2,1)S(1)}) all-reduce(f32[2048]{0:T(1024)S(1)} %bitcast.80, f32[128]{0:T(128)S(1)} %bitcast.84, f32[2048]{0:T(1024)S(1)} %bitcast.79), channel_id=1, replica_groups=mesh['shard'=4,'context'=2,'tensor'=4] {'tensor'}, use_global_device_ids=true, to_apply=%region_2.3 | all-reduce | flops 4224 | bytes 25344 | tf_op jit(solution)/shard_map/psum | solution.py:842
  764.1 12.8 %all-reduce.5 = (bf16[2048]{0:T(1024)(128)(2,1)S(1)}, bf16[128]{0:T(256)(128)(2,1)S(1)}, bf16[2048]{0:T(1024)(128)(2,1)S(1)}) all-reduce(bf16[2048]{0:T(1024)(128)(2,1)S(1)} %get-tuple-element.56, bf16[128]{0:T(256)(128)(2,1)S(1)} %get-tuple-element.57, ...), channel_id=2, replica_groups=mesh['shard'=4,'context'=2,'tensor'=4] {'shard','context'}, use_global_device_ids=true, to_apply=%region_3.4.clone | all-reduce | flops 4224 | bytes 16896
  778.1 0.8 copy.48
  779.5 1.8 convert_element_type.143
  781.2 2.3 convert_element_type.147
  783.5 2.3 convert_element_type.149
  785.8 2.3 convert_element_type.151
  788.2 2.8 fusion.13
  791.1 2.1 copy.51
  793.2 1.6 copy-done.10
  794.8 2.0 copy.52
  (100 shorter events, 9.8 us)
Async XLA Ops:
  7.2 5.1 copy-start.11
  7.2 9.9 %copy-start.12 = (f32[4,128]{1,0:T(4,128)S(1)}, f32[4,128]{1,0:T(4,128)}, u32[]{:S(2)}) copy-start(f32[4,128]{1,0:T(4,128)} %param.22) | copy-start | bytes 6148
  7.2 60.4 %all-gather.6.cloned.1.call-start = ((), (), s32[]{:S(2)}) async-start(), calls=%async_computation.6 | async-start | bytes 9437184 | tf_op jit(solution)/shard_map/all_gather | solution.py:751
  9.6 58.1 %copy-start.5 = (f32[2048]{0:T(1024)S(1)}, f32[2048]{0:T(1024)}, u32[]{:S(2)}) copy-start(f32[2048]{0:T(1024)} %param.17) | copy-start | bytes 24580
  9.6 95.1 %all-gather.8.cloned.1.call-start = ((), (), s32[]{:S(2)}) async-start(), calls=%async_computation.7 | async-start | bytes 2359296 | tf_op jit(solution)/shard_map/all_gather | solution.py:754
  10.3 217.2 %all-gather.10.cloned.1.call-start = ((), (), s32[]{:S(2)}) async-start(), calls=%async_computation.8 | async-start | bytes 6488064 | tf_op jit(solution)/shard_map/all_gather | solution.py:755
  11.1 228.1 %all-gather.12.cloned.1.call-start = ((), (), s32[]{:S(2)}) async-start(), calls=%async_computation.9 | async-start | bytes 6488064 | tf_op jit(solution)/shard_map/all_gather | solution.py:756
  11.6 239.2 %all-gather.14.cloned.1.call-start = ((), (), s32[]{:S(2)}) async-start(), calls=%async_computation.10 | async-start | bytes 6488064 | tf_op jit(solution)/shard_map/all_gather | solution.py:757
  12.2 765.9 %reduce-scatter.19.cloned.1.call-start = ((), (), s32[]{:S(2)}) async-start(), calls=%async_computation.16 | async-start | bytes 36864
  82.2 17.1 %copy-start.6 = (f32[128]{0:T(128)S(1)}, f32[128]{0:T(128)}, u32[]{:S(2)}) copy-start(f32[128]{0:T(128)} %param.23) | copy-start | bytes 1540
  91.8 1.4 copy-start
  93.3 3.4 collective-permute-start
  103.3 1.3 copy-start.2
  104.7 6.0 copy-start.4
  266.4 10.9 %copy-start.17 = (bf16[1024,1408]{1,0:T(8,128)(2,1)}, bf16[1024,1408]{1,0:T(8,128)(2,1)S(1)}, u32[]{:S(2)}) copy-start(bf16[1024,1408]{1,0:T(8,128)(2,1)S(1)} %get-tuple-element.63) | copy-start | bytes 8650756
  266.4 10.9 %copy-start.18 = (bf16[1024,1408]{1,0:T(8,128)(2,1)}, bf16[1024,1408]{1,0:T(8,128)(2,1)S(1)}, u32[]{:S(2)}) copy-start(bf16[1024,1408]{1,0:T(8,128)(2,1)S(1)} %get-tuple-element.62) | copy-start | bytes 8650756
  266.4 10.9 %copy-start.13 = (bf16[2048,1408]{1,0:T(8,128)(2,1)S(1)}, bf16[2048,1408]{1,0:T(8,128)(2,1)}, u32[]{:S(2)}) copy-start(bf16[2048,1408]{1,0:T(8,128)(2,1)} %all-gather.12.cloned.1.call-done) | copy-start | bytes 17301508
  285.7 115.6 %copy-start.14 = (bf16[512,2048]{1,0:T(8,128)(2,1)S(1)}, bf16[512,2048]{1,0:T(8,128)(2,1)}, u32[]{:S(2)}) copy-start(bf16[512,2048]{1,0:T(8,128)(2,1)} %all-gather.8.cloned.1.call-done) | copy-start | bytes 6291460
  401.4 4.7 copy-start.3
  406.1 9.7 %copy-start.1 = (f32[8,4,128,128]{3,2,1,0:T(8,128)S(1)}, f32[8,4,128,128]{3,2,1,0:T(8,128)}, u32[]{:S(2)}) copy-start(f32[8,4,128,128]{3,2,1,0:T(8,128)} %copy-done) | copy-start | bytes 6291460
  412.4 3.4 collective-permute-start.1
  430.4 2.0 copy-start.7
  433.2 346.2 %reduce-scatter.11.cloned.1.call-start = ((), (), s32[]{:S(2)}) async-start(), calls=%async_computation.12 | async-start | bytes 2359296 | tf_op jit(solution)/shard_map/reduce_scatter | solution.py:848
  439.2 342.0 %reduce-scatter.13.cloned.1.call-start = ((), (), s32[]{:S(2)}) async-start(), calls=%async_computation.13 | async-start | bytes 6488064 | tf_op jit(solution)/shard_map/reduce_scatter | solution.py:848
  450.5 1.8 copy-start.19
  450.5 333.0 %reduce-scatter.15.cloned.1.call-start = ((), (), s32[]{:S(2)}) async-start(), calls=%async_computation.14 | async-start | bytes 6488064 | tf_op jit(solution)/shard_map/reduce_scatter | solution.py:848
  463.2 1.8 copy-start.16
  463.2 322.6 %reduce-scatter.17.cloned.1.call-start = ((), (), s32[]{:S(2)}) async-start(), calls=%async_computation.15 | async-start | bytes 6488064 | tf_op jit(solution)/shard_map/reduce_scatter | solution.py:848
  475.7 312.4 %reduce-scatter.9.cloned.1.call-start = ((), (), s32[]{:S(2)}) async-start(), calls=%async_computation.11 | async-start | bytes 9437184 | tf_op jit(solution)/shard_map/reduce_scatter | solution.py:848
  490.7 0.7 copy-start.15
  504.3 114.4 %copy-start.8 = (bf16[1024,2048]{1,0:T(8,128)(2,1)S(1)}, bf16[1024,2048]{1,0:T(8,128)(2,1)}, u32[]{:S(2)}) copy-start(bf16[1024,2048]{1,0:T(8,128)(2,1)} %copy-done.7) | copy-start | bytes 12582916
  788.2 2.9 copy-start.9
  791.1 3.7 copy-start.10
Sparse Core Ops, SparseCore 0:
  10.5 57.0 all-gather.5
  69.5 28.1 all-gather.7
  99.6 43.3 all-gather.9
  144.7 43.3 all-gather.11
  189.8 44.3 all-gather.13
  433.3 30.7 reduce-scatter.18
  467.7 41.2 reduce-scatter.10
  512.5 59.0 reduce-scatter.12
  575.4 59.0 reduce-scatter.14
  637.8 59.0 reduce-scatter.16
  700.7 71.5 reduce-scatter.8

commit v4 on v2

--- a/solution.py
+++ b/solution.py
@@ -508,14 +508,436 @@
     return total
 
 
-def scatter_sum(values):
-    return lax.psum_scatter(
-        values.astype(jnp.bfloat16), "tensor", scatter_dimension=0, tiled=True
-    ).astype(jnp.float32)
-
-
-def gather_rows(values):
-    return lax.all_gather(values, "tensor", axis=0, tiled=True)
+CHUNK = 32
+LAG = 2
+MESH_ID = pl.DeviceIdType.MESH
+
+
+class Line:
+    def __init__(self, mesh_axes, part, arrived, out, sems, transform):
+        self.mesh_axes = mesh_axes
+        self.part, self.arrived, self.out = part, arrived, out
+        self.sum_send, self.sum_recv, self.back_send, self.back_recv = sems
+        self.transform = transform
+        self.half = part.shape[0] // 2
+        self.chunks = self.half // CHUNK
+        self.size = lax.axis_size("tensor")
+        self.place = lax.axis_index("tensor")
+        self.lines = ((self.size - 1 - self.place, -1), (self.place, 1))
+        self.steps = self.chunks + 2 * LAG * (self.size - 1)
+
+    def device(self, position):
+        return tuple(
+            jnp.clip(position, 0, self.size - 1) if axis == "tensor" else lax.axis_index(axis)
+            for axis in self.mesh_axes
+        )
+
+    def greet(self, barrier):
+        for step in (-1, 1):
+            inside = jnp.logical_and(self.place + step >= 0, self.place + step < self.size)
+
+            @pl.when(inside)
+            def _(step=step):
+                pl.semaphore_signal(
+                    barrier, inc=1, device_id=self.device(self.place + step), device_id_type=MESH_ID
+                )
+
+        at_end = jnp.logical_or(self.place == 0, self.place == self.size - 1)
+        return jnp.where(at_end, 1, 2)
+
+    def rows_of(self, side, index):
+        return pl.ds(pl.multiple_of(side * self.half + index * CHUNK, CHUNK), CHUNK)
+
+    def sum_copy(self, side, index, source):
+        rows = self.rows_of(side, index)
+        return pltpu.make_async_remote_copy(
+            source.at[rows],
+            self.arrived.at[rows],
+            self.sum_send.at[side, index],
+            self.sum_recv.at[side, index],
+            device_id=self.device(self.place + self.lines[side][1]),
+            device_id_type=MESH_ID,
+        )
+
+    def back_copy(self, side, index):
+        rows = self.rows_of(side, index)
+        return pltpu.make_async_remote_copy(
+            self.out.at[rows],
+            self.out.at[rows],
+            self.back_send.at[side, index],
+            self.back_recv.at[side, index],
+            device_id=self.device(self.place - self.lines[side][1]),
+            device_id_type=MESH_ID,
+        )
+
+    def step(self, time):
+        for side in (0, 1):
+            hops = self.lines[side][0]
+            index = time - LAG * hops
+            valid = jnp.logical_and(index >= 0, index < self.chunks)
+            at_source, at_owner = hops == 0, hops == self.size - 1
+            index = jnp.clip(index, 0, self.chunks - 1)
+            rows = self.rows_of(side, index)
+
+            @pl.when(jnp.logical_and(valid, at_source))
+            def _(side=side, index=index):
+                self.sum_copy(side, index, self.part).start()
+
+            @pl.when(jnp.logical_and(valid, jnp.logical_not(at_source)))
+            def _(side=side, index=index):
+                self.sum_copy(side, index, self.arrived).wait_recv()
+
+            between = jnp.logical_and(jnp.logical_not(at_source), jnp.logical_not(at_owner))
+
+            @pl.when(jnp.logical_and(valid, between))
+            def _(side=side, index=index, rows=rows):
+                total = self.part[rows].astype(F32) + self.arrived[rows].astype(F32)
+                self.arrived[rows] = total.astype(BF16)
+                self.sum_copy(side, index, self.arrived).start()
+
+            @pl.when(jnp.logical_and(valid, at_owner))
+            def _(side=side, index=index, rows=rows):
+                total = self.part[rows].astype(F32) + self.arrived[rows].astype(F32)
+                own = pl.ds(pl.multiple_of(index * CHUNK, CHUNK), CHUNK)
+                self.transform(total, rows, own)
+                self.back_copy(side, index).start()
+
+            away = self.size - 1 - hops
+            index = time - LAG * (self.size - 1 + away)
+            valid = jnp.logical_and(jnp.logical_and(index >= 0, index < self.chunks), away > 0)
+            index = jnp.clip(index, 0, self.chunks - 1)
+
+            @pl.when(valid)
+            def _(side=side, index=index):
+                self.back_copy(side, index).wait_recv()
+
+            @pl.when(jnp.logical_and(valid, away < self.size - 1))
+            def _(side=side, index=index):
+                self.back_copy(side, index).start()
+
+    def run(self, first, last):
+        def body(time, _):
+            self.step(time)
+            return 0
+
+        lax.fori_loop(first, last, body, 0)
+
+    def finish(self):
+        def body(index, _):
+            for side in (0, 1):
+                hops = self.lines[side][0]
+
+                @pl.when(hops < self.size - 1)
+                def _(side=side):
+                    self.sum_copy(side, index, self.arrived).wait_send()
+
+                @pl.when(hops > 0)
+                def _(side=side):
+                    self.back_copy(side, index).wait_send()
+
+            return 0
+
+        lax.fori_loop(0, self.chunks, body, 0)
+
+
+def line_sems(tokens):
+    return [pltpu.SemaphoreType.DMA((2, tokens // 2 // CHUNK))] * 4
+
+
+def line_exchange_kernel(transform, mesh_axes, n_in, n_out, *refs):
+    part, extra_in = refs[0], refs[1 : 1 + n_in]
+    out, extra_out = refs[1 + n_in], refs[2 + n_in : 2 + n_in + n_out]
+    arrived, *sems = refs[2 + n_in + n_out :]
+    if transform is norm_one_back:
+        extra_out[0][...] = jnp.zeros_like(extra_out[0])
+
+    def turn(total, rows, own):
+        transform(total, rows, own, extra_in, out, extra_out)
+
+    line = Line(mesh_axes, part, arrived, out, sems, turn)
+    barrier = pltpu.get_barrier_semaphore()
+    pl.semaphore_wait(barrier, line.greet(barrier))
+    line.run(0, line.steps)
+    line.finish()
+
+
+def line_exchange(transform, mesh_axes, collective, part, extras, extra_shapes, name):
+    tokens, width = part.shape
+    whole = pl.BlockSpec(memory_space=pltpu.VMEM)
+    return pl.pallas_call(
+        partial(line_exchange_kernel, transform, mesh_axes, len(extras), len(extra_shapes)),
+        in_specs=[whole] * (1 + len(extras)),
+        out_specs=[whole] * (1 + len(extra_shapes)),
+        out_shape=[jax.ShapeDtypeStruct((tokens, width), BF16)] + list(extra_shapes),
+        scratch_shapes=[pltpu.VMEM((tokens, width), BF16)] + line_sems(tokens),
+        compiler_params=pltpu.CompilerParams(
+            collective_id=collective, has_side_effects=True, vmem_limit_bytes=52 << 20
+        ),
+        cost_estimate=pl.CostEstimate(
+            flops=tokens * width * 8, bytes_accessed=360_000_000, transcendentals=0
+        ),
+        name=name,
+    )(part, *extras)
+
+
+def inverse_rms(values):
+    return lax.rsqrt(jnp.mean(values * values, axis=-1, keepdims=True) + EPSILON)
+
+
+def residual_norm(total, rows, own, extra_in, out, extra_out):
+    hidden, gain = extra_in
+    residual = hidden[rows].astype(F32) + total
+    extra_out[0][own] = residual
+    out[rows] = (residual * inverse_rms(residual) * gain[...]).astype(BF16)
+
+
+def residual_out(total, rows, own, extra_in, out, extra_out):
+    out[rows] = (extra_in[0][own] + total).astype(BF16)
+
+
+def norm_one_back(total, rows, own, extra_in, out, extra_out):
+    hidden, residual_grad, gain = extra_in
+    gain_grad = extra_out[0]
+    values = hidden[rows].astype(F32)
+    inverse = inverse_rms(values)
+    unit = values * inverse
+    gain_grad[...] += jnp.sum(total * unit, axis=0, keepdims=True)
+    lifted = total * gain[...]
+    mean = jnp.mean(lifted * unit, axis=-1, keepdims=True)
+    grad = residual_grad[own] + inverse * (lifted - unit * mean)
+    out[rows] = grad.astype(BF16)
+
+
+GROUP = 128
+TILE = 256
+
+
+def feed_kernel(
+    mesh_axes,
+    normed_ref,
+    cotangent_ref,
+    residual_hbm,
+    gain_ref,
+    gate_hbm,
+    up_hbm,
+    down_hbm,
+    out_ref,
+    gain_grad,
+    hidden_hbm,
+    grad_gate_hbm,
+    grad_up_hbm,
+    feed_hbm,
+    grad_hbm,
+    gate_w,
+    up_w,
+    down_w,
+    part,
+    arrived,
+    residual,
+    stage_hidden,
+    stage_gate,
+    stage_up,
+    stage_feed,
+    weight_sem,
+    residual_sem,
+    stage_sem,
+    grad_sem,
+    *sems,
+):
+    tokens, model_width = normed_ref.shape
+    half = tokens // 2
+    hidden_width = gate_hbm.shape[1]
+    padded = gate_w.shape[1]
+    groups = half // GROUP
+    loads = [
+        pltpu.make_async_copy(gate_hbm, gate_w.at[:, pl.ds(0, hidden_width)], weight_sem.at[0]),
+        pltpu.make_async_copy(up_hbm, up_w.at[:, pl.ds(0, hidden_width)], weight_sem.at[1]),
+        pltpu.make_async_copy(down_hbm, down_w.at[pl.ds(0, hidden_width)], weight_sem.at[2]),
+    ]
+    for load in loads:
+        load.start()
+    residual_load = pltpu.make_async_copy(residual_hbm, residual, residual_sem.at[0])
+    residual_load.start()
+    if padded > hidden_width:
+        spare = slice(hidden_width, padded)
+        gate_w[:, spare] = jnp.zeros((model_width, padded - hidden_width), BF16)
+        up_w[:, spare] = jnp.zeros((model_width, padded - hidden_width), BF16)
+        down_w[spare, :] = jnp.zeros((padded - hidden_width, model_width), BF16)
+    gain_grad[...] = jnp.zeros_like(gain_grad)
+
+    def turn(total, rows, own):
+        values = residual[own]
+        inverse = inverse_rms(values)
+        unit = values * inverse
+        gain_grad[...] += jnp.sum(total * unit, axis=0, keepdims=True)
+        lifted = total * gain_ref[...]
+        mean = jnp.mean(lifted * unit, axis=-1, keepdims=True)
+        grad = cotangent_ref[rows].astype(F32) + inverse * (lifted - unit * mean)
+        residual[own] = grad
+        out_ref[rows] = grad.astype(BF16)
+
+    line = Line(mesh_axes, part, arrived, out_ref, sems, turn)
+    barrier = pltpu.get_barrier_semaphore()
+    pl.semaphore_wait(barrier, line.greet(barrier))
+    residual_load.wait()
+    for load in loads:
+        load.wait()
+
+    def both(ref, group):
+        first = pl.ds(pl.multiple_of(group * GROUP, GROUP), GROUP)
+        second = pl.ds(pl.multiple_of(half + group * GROUP, GROUP), GROUP)
+        return first, second
+
+    def stage_copies(group):
+        slot = lax.rem(group, 2)
+        copies = []
+        for side, rows in enumerate(both(None, group)):
+            from_rows = pl.ds(side * GROUP, GROUP)
+            columns = pl.ds(0, hidden_width)
+            for which, (stage, target) in enumerate(
+                (
+                    (stage_hidden, hidden_hbm),
+                    (stage_gate, grad_gate_hbm),
+                    (stage_up, grad_up_hbm),
+                )
+            ):
+                copies.append(
+                    pltpu.make_async_copy(
+                        stage.at[slot, from_rows, columns],
+                        target.at[rows],
+                        stage_sem.at[slot, which, side],
+                    )
+                )
+            copies.append(
+                pltpu.make_async_copy(
+                    stage_feed.at[slot, from_rows], feed_hbm.at[rows], stage_sem.at[slot, 3, side]
+                )
+            )
+        return copies
+
+    def hidden_tile(group, tile):
+        first, second = both(normed_ref, group)
+        slot = lax.rem(group, 2)
+        columns = pl.ds(pl.multiple_of(tile * TILE, TILE), TILE)
+        rows = jnp.concatenate([normed_ref[first], normed_ref[second]], axis=0)
+        gate = mm_nn(rows, gate_w[:, columns])
+        up = mm_nn(rows, up_w[:, columns])
+        grads = jnp.concatenate([cotangent_ref[first], cotangent_ref[second]], axis=0)
+        grad = mm_nt(grads, down_w[columns, :])
+        sigma = jax.nn.sigmoid(gate)
+        active = gate * sigma
+        stage_hidden[slot, :, columns] = (active * up).astype(BF16)
+        stage_gate[slot, :, columns] = (grad * up * sigma * (1.0 + gate * (1.0 - sigma))).astype(
+            BF16
+        )
+        stage_up[slot, :, columns] = (grad * active).astype(BF16)
+
+    def model_tile(group, tile):
+        first, second = both(part, group)
+        slot = lax.rem(group, 2)
+        columns = pl.ds(pl.multiple_of(tile * TILE, TILE), TILE)
+        back = mm_nt(stage_gate[slot], gate_w[columns, :])
+        back = (back + mm_nt(stage_up[slot], up_w[columns, :])).astype(BF16)
+        part[first, columns] = back[:GROUP]
+        part[second, columns] = back[GROUP:]
+        stage_feed[slot, :, columns] = mm_nn(stage_hidden[slot], down_w[:, columns]).astype(BF16)
+
+    hidden_tiles, model_tiles = padded // TILE, model_width // TILE
+    ticks = hidden_tiles + model_tiles
+    pace = GROUP // CHUNK
+    piece = -(-ticks // pace)
+
+    def group_body(group, _):
+        @pl.when(group >= 2)
+        def _():
+            for copy in stage_copies(group - 2):
+                copy.wait()
+
+        def piece_body(index, _):
+            def tick_body(offset, _):
+                tick = index * piece + offset
+
+                @pl.when(tick < hidden_tiles)
+                def _():
+                    hidden_tile(group, tick)
+
+                @pl.when(jnp.logical_and(tick >= hidden_tiles, tick < ticks))
+                def _():
+                    model_tile(group, tick - hidden_tiles)
+
+                return 0
+
+            lax.fori_loop(0, piece, tick_body, 0)
+
+            @pl.when(group >= 1)
+            def _():
+                line.step((group - 1) * pace + index)
+
+            return 0
+
+        lax.fori_loop(0, pace, piece_body, 0)
+        for copy in stage_copies(group):
+            copy.start()
+        return 0
+
+    lax.fori_loop(0, groups, group_body, 0)
+    line.run((groups - 1) * pace, line.steps)
+    save = pltpu.make_async_copy(residual, grad_hbm, grad_sem.at[0])
+    save.start()
+    for group in range(max(groups - 2, 0), groups):
+        for copy in stage_copies(group):
+            copy.wait()
+    line.finish()
+    save.wait()
+
+
+def feed_line(mesh_axes, collective, normed, cotangent, residual, gain, gate_w, up_w, down_w):
+    tokens, model_width = normed.shape
+    hidden_width = gate_w.shape[1]
+    padded = -(-hidden_width // TILE) * TILE
+    whole = pl.BlockSpec(memory_space=pltpu.VMEM)
+    remote = pl.BlockSpec(memory_space=pl.ANY)
+    group_rows = 2 * GROUP
+    return pl.pallas_call(
+        partial(feed_kernel, mesh_axes),
+        in_specs=[whole, whole, remote, whole, remote, remote, remote],
+        out_specs=[whole, whole] + [remote] * 5,
+        out_shape=[
+            jax.ShapeDtypeStruct((tokens, model_width), BF16),
+            jax.ShapeDtypeStruct((1, model_width), F32),
+            jax.ShapeDtypeStruct((tokens, hidden_width), BF16),
+            jax.ShapeDtypeStruct((tokens, hidden_width), BF16),
+            jax.ShapeDtypeStruct((tokens, hidden_width), BF16),
+            jax.ShapeDtypeStruct((tokens, model_width), BF16),
+            jax.ShapeDtypeStruct((tokens // 2, model_width), F32),
+        ],
+        scratch_shapes=[
+            pltpu.VMEM((model_width, padded), BF16),
+            pltpu.VMEM((model_width, padded), BF16),
+            pltpu.VMEM((padded, model_width), BF16),
+            pltpu.VMEM((tokens, model_width), BF16),
+            pltpu.VMEM((tokens, model_width), BF16),
+            pltpu.VMEM((tokens // 2, model_width), F32),
+            pltpu.VMEM((2, group_rows, padded), BF16),
+            pltpu.VMEM((2, group_rows, padded), BF16),
+            pltpu.VMEM((2, group_rows, padded), BF16),
+            pltpu.VMEM((2, group_rows, model_width), BF16),
+            pltpu.SemaphoreType.DMA((3,)),
+            pltpu.SemaphoreType.DMA((1,)),
+            pltpu.SemaphoreType.DMA((2, 4, 2)),
+            pltpu.SemaphoreType.DMA((1,)),
+        ]
+        + line_sems(tokens),
+        compiler_params=pltpu.CompilerParams(
+            collective_id=collective, has_side_effects=True, vmem_limit_bytes=58 << 20
+        ),
+        cost_estimate=pl.CostEstimate(
+            flops=tokens * model_width * hidden_width * 12,
+            bytes_accessed=360_000_000,
+            transcendentals=tokens * hidden_width,
+        ),
+        name="feed_and_norm_two_line",
+    )(normed, cotangent, residual, gain, gate_w, up_w, down_w)
 
 
 def rms_parts(values):
@@ -524,6 +946,7 @@
 
 
 def local(
+    mesh_axes,
     hidden,
     segment_ids,
     norm1_gain,
@@ -553,12 +976,9 @@
     gate_full = lax.all_gather(w_ffn_gate, both, axis=0, tiled=True)
     up_full = lax.all_gather(w_ffn_up, both, axis=0, tiled=True)
     down_full = lax.all_gather(w_ffn_down, both, axis=1, tiled=True)
-    part_rows = tokens // lax.axis_size("tensor")
-    place = lax.axis_index("tensor") * part_rows
-
-    def own_rows(values):
-        return lax.dynamic_slice_in_dim(values, place, part_rows, 0)
-
+    gain_one, gain_two = norm1_gain.reshape(1, -1), norm2_gain.reshape(1, -1)
+    half_wide = jax.ShapeDtypeStruct((tokens // 2, model_width), F32)
+    one_row = jax.ShapeDtypeStruct((1, model_width), F32)
     hidden_rows = hidden.reshape(tokens, model_width)
     unit_rows, _ = rms_parts(hidden_rows.astype(F32))
     normed_one = (unit_rows * norm1_gain).astype(BF16)
@@ -575,39 +995,22 @@
     mixed, gated_low = gate_forward(
         mixed_local, lead, carry.astype(BF16), pre, gain_row, keep, key_scale
     )
-    mix_part = jnp.dot(gated_low, out_full, preferred_element_type=F32)
-    inputs_own = own_rows(hidden_rows).astype(F32)
-    residual = inputs_own + scatter_sum(mix_part)
-    unit_two, inverse_two = rms_parts(residual)
-    normed_two = gather_rows((unit_two * norm2_gain).astype(BF16))
-    gate_ffn = jnp.dot(normed_two, gate_full, preferred_element_type=F32)
-    up_ffn = jnp.dot(normed_two, up_full, preferred_element_type=F32)
-    sigma_gate = jax.nn.sigmoid(gate_ffn)
-    active = gate_ffn * sigma_gate
-    hidden_low = (active * up_ffn).astype(BF16)
-    feed_part = jnp.dot(hidden_low, down_full, preferred_element_type=F32)
-    output_rows = gather_rows((residual + scatter_sum(feed_part)).astype(BF16))
+    mix_part = jnp.dot(gated_low, out_full, preferred_element_type=F32).astype(BF16)
+    normed_two, residual = line_exchange(
+        residual_norm, mesh_axes, 0, mix_part, (hidden_rows, gain_two), [half_wide], "mix_line"
+    )
     grad_rows = out_grad.reshape(tokens, model_width)
+    grad_mix_low, grad_norm_two, hidden_low, grad_gate_low, grad_up_low, feed_part, grad_residual = (
+        feed_line(
+            mesh_axes, 2, normed_two, grad_rows, residual, gain_two, gate_full, up_full, down_full
+        )
+    )
+    (output_rows,) = line_exchange(
+        residual_out, mesh_axes, 1, feed_part, (residual,), [], "feed_line"
+    )
     grad_down = jnp.einsum("tf,td->fd", hidden_low, grad_rows, preferred_element_type=F32)
-    grad_hidden = jnp.einsum("td,fd->tf", grad_rows, down_full, preferred_element_type=F32)
-    grad_gate_low = (
-        grad_hidden * up_ffn * sigma_gate * (1.0 + gate_ffn * (1.0 - sigma_gate))
-    ).astype(BF16)
-    grad_up_low = (grad_hidden * active).astype(BF16)
     grad_gate = jnp.einsum("td,tf->df", normed_two, grad_gate_low, preferred_element_type=F32)
     grad_up = jnp.einsum("td,tf->df", normed_two, grad_up_low, preferred_element_type=F32)
-    back_two = jnp.einsum("tf,df->td", grad_gate_low, gate_full, preferred_element_type=F32)
-    back_two = back_two + jnp.einsum(
-        "tf,df->td", grad_up_low, up_full, preferred_element_type=F32
-    )
-    grad_normed_two = scatter_sum(back_two)
-    cotangent_rows = own_rows(grad_rows).astype(F32)
-    grad_norm_two = jnp.sum(grad_normed_two * unit_two, axis=0)
-    lifted_two = grad_normed_two * norm2_gain
-    grad_residual = cotangent_rows + inverse_two * (
-        lifted_two - unit_two * jnp.mean(lifted_two * unit_two, axis=-1, keepdims=True)
-    )
-    grad_mix_low = gather_rows(grad_residual.astype(BF16))
     grad_out = jnp.einsum("tv,td->vd", gated_low, grad_mix_low, preferred_element_type=F32)
     grad_gated = jnp.einsum("td,vd->tv", grad_mix_low, out_full, preferred_element_type=F32)
     grad_mixed, grad_gate_pre, grad_head_part, back = gate_backward(
@@ -629,17 +1032,19 @@
     )
     grad_mixer = jnp.einsum("td,tk->dk", normed_one, grad_pre, preferred_element_type=F32)
     back_one = jnp.einsum("tk,dk->td", grad_pre, mixer_full, preferred_element_type=F32)
-    grad_normed_one = scatter_sum(back_one)
-    unit_one, inverse_one = rms_parts(inputs_own)
-    grad_norm_one = jnp.sum(grad_normed_one * unit_one, axis=0)
+    input_rows, grad_norm_one = line_exchange(
+        norm_one_back,
+        mesh_axes,
+        3,
+        back_one.astype(BF16),
+        (hidden_rows, grad_residual, gain_one),
+        [one_row],
+        "norm_one_line",
+    )
     grad_norm_one, grad_norm_two, head_total = lax.psum(
-        (grad_norm_one, grad_norm_two, grad_head_part.reshape(-1)), "tensor"
-    )
-    lifted_one = grad_normed_one * norm1_gain
-    grad_inputs = grad_residual + inverse_one * (
-        lifted_one - unit_one * jnp.mean(lifted_one * unit_one, axis=-1, keepdims=True)
-    )
-    input_rows = gather_rows(grad_inputs.astype(BF16))
+        (grad_norm_one.reshape(-1), grad_norm_two.reshape(-1), grad_head_part.reshape(-1)),
+        "tensor",
+    )
 
     def share(values, dim):
         return lax.psum_scatter(
@@ -699,4 +1104,5 @@
         P(("shard", "context"), "tensor"),
         P("tensor", ("shard", "context")),
     )
-    return jax.shard_map(local, mesh=mesh, in_specs=in_specs, out_specs=out_specs, check_vma=False)
+    return jax.shard_map(
+        partial(local, mesh.axis_names), mesh=mesh, in_specs=in_specs, out_specs=out_specs, check_vma=False)

time: 1330 us -> 779 us (0.59)
  waiting for transfers between devices: 1020 us -> 59.6 us
  Pallas kernels: 34.4 us -> 526 us
  matrix products: 158 us -> 91.1 us
  other arithmetic: 38.7 us -> 16.6 us
    pallas_call x0 -> x4, Pallas kernels: none -> 492 us  [the longest x3 346 us: line_exchange(): pl.pallas_call(partial(line_exchange_kernel, transform, mesh_axes, len(ex...]
    all_gather x4 -> x0, waiting for transfers between devices: 326 us -> none  [gather_rows(): return lax.all_gather(values, 'tensor', axis=0, tiled=True)]
    reduce_scatter x5, waiting for transfers between devices: 259 us -> 0.01 us  [share(): lax.psum_scatter(values.astype(BF16), both, scatter_dimension=dim, tiled=...]
    reduce_scatter x4 -> x0, waiting for transfers between devices: 241 us -> none  [scatter_sum(): lax.psum_scatter(values.astype(jnp.bfloat16), 'tensor', scatter_dimension...]
    dot_general x7 -> x1, matrix products: 75.2 us -> 6.02 us  [local(): jnp.dot(gated_low, out_full, preferred_element_type=F32).astype(BF16)]
    all_gather x1, waiting for transfers between devices: 39 us -> 0.02 us  [local(): gate_full = lax.all_gather(w_ffn_gate, both, axis=0, tiled=True)]
    unnamed x20 -> x12, waiting for transfers between devices: 36 us -> 2.55 us
    all_gather x1, waiting for transfers between devices: 32.1 us -> 0.02 us  [local(): up_full = lax.all_gather(w_ffn_up, both, axis=0, tiled=True)]
  transfers between devices with their start and end apart: 21 -> 13, of which waited for: 20 -> 4; matrix products, arithmetic and copies ran while one was open for 11% -> 14% of each run, Pallas kernels for 1% -> 47%
where the time goes in v4:
time: 779 us; the launch traced here: 772 us
  Pallas kernels  526 us (68%)
  matrix products  91.1 us (12%)
  waiting for transfers between devices  59.6 us (8%)
  blocking collectives  31.3 us (4%)
  local copies, waits for them, and re-layouts  23.7 us (3%)
  between operations  18.6 us (2%)
  other arithmetic  16.6 us (2%)
    pallas_call x3, Pallas kernels, line_exchange(): pl.pallas_call(partial(line_exchange_kernel, transform, mesh_axes, len(ex...  346 us
    pallas_call x1, Pallas kernels, feed_line(): pl.pallas_call(partial(feed_kernel, mesh_axes), in_specs=[whole, whole, r...  145 us
    all_gather x1, waiting for transfers between devices, local(): lax.all_gather(jnp.concatenate([w_query, w_forget, w_input, w_gate_out],...  47.4 us
    psum x1, blocking collectives, local(): lax.psum((grad_norm_one.reshape(-1), grad_norm_two.reshape(-1), grad_head...  18.4 us
    unnamed x41, local copies, waits for them, and re-layouts  16.8 us
  transfers between devices with their start and end apart: 13, of which 4 were waited for; matrix products, arithmetic and copies ran while one was open for 14% of the time, Pallas kernels for 47%

profile of v4, /device:TPU:0, one launch (start us, length us, event | category | flops | bytes accessed | tf_op | source)
XLA Modules:
  0.0 771.5 jit_solution(6423624933201501892)
XLA Ops:
  7.2 2.3 pad_maximum_fusion
  9.6 0.7 all-gather.8.cloned.1.call-update
  10.4 0.7 all-gather.10.cloned.1.call-update
  15.0 1.4 stack.11
  17.1 3.1 fusion
  20.2 47.4 %all-gather.6.cloned.1.call-done = bf16[2048,2048]{1,0:T(8,128)(2,1)} async-done(((bf16[256,2048]{1,0:T(8,128)(2,1)}), bf16[2048,2048]{1,0:T(8,128)(2,1)}) %all-gather.6.cloned.1.call-update) | async-done | bytes 8388624 | tf_op jit(solution)/shard_map/all_gather | solution.py:972
  67.6 14.6 %fusion.4.pre_ref.gate_ref = f32[1024,2048]{1,0:T(8,128)} fusion(bf16[2048,2048]{1,0:T(8,128)(2,1)} %all-gather.6.cloned.1.call-done, f32[2048]{0:T(1024)S(1)} %copy-done.5, f32[1024]{0:T(1024)S(1)} %add_rsqrt_fusion, bf16[1,1024,2048]{2,1,0:T(8,128)(2,1)} %param.15), kind=kOutput, calls=%fused_computation.14 | convolution fusion | flops 8598323200 | bytes 20983808 | tf_op jit(solution)/shard_map/dot_general | solution.py:985
  82.3 9.6 %mixer_forward.1 = (f32[1024,512]{1,0:T(8,128)S(1)}, bf16[1024,512]{1,0:T(8,128)(2,1)S(1)}, f32[8,4,128,128]{3,2,1,0:T(8,128)S(1)}, f32[8,1,512]{2,1,0:T(1,128)S...) custom-call(f32[1024,2048]{1,0:T(8,128)} %fusion.4.pre_ref.gate_ref, f32[1,512]{1,0:T(1,128)S(1)} %bitcast.60, ...), custom_call_target="tpu_custom_call" | custom-call | flops 805306368 | bytes 15728640 | tf_op jit(solution)/shard_map/mixer_forward/pallas_call | solution.py:115
  91.9 1.3 copy-done
  93.3 2.2 collective-permute-start
  95.6 1.1 collective-permute-done
  99.2 4.1 gate_forward.1
  103.3 1.3 copy-done.2
  104.7 6.0 convolution_convert_fusion.5.refs_0_
  110.7 117.1 %mix_line.1 = (bf16[1024,2048]{1,0:T(8,128)(2,1)}, f32[512,2048]{1,0:T(8,128)}) custom-call(bf16[1024,2048]{1,0:T(8,128)(2,1)} %convolution_convert_fusion.5.refs_0_, bf16[1024,2048]{1,0:T(8,128)(2,1)} %bitcast.69, f32[1,2048]{1,0:T(1,128)S(1)} %bitcast.63), custom_call_target="tpu_custom_call" | custom-call | flops 16777216 | bytes 360000000 | tf_op jit(solution)/shard_map/mix_line/pallas_call | solution.py:667
  227.9 6.3 all-gather.14.cloned.1.call-done.down_hbm
  234.2 145.4 %feed_and_norm_two_line.1 = (bf16[1024,2048]{1,0:T(8,128)(2,1)}, f32[1,2048]{1,0:T(1,128)}, bf16[1024,1408]{1,0:T(8,128)(2,1)}, bf16[1024,1408]{1,0:T(8,128)(2,1...) custom-call(bf16[1024,2048]{1,0:T(8,128)(2,1)} %get-tuple-element.44.normed_ref, ...), custom_call_target="tpu_custom_call" | custom-call | flops 35433480192 | bytes 360000000 | tf_op jit(solution)/shard_map/feed_and_norm_two_line/pallas_call | solution.py:901
  379.6 4.7 fusion.13.grad_ref
  384.3 6.2 gate_backward.1
  390.6 1.3 collective-permute-start.1
  391.9 2.1 collective-permute-done.1
  394.1 14.6 %mixer_backward.1 = (bf16[1024,2048]{1,0:T(8,128)(2,1)S(1)}, f32[1,512]{1,0:T(1,128)S(1)}) custom-call(f32[1024,2048]{1,0:T(8,128)} %fusion.4.pre_ref.gate_ref, bf16[1024,512]{1,0:T(8,128)(2,1)S(1)} %get-tuple-element.49.grad_mixed_ref, bf16[1024,512]{1,0:T(8,128)(2,1)S(1)} %get-tuple-element.50.grad_gate_ref, f32[8,4,128,128]{3,2,1,0:T(8,128)S(1)} %copy-done.1, ...), custom_call_target="tpu_custom_call" | custom-call | flops 2013265920 | bytes 18874368 | tf_op jit(solution)/shard_map/mixer_backward/pallas_call | solution.py:392
  408.7 2.0 copy-done.7
  410.7 0.7 copy.47
  411.5 5.9 convolution_convert_fusion.6
  417.7 11.0 %convolution_convert_fusion.2 = bf16[2048,1408]{1,0:T(8,128)(2,1)} fusion(bf16[1024,2048]{1,0:T(8,128)(2,1)} %get-tuple-element.44.normed_ref, bf16[1024,1408]{1,0:T(8,128)(2,1)} %get-tuple-element.61), kind=kOutput, calls=%fused_computation.7 | convolution fusion | flops 5908463616 | bytes 12845056 | tf_op jit(solution)/shard_map/td,tf->df/dot_general | solution.py:1012
  428.8 1.8 copy-done.17
  430.5 10.9 %convolution_convert_fusion.1 = bf16[2048,1408]{1,0:T(8,128)(2,1)} fusion(bf16[1024,2048]{1,0:T(8,128)(2,1)} %get-tuple-element.44.normed_ref, bf16[1024,1408]{1,0:T(8,128)(2,1)S(1)} %copy-done.17), kind=kOutput, calls=%fused_computation.6 | convolution fusion | flops 5908463616 | bytes 12845056 | tf_op jit(solution)/shard_map/td,tf->df/dot_general | solution.py:1013
  441.5 1.8 copy-done.16
  443.2 10.7 %convolution_convert_fusion = bf16[1408,2048]{1,0:T(8,128)(2,1)} fusion(bf16[1024,1408]{1,0:T(8,128)(2,1)S(1)} %copy-done.16, bf16[1,1024,2048]{2,1,0:T(8,128)(2,1)} %param.29), kind=kOutput, calls=%fused_computation.5 | convolution fusion | flops 5908463616 | bytes 12845056 | tf_op jit(solution)/shard_map/tf,td->fd/dot_general | solution.py:1011
  454.2 14.7 %convolution_convert_fusion.3 = bf16[2048,2048]{1,0:T(8,128)(2,1)} fusion(bf16[1024,2048]{1,0:T(8,128)(2,1)} %copy-done.7, f32[2048]{0:T(1024)S(1)} %copy-done.5, f32[1024]{0:T(1024)S(1)} %add_rsqrt_fusion, bf16[1,1024,2048]{2,1,0:T(8,128)(2,1)} %param.15), kind=kOutput, calls=%fused_computation.8 | convolution fusion | flops 8602517504 | bytes 16789504 | tf_op jit(solution)/shard_map/td,tk->dk/dot_general | solution.py:1033
  468.9 0.6 copy-done.15
  471.4 114.4 %feed_line.1 = bf16[1024,2048]{1,0:T(8,128)(2,1)} custom-call(bf16[1024,2048]{1,0:T(8,128)(2,1)} %get-tuple-element.46.refs_0_, f32[512,2048]{1,0:T(8,128)} %get-tuple-element.45.residual_hbm.refs_1_), custom_call_target="tpu_custom_call" | custom-call | flops 16777216 | bytes 360000000 | tf_op jit(solution)/shard_map/feed_line/pallas_call | solution.py:667
  585.8 12.6 %convolution_convert_fusion.4.refs_0_ = bf16[1024,2048]{1,0:T(8,128)(2,1)} fusion(bf16[1024,2048]{1,0:T(8,128)(2,1)S(1)} %copy-done.8, bf16[2048,2048]{1,0:T(8,128)(2,1)} %all-gather.6.cloned.1.call-done), kind=kOutput, calls=%fused_computation.11 | convolution fusion | flops 8592031744 | bytes 16777216 | tf_op jit(solution)/shard_map/tk,dk->td/dot_general | solution.py:1034
  598.4 114.8 %norm_one_line.1 = (bf16[1024,2048]{1,0:T(8,128)(2,1)}, f32[1,2048]{1,0:T(1,128)S(1)}) custom-call(bf16[1024,2048]{1,0:T(8,128)(2,1)} %convolution_convert_fusion.4.refs_0_, bf16[1024,2048]{1,0:T(8,128)(2,1)} %bitcast.70, f32[512,2048]{1,0:T(8,128)} %get-tuple-element.55.refs_2_, f32[1,2048]{1,0:T(1,128)S(1)} %bitcast.65), custom_call_target="tpu_custom_call" | custom-call | flops 16777216 | bytes 360000000 | tf_op jit(solution)/shard_map/norm_one_line/pallas_call | solution.py:667
  713.3 18.4 %all-reduce.4 = (bf16[2048]{0:T(1024)(128)(2,1)S(1)}, bf16[128]{0:T(256)(128)(2,1)S(1)}, bf16[2048]{0:T(1024)(128)(2,1)S(1)}) all-reduce(f32[2048]{0:T(1024)S(1)} %bitcast.64, f32[128]{0:T(128)S(1)} %bitcast.68, f32[2048]{0:T(1024)S(1)} %bitcast.81), channel_id=1, replica_groups=mesh['shard'=4,'context'=2,'tensor'=4] {'tensor'}, use_global_device_ids=true, to_apply=%region_2.3 | all-reduce | flops 4224 | bytes 25344 | tf_op jit(solution)/shard_map/psum | solution.py:1044
  731.7 12.9 %all-reduce.5 = (bf16[2048]{0:T(1024)(128)(2,1)S(1)}, bf16[128]{0:T(256)(128)(2,1)S(1)}, bf16[2048]{0:T(1024)(128)(2,1)S(1)}) all-reduce(bf16[2048]{0:T(1024)(128)(2,1)S(1)} %get-tuple-element.64, bf16[128]{0:T(256)(128)(2,1)S(1)} %get-tuple-element.65, ...), channel_id=2, replica_groups=mesh['shard'=4,'context'=2,'tensor'=4] {'shard','context'}, use_global_device_ids=true, to_apply=%region_3.4.clone | all-reduce | flops 4224 | bytes 16896
  744.6 0.6 dynamic-slice_convert_fusion.1
  745.2 0.6 dynamic-slice_convert_fusion
  745.8 0.8 copy.48
  747.2 1.8 convert_element_type.123
  749.0 2.3 convert_element_type.127
  751.3 2.3 convert_element_type.129
  753.6 2.3 convert_element_type.131
  755.9 2.8 fusion.10
  758.8 2.1 copy.51
  761.0 1.6 copy-done.10
  762.5 2.0 copy.52
  (90 shorter events, 7.0 us)
Async XLA Ops:
  7.2 5.1 copy-start.11
  7.2 9.9 %copy-start.13 = (f32[4,128]{1,0:T(4,128)S(1)}, f32[4,128]{1,0:T(4,128)}, u32[]{:S(2)}) copy-start(f32[4,128]{1,0:T(4,128)} %param.22) | copy-start | bytes 6148
  7.2 60.4 %all-gather.6.cloned.1.call-start = ((), (), s32[]{:S(2)}) async-start(), calls=%async_computation.6 | async-start | bytes 9437184 | tf_op jit(solution)/shard_map/all_gather | solution.py:972
  9.6 58.1 %copy-start.5 = (f32[2048]{0:T(1024)S(1)}, f32[2048]{0:T(1024)}, u32[]{:S(2)}) copy-start(f32[2048]{0:T(1024)} %param.17) | copy-start | bytes 24580
  9.6 95.1 %all-gather.8.cloned.1.call-start = ((), (), s32[]{:S(2)}) async-start(), calls=%async_computation.7 | async-start | bytes 2359296 | tf_op jit(solution)/shard_map/all_gather | solution.py:975
  10.3 217.5 %all-gather.10.cloned.1.call-start = ((), (), s32[]{:S(2)}) async-start(), calls=%async_computation.8 | async-start | bytes 6488064 | tf_op jit(solution)/shard_map/all_gather | solution.py:976
  11.1 216.8 %all-gather.12.cloned.1.call-start = ((), (), s32[]{:S(2)}) async-start(), calls=%async_computation.9 | async-start | bytes 6488064 | tf_op jit(solution)/shard_map/all_gather | solution.py:977
  11.6 222.5 %all-gather.14.cloned.1.call-start = ((), (), s32[]{:S(2)}) async-start(), calls=%async_computation.10 | async-start | bytes 6488064 | tf_op jit(solution)/shard_map/all_gather | solution.py:978
  12.2 733.6 %reduce-scatter.19.cloned.1.call-start = ((), (), s32[]{:S(2)}) async-start(), calls=%async_computation.16 | async-start | bytes 36864
  82.3 17.0 %copy-start.6 = (f32[128]{0:T(128)S(1)}, f32[128]{0:T(128)}, u32[]{:S(2)}) copy-start(f32[128]{0:T(128)} %param.23) | copy-start | bytes 1540
  91.8 1.3 copy-start
  93.3 3.4 collective-permute-start
  103.3 1.3 copy-start.2
  104.6 6.0 copy-start.4
  234.2 145.4 %copy-start.14 = (bf16[512,2048]{1,0:T(8,128)(2,1)S(1)}, bf16[512,2048]{1,0:T(8,128)(2,1)}, u32[]{:S(2)}) copy-start(bf16[512,2048]{1,0:T(8,128)(2,1)} %all-gather.8.cloned.1.call-done) | copy-start | bytes 6291460
  379.6 4.7 copy-start.3
  384.3 9.7 %copy-start.1 = (f32[8,4,128,128]{3,2,1,0:T(8,128)S(1)}, f32[8,4,128,128]{3,2,1,0:T(8,128)}, u32[]{:S(2)}) copy-start(f32[8,4,128,128]{3,2,1,0:T(8,128)} %copy-done) | copy-start | bytes 6291460
  390.6 3.4 collective-permute-start.1
  408.6 2.0 copy-start.7
  411.4 335.8 %reduce-scatter.11.cloned.1.call-start = ((), (), s32[]{:S(2)}) async-start(), calls=%async_computation.12 | async-start | bytes 2359296 | tf_op jit(solution)/shard_map/reduce_scatter | solution.py:1050
  417.4 331.6 %reduce-scatter.13.cloned.1.call-start = ((), (), s32[]{:S(2)}) async-start(), calls=%async_computation.13 | async-start | bytes 6488064 | tf_op jit(solution)/shard_map/reduce_scatter | solution.py:1050
  428.7 1.8 copy-start.17
  428.7 322.6 %reduce-scatter.15.cloned.1.call-start = ((), (), s32[]{:S(2)}) async-start(), calls=%async_computation.14 | async-start | bytes 6488064 | tf_op jit(solution)/shard_map/reduce_scatter | solution.py:1050
  441.4 1.8 copy-start.16
  441.4 312.2 %reduce-scatter.17.cloned.1.call-start = ((), (), s32[]{:S(2)}) async-start(), calls=%async_computation.15 | async-start | bytes 6488064 | tf_op jit(solution)/shard_map/reduce_scatter | solution.py:1050
  453.9 302.0 %reduce-scatter.9.cloned.1.call-start = ((), (), s32[]{:S(2)}) async-start(), calls=%async_computation.11 | async-start | bytes 9437184 | tf_op jit(solution)/shard_map/reduce_scatter | solution.py:1050
  468.9 0.7 copy-start.15
  471.4 114.4 %copy-start.8 = (bf16[1024,2048]{1,0:T(8,128)(2,1)S(1)}, bf16[1024,2048]{1,0:T(8,128)(2,1)}, u32[]{:S(2)}) copy-start(bf16[1024,2048]{1,0:T(8,128)(2,1)} %copy-done.7) | copy-start | bytes 12582916
  598.4 114.8 %copy-start.12 = (f32[1,2048]{1,0:T(1,128)S(1)}, f32[1,2048]{1,0:T(1,128)}, u32[]{:S(2)}) copy-start(f32[1,2048]{1,0:T(1,128)} %get-tuple-element.60) | copy-start | bytes 24580
  755.9 2.9 copy-start.9
  758.8 3.7 copy-start.10
Sparse Core Ops, SparseCore 0:
  10.5 57.0 all-gather.5
  69.5 28.1 all-gather.7
  99.6 43.3 all-gather.9
  144.7 43.3 all-gather.11
  189.8 44.3 all-gather.13
  411.6 30.9 reduce-scatter.18
  446.7 41.2 reduce-scatter.10
  491.5 59.0 reduce-scatter.12
  554.4 59.0 reduce-scatter.14
  616.8 59.0 reduce-scatter.16
  679.7 71.6 reduce-scatter.8

commit v5 on v4

--- a/solution.py
+++ b/solution.py
@@ -615,9 +615,11 @@
             def _(side=side, index=index):
                 self.back_copy(side, index).start()
 
-    def run(self, first, last):
+    def run(self, first, last, beside=None):
         def body(time, _):
             self.step(time)
+            if beside is not None:
+                beside(time)
             return 0
 
         lax.fori_loop(first, last, body, 0)
@@ -648,9 +650,6 @@
     part, extra_in = refs[0], refs[1 : 1 + n_in]
     out, extra_out = refs[1 + n_in], refs[2 + n_in : 2 + n_in + n_out]
     arrived, *sems = refs[2 + n_in + n_out :]
-    if transform is norm_one_back:
-        extra_out[0][...] = jnp.zeros_like(extra_out[0])
-
     def turn(total, rows, own):
         transform(total, rows, own, extra_in, out, extra_out)
 
@@ -689,23 +688,6 @@
     residual = hidden[rows].astype(F32) + total
     extra_out[0][own] = residual
     out[rows] = (residual * inverse_rms(residual) * gain[...]).astype(BF16)
-
-
-def residual_out(total, rows, own, extra_in, out, extra_out):
-    out[rows] = (extra_in[0][own] + total).astype(BF16)
-
-
-def norm_one_back(total, rows, own, extra_in, out, extra_out):
-    hidden, residual_grad, gain = extra_in
-    gain_grad = extra_out[0]
-    values = hidden[rows].astype(F32)
-    inverse = inverse_rms(values)
-    unit = values * inverse
-    gain_grad[...] += jnp.sum(total * unit, axis=0, keepdims=True)
-    lifted = total * gain[...]
-    mean = jnp.mean(lifted * unit, axis=-1, keepdims=True)
-    grad = residual_grad[own] + inverse * (lifted - unit * mean)
-    out[rows] = grad.astype(BF16)
 
 
 GROUP = 128
@@ -940,6 +922,297 @@
     )(normed, cotangent, residual, gain, gate_w, up_w, down_w)
 
 
+def output_kernel(
+    mesh_axes,
+    part,
+    residual,
+    normed_ref,
+    cotangent_ref,
+    hidden_ref,
+    grad_gate_ref,
+    grad_up_ref,
+    out_ref,
+    grads_hbm,
+    arrived,
+    stage,
+    stage_sem,
+    *sems,
+):
+    model_width = normed_ref.shape[1]
+    tiles = model_width // TILE
+
+    def turn(total, rows, own):
+        out_ref[rows] = (residual[own] + total).astype(BF16)
+
+    line = Line(mesh_axes, part, arrived, out_ref, sems, turn)
+    barrier = pltpu.get_barrier_semaphore()
+    pl.semaphore_wait(barrier, line.greet(barrier))
+
+    def stage_copy(tile):
+        rows = pl.ds(pl.multiple_of(tile * TILE, TILE), TILE)
+        slot = lax.rem(tile, 2)
+        return pltpu.make_async_copy(stage.at[slot], grads_hbm.at[:, rows], stage_sem.at[slot])
+
+    def weight_tile(time):
+        tile = jnp.clip(time, 0, tiles - 1)
+        slot = lax.rem(tile, 2)
+        columns = pl.ds(pl.multiple_of(tile * TILE, TILE), TILE)
+
+        @pl.when(jnp.logical_and(time < tiles, time >= 2))
+        def _():
+            stage_copy(tile - 2).wait()
+
+        @pl.when(time < tiles)
+        def _():
+            rows = normed_ref[:, columns]
+            stage[slot, 0] = mm_tn(rows, grad_gate_ref[...]).astype(BF16)
+            stage[slot, 1] = mm_tn(rows, grad_up_ref[...]).astype(BF16)
+            stage[slot, 2] = mm_tn(cotangent_ref[:, columns], hidden_ref[...]).astype(BF16)
+            stage_copy(tile).start()
+
+    line.run(0, line.steps, weight_tile)
+    for tile in range(max(tiles - 2, 0), tiles):
+        stage_copy(tile).wait()
+    line.finish()
+
+
+def output_line(
+    mesh_axes, collective, part, residual, normed, cotangent, hidden_low, grad_gate, grad_up
+):
+    tokens, model_width = part.shape
+    hidden_width = hidden_low.shape[1]
+    whole = pl.BlockSpec(memory_space=pltpu.VMEM)
+    return pl.pallas_call(
+        partial(output_kernel, mesh_axes),
+        in_specs=[whole] * 7,
+        out_specs=[whole, pl.BlockSpec(memory_space=pl.ANY)],
+        out_shape=[
+            jax.ShapeDtypeStruct((tokens, model_width), BF16),
+            jax.ShapeDtypeStruct((3, model_width, hidden_width), BF16),
+        ],
+        scratch_shapes=[
+            pltpu.VMEM((tokens, model_width), BF16),
+            pltpu.VMEM((2, 3, TILE, hidden_width), BF16),
+            pltpu.SemaphoreType.DMA((2,)),
+        ]
+        + line_sems(tokens),
+        compiler_params=pltpu.CompilerParams(
+            collective_id=collective, has_side_effects=True, vmem_limit_bytes=56 << 20
+        ),
+        cost_estimate=pl.CostEstimate(
+            flops=tokens * model_width * hidden_width * 6,
+            bytes_accessed=360_000_000,
+            transcendentals=0,
+        ),
+        name="output_line",
+    )(part, residual, normed, cotangent, hidden_low, grad_gate, grad_up)
+
+
+class Plane:
+    def __init__(self, mesh_axes):
+        self.mesh_axes = mesh_axes
+        self.context = lax.axis_size("context")
+        self.per_row = self.context // 2
+        self.chips = lax.axis_size("shard") * self.per_row
+        context_place = lax.axis_index("context")
+        self.core = lax.rem(context_place, 2)
+        self.chip = lax.axis_index("shard") * self.per_row + context_place // 2
+
+    def device(self, chip, core):
+        places = {
+            "shard": chip // self.per_row,
+            "context": 2 * lax.rem(chip, self.per_row) + core,
+            "tensor": lax.axis_index("tensor"),
+        }
+        return tuple(places[axis] for axis in self.mesh_axes)
+
+    def ahead(self, distance):
+        return lax.rem(self.chip + distance, self.chips)
+
+    def greet(self, barrier):
+        targets = [self.device(self.chip, 1 - self.core)]
+        targets += [self.device(self.ahead(step), self.core) for step in range(1, self.chips)]
+        for target in targets:
+            pl.semaphore_signal(barrier, inc=1, device_id=target, device_id_type=MESH_ID)
+        return len(targets)
+
+
+def input_kernel(
+    mesh_axes,
+    part,
+    hidden_ref,
+    residual_grad,
+    gain_ref,
+    grads_hbm,
+    out_ref,
+    gain_grad,
+    share_gate,
+    share_up,
+    share_down,
+    arrived,
+    own,
+    other,
+    remote,
+    load_sem,
+    pair_send,
+    pair_recv,
+    chip_send,
+    chip_recv,
+    *sems,
+):
+    plane = Plane(mesh_axes)
+    chips = plane.chips
+    block = own.shape[2]
+    gain_grad[...] = jnp.zeros_like(gain_grad)
+
+    def turn(total, rows, own_rows):
+        values = hidden_ref[rows].astype(F32)
+        inverse = inverse_rms(values)
+        unit = values * inverse
+        gain_grad[...] += jnp.sum(total * unit, axis=0, keepdims=True)
+        lifted = total * gain_ref[...]
+        mean = jnp.mean(lifted * unit, axis=-1, keepdims=True)
+        grad = residual_grad[own_rows] + inverse * (lifted - unit * mean)
+        out_ref[rows] = grad.astype(BF16)
+
+    line = Line(mesh_axes, part, arrived, out_ref, sems, turn)
+    barrier = pltpu.get_barrier_semaphore()
+    expected = line.greet(barrier) + plane.greet(barrier)
+    pl.semaphore_wait(barrier, expected)
+
+    def rows_of(slot, core):
+        return pl.ds(pl.multiple_of((2 * plane.ahead(slot) + core) * block, block), block)
+
+    def load(slot):
+        return pltpu.make_async_copy(
+            grads_hbm.at[:, rows_of(slot, plane.core)], own.at[slot], load_sem.at[slot]
+        )
+
+    def pair_copy(slot):
+        return pltpu.make_async_remote_copy(
+            grads_hbm.at[:, rows_of(slot, 1 - plane.core)],
+            other.at[slot],
+            pair_send.at[slot],
+            pair_recv.at[slot],
+            device_id=plane.device(plane.chip, 1 - plane.core),
+            device_id_type=MESH_ID,
+        )
+
+    def chip_copy(slot):
+        return pltpu.make_async_remote_copy(
+            own.at[slot],
+            remote.at[slot - 1],
+            chip_send.at[slot - 1],
+            chip_recv.at[slot - 1],
+            device_id=plane.device(plane.ahead(slot), plane.core),
+            device_id_type=MESH_ID,
+        )
+
+    def start(index, _):
+        slot = lax.rem(index + 1, chips)
+        pair_copy(slot).start()
+        load(slot).start()
+        return 0
+
+    lax.fori_loop(0, chips, start, 0)
+    strip = 32
+
+    def combine(time):
+        slot = lax.rem(jnp.clip(time, 0, chips - 1) + 1, chips)
+
+        @pl.when(time < chips)
+        def _():
+            load(slot).wait()
+            pair_copy(slot).wait_recv()
+
+            def add(index, _):
+                rows = pl.ds(pl.multiple_of(index * strip, strip), strip)
+                for which in range(3):
+                    total = own[slot, which, rows].astype(F32) + other[slot, which, rows].astype(F32)
+                    own[slot, which, rows] = total.astype(BF16)
+                return 0
+
+            lax.fori_loop(0, block // strip, add, 0)
+
+        @pl.when(time < chips - 1)
+        def _():
+            chip_copy(slot).start()
+
+    line.run(0, line.steps, combine)
+
+    def arrive(index, _):
+        chip_copy(index).wait_recv()
+        return 0
+
+    lax.fori_loop(1, chips, arrive, 0)
+
+    def total(index, _):
+        rows = pl.ds(pl.multiple_of(index * strip, strip), strip)
+
+        def whole(which):
+            def add(slot, value):
+                return value + remote[slot, which, rows].astype(F32)
+
+            return lax.fori_loop(0, chips - 1, add, own[0, which, rows].astype(F32))
+
+        share_gate[rows] = whole(0)
+        share_up[rows] = whole(1)
+        share_down[rows] = whole(2)
+        return 0
+
+    lax.fori_loop(0, block // strip, total, 0)
+
+    def sent(index, _):
+        pair_copy(index).wait_send()
+        return 0
+
+    lax.fori_loop(0, chips, sent, 0)
+
+    def chip_sent(index, _):
+        chip_copy(index).wait_send()
+        return 0
+
+    lax.fori_loop(1, chips, chip_sent, 0)
+    line.finish()
+
+
+def input_line(mesh_axes, collective, part, hidden, residual_grad, gain, grads):
+    tokens, model_width = part.shape
+    hidden_width = grads.shape[2]
+    chips = lax.axis_size("shard") * lax.axis_size("context") // 2
+    block = model_width // (2 * chips)
+    whole = pl.BlockSpec(memory_space=pltpu.VMEM)
+    return pl.pallas_call(
+        partial(input_kernel, mesh_axes),
+        in_specs=[whole] * 4 + [pl.BlockSpec(memory_space=pl.ANY)],
+        out_specs=[whole] * 5,
+        out_shape=[
+            jax.ShapeDtypeStruct((tokens, model_width), BF16),
+            jax.ShapeDtypeStruct((1, model_width), F32),
+        ]
+        + [jax.ShapeDtypeStruct((block, hidden_width), F32)] * 3,
+        scratch_shapes=[
+            pltpu.VMEM((tokens, model_width), BF16),
+            pltpu.VMEM((chips, 3, block, hidden_width), BF16),
+            pltpu.VMEM((chips, 3, block, hidden_width), BF16),
+            pltpu.VMEM((chips - 1, 3, block, hidden_width), BF16),
+            pltpu.SemaphoreType.DMA((chips,)),
+            pltpu.SemaphoreType.DMA((chips,)),
+            pltpu.SemaphoreType.DMA((chips,)),
+            pltpu.SemaphoreType.DMA((chips - 1,)),
+            pltpu.SemaphoreType.DMA((chips - 1,)),
+        ]
+        + line_sems(tokens),
+        compiler_params=pltpu.CompilerParams(
+            collective_id=collective, has_side_effects=True, vmem_limit_bytes=58 << 20
+        ),
+        cost_estimate=pl.CostEstimate(
+            flops=tokens * model_width * 8, bytes_accessed=360_000_000, transcendentals=0
+        ),
+        name="input_line",
+    )(part, hidden, residual_grad, gain, grads)
+
+
 def rms_parts(values):
     inverse = lax.rsqrt(jnp.mean(values * values, axis=-1, keepdims=True) + EPSILON)
     return (values * inverse, inverse)
@@ -978,7 +1251,6 @@
     down_full = lax.all_gather(w_ffn_down, both, axis=1, tiled=True)
     gain_one, gain_two = norm1_gain.reshape(1, -1), norm2_gain.reshape(1, -1)
     half_wide = jax.ShapeDtypeStruct((tokens // 2, model_width), F32)
-    one_row = jax.ShapeDtypeStruct((1, model_width), F32)
     hidden_rows = hidden.reshape(tokens, model_width)
     unit_rows, _ = rms_parts(hidden_rows.astype(F32))
     normed_one = (unit_rows * norm1_gain).astype(BF16)
@@ -1005,12 +1277,17 @@
             mesh_axes, 2, normed_two, grad_rows, residual, gain_two, gate_full, up_full, down_full
         )
     )
-    (output_rows,) = line_exchange(
-        residual_out, mesh_axes, 1, feed_part, (residual,), [], "feed_line"
-    )
-    grad_down = jnp.einsum("tf,td->fd", hidden_low, grad_rows, preferred_element_type=F32)
-    grad_gate = jnp.einsum("td,tf->df", normed_two, grad_gate_low, preferred_element_type=F32)
-    grad_up = jnp.einsum("td,tf->df", normed_two, grad_up_low, preferred_element_type=F32)
+    output_rows, grads_ffn = output_line(
+        mesh_axes,
+        1,
+        feed_part,
+        residual,
+        normed_two,
+        grad_rows,
+        hidden_low,
+        grad_gate_low,
+        grad_up_low,
+    )
     grad_out = jnp.einsum("tv,td->vd", gated_low, grad_mix_low, preferred_element_type=F32)
     grad_gated = jnp.einsum("td,vd->tv", grad_mix_low, out_full, preferred_element_type=F32)
     grad_mixed, grad_gate_pre, grad_head_part, back = gate_backward(
@@ -1032,14 +1309,8 @@
     )
     grad_mixer = jnp.einsum("td,tk->dk", normed_one, grad_pre, preferred_element_type=F32)
     back_one = jnp.einsum("tk,dk->td", grad_pre, mixer_full, preferred_element_type=F32)
-    input_rows, grad_norm_one = line_exchange(
-        norm_one_back,
-        mesh_axes,
-        3,
-        back_one.astype(BF16),
-        (hidden_rows, grad_residual, gain_one),
-        [one_row],
-        "norm_one_line",
+    input_rows, grad_norm_one, share_gate, share_up, share_down = input_line(
+        mesh_axes, 3, back_one.astype(BF16), hidden_rows, grad_residual, gain_one, grads_ffn
     )
     grad_norm_one, grad_norm_two, head_total = lax.psum(
         (grad_norm_one.reshape(-1), grad_norm_two.reshape(-1), grad_head_part.reshape(-1)),
@@ -1064,9 +1335,9 @@
         share(head_total, 0),
         share(grad_out, 1),
         share(grad_norm_two, 0),
-        share(grad_gate, 0),
-        share(grad_up, 0),
-        share(grad_down, 1),
+        share_gate,
+        share_up,
+        share_down.T,
     )
 
 

time: 779 us -> 746 us (0.958)
  matrix products: 91.1 us -> 58.1 us
  Pallas kernels: 526 us -> 538 us
    pallas_call x0 -> x2, Pallas kernels: none -> 242 us  [the longest x1 122 us: input_line(): pl.pallas_call(partial(input_kernel, mesh_axes), in_specs=[whole] * 4 + [...]
    pallas_call x3 -> x1, Pallas kernels: 346 us -> 117 us  [line_exchange(): pl.pallas_call(partial(line_exchange_kernel, transform, mesh_axes, len(ex...]
    dot_general x3 -> x0, matrix products: 32.6 us -> none  [the longest x1 11 us: local(): jnp.einsum('td,tf->df', normed_two, grad_gate_low, preferred_element_type...]
    unnamed x41 -> x44, local copies, waits for them, and re-layouts: 16.8 us -> 18.7 us
  transfers between devices with their start and end apart: 13 -> 10, of which waited for: 4 -> 4; matrix products, arithmetic and copies ran while one was open for 14% -> 9% of each run, Pallas kernels for 47% -> 50%
where the time goes in v5:
time: 746 us; the launch traced here: 745 us
  Pallas kernels  538 us (72%)
  waiting for transfers between devices  59.9 us (8%)
  matrix products  58.1 us (8%)
  blocking collectives  31 us (4%)
  local copies, waits for them, and re-layouts  25.7 us (3%)
  between operations  18.4 us (2%)
  other arithmetic  9.65 us (1%)
    pallas_call x1, Pallas kernels, feed_line(): pl.pallas_call(partial(feed_kernel, mesh_axes), in_specs=[whole, whole, r...  145 us
    pallas_call x1, Pallas kernels, input_line(): pl.pallas_call(partial(input_kernel, mesh_axes), in_specs=[whole] * 4 + [...  122 us
    pallas_call x1, Pallas kernels, output_line(): pl.pallas_call(partial(output_kernel, mesh_axes), in_specs=[whole] * 7, o...  119 us
    pallas_call x1, Pallas kernels, line_exchange(): pl.pallas_call(partial(line_exchange_kernel, transform, mesh_axes, len(ex...  117 us
    all_gather x1, waiting for transfers between devices, local(): lax.all_gather(jnp.concatenate([w_query, w_forget, w_input, w_gate_out],...  47.4 us
    unnamed x44, local copies, waits for them, and re-layouts  18.7 us
    psum x1, blocking collectives, local(): lax.psum((grad_norm_one.reshape(-1), grad_norm_two.reshape(-1), grad_head...  18.7 us
  transfers between devices with their start and end apart: 10, of which 4 were waited for; matrix products, arithmetic and copies ran while one was open for 9% of the time, Pallas kernels for 50%

profile of v5, /device:TPU:0, one launch (start us, length us, event | category | flops | bytes accessed | tf_op | source)
XLA Modules:
  0.0 745.1 jit_solution(13745118376733451478)
XLA Ops:
  7.2 2.3 pad_maximum_fusion
  9.6 0.7 all-gather.8.cloned.1.call-update
  10.4 0.7 all-gather.10.cloned.1.call-update
  11.7 0.5 all-gather.14.cloned.1.call-update
  13.2 0.6 slice.72
  14.4 0.6 fusion.11
  15.0 1.4 stack.11
  17.1 3.1 fusion
  20.2 47.4 %all-gather.6.cloned.1.call-done = bf16[2048,2048]{1,0:T(8,128)(2,1)} async-done(((bf16[256,2048]{1,0:T(8,128)(2,1)}), bf16[2048,2048]{1,0:T(8,128)(2,1)}) %all-gather.6.cloned.1.call-update) | async-done | bytes 8388624 | tf_op jit(solution)/shard_map/all_gather | solution.py:1245
  67.6 14.5 %fusion.4.pre_ref.gate_ref = f32[1024,2048]{1,0:T(8,128)} fusion(bf16[2048,2048]{1,0:T(8,128)(2,1)} %all-gather.6.cloned.1.call-done, f32[2048]{0:T(1024)S(1)} %copy-done.14, f32[1024]{0:T(1024)S(1)} %add_rsqrt_fusion, bf16[1,1024,2048]{2,1,0:T(8,128)(2,1)} %param.15), kind=kOutput, calls=%fused_computation.11 | convolution fusion | flops 8598323200 | bytes 20983808 | tf_op jit(solution)/shard_map/dot_general | solution.py:1257
  82.2 9.6 %mixer_forward.1 = (f32[1024,512]{1,0:T(8,128)S(1)}, bf16[1024,512]{1,0:T(8,128)(2,1)S(1)}, f32[8,4,128,128]{3,2,1,0:T(8,128)S(1)}, f32[8,1,512]{2,1,0:T(1,128)S...) custom-call(f32[1024,2048]{1,0:T(8,128)} %fusion.4.pre_ref.gate_ref, f32[1,512]{1,0:T(1,128)S(1)} %bitcast.54, ...), custom_call_target="tpu_custom_call" | custom-call | flops 805306368 | bytes 15728640 | tf_op jit(solution)/shard_map/mixer_forward/pallas_call | solution.py:115
  91.8 1.3 copy-done
  93.3 2.2 collective-permute-start
  95.5 1.1 collective-permute-done
  99.2 4.1 gate_forward.1
  103.3 1.3 copy-done.2
  104.6 6.0 convolution_convert_fusion.2.refs_0_
  110.6 116.8 %mix_line.1 = (bf16[1024,2048]{1,0:T(8,128)(2,1)}, f32[512,2048]{1,0:T(8,128)}) custom-call(bf16[1024,2048]{1,0:T(8,128)(2,1)} %convolution_convert_fusion.2.refs_0_, bf16[1024,2048]{1,0:T(8,128)(2,1)} %bitcast.61, f32[1,2048]{1,0:T(1,128)S(1)} %bitcast.57), custom_call_target="tpu_custom_call" | custom-call | flops 16777216 | bytes 360000000 | tf_op jit(solution)/shard_map/mix_line/pallas_call | solution.py:666
  227.5 6.7 all-gather.14.cloned.1.call-done.down_hbm
  234.2 145.2 %feed_and_norm_two_line.1 = (bf16[1024,2048]{1,0:T(8,128)(2,1)}, f32[1,2048]{1,0:T(1,128)}, bf16[1024,1408]{1,0:T(8,128)(2,1)}, bf16[1024,1408]{1,0:T(8,128)(2,1...) custom-call(bf16[1024,2048]{1,0:T(8,128)(2,1)} %get-tuple-element.49.normed_ref, ...), custom_call_target="tpu_custom_call" | custom-call | flops 35433480192 | bytes 360000000 | tf_op jit(solution)/shard_map/feed_and_norm_two_line/pallas_call | solution.py:883
  379.4 4.7 fusion.12.grad_ref
  384.2 6.0 gate_backward.1
  390.3 1.3 collective-permute-start.1
  391.6 2.1 collective-permute-done.1
  393.7 14.5 %mixer_backward.1 = (bf16[1024,2048]{1,0:T(8,128)(2,1)S(1)}, f32[1,512]{1,0:T(1,128)S(1)}) custom-call(f32[1024,2048]{1,0:T(8,128)} %fusion.4.pre_ref.gate_ref, bf16[1024,512]{1,0:T(8,128)(2,1)S(1)} %get-tuple-element.58.grad_mixed_ref, bf16[1024,512]{1,0:T(8,128)(2,1)S(1)} %get-tuple-element.59.grad_gate_ref, f32[8,4,128,128]{3,2,1,0:T(8,128)S(1)} %copy-done.1, ...), custom_call_target="tpu_custom_call" | custom-call | flops 2013265920 | bytes 18874368 | tf_op jit(solution)/shard_map/mixer_backward/pallas_call | solution.py:392
  408.3 2.0 copy-done.6
  410.3 0.7 copy.51
  411.1 5.9 convolution_convert_fusion.3
  417.3 14.4 %convolution_convert_fusion = bf16[2048,2048]{1,0:T(8,128)(2,1)} fusion(bf16[1024,2048]{1,0:T(8,128)(2,1)} %copy-done.6, f32[2048]{0:T(1024)S(1)} %copy-done.14, f32[1024]{0:T(1024)S(1)} %add_rsqrt_fusion, bf16[1,1024,2048]{2,1,0:T(8,128)(2,1)} %param.15), kind=kOutput, calls=%fused_computation.5 | convolution fusion | flops 8602517504 | bytes 16789504 | tf_op jit(solution)/shard_map/td,tk->dk/dot_general | solution.py:1310
  431.7 0.6 copy-done.17
  432.4 0.6 dynamic-slice
  434.3 119.4 %output_line.1 = (bf16[1024,2048]{1,0:T(8,128)(2,1)}, bf16[3,2048,1408]{2,1,0:T(8,128)(2,1)}) custom-call(bf16[1024,2048]{1,0:T(8,128)(2,1)} %get-tuple-element.51.part, f32[512,2048]{1,0:T(8,128)} %get-tuple-element.50.residual_hbm.residual, bf16[1024,2048]{1,0:T(8,128)(2,1)} %get-tuple-element.49.normed_ref, bf16[1024,2048]{1,0:T(8,128)(2,1)} %bitcast.80, ...), custom_call_target="tpu_custom_call" | custom-call | flops 17716740096 | bytes 360000000 | tf_op jit(solution)/shard_map/output_line/pallas_call | solution.py:985
  553.7 12.6 %convolution_convert_fusion.1.part = bf16[1024,2048]{1,0:T(8,128)(2,1)} fusion(bf16[1024,2048]{1,0:T(8,128)(2,1)S(1)} %copy-done.7, bf16[2048,2048]{1,0:T(8,128)(2,1)} %all-gather.6.cloned.1.call-done), kind=kOutput, calls=%fused_computation.8 | convolution fusion | flops 8592031744 | bytes 16777216 | tf_op jit(solution)/shard_map/tk,dk->td/dot_general | solution.py:1311
  566.3 122.5 %input_line.1 = (bf16[1024,2048]{1,0:T(8,128)(2,1)}, f32[1,2048]{1,0:T(1,128)}, f32[256,1408]{1,0:T(8,128)}, f32[256,1408]{1,0:T(8,128)}, f32[256,1408]{1,0:T(8,128)}) custom-call(bf16[1024,2048]{1,0:T(8,128)(2,1)} %convolution_convert_fusion.1.part, bf16[1024,2048]{1,0:T(8,128)(2,1)} %bitcast.62, f32[512,2048]{1,0:T(8,128)} %get-tuple-element.64.residual_grad, ...), custom_call_target="tpu_custom_call" | custom-call | flops 16777216 | bytes 360000000 | tf_op jit(solution)/shard_map/input_line/pallas_call | solution.py:1185
  688.8 2.9 copy.50
  691.7 18.7 %all-reduce.4 = (bf16[2048]{0:T(1024)(128)(2,1)S(1)}, bf16[128]{0:T(256)(128)(2,1)S(1)}, bf16[2048]{0:T(1024)(128)(2,1)S(1)}) all-reduce(f32[2048]{0:T(1024)} %bitcast.75, f32[128]{0:T(128)S(1)} %bitcast.60, f32[2048]{0:T(1024)S(1)} %bitcast.74), channel_id=1, replica_groups=mesh['shard'=4,'context'=2,'tensor'=4] {'tensor'}, use_global_device_ids=true, to_apply=%region_2.3 | all-reduce | flops 4224 | bytes 25344 | tf_op jit(solution)/shard_map/psum | solution.py:1315
  710.4 12.3 %all-reduce.5 = (bf16[2048]{0:T(1024)(128)(2,1)S(1)}, bf16[128]{0:T(256)(128)(2,1)S(1)}, bf16[2048]{0:T(1024)(128)(2,1)S(1)}) all-reduce(bf16[2048]{0:T(1024)(128)(2,1)S(1)} %get-tuple-element.130, bf16[128]{0:T(256)(128)(2,1)S(1)} %get-tuple-element.131, ...), channel_id=2, replica_groups=mesh['shard'=4,'context'=2,'tensor'=4] {'shard','context'}, use_global_device_ids=true, to_apply=%region_3.4.clone | all-reduce | flops 4224 | bytes 16896
  722.7 0.6 dynamic-slice_convert_fusion.1
  723.3 0.6 dynamic-slice_convert_fusion
  723.9 0.8 copy.52
  724.7 0.6 convert_element_type.101
  725.2 1.8 convert_element_type.105
  727.0 2.8 fusion.9
  729.9 2.1 copy.57
  732.1 1.6 copy-done.9
  733.6 2.1 copy.58
  736.0 1.1 copy.59
  737.1 1.1 copy.60
  (78 shorter events, 4.0 us)
Async XLA Ops:
  7.2 5.1 copy-start.12
  7.2 9.9 %copy-start.15 = (f32[4,128]{1,0:T(4,128)S(1)}, f32[4,128]{1,0:T(4,128)}, u32[]{:S(2)}) copy-start(f32[4,128]{1,0:T(4,128)} %param.22) | copy-start | bytes 6148
  7.2 60.4 %all-gather.6.cloned.1.call-start = ((), (), s32[]{:S(2)}) async-start(), calls=%async_computation.3 | async-start | bytes 9437184 | tf_op jit(solution)/shard_map/all_gather | solution.py:1245
  9.6 58.1 %copy-start.14 = (f32[2048]{0:T(1024)S(1)}, f32[2048]{0:T(1024)}, u32[]{:S(2)}) copy-start(f32[2048]{0:T(1024)} %param.17) | copy-start | bytes 24580
  9.6 95.0 %all-gather.8.cloned.1.call-start = ((), (), s32[]{:S(2)}) async-start(), calls=%async_computation.4 | async-start | bytes 2359296 | tf_op jit(solution)/shard_map/all_gather | solution.py:1248
  10.3 217.1 %all-gather.10.cloned.1.call-start = ((), (), s32[]{:S(2)}) async-start(), calls=%async_computation.5 | async-start | bytes 6488064 | tf_op jit(solution)/shard_map/all_gather | solution.py:1249
  11.1 216.4 %all-gather.12.cloned.1.call-start = ((), (), s32[]{:S(2)}) async-start(), calls=%async_computation.6 | async-start | bytes 6488064 | tf_op jit(solution)/shard_map/all_gather | solution.py:1250
  11.6 222.6 %all-gather.14.cloned.1.call-start = ((), (), s32[]{:S(2)}) async-start(), calls=%async_computation.7 | async-start | bytes 6488064 | tf_op jit(solution)/shard_map/all_gather | solution.py:1251
  12.2 711.7 %reduce-scatter.10.cloned.1.call-start = ((), (), s32[]{:S(2)}) async-start(), calls=%async_computation.10 | async-start | bytes 36864
  82.2 17.0 %copy-start.5 = (f32[128]{0:T(128)S(1)}, f32[128]{0:T(128)}, u32[]{:S(2)}) copy-start(f32[128]{0:T(128)} %param.23) | copy-start | bytes 1540
  91.8 1.3 copy-start
  93.3 3.4 collective-permute-start
  103.3 1.3 copy-start.2
  104.6 6.0 copy-start.4
  234.2 145.2 %copy-start.16 = (bf16[512,2048]{1,0:T(8,128)(2,1)S(1)}, bf16[512,2048]{1,0:T(8,128)(2,1)}, u32[]{:S(2)}) copy-start(bf16[512,2048]{1,0:T(8,128)(2,1)} %all-gather.8.cloned.1.call-done) | copy-start | bytes 6291460
  379.4 4.7 copy-start.3
  384.2 9.6 %copy-start.1 = (f32[8,4,128,128]{3,2,1,0:T(8,128)S(1)}, f32[8,4,128,128]{3,2,1,0:T(8,128)}, u32[]{:S(2)}) copy-start(f32[8,4,128,128]{3,2,1,0:T(8,128)} %copy-done) | copy-start | bytes 6291460
  390.3 3.4 collective-permute-start.1
  408.3 2.0 copy-start.6
  411.1 314.2 %reduce-scatter.8.cloned.1.call-start = ((), (), s32[]{:S(2)}) async-start(), calls=%async_computation.9 | async-start | bytes 2359296 | tf_op jit(solution)/shard_map/reduce_scatter | solution.py:1321
  417.0 310.0 %reduce-scatter.6.cloned.1.call-start = ((), (), s32[]{:S(2)}) async-start(), calls=%async_computation.8 | async-start | bytes 9437184 | tf_op jit(solution)/shard_map/reduce_scatter | solution.py:1321
  431.7 0.7 copy-start.17
  434.2 119.4 %copy-start.7 = (bf16[1024,2048]{1,0:T(8,128)(2,1)S(1)}, bf16[1024,2048]{1,0:T(8,128)(2,1)}, u32[]{:S(2)}) copy-start(bf16[1024,2048]{1,0:T(8,128)(2,1)} %copy-done.6) | copy-start | bytes 12582916
  566.3 125.4 %copy-start.13 = (f32[1,2048]{1,0:T(1,128)S(1)}, f32[1,2048]{1,0:T(1,128)}, u32[]{:S(2)}) copy-start(f32[1,2048]{1,0:T(1,128)} %get-tuple-element.70) | copy-start | bytes 24580
  727.0 2.9 copy-start.8
  729.9 3.7 copy-start.9
  733.6 2.4 copy-start.11
  733.6 3.5 copy-start.10
Sparse Core Ops, SparseCore 0:
  10.5 57.0 all-gather.5
  69.5 28.1 all-gather.7
  99.6 43.3 all-gather.9
  144.7 43.3 all-gather.11
  189.8 44.3 all-gather.13
  411.2 30.9 reduce-scatter.9
  446.4 41.2 reduce-scatter.7
  491.2 71.2 reduce-scatter.5

commit v6 on v5

--- a/solution.py
+++ b/solution.py
@@ -1213,9 +1213,306 @@
     )(part, hidden, residual_grad, gain, grads)
 
 
-def rms_parts(values):
-    inverse = lax.rsqrt(jnp.mean(values * values, axis=-1, keepdims=True) + EPSILON)
-    return (values * inverse, inverse)
+def front_kernel(
+    mesh_axes,
+    hidden_ref,
+    gain_ref,
+    query_ref,
+    forget_ref,
+    input_ref,
+    gate_ref,
+    normed_hbm,
+    pre_hbm,
+    full_hbm,
+    normed,
+    pre,
+    full,
+    save_sem,
+    normed_sem,
+    pre_sem,
+    send_sem,
+    recv_sem,
+    pair_send,
+    pair_recv,
+):
+    plane = Plane(mesh_axes)
+    chips = plane.chips
+    tokens, model_width = hidden_ref.shape
+    block, width = query_ref.shape
+    part = block // 2
+    relayed = chips == 4
+
+    def partner(distance):
+        return jnp.bitwise_xor(plane.chip, distance)
+
+    def rows_of(chip, core, half):
+        return pl.ds(pl.multiple_of((2 * chip + core) * block + half * part, part), part)
+
+    def copy(rows, distance, half, chip):
+        return pltpu.make_async_remote_copy(
+            full.at[rows],
+            full.at[rows],
+            send_sem.at[distance - 1, half],
+            recv_sem.at[distance - 1, half],
+            device_id=plane.device(chip, plane.core),
+            device_id_type=MESH_ID,
+        )
+
+    def send(distance, half):
+        if relayed and distance == 3:
+            through, target = (2, 1) if half == 0 else (1, 2)
+            return copy(
+                rows_of(partner(through), plane.core, half), 3, half, partner(target)
+            )
+        return copy(rows_of(plane.chip, plane.core, half), distance, half, partner(distance))
+
+    def forward(distance, half):
+        rows = rows_of(partner(distance), plane.core, half)
+        return pltpu.make_async_remote_copy(
+            full.at[rows],
+            full.at[rows],
+            pair_send.at[distance, half],
+            pair_recv.at[distance, half],
+            device_id=plane.device(plane.chip, 1 - plane.core),
+            device_id_type=MESH_ID,
+        )
+
+    own = pl.ds(pl.multiple_of((2 * plane.chip + plane.core) * block, block), block)
+    for which, ref in enumerate((query_ref, forget_ref, input_ref, gate_ref)):
+        full[own, which * width : (which + 1) * width] = ref[...]
+    barrier = pltpu.get_barrier_semaphore()
+    targets = [plane.device(plane.chip, 1 - plane.core)]
+    targets += [
+        plane.device(partner(step), plane.core)
+        for step in range(1, 3 if relayed else chips)
+    ]
+    for target in targets:
+        pl.semaphore_signal(barrier, inc=1, device_id=target, device_id_type=MESH_ID)
+    pl.semaphore_wait(barrier, len(targets))
+    if relayed:
+        for distance, half in ((1, 1), (2, 0), (1, 0), (2, 1)):
+            send(distance, half).start()
+    else:
+        for distance in range(1, chips):
+            send(distance, 0).start()
+            send(distance, 1).start()
+    for half in range(2):
+        forward(0, half).start()
+
+    def norm(index, _):
+        rows = pl.ds(pl.multiple_of(index * 128, 128), 128)
+        values = hidden_ref[rows].astype(F32)
+        normed[rows] = (values * inverse_rms(values) * gain_ref[...]).astype(BF16)
+        return 0
+
+    lax.fori_loop(0, tokens // 128, norm, 0)
+    normed_save = pltpu.make_async_copy(normed, normed_hbm, normed_sem.at[0])
+    normed_save.start()
+    row_tile, column_tile = 256, 512
+
+    def pre_save(index):
+        rows = pl.ds(pl.multiple_of(index * row_tile, row_tile), row_tile)
+        return pltpu.make_async_copy(pre.at[rows], pre_hbm.at[rows], pre_sem.at[index])
+
+    def product(distance):
+        depth = pl.ds(pl.multiple_of(2 * partner(distance) * block, 2 * block), 2 * block)
+
+        def row_body(index, _):
+            rows = pl.ds(pl.multiple_of(index * row_tile, row_tile), row_tile)
+            left = normed[rows, depth]
+
+            def column_body(column, _):
+                columns = pl.ds(pl.multiple_of(column * column_tile, column_tile), column_tile)
+                value = mm_nn(left, full[depth, columns])
+                if distance > 0:
+                    value = value + pre[rows, columns]
+                pre[rows, columns] = value
+                return 0
+
+            lax.fori_loop(0, full.shape[1] // column_tile, column_body, 0)
+            if distance == chips - 1:
+                pre_save(index).start()
+            return 0
+
+        lax.fori_loop(0, tokens // row_tile, row_body, 0)
+
+    def full_save(distance):
+        depth = pl.ds(pl.multiple_of(2 * partner(distance) * block, 2 * block), 2 * block)
+        return pltpu.make_async_copy(full.at[depth], full_hbm.at[depth], save_sem.at[distance])
+
+    def use(distance):
+        for half in range(2):
+            forward(distance, half).wait_recv()
+        full_save(distance).start()
+        product(distance)
+
+    use(0)
+    if relayed:
+        for distance, half in ((1, 1), (2, 0), (1, 0), (2, 1)):
+            send(distance, half).wait_recv()
+            if (distance, half) in ((1, 1), (2, 0)):
+                send(3, half).start()
+            forward(distance, half).start()
+        use(1)
+        use(2)
+        for half in range(2):
+            send(3, half).wait_recv()
+            forward(3, half).start()
+        use(3)
+    else:
+        for distance in range(1, chips):
+            for half in range(2):
+                send(distance, half).wait_recv()
+                forward(distance, half).start()
+            if distance > 1:
+                use(distance - 1)
+        use(chips - 1)
+    for distance in range(chips):
+        for half in range(2):
+            if distance > 0:
+                send(distance, half).wait_send()
+            forward(distance, half).wait_send()
+        full_save(distance).wait()
+    normed_save.wait()
+    for index in range(tokens // row_tile):
+        pre_save(index).wait()
+
+
+def front(mesh_axes, collective, hidden, gain, shards):
+    tokens, model_width = hidden.shape
+    block, width = shards[0].shape
+    all_width = width * len(shards)
+    chips = lax.axis_size("shard") * lax.axis_size("context") // 2
+    whole = pl.BlockSpec(memory_space=pltpu.VMEM)
+    remote = pl.BlockSpec(memory_space=pl.ANY)
+    return pl.pallas_call(
+        partial(front_kernel, mesh_axes),
+        in_specs=[whole] * 6,
+        out_specs=[remote] * 3,
+        out_shape=[
+            jax.ShapeDtypeStruct((tokens, model_width), BF16),
+            jax.ShapeDtypeStruct((tokens, all_width), F32),
+            jax.ShapeDtypeStruct((model_width, all_width), BF16),
+        ],
+        scratch_shapes=[
+            pltpu.VMEM((tokens, model_width), BF16),
+            pltpu.VMEM((tokens, all_width), F32),
+            pltpu.VMEM((model_width, all_width), BF16),
+            pltpu.SemaphoreType.DMA((chips,)),
+            pltpu.SemaphoreType.DMA((1,)),
+            pltpu.SemaphoreType.DMA((tokens // 256,)),
+            pltpu.SemaphoreType.DMA((chips - 1, 2)),
+            pltpu.SemaphoreType.DMA((chips - 1, 2)),
+            pltpu.SemaphoreType.DMA((chips, 2)),
+            pltpu.SemaphoreType.DMA((chips, 2)),
+        ],
+        compiler_params=pltpu.CompilerParams(
+            collective_id=collective, has_side_effects=True, vmem_limit_bytes=48 << 20
+        ),
+        cost_estimate=pl.CostEstimate(
+            flops=2 * tokens * model_width * all_width,
+            bytes_accessed=160_000_000,
+            transcendentals=0,
+        ),
+        name="front",
+    )(hidden, gain, *shards)
+
+
+def small_sum_kernel(
+    mesh_axes, value, local_ref, total_ref, near, far, near_send, near_recv, far_send, far_recv
+):
+    shard_size, context_size = lax.axis_size("shard"), lax.axis_size("context")
+    line_size = lax.axis_size("tensor")
+    group = shard_size * context_size
+    place = lax.axis_index("shard") * context_size + lax.axis_index("context")
+    line_place = lax.axis_index("tensor")
+
+    def device(position, line_position):
+        places = {
+            "shard": position // context_size,
+            "context": lax.rem(position, context_size),
+            "tensor": line_position,
+        }
+        return tuple(places[axis] for axis in mesh_axes)
+
+    def near_target(step):
+        return device(lax.rem(place + step, group), line_place)
+
+    def far_target(step):
+        return device(place, lax.rem(line_place + step, line_size))
+
+    def near_copy(step):
+        return pltpu.make_async_remote_copy(
+            value,
+            near.at[step - 1],
+            near_send.at[step - 1],
+            near_recv.at[step - 1],
+            device_id=near_target(step),
+            device_id_type=MESH_ID,
+        )
+
+    def far_copy(step):
+        return pltpu.make_async_remote_copy(
+            local_ref,
+            far.at[step - 1],
+            far_send.at[step - 1],
+            far_recv.at[step - 1],
+            device_id=far_target(step),
+            device_id_type=MESH_ID,
+        )
+
+    barrier = pltpu.get_barrier_semaphore()
+    for step in range(1, group):
+        pl.semaphore_signal(barrier, inc=1, device_id=near_target(step), device_id_type=MESH_ID)
+    for step in range(1, line_size):
+        pl.semaphore_signal(barrier, inc=1, device_id=far_target(step), device_id_type=MESH_ID)
+    pl.semaphore_wait(barrier, group + line_size - 2)
+    for step in range(1, group):
+        near_copy(step).start()
+    total = value[...]
+    for step in range(1, group):
+        near_copy(step).wait_recv()
+        total = total + near[step - 1]
+    local_ref[...] = total
+    for step in range(1, line_size):
+        far_copy(step).start()
+    for step in range(1, line_size):
+        far_copy(step).wait_recv()
+        total = total + far[step - 1]
+    total_ref[...] = total
+    for step in range(1, group):
+        near_copy(step).wait_send()
+    for step in range(1, line_size):
+        far_copy(step).wait_send()
+
+
+def small_sum(mesh_axes, collective, values):
+    flat = jnp.concatenate([value.reshape(-1) for value in values])
+    lanes = -(-flat.shape[0] // 1024) * 128
+    flat = jnp.pad(flat, (0, 8 * lanes - flat.shape[0])).reshape(8, lanes)
+    group = lax.axis_size("shard") * lax.axis_size("context")
+    line_size = lax.axis_size("tensor")
+    whole = pl.BlockSpec(memory_space=pltpu.VMEM)
+    local, total = pl.pallas_call(
+        partial(small_sum_kernel, mesh_axes),
+        in_specs=[whole],
+        out_specs=[whole] * 2,
+        out_shape=[jax.ShapeDtypeStruct((8, lanes), F32)] * 2,
+        scratch_shapes=[
+            pltpu.VMEM((group - 1, 8, lanes), F32),
+            pltpu.VMEM((line_size - 1, 8, lanes), F32),
+            pltpu.SemaphoreType.DMA((group - 1,)),
+            pltpu.SemaphoreType.DMA((group - 1,)),
+            pltpu.SemaphoreType.DMA((line_size - 1,)),
+            pltpu.SemaphoreType.DMA((line_size - 1,)),
+        ],
+        compiler_params=pltpu.CompilerParams(collective_id=collective, has_side_effects=True),
+        cost_estimate=pl.CostEstimate(
+            flops=8 * lanes * group, bytes_accessed=20_000_000, transcendentals=0
+        ),
+        name="small_sum",
+    )(flat)
+    return local.reshape(-1), total.reshape(-1)
 
 
 def local(
@@ -1242,19 +1539,19 @@
     width = head_count * key_dim
     key_scale = key_dim ** (-0.5)
     both = ("shard", "context")
-    mixer_full = lax.all_gather(
-        jnp.concatenate([w_query, w_forget, w_input, w_gate_out], axis=1), both, axis=0, tiled=True
+    gain_one, gain_two = norm1_gain.reshape(1, -1), norm2_gain.reshape(1, -1)
+    half_wide = jax.ShapeDtypeStruct((tokens // 2, model_width), F32)
+    hidden_rows = hidden.reshape(tokens, model_width)
+    normed_one, pre, mixer_full = front(
+        mesh_axes, 4, hidden_rows, gain_one, (w_query, w_forget, w_input, w_gate_out)
+    )
+    pre, w_out, w_ffn_gate, w_ffn_up, w_ffn_down = lax.optimization_barrier(
+        (pre, w_out, w_ffn_gate, w_ffn_up, w_ffn_down)
     )
     out_full = lax.all_gather(w_out, both, axis=1, tiled=True)
     gate_full = lax.all_gather(w_ffn_gate, both, axis=0, tiled=True)
     up_full = lax.all_gather(w_ffn_up, both, axis=0, tiled=True)
     down_full = lax.all_gather(w_ffn_down, both, axis=1, tiled=True)
-    gain_one, gain_two = norm1_gain.reshape(1, -1), norm2_gain.reshape(1, -1)
-    half_wide = jax.ShapeDtypeStruct((tokens // 2, model_width), F32)
-    hidden_rows = hidden.reshape(tokens, model_width)
-    unit_rows, _ = rms_parts(hidden_rows.astype(F32))
-    normed_one = (unit_rows * norm1_gain).astype(BF16)
-    pre = jnp.dot(normed_one, mixer_full, preferred_element_type=F32)
     open_part = (1.0 - forget_floor).reshape(1, width)
     counts, keep, flags, last_count = row_flags(segment_ids)
     mixed_local, lead, starts, runs, state_end, run_end = mixer_forward(
@@ -1312,10 +1609,18 @@
     input_rows, grad_norm_one, share_gate, share_up, share_down = input_line(
         mesh_axes, 3, back_one.astype(BF16), hidden_rows, grad_residual, gain_one, grads_ffn
     )
-    grad_norm_one, grad_norm_two, head_total = lax.psum(
-        (grad_norm_one.reshape(-1), grad_norm_two.reshape(-1), grad_head_part.reshape(-1)),
-        "tensor",
-    )
+    near, total = small_sum(
+        mesh_axes, 5, (grad_norm_one, grad_norm_two, grad_head_part, grad_floor_part)
+    )
+    shares = lax.axis_size("shard") * lax.axis_size("context")
+    position = lax.axis_index("shard") * lax.axis_size("context") + lax.axis_index("context")
+
+    def own_slice(values, first, length):
+        values = values[first : first + length].reshape(shares, length // shares)
+        return lax.dynamic_index_in_dim(values, position, 0, False)
+
+    floor_total = near[2 * model_width + key_dim : 2 * model_width + key_dim + width]
+    floor_total = floor_total.reshape(head_count, shares, key_dim // shares)
 
     def share(values, dim):
         return lax.psum_scatter(
@@ -1326,15 +1631,15 @@
     return (
         output_rows.reshape(hidden.shape),
         input_rows.reshape(hidden.shape),
-        share(grad_norm_one, 0),
+        own_slice(total, 0, model_width),
         share_mixer[:, :width],
         share_mixer[:, width : 2 * width],
         share_mixer[:, 2 * width : 3 * width],
         share_mixer[:, 3 * width :],
-        share(grad_floor_part.reshape(head_count, key_dim), 1),
-        share(head_total, 0),
+        lax.dynamic_index_in_dim(floor_total, position, 1, False),
+        own_slice(total, 2 * model_width, key_dim),
         share(grad_out, 1),
-        share(grad_norm_two, 0),
+        own_slice(total, model_width, model_width),
         share_gate,
         share_up,
         share_down.T,

time: 746 us -> 722 us (0.968)
  Pallas kernels: 538 us -> 603 us
  waiting for transfers between devices: 59.9 us -> 19.1 us
  blocking collectives: 31 us -> 0 us
  matrix products: 58.1 us -> 41 us
  local copies, waits for them, and re-layouts: 25.7 us -> 34.2 us
    pallas_call x0 -> x2, Pallas kernels: none -> 64.4 us  [the longest x1 51.5 us: front(): pl.pallas_call(partial(front_kernel, mesh_axes), in_specs=[whole] * 6, ou...]
    all_gather x1 -> x0, waiting for transfers between devices: 47.4 us -> none  [local(): lax.all_gather(jnp.concatenate([w_query, w_forget, w_input, w_gate_out],...]
    psum x1 -> x0, blocking collectives: 18.7 us -> none  [local(): lax.psum((grad_norm_one.reshape(-1), grad_norm_two.reshape(-1), grad_head...]
    dot_general x1 -> x0, matrix products: 14.5 us -> none  [local(): pre = jnp.dot(normed_one, mixer_full, preferred_element_type=F32)]
    all_gather x1, waiting for transfers between devices: 0.02 us -> 13.6 us  [local(): up_full = lax.all_gather(w_ffn_up, both, axis=0, tiled=True)]
    unnamed x1 -> x0, blocking collectives: 12.3 us -> none
    unnamed x44 -> x49, local copies, waits for them, and re-layouts: 18.7 us -> 22.5 us
  transfers between devices with their start and end apart: 10 -> 8, of which waited for: 4 -> 4; matrix products, arithmetic and copies ran while one was open for 9% -> 7% of each run, Pallas kernels for 50% -> 56%
where the time goes in v6:
time: 722 us; the launch traced here: 721 us
  Pallas kernels  603 us (84%)
  matrix products  41 us (6%)
  local copies, waits for them, and re-layouts  34.2 us (5%)
  waiting for transfers between devices  19.1 us (3%)
  between operations  17.1 us (2%)
    pallas_call x1, Pallas kernels, feed_line(): pl.pallas_call(partial(feed_kernel, mesh_axes), in_specs=[whole, whole, r...  145 us
    pallas_call x1, Pallas kernels, input_line(): pl.pallas_call(partial(input_kernel, mesh_axes), in_specs=[whole] * 4 + [...  122 us
    pallas_call x1, Pallas kernels, output_line(): pl.pallas_call(partial(output_kernel, mesh_axes), in_specs=[whole] * 7, o...  120 us
    pallas_call x1, Pallas kernels, line_exchange(): pl.pallas_call(partial(line_exchange_kernel, transform, mesh_axes, len(ex...  117 us
    pallas_call x1, Pallas kernels, front(): pl.pallas_call(partial(front_kernel, mesh_axes), in_specs=[whole] * 6, ou...  51.5 us
    unnamed x49, local copies, waits for them, and re-layouts  22.5 us
    pallas_call x1, Pallas kernels, mixer_backward(): pl.pallas_call(partial(mixer_backward_kernel, head_count), grid=(blocks,)...  14.6 us
  transfers between devices with their start and end apart: 8, of which 4 were waited for; matrix products, arithmetic and copies ran while one was open for 7% of the time, Pallas kernels for 56%

profile of v6, /device:TPU:0, one launch (start us, length us, event | category | flops | bytes accessed | tf_op | source)
XLA Modules:
  0.0 720.7 jit_solution(17209603129534162143)
XLA Ops:
  7.2 0.7 copy-done.5
  7.9 0.9 copy-done.9
  8.9 0.9 copy-done.10
  9.8 0.9 copy-done.11
  10.8 0.9 copy-done.12
  11.7 51.5 %front.1 = (bf16[1024,2048]{1,0:T(8,128)(2,1)S(1)}, f32[1024,2048]{1,0:T(8,128)}, bf16[2048,2048]{1,0:T(8,128)(2,1)}) custom-call(bf16[1024,2048]{1,0:T(8,128)(2,1)} %bitcast.57, f32[1,2048]{1,0:T(1,128)S(1)} %bitcast.52, bf16[256,512]{1,0:T(8,128)(2,1)S(1)} %copy-done.9, bf16[256,512]{1,0:T(8,128)(2,1)S(1)} %copy-done.10, bf16[256,512]{1,0:T(8,128)(2,1)S(1)} %copy-done.11, ...), custom_call_target="tpu_custom_call" | custom-call | flops 8589934592 | bytes 160000000 | tf_op jit(solution)/shard_map/front/pallas_call | solution.py:1388
  63.2 2.0 copy-done.13
  65.3 0.7 all-gather.11.cloned.1.call-update
  66.1 0.7 all-gather.7.cloned.1.call-update
  68.3 0.6 slice.94
  69.5 0.6 fusion.5
  70.1 1.4 stack.11
  72.2 9.5 %mixer_forward.1 = (f32[1024,512]{1,0:T(8,128)S(1)}, bf16[1024,512]{1,0:T(8,128)(2,1)S(1)}, f32[8,4,128,128]{3,2,1,0:T(8,128)S(1)}, f32[8,1,512]{2,1,0:T(1,128)S...) custom-call(f32[1024,2048]{1,0:T(8,128)} %get-tuple-element.55.pre_ref.gate_ref, f32[1,512]{1,0:T(1,128)S(1)} %bitcast.47, ...), custom_call_target="tpu_custom_call" | custom-call | flops 805306368 | bytes 15728640 | tf_op jit(solution)/shard_map/mixer_forward/pallas_call | solution.py:115
  81.8 1.3 copy-done
  83.3 1.3 collective-permute-start
  84.6 1.1 collective-permute-done
  88.2 4.1 gate_forward.1
  92.3 1.3 copy-done.2
  93.9 6.0 convolution_convert_fusion.2.refs_0_
  99.8 117.0 %mix_line.1 = (bf16[1024,2048]{1,0:T(8,128)(2,1)}, f32[512,2048]{1,0:T(8,128)}) custom-call(bf16[1024,2048]{1,0:T(8,128)(2,1)} %convolution_convert_fusion.2.refs_0_, bf16[1024,2048]{1,0:T(8,128)(2,1)} %bitcast.58, f32[1,2048]{1,0:T(1,128)S(1)} %bitcast.50), custom_call_target="tpu_custom_call" | custom-call | flops 16777216 | bytes 360000000 | tf_op jit(solution)/shard_map/mix_line/pallas_call | solution.py:666
  216.9 13.6 %all-gather.9.cloned.1.call-done.up_hbm = bf16[2048,1408]{1,0:T(8,128)(2,1)} async-done(((bf16[256,1408]{1,0:T(8,128)(2,1)}), bf16[2048,1408]{1,0:T(8,128)(2,1)}) %all-gather.9.cloned.1.call-update) | async-done | bytes 5767184 | tf_op jit(solution)/shard_map/all_gather | solution.py:1553
  230.5 145.0 %feed_and_norm_two_line.1 = (bf16[1024,2048]{1,0:T(8,128)(2,1)}, f32[1,2048]{1,0:T(1,128)}, bf16[1024,1408]{1,0:T(8,128)(2,1)}, bf16[1024,1408]{1,0:T(8,128)(2,1...) custom-call(bf16[1024,2048]{1,0:T(8,128)(2,1)} %get-tuple-element.62.normed_ref, ...), custom_call_target="tpu_custom_call" | custom-call | flops 35433480192 | bytes 360000000 | tf_op jit(solution)/shard_map/feed_and_norm_two_line/pallas_call | solution.py:883
  375.5 5.9 convolution_convert_fusion.3
  381.6 5.4 fusion.6.grad_ref
  387.0 6.1 gate_backward.1
  393.2 1.3 collective-permute-start.1
  394.5 2.1 collective-permute-done.1
  396.6 14.6 %mixer_backward.1 = (bf16[1024,2048]{1,0:T(8,128)(2,1)S(1)}, f32[1,512]{1,0:T(1,128)S(1)}) custom-call(f32[1024,2048]{1,0:T(8,128)} %get-tuple-element.55.pre_ref.gate_ref, bf16[1024,512]{1,0:T(8,128)(2,1)S(1)} %get-tuple-element.74.grad_mixed_ref, bf16[1024,512]{1,0:T(8,128)(2,1)S(1)} %get-tuple-element.75.grad_gate_ref, f32[8,4,128,128]{3,2,1,0:T(8,128)S(1)} %copy-done.1, ...), custom_call_target="tpu_custom_call" | custom-call | flops 2013265920 | bytes 18874368 | tf_op jit(solution)/shard_map/mixer_backward/pallas_call | solution.py:392
  411.3 2.0 copy-done.7
  413.3 11.2 %convolution_convert_fusion = bf16[2048,2048]{1,0:T(8,128)(2,1)} fusion(bf16[1024,2048]{1,0:T(8,128)(2,1)S(1)} %copy-done.14, bf16[1024,2048]{1,0:T(8,128)(2,1)S(1)} %get-tuple-element.79), kind=kOutput, calls=%fused_computation | convolution fusion | flops 8594128896 | bytes 16777216 | tf_op jit(solution)/shard_map/td,tk->dk/dot_general | solution.py:1607
  424.5 120.1 %output_line.1 = (bf16[1024,2048]{1,0:T(8,128)(2,1)}, bf16[3,2048,1408]{2,1,0:T(8,128)(2,1)}) custom-call(bf16[1024,2048]{1,0:T(8,128)(2,1)} %get-tuple-element.67.part, f32[512,2048]{1,0:T(8,128)} %get-tuple-element.63.residual_hbm.residual, bf16[1024,2048]{1,0:T(8,128)(2,1)} %get-tuple-element.62.normed_ref, bf16[1024,2048]{1,0:T(8,128)(2,1)} %bitcast.76, ...), custom_call_target="tpu_custom_call" | custom-call | flops 17716740096 | bytes 360000000 | tf_op jit(solution)/shard_map/output_line/pallas_call | solution.py:985
  544.6 12.6 %convolution_convert_fusion.1.part = bf16[1024,2048]{1,0:T(8,128)(2,1)} fusion(bf16[1024,2048]{1,0:T(8,128)(2,1)S(1)} %copy-done.8, bf16[2048,2048]{1,0:T(8,128)(2,1)} %get-tuple-element.80), kind=kOutput, calls=%fused_computation.3 | convolution fusion | flops 8592031744 | bytes 16777216 | tf_op jit(solution)/shard_map/tk,dk->td/dot_general | solution.py:1608
  557.2 122.4 %input_line.1 = (bf16[1024,2048]{1,0:T(8,128)(2,1)}, f32[1,2048]{1,0:T(1,128)}, f32[256,1408]{1,0:T(8,128)}, f32[256,1408]{1,0:T(8,128)}, f32[256,1408]{1,0:T(8,128)}) custom-call(bf16[1024,2048]{1,0:T(8,128)(2,1)} %convolution_convert_fusion.1.part, bf16[1024,2048]{1,0:T(8,128)(2,1)} %bitcast.59, f32[512,2048]{1,0:T(8,128)} %get-tuple-element.81.residual_grad, ...), custom_call_target="tpu_custom_call" | custom-call | flops 16777216 | bytes 360000000 | tf_op jit(solution)/shard_map/input_line/pallas_call | solution.py:1185
  679.6 0.7 select_maximum_fusion
  680.3 0.6 reshape.159.value
  680.9 12.9 %small_sum.1 = (f32[8,640]{1,0:T(8,128)}, f32[8,640]{1,0:T(8,128)}) custom-call(f32[8,640]{1,0:T(8,128)} %reshape.159.value), custom_call_target="tpu_custom_call" | custom-call | flops 40960 | bytes 20000000 | tf_op jit(solution)/shard_map/small_sum/pallas_call | solution.py:1496
  693.8 0.8 slice.111
  694.7 0.7 slice.103
  695.4 0.8 slice.109
  696.3 2.9 copy.44
  699.7 0.6 constant_dynamic-slice_fusion.2
  700.8 1.8 convert_element_type.65
  702.6 2.8 fusion.2
  705.5 2.1 copy.49
  707.7 1.6 copy-done.16
  709.2 2.1 copy.50
  711.6 1.1 copy.51
  712.7 1.1 copy.52
  (80 shorter events, 5.2 us)
Async XLA Ops:
  7.2 86.7 %all-gather.5.cloned.1.call-start = ((), (), s32[]{:S(2)}) async-start(), calls=%async_computation.2 | async-start | bytes 2359296 | tf_op jit(solution)/shard_map/all_gather | solution.py:1551
  7.2 0.7 copy-start.5
  7.9 0.9 copy-start.9
  8.9 0.9 copy-start.10
  9.8 0.9 copy-start.11
  10.8 0.9 copy-start.12
  11.7 55.6 %copy-start.19 = (s32[1,1024]{1,0:T(1,128)S(1)}, s32[1,1024]{1,0:T(1,128)}, u32[]{:S(2)}) copy-start(s32[1,1024]{1,0:T(1,128)} %param.16) | copy-start | bytes 12292
  11.7 60.5 %copy-start.21 = (f32[4,128]{1,0:T(4,128)S(1)}, f32[4,128]{1,0:T(4,128)}, u32[]{:S(2)}) copy-start(f32[4,128]{1,0:T(4,128)} %param.22) | copy-start | bytes 6148
  63.2 2.0 copy-start.13
  65.3 151.6 %all-gather.11.cloned.1.call-start = ((), (), s32[]{:S(2)}) async-start(), calls=%async_computation.5 | async-start | bytes 6488064 | tf_op jit(solution)/shard_map/all_gather | solution.py:1554
  66.0 150.9 %all-gather.7.cloned.1.call-start = ((), (), s32[]{:S(2)}) async-start(), calls=%async_computation.3 | async-start | bytes 6488064 | tf_op jit(solution)/shard_map/all_gather | solution.py:1552
  66.7 163.8 %all-gather.9.cloned.1.call-start = ((), (), s32[]{:S(2)}) async-start(), calls=%async_computation.4 | async-start | bytes 6488064 | tf_op jit(solution)/shard_map/all_gather | solution.py:1553
  67.3 633.5 %reduce-scatter.5.cloned.1.call-start = ((), (), s32[]{:S(2)}) async-start(), calls=%async_computation.7 | async-start | bytes 2359296 | tf_op jit(solution)/shard_map/reduce_scatter | solution.py:1626
  72.2 16.0 %copy-start.6 = (f32[128]{0:T(128)S(1)}, f32[128]{0:T(128)}, u32[]{:S(2)}) copy-start(f32[128]{0:T(128)} %param.23) | copy-start | bytes 1540
  81.8 1.3 copy-start
  83.3 2.5 collective-permute-start
  92.3 1.3 copy-start.2
  93.9 6.0 copy-start.4
  381.4 321.2 %reduce-scatter.3.cloned.1.call-start = ((), (), s32[]{:S(2)}) async-start(), calls=%async_computation.6 | async-start | bytes 9437184 | tf_op jit(solution)/shard_map/reduce_scatter | solution.py:1626
  381.6 5.4 copy-start.3
  387.0 9.6 %copy-start.1 = (f32[8,4,128,128]{3,2,1,0:T(8,128)S(1)}, f32[8,4,128,128]{3,2,1,0:T(8,128)}, u32[]{:S(2)}) copy-start(f32[8,4,128,128]{3,2,1,0:T(8,128)} %copy-done) | copy-start | bytes 6291460
  393.2 3.4 collective-permute-start.1
  396.6 16.6 %copy-start.14 = (bf16[1024,2048]{1,0:T(8,128)(2,1)S(1)}, bf16[1024,2048]{1,0:T(8,128)(2,1)}, u32[]{:S(2)}) copy-start(bf16[1024,2048]{1,0:T(8,128)(2,1)} %copy-done.13) | copy-start | bytes 12582916
  411.2 2.0 copy-start.7
  424.5 120.1 %copy-start.8 = (bf16[1024,2048]{1,0:T(8,128)(2,1)S(1)}, bf16[1024,2048]{1,0:T(8,128)(2,1)}, u32[]{:S(2)}) copy-start(bf16[1024,2048]{1,0:T(8,128)(2,1)} %copy-done.7) | copy-start | bytes 12582916
  557.2 122.4 %copy-start.20 = (f32[1,2048]{1,0:T(1,128)S(1)}, f32[1,2048]{1,0:T(1,128)}, u32[]{:S(2)}) copy-start(f32[1,2048]{1,0:T(1,128)} %get-tuple-element.85) | copy-start | bytes 24580
  702.6 2.9 copy-start.15
  705.5 3.7 copy-start.16
  709.2 2.4 copy-start.18
  709.2 3.5 copy-start.17
Sparse Core Ops, SparseCore 0:
  65.4 28.4 all-gather.4
  95.7 44.3 all-gather.10
  142.0 43.3 all-gather.6
  187.1 43.3 all-gather.8
  381.5 40.8 reduce-scatter.4
  426.2 71.2 reduce-scatter.2

commit v7 on v6

--- a/solution.py
+++ b/solution.py
@@ -624,12 +624,27 @@
 
         lax.fori_loop(first, last, body, 0)
 
-    def finish(self):
+    def source_sent(self, first, last):
+        def body(index, _):
+            for side in (0, 1):
+
+                @pl.when(self.lines[side][0] == 0)
+                def _(side=side):
+                    self.sum_copy(side, index, self.part).wait_send()
+
+            return 0
+
+        lax.fori_loop(first, last, body, 0)
+
+    def finish(self, source_waits=True):
         def body(index, _):
             for side in (0, 1):
                 hops = self.lines[side][0]
-
-                @pl.when(hops < self.size - 1)
+                passed = hops < self.size - 1
+                if not source_waits:
+                    passed = jnp.logical_and(passed, hops > 0)
+
+                @pl.when(passed)
                 def _(side=side):
                     self.sum_copy(side, index, self.arrived).wait_send()
 
@@ -646,65 +661,206 @@
     return [pltpu.SemaphoreType.DMA((2, tokens // 2 // CHUNK))] * 4
 
 
-def line_exchange_kernel(transform, mesh_axes, n_in, n_out, *refs):
-    part, extra_in = refs[0], refs[1 : 1 + n_in]
-    out, extra_out = refs[1 + n_in], refs[2 + n_in : 2 + n_in + n_out]
-    arrived, *sems = refs[2 + n_in + n_out :]
-    def turn(total, rows, own):
-        transform(total, rows, own, extra_in, out, extra_out)
-
-    line = Line(mesh_axes, part, arrived, out, sems, turn)
-    barrier = pltpu.get_barrier_semaphore()
-    pl.semaphore_wait(barrier, line.greet(barrier))
-    line.run(0, line.steps)
-    line.finish()
-
-
-def line_exchange(transform, mesh_axes, collective, part, extras, extra_shapes, name):
-    tokens, width = part.shape
-    whole = pl.BlockSpec(memory_space=pltpu.VMEM)
-    return pl.pallas_call(
-        partial(line_exchange_kernel, transform, mesh_axes, len(extras), len(extra_shapes)),
-        in_specs=[whole] * (1 + len(extras)),
-        out_specs=[whole] * (1 + len(extra_shapes)),
-        out_shape=[jax.ShapeDtypeStruct((tokens, width), BF16)] + list(extra_shapes),
-        scratch_shapes=[pltpu.VMEM((tokens, width), BF16)] + line_sems(tokens),
-        compiler_params=pltpu.CompilerParams(
-            collective_id=collective, has_side_effects=True, vmem_limit_bytes=52 << 20
-        ),
-        cost_estimate=pl.CostEstimate(
-            flops=tokens * width * 8, bytes_accessed=360_000_000, transcendentals=0
-        ),
-        name=name,
-    )(part, *extras)
-
-
 def inverse_rms(values):
     return lax.rsqrt(jnp.mean(values * values, axis=-1, keepdims=True) + EPSILON)
 
 
-def residual_norm(total, rows, own, extra_in, out, extra_out):
-    hidden, gain = extra_in
-    residual = hidden[rows].astype(F32) + total
-    extra_out[0][own] = residual
-    out[rows] = (residual * inverse_rms(residual) * gain[...]).astype(BF16)
+class Plane:
+    def __init__(self, mesh_axes):
+        self.mesh_axes = mesh_axes
+        self.context = lax.axis_size("context")
+        self.per_row = self.context // 2
+        self.chips = lax.axis_size("shard") * self.per_row
+        context_place = lax.axis_index("context")
+        self.core = lax.rem(context_place, 2)
+        self.chip = lax.axis_index("shard") * self.per_row + context_place // 2
+
+    def device(self, chip, core):
+        places = {
+            "shard": chip // self.per_row,
+            "context": 2 * lax.rem(chip, self.per_row) + core,
+            "tensor": lax.axis_index("tensor"),
+        }
+        return tuple(places[axis] for axis in self.mesh_axes)
+
+    def ahead(self, distance):
+        return lax.rem(self.chip + distance, self.chips)
+
+    def greet(self, barrier):
+        targets = [self.device(self.chip, 1 - self.core)]
+        targets += [self.device(self.ahead(step), self.core) for step in range(1, self.chips)]
+        for target in targets:
+            pl.semaphore_signal(barrier, inc=1, device_id=target, device_id_type=MESH_ID)
+        return len(targets)
+
+
+class Gather:
+    def __init__(self, plane, sources, targets, sems):
+        self.plane, self.sources, self.targets = plane, sources, targets
+        self.load_sem, self.send_sem, self.recv_sem, self.pair_send, self.pair_recv = sems
+        self.block = sources[0].shape[0]
+        self.part = self.block // 2
+        self.relayed = plane.chips == 4
+        self.arrays = range(len(sources))
+
+    def partner(self, distance):
+        return jnp.bitwise_xor(self.plane.chip, distance)
+
+    def greet(self, barrier):
+        plane = self.plane
+        targets = [plane.device(plane.chip, 1 - plane.core)]
+        targets += [
+            plane.device(self.partner(step), plane.core)
+            for step in range(1, 3 if self.relayed else plane.chips)
+        ]
+        for target in targets:
+            pl.semaphore_signal(barrier, inc=1, device_id=target, device_id_type=MESH_ID)
+        return len(targets)
+
+    def place(self, array, chip, core, half):
+        first = (2 * chip + core) * self.block + half * self.part
+        rows = pl.ds(pl.multiple_of(first, self.part), self.part)
+        return self.targets[array].at[rows, pl.ds(0, self.sources[array].shape[1])]
+
+    def mine(self, array, half):
+        return self.sources[array].at[pl.ds(half * self.part, self.part)]
+
+    def loads(self):
+        plane = self.plane
+        return [
+            pltpu.make_async_copy(
+                self.mine(array, half),
+                self.place(array, plane.chip, plane.core, half),
+                self.load_sem.at[array, half],
+            )
+            for array in self.arrays
+            for half in range(2)
+        ]
+
+    def send(self, distance, half):
+        plane = self.plane
+        copies = []
+        for array in self.arrays:
+            chip, target = plane.chip, self.partner(distance)
+            source = self.mine(array, half)
+            if self.relayed and distance == 3:
+                chip = self.partner(2 if half == 0 else 1)
+                target = self.partner(1 if half == 0 else 2)
+                source = self.place(array, chip, plane.core, half)
+            copies.append(
+                pltpu.make_async_remote_copy(
+                    source,
+                    self.place(array, chip, plane.core, half),
+                    self.send_sem.at[array, distance - 1, half],
+                    self.recv_sem.at[array, distance - 1, half],
+                    device_id=plane.device(target, plane.core),
+                    device_id_type=MESH_ID,
+                )
+            )
+        return copies
+
+    def forward(self, distance, half):
+        plane = self.plane
+        copies = []
+        for array in self.arrays:
+            place = self.place(array, self.partner(distance), plane.core, half)
+            copies.append(
+                pltpu.make_async_remote_copy(
+                    self.mine(array, half) if distance == 0 else place,
+                    place,
+                    self.pair_send.at[array, distance, half],
+                    self.pair_recv.at[array, distance, half],
+                    device_id=plane.device(plane.chip, 1 - plane.core),
+                    device_id_type=MESH_ID,
+                )
+            )
+        return copies
+
+    def start(self):
+        if self.relayed:
+            order = ((1, 1), (2, 0), (1, 0), (2, 1))
+        else:
+            order = [(step, half) for step in range(1, self.plane.chips) for half in range(2)]
+        for distance, half in order:
+            for copy in self.send(distance, half):
+                copy.start()
+        for copy in self.loads():
+            copy.start()
+        for half in range(2):
+            for copy in self.forward(0, half):
+                copy.start()
+
+    def take(self, distance, half, relay):
+        for copy in self.send(distance, half):
+            copy.wait_recv()
+        if relay:
+            for copy in self.send(3, half):
+                copy.start()
+        for copy in self.forward(distance, half):
+            copy.start()
+
+    def stage(self, number):
+        if self.relayed:
+            if number == 0:
+                self.take(1, 1, True)
+                self.take(2, 0, True)
+            elif number == 1:
+                self.take(1, 0, False)
+                self.take(2, 1, False)
+            else:
+                self.take(3, 0, False)
+                self.take(3, 1, False)
+        elif number == 2:
+            for distance in range(1, self.plane.chips):
+                for half in range(2):
+                    self.take(distance, half, False)
+
+    def arrive(self):
+        for copy in self.loads():
+            copy.wait()
+        for distance in range(self.plane.chips):
+            for half in range(2):
+                for copy in self.forward(distance, half):
+                    copy.wait_recv()
+
+    def finish(self):
+        for distance in range(self.plane.chips):
+            for half in range(2):
+                for copy in self.forward(distance, half):
+                    copy.wait_send()
+                if distance > 0:
+                    for copy in self.send(distance, half):
+                        copy.wait_send()
+
+
+def gather_sems(arrays):
+    chips = lax.axis_size("shard") * lax.axis_size("context") // 2
+    return [
+        pltpu.SemaphoreType.DMA((arrays, 2)),
+        pltpu.SemaphoreType.DMA((arrays, chips - 1, 2)),
+        pltpu.SemaphoreType.DMA((arrays, chips - 1, 2)),
+        pltpu.SemaphoreType.DMA((arrays, chips, 2)),
+        pltpu.SemaphoreType.DMA((arrays, chips, 2)),
+    ]
 
 
 GROUP = 128
 TILE = 256
 
 
-def feed_kernel(
+def middle_kernel(
     mesh_axes,
-    normed_ref,
+    mix_hbm,
     cotangent_ref,
-    residual_hbm,
+    input_hbm,
     gain_ref,
     gate_hbm,
     up_hbm,
     down_hbm,
+    normed_ref,
     out_ref,
     gain_grad,
+    residual_hbm,
     hidden_hbm,
     grad_gate_hbm,
     grad_up_hbm,
@@ -714,14 +870,17 @@
     up_w,
     down_w,
     part,
+    mix_arrived,
     arrived,
+    inputs,
     residual,
     stage_hidden,
     stage_gate,
     stage_up,
     stage_feed,
-    weight_sem,
-    residual_sem,
+    part_sem,
+    input_sem,
+    save_sem,
     stage_sem,
     grad_sem,
     *sems,
@@ -731,21 +890,23 @@
     hidden_width = gate_hbm.shape[1]
     padded = gate_w.shape[1]
     groups = half // GROUP
-    loads = [
-        pltpu.make_async_copy(gate_hbm, gate_w.at[:, pl.ds(0, hidden_width)], weight_sem.at[0]),
-        pltpu.make_async_copy(up_hbm, up_w.at[:, pl.ds(0, hidden_width)], weight_sem.at[1]),
-        pltpu.make_async_copy(down_hbm, down_w.at[pl.ds(0, hidden_width)], weight_sem.at[2]),
-    ]
-    for load in loads:
-        load.start()
-    residual_load = pltpu.make_async_copy(residual_hbm, residual, residual_sem.at[0])
-    residual_load.start()
+    place, line_size = lax.axis_index("tensor"), lax.axis_size("tensor")
+    own_half = pl.ds(pl.multiple_of(jnp.where(place == 0, 0, half), half), half)
+    part_load = pltpu.make_async_copy(mix_hbm, part, part_sem.at[0])
+    part_load.start()
+    input_load = pltpu.make_async_copy(input_hbm.at[own_half], inputs, input_sem.at[0])
+    input_load.start()
     if padded > hidden_width:
         spare = slice(hidden_width, padded)
         gate_w[:, spare] = jnp.zeros((model_width, padded - hidden_width), BF16)
         up_w[:, spare] = jnp.zeros((model_width, padded - hidden_width), BF16)
-        down_w[spare, :] = jnp.zeros((padded - hidden_width, model_width), BF16)
+        down_w[:, spare] = jnp.zeros((model_width, padded - hidden_width), BF16)
     gain_grad[...] = jnp.zeros_like(gain_grad)
+
+    def mix_turn(total, rows, own):
+        values = inputs[own].astype(F32) + total
+        residual[own] = values
+        normed_ref[rows] = (values * inverse_rms(values) * gain_ref[...]).astype(BF16)
 
     def turn(total, rows, own):
         values = residual[own]
@@ -758,12 +919,26 @@
         residual[own] = grad
         out_ref[rows] = grad.astype(BF16)
 
-    line = Line(mesh_axes, part, arrived, out_ref, sems, turn)
+    mix_line = Line(mesh_axes, part, mix_arrived, normed_ref, sems[:4], mix_turn)
+    line = Line(mesh_axes, part, arrived, out_ref, sems[4:8], turn)
+    gather = Gather(
+        Plane(mesh_axes), (gate_hbm, up_hbm, down_hbm), (gate_w, up_w, down_w), sems[8:]
+    )
     barrier = pltpu.get_barrier_semaphore()
-    pl.semaphore_wait(barrier, line.greet(barrier))
-    residual_load.wait()
-    for load in loads:
-        load.wait()
+    expected = mix_line.greet(barrier) + gather.greet(barrier)
+    pl.semaphore_wait(barrier, expected)
+    gather.start()
+    part_load.wait()
+    input_load.wait()
+    pace = GROUP // CHUNK
+    begin = pace + 2 * LAG * (line_size - 1) + 4
+    mix_line.run(0, begin - 10)
+    gather.stage(0)
+    mix_line.run(begin - 10, begin - 4)
+    gather.stage(1)
+    mix_line.run(begin - 4, begin)
+    gather.stage(2)
+    gather.arrive()
 
     def both(ref, group):
         first = pl.ds(pl.multiple_of(group * GROUP, GROUP), GROUP)
@@ -805,7 +980,7 @@
         gate = mm_nn(rows, gate_w[:, columns])
         up = mm_nn(rows, up_w[:, columns])
         grads = jnp.concatenate([cotangent_ref[first], cotangent_ref[second]], axis=0)
-        grad = mm_nt(grads, down_w[columns, :])
+        grad = mm_nn(grads, down_w[:, columns])
         sigma = jax.nn.sigmoid(gate)
         active = gate * sigma
         stage_hidden[slot, :, columns] = (active * up).astype(BF16)
@@ -822,14 +997,24 @@
         back = (back + mm_nt(stage_up[slot], up_w[columns, :])).astype(BF16)
         part[first, columns] = back[:GROUP]
         part[second, columns] = back[GROUP:]
-        stage_feed[slot, :, columns] = mm_nn(stage_hidden[slot], down_w[:, columns]).astype(BF16)
+        stage_feed[slot, :, columns] = mm_nt(stage_hidden[slot], down_w[columns, :]).astype(BF16)
 
     hidden_tiles, model_tiles = padded // TILE, model_width // TILE
     ticks = hidden_tiles + model_tiles
-    pace = GROUP // CHUNK
     piece = -(-ticks // pace)
+    save = pltpu.make_async_copy(residual, residual_hbm, save_sem.at[0])
 
     def group_body(group, _):
+        mix_line.source_sent(group * pace, (group + 1) * pace)
+
+        @pl.when(group == 1)
+        def _():
+            save.start()
+
+        @pl.when(group == 2)
+        def _():
+            save.wait()
+
         @pl.when(group >= 2)
         def _():
             for copy in stage_copies(group - 2):
@@ -851,6 +1036,12 @@
 
             lax.fori_loop(0, piece, tick_body, 0)
 
+            mix_time = begin + group * pace + index
+
+            @pl.when(mix_time < mix_line.steps)
+            def _():
+                mix_line.step(mix_time)
+
             @pl.when(group >= 1)
             def _():
                 line.step((group - 1) * pace + index)
@@ -864,29 +1055,33 @@
 
     lax.fori_loop(0, groups, group_body, 0)
     line.run((groups - 1) * pace, line.steps)
-    save = pltpu.make_async_copy(residual, grad_hbm, grad_sem.at[0])
-    save.start()
+    grad_save = pltpu.make_async_copy(residual, grad_hbm, grad_sem.at[0])
+    grad_save.start()
     for group in range(max(groups - 2, 0), groups):
         for copy in stage_copies(group):
             copy.wait()
+    gather.finish()
+    mix_line.finish(source_waits=False)
     line.finish()
-    save.wait()
-
-
-def feed_line(mesh_axes, collective, normed, cotangent, residual, gain, gate_w, up_w, down_w):
-    tokens, model_width = normed.shape
+    grad_save.wait()
+
+
+def middle(mesh_axes, collective, mix, cotangent, inputs, gain, gate_w, up_w, down_w):
+    tokens, model_width = mix.shape
     hidden_width = gate_w.shape[1]
     padded = -(-hidden_width // TILE) * TILE
     whole = pl.BlockSpec(memory_space=pltpu.VMEM)
     remote = pl.BlockSpec(memory_space=pl.ANY)
     group_rows = 2 * GROUP
     return pl.pallas_call(
-        partial(feed_kernel, mesh_axes),
-        in_specs=[whole, whole, remote, whole, remote, remote, remote],
-        out_specs=[whole, whole] + [remote] * 5,
+        partial(middle_kernel, mesh_axes),
+        in_specs=[remote, whole, remote, whole, remote, remote, remote],
+        out_specs=[whole, whole, whole] + [remote] * 6,
         out_shape=[
             jax.ShapeDtypeStruct((tokens, model_width), BF16),
+            jax.ShapeDtypeStruct((tokens, model_width), BF16),
             jax.ShapeDtypeStruct((1, model_width), F32),
+            jax.ShapeDtypeStruct((tokens // 2, model_width), F32),
             jax.ShapeDtypeStruct((tokens, hidden_width), BF16),
             jax.ShapeDtypeStruct((tokens, hidden_width), BF16),
             jax.ShapeDtypeStruct((tokens, hidden_width), BF16),
@@ -896,30 +1091,35 @@
         scratch_shapes=[
             pltpu.VMEM((model_width, padded), BF16),
             pltpu.VMEM((model_width, padded), BF16),
-            pltpu.VMEM((padded, model_width), BF16),
+            pltpu.VMEM((model_width, padded), BF16),
             pltpu.VMEM((tokens, model_width), BF16),
             pltpu.VMEM((tokens, model_width), BF16),
+            pltpu.VMEM((tokens, model_width), BF16),
+            pltpu.VMEM((tokens // 2, model_width), BF16),
             pltpu.VMEM((tokens // 2, model_width), F32),
             pltpu.VMEM((2, group_rows, padded), BF16),
             pltpu.VMEM((2, group_rows, padded), BF16),
             pltpu.VMEM((2, group_rows, padded), BF16),
             pltpu.VMEM((2, group_rows, model_width), BF16),
-            pltpu.SemaphoreType.DMA((3,)),
+            pltpu.SemaphoreType.DMA((1,)),
+            pltpu.SemaphoreType.DMA((1,)),
             pltpu.SemaphoreType.DMA((1,)),
             pltpu.SemaphoreType.DMA((2, 4, 2)),
             pltpu.SemaphoreType.DMA((1,)),
         ]
-        + line_sems(tokens),
+        + line_sems(tokens)
+        + line_sems(tokens)
+        + gather_sems(3),
         compiler_params=pltpu.CompilerParams(
-            collective_id=collective, has_side_effects=True, vmem_limit_bytes=58 << 20
+            collective_id=collective, has_side_effects=True, vmem_limit_bytes=61 << 20
         ),
         cost_estimate=pl.CostEstimate(
             flops=tokens * model_width * hidden_width * 12,
             bytes_accessed=360_000_000,
             transcendentals=tokens * hidden_width,
         ),
-        name="feed_and_norm_two_line",
-    )(normed, cotangent, residual, gain, gate_w, up_w, down_w)
+        name="middle",
+    )(mix, cotangent, inputs, gain, gate_w, up_w, down_w)
 
 
 def output_kernel(
@@ -1006,35 +1206,6 @@
         ),
         name="output_line",
     )(part, residual, normed, cotangent, hidden_low, grad_gate, grad_up)
-
-
-class Plane:
-    def __init__(self, mesh_axes):
-        self.mesh_axes = mesh_axes
-        self.context = lax.axis_size("context")
-        self.per_row = self.context // 2
-        self.chips = lax.axis_size("shard") * self.per_row
-        context_place = lax.axis_index("context")
-        self.core = lax.rem(context_place, 2)
-        self.chip = lax.axis_index("shard") * self.per_row + context_place // 2
-
-    def device(self, chip, core):
-        places = {
-            "shard": chip // self.per_row,
-            "context": 2 * lax.rem(chip, self.per_row) + core,
-            "tensor": lax.axis_index("tensor"),
-        }
-        return tuple(places[axis] for axis in self.mesh_axes)
-
-    def ahead(self, distance):
-        return lax.rem(self.chip + distance, self.chips)
-
-    def greet(self, barrier):
-        targets = [self.device(self.chip, 1 - self.core)]
-        targets += [self.device(self.ahead(step), self.core) for step in range(1, self.chips)]
-        for target in targets:
-            pl.semaphore_signal(barrier, inc=1, device_id=target, device_id_type=MESH_ID)
-        return len(targets)
 
 
 def input_kernel(
@@ -1540,18 +1711,12 @@
     key_scale = key_dim ** (-0.5)
     both = ("shard", "context")
     gain_one, gain_two = norm1_gain.reshape(1, -1), norm2_gain.reshape(1, -1)
-    half_wide = jax.ShapeDtypeStruct((tokens // 2, model_width), F32)
     hidden_rows = hidden.reshape(tokens, model_width)
     normed_one, pre, mixer_full = front(
         mesh_axes, 4, hidden_rows, gain_one, (w_query, w_forget, w_input, w_gate_out)
     )
-    pre, w_out, w_ffn_gate, w_ffn_up, w_ffn_down = lax.optimization_barrier(
-        (pre, w_out, w_ffn_gate, w_ffn_up, w_ffn_down)
-    )
+    pre, w_out = lax.optimization_barrier((pre, w_out))
     out_full = lax.all_gather(w_out, both, axis=1, tiled=True)
-    gate_full = lax.all_gather(w_ffn_gate, both, axis=0, tiled=True)
-    up_full = lax.all_gather(w_ffn_up, both, axis=0, tiled=True)
-    down_full = lax.all_gather(w_ffn_down, both, axis=1, tiled=True)
     open_part = (1.0 - forget_floor).reshape(1, width)
     counts, keep, flags, last_count = row_flags(segment_ids)
     mixed_local, lead, starts, runs, state_end, run_end = mixer_forward(
@@ -1565,14 +1730,27 @@
         mixed_local, lead, carry.astype(BF16), pre, gain_row, keep, key_scale
     )
     mix_part = jnp.dot(gated_low, out_full, preferred_element_type=F32).astype(BF16)
-    normed_two, residual = line_exchange(
-        residual_norm, mesh_axes, 0, mix_part, (hidden_rows, gain_two), [half_wide], "mix_line"
-    )
     grad_rows = out_grad.reshape(tokens, model_width)
-    grad_mix_low, grad_norm_two, hidden_low, grad_gate_low, grad_up_low, feed_part, grad_residual = (
-        feed_line(
-            mesh_axes, 2, normed_two, grad_rows, residual, gain_two, gate_full, up_full, down_full
-        )
+    (
+        normed_two,
+        grad_mix_low,
+        grad_norm_two,
+        residual,
+        hidden_low,
+        grad_gate_low,
+        grad_up_low,
+        feed_part,
+        grad_residual,
+    ) = middle(
+        mesh_axes,
+        2,
+        mix_part,
+        grad_rows,
+        hidden_rows,
+        gain_two,
+        w_ffn_gate,
+        w_ffn_up,
+        w_ffn_down.T,
     )
     output_rows, grads_ffn = output_line(
         mesh_axes,

time: 722 us -> 677 us (0.938)
  Pallas kernels: 603 us -> 568 us
  waiting for transfers between devices: 19.1 us -> 1.97 us
    pallas_call x2 -> x1, Pallas kernels: 262 us -> 229 us  [middle(): pl.pallas_call(partial(middle_kernel, mesh_axes), in_specs=[remote, whole...]
    all_gather x3 -> x0, waiting for transfers between devices: 13.7 us -> none  [the longest x1 13.6 us: local(): up_full = lax.all_gather(w_ffn_up, both, axis=0, tiled=True)]
    unnamed x49 -> x56, local copies, waits for them, and re-layouts: 22.5 us -> 27.5 us
  transfers between devices with their start and end apart: 8 -> 5, of which waited for: 4 -> 1; matrix products, arithmetic and copies ran while one was open for 7% -> 7% of each run, Pallas kernels for 56% -> 43%
where the time goes in v7:
time: 677 us; the launch traced here: 676 us
  Pallas kernels  568 us (84%)
  matrix products  41.6 us (6%)
  local copies, waits for them, and re-layouts  39.9 us (6%)
  between operations  16.8 us (2%)
    pallas_call x1, Pallas kernels, middle(): pl.pallas_call(partial(middle_kernel, mesh_axes), in_specs=[remote, whole...  229 us
    pallas_call x1, Pallas kernels, input_line(): pl.pallas_call(partial(input_kernel, mesh_axes), in_specs=[whole] * 4 + [...  122 us
    pallas_call x1, Pallas kernels, output_line(): pl.pallas_call(partial(output_kernel, mesh_axes), in_specs=[whole] * 7, o...  121 us
    pallas_call x1, Pallas kernels, front(): pl.pallas_call(partial(front_kernel, mesh_axes), in_specs=[whole] * 6, ou...  51.5 us
    unnamed x56, local copies, waits for them, and re-layouts  27.5 us
    pallas_call x1, Pallas kernels, mixer_backward(): pl.pallas_call(partial(mixer_backward_kernel, head_count), grid=(blocks,)...  14.7 us
  transfers between devices with their start and end apart: 5, of which 1 were waited for; matrix products, arithmetic and copies ran while one was open for 7% of the time, Pallas kernels for 43%

profile of v7, /device:TPU:0, one launch (start us, length us, event | category | flops | bytes accessed | tf_op | source)
XLA Modules:
  0.0 675.9 jit_solution(11050865482427259197)
XLA Ops:
  7.2 0.7 copy-done.6
  7.9 0.9 copy-done.11
  8.9 0.9 copy-done.12
  9.8 0.9 copy-done.13
  10.8 0.9 copy-done.14
  11.7 51.5 %front.1 = (bf16[1024,2048]{1,0:T(8,128)(2,1)S(1)}, f32[1024,2048]{1,0:T(8,128)}, bf16[2048,2048]{1,0:T(8,128)(2,1)}) custom-call(bf16[1024,2048]{1,0:T(8,128)(2,1)} %bitcast.58, f32[1,2048]{1,0:T(1,128)S(1)} %bitcast.51, bf16[256,512]{1,0:T(8,128)(2,1)S(1)} %copy-done.11, bf16[256,512]{1,0:T(8,128)(2,1)S(1)} %copy-done.12, bf16[256,512]{1,0:T(8,128)(2,1)S(1)} %copy-done.13, ...), custom_call_target="tpu_custom_call" | custom-call | flops 8589934592 | bytes 160000000 | tf_op jit(solution)/shard_map/front/pallas_call | solution.py:1559
  63.2 2.0 copy-done.15
  66.2 0.6 slice.94
  67.4 0.6 fusion.5
  68.0 1.4 stack.11
  70.2 9.6 %mixer_forward.1 = (f32[1024,512]{1,0:T(8,128)S(1)}, bf16[1024,512]{1,0:T(8,128)(2,1)S(1)}, f32[8,4,128,128]{3,2,1,0:T(8,128)S(1)}, f32[8,1,512]{2,1,0:T(1,128)S...) custom-call(f32[1024,2048]{1,0:T(8,128)} %get-tuple-element.52.pre_ref.gate_ref, f32[1,512]{1,0:T(1,128)S(1)} %bitcast.48, ...), custom_call_target="tpu_custom_call" | custom-call | flops 805306368 | bytes 15728640 | tf_op jit(solution)/shard_map/mixer_forward/pallas_call | solution.py:115
  79.8 1.3 copy-done
  81.1 1.3 copy-done.4
  82.5 2.0 collective-permute-start
  84.5 1.1 copy.43
  85.7 1.3 fusion.3
  88.9 1.0 slice_multiply_fusion
  89.9 1.6 copy-done.5
  91.5 4.1 gate_forward.1
  95.6 1.3 copy-done.2
  96.9 1.0 copy-done.10
  97.9 6.3 convolution_convert_fusion.2.mix_hbm
  104.1 229.0 %middle.1 = (bf16[1024,2048]{1,0:T(8,128)(2,1)}, bf16[1024,2048]{1,0:T(8,128)(2,1)}, f32[1,2048]{1,0:T(1,128)}, f32[512,2048]{1,0:T(8,128)}, bf16[1024,1408]{1,0...) custom-call(bf16[1024,2048]{1,0:T(8,128)(2,1)} %convolution_convert_, ...), custom_call_target="tpu_custom_call" | custom-call | flops 35433480192 | bytes 360000000 | tf_op jit(solution)/shard_map/middle/pallas_call | solution.py:1076
  333.2 6.2 convolution_convert_fusion.3
  339.4 5.4 fusion.6.grad_ref
  344.8 6.1 gate_backward.1
  351.0 1.5 collective-permute-start.1
  352.5 1.9 collective-permute-done.1
  354.5 14.7 %mixer_backward.1 = (bf16[1024,2048]{1,0:T(8,128)(2,1)S(1)}, f32[1,512]{1,0:T(1,128)S(1)}) custom-call(f32[1024,2048]{1,0:T(8,128)} %get-tuple-element.52.pre_ref.gate_ref, bf16[1024,512]{1,0:T(8,128)(2,1)S(1)} %get-tuple-element.68.grad_mixed_ref, bf16[1024,512]{1,0:T(8,128)(2,1)S(1)} %get-tuple-element.69.grad_gate_ref, f32[8,4,128,128]{3,2,1,0:T(8,128)S(1)} %copy-done.1, ...), custom_call_target="tpu_custom_call" | custom-call | flops 2013265920 | bytes 18874368 | tf_op jit(solution)/shard_map/mixer_backward/pallas_call | solution.py:392
  369.2 2.0 copy-done.8
  371.2 11.2 %convolution_convert_fusion = bf16[2048,2048]{1,0:T(8,128)(2,1)} fusion(bf16[1024,2048]{1,0:T(8,128)(2,1)S(1)} %copy-done.16, bf16[1024,2048]{1,0:T(8,128)(2,1)S(1)} %get-tuple-element.73), kind=kOutput, calls=%fused_computation | convolution fusion | flops 8594128896 | bytes 16777216 | tf_op jit(solution)/shard_map/td,tk->dk/dot_general | solution.py:1785
  382.4 121.1 %output_line.1 = (bf16[1024,2048]{1,0:T(8,128)(2,1)}, bf16[3,2048,1408]{2,1,0:T(8,128)(2,1)}) custom-call(bf16[1024,2048]{1,0:T(8,128)(2,1)} %get-tuple-element.59.part, f32[512,2048]{1,0:T(8,128)} %get-tuple-element.60.residual, bf16[1024,2048]{1,0:T(8,128)(2,1)} %get-tuple-element.61.normed_ref, bf16[1024,2048]{1,0:T(8,128)(2,1)} %bitcast.76, ...), custom_call_target="tpu_custom_call" | custom-call | flops 17716740096 | bytes 360000000 | tf_op jit(solution)/shard_map/output_line/pallas_call | solution.py:1185
  503.5 12.6 %convolution_convert_fusion.1.part = bf16[1024,2048]{1,0:T(8,128)(2,1)} fusion(bf16[1024,2048]{1,0:T(8,128)(2,1)S(1)} %copy-done.9, bf16[2048,2048]{1,0:T(8,128)(2,1)} %get-tuple-element.74), kind=kOutput, calls=%fused_computation.3 | convolution fusion | flops 8592031744 | bytes 16777216 | tf_op jit(solution)/shard_map/tk,dk->td/dot_general | solution.py:1786
  516.1 122.5 %input_line.1 = (bf16[1024,2048]{1,0:T(8,128)(2,1)}, f32[1,2048]{1,0:T(1,128)}, f32[256,1408]{1,0:T(8,128)}, f32[256,1408]{1,0:T(8,128)}, f32[256,1408]{1,0:T(8,128)}) custom-call(bf16[1024,2048]{1,0:T(8,128)(2,1)} %convolution_convert_fusion.1.part, bf16[1024,2048]{1,0:T(8,128)(2,1)} %bitcast.60, f32[512,2048]{1,0:T(8,128)} %get-tuple-element.75.residual_grad, ...), custom_call_target="tpu_custom_call" | custom-call | flops 16777216 | bytes 360000000 | tf_op jit(solution)/shard_map/input_line/pallas_call | solution.py:1356
  638.6 0.7 select_maximum_fusion
  639.3 0.6 reshape.159.value
  639.9 9.5 %small_sum.1 = (f32[8,640]{1,0:T(8,128)}, f32[8,640]{1,0:T(8,128)}) custom-call(f32[8,640]{1,0:T(8,128)} %reshape.159.value), custom_call_target="tpu_custom_call" | custom-call | flops 40960 | bytes 20000000 | tf_op jit(solution)/shard_map/small_sum/pallas_call | solution.py:1667
  649.4 0.8 slice.111
  650.3 0.7 slice.103
  651.0 0.8 slice.109
  651.9 2.9 copy.47
  656.4 1.8 convert_element_type.65
  658.2 2.8 fusion.2
  661.1 2.1 copy.52
  663.3 1.6 copy-done.18
  664.8 2.1 copy.53
  667.2 1.1 copy.54
  668.3 1.1 copy.55
  (77 shorter events, 4.1 us)
Async XLA Ops:
  7.2 90.7 %all-gather.2.cloned.1.call-start = ((), (), s32[]{:S(2)}) async-start(), calls=%async_computation.2 | async-start | bytes 2359296 | tf_op jit(solution)/shard_map/all_gather | solution.py:1719
  7.2 0.7 copy-start.6
  7.9 0.9 copy-start.11
  8.9 0.9 copy-start.12
  9.8 0.9 copy-start.13
  10.8 0.9 copy-start.14
  11.7 53.6 %copy-start.22 = (s32[1,1024]{1,0:T(1,128)S(1)}, s32[1,1024]{1,0:T(1,128)}, u32[]{:S(2)}) copy-start(s32[1,1024]{1,0:T(1,128)} %param.16) | copy-start | bytes 12292
  11.7 58.4 %copy-start.24 = (f32[4,128]{1,0:T(4,128)S(1)}, f32[4,128]{1,0:T(4,128)}, u32[]{:S(2)}) copy-start(f32[4,128]{1,0:T(4,128)} %param.22) | copy-start | bytes 6148
  63.2 2.0 copy-start.15
  65.2 591.2 %reduce-scatter.5.cloned.1.call-start = ((), (), s32[]{:S(2)}) async-start(), calls=%async_computation.4 | async-start | bytes 2359296 | tf_op jit(solution)/shard_map/reduce_scatter | solution.py:1804
  70.1 14.4 %copy-start.21 = (bf16[1408,256]{1,0:T(8,128)(2,1)S(1)}, bf16[1408,256]{1,0:T(8,128)(2,1)}, u32[]{:S(2)}) copy-start(bf16[1408,256]{1,0:T(8,128)(2,1)} %param.28) | copy-start | bytes 2162692
  70.1 19.7 %copy-start.7 = (f32[128]{0:T(128)S(1)}, f32[128]{0:T(128)}, u32[]{:S(2)}) copy-start(f32[128]{0:T(128)} %param.23) | copy-start | bytes 1540
  79.8 1.3 copy-start
  81.1 1.3 copy-start.4
  82.5 3.1 collective-permute-start
  89.9 1.6 copy-start.5
  95.6 1.3 copy-start.2
  96.9 1.0 copy-start.10
  339.4 318.8 %reduce-scatter.3.cloned.1.call-start = ((), (), s32[]{:S(2)}) async-start(), calls=%async_computation.3 | async-start | bytes 9437184 | tf_op jit(solution)/shard_map/reduce_scatter | solution.py:1804
  339.4 5.4 copy-start.3
  344.8 9.6 %copy-start.1 = (f32[8,4,128,128]{3,2,1,0:T(8,128)S(1)}, f32[8,4,128,128]{3,2,1,0:T(8,128)}, u32[]{:S(2)}) copy-start(f32[8,4,128,128]{3,2,1,0:T(8,128)} %copy-done) | copy-start | bytes 6291460
  351.0 3.4 collective-permute-start.1
  354.5 16.7 %copy-start.16 = (bf16[1024,2048]{1,0:T(8,128)(2,1)S(1)}, bf16[1024,2048]{1,0:T(8,128)(2,1)}, u32[]{:S(2)}) copy-start(bf16[1024,2048]{1,0:T(8,128)(2,1)} %copy-done.15) | copy-start | bytes 12582916
  369.2 2.0 copy-start.8
  382.4 121.1 %copy-start.9 = (bf16[1024,2048]{1,0:T(8,128)(2,1)S(1)}, bf16[1024,2048]{1,0:T(8,128)(2,1)}, u32[]{:S(2)}) copy-start(bf16[1024,2048]{1,0:T(8,128)(2,1)} %copy-done.8) | copy-start | bytes 12582916
  516.1 122.5 %copy-start.23 = (f32[1,2048]{1,0:T(1,128)S(1)}, f32[1,2048]{1,0:T(1,128)}, u32[]{:S(2)}) copy-start(f32[1,2048]{1,0:T(1,128)} %get-tuple-element.79) | copy-start | bytes 24580
  658.2 2.9 copy-start.17
  661.1 3.7 copy-start.18
  664.8 2.4 copy-start.20
  664.8 3.5 copy-start.19
Sparse Core Ops, SparseCore 0:
  65.4 28.4 all-gather.1
  339.5 39.0 reduce-scatter.4
  382.5 71.1 reduce-scatter.2

commit v8 on v7

--- a/solution.py
+++ b/solution.py
@@ -46,171 +46,6 @@
     tail = (counts == flags_row[2:3, 0:1]).astype(F32)
     closing = (flags_row[1:2, 0:1] == flags_row[2:3, 0:1]).astype(F32)
     return row_ids, col_ids, linked, fresh, tail, closing
-
-
-def mixer_forward_kernel(
-    head_count,
-    key_scale,
-    pre_ref,
-    open_ref,
-    count_ref,
-    keep_ref,
-    flags_ref,
-    mixed_ref,
-    lead_ref,
-    start_ref,
-    run_ref,
-    end_ref,
-    total_ref,
-    state_scr,
-    run_scr,
-):
-    step = pl.program_id(0)
-    width = open_ref.shape[1]
-    lanes = width // head_count
-
-    @pl.when(step == 0)
-    def _():
-        state_scr[...] = jnp.zeros_like(state_scr)
-        run_scr[...] = jnp.zeros_like(run_scr)
-
-    counts, keep = count_ref[...], keep_ref[...]
-    row_ids, col_ids, linked, fresh, tail, closing = block_masks(counts, flags_ref[0])
-    tri = (row_ids >= col_ids).astype(BF16)
-    query_pre = pre_ref[:, :width]
-    values = pre_ref[:, 2 * width : 3 * width].astype(BF16)
-    keys = open_ref[...] * jax.nn.sigmoid(-pre_ref[:, width : 2 * width])
-    cum = split_sum(tri, jnp.log1p(-keys))
-    rows = cum.shape[0]
-    ending = cum[rows - 1 : rows, :]
-    lifted = query_pre * jax.nn.sigmoid(query_pre) * jnp.exp(cum)
-    lowered = (keys * jnp.exp(-cum) * keep).astype(BF16)
-    moved = (keys * jnp.exp(ending - cum) * (keep * tail)).astype(BF16)
-    run = run_scr[...]
-    lead_ref[...] = (lifted * jnp.exp(run) * (counts == 0).astype(F32)).astype(BF16)
-    run_ref[0] = run
-    run_scr[...] = run + ending
-    total_ref[...] = run + ending
-    fresh_lifted = (lifted * fresh).astype(BF16)
-    lifted = lifted.astype(BF16)
-    end_decay = jnp.exp(ending) * closing
-    for head in range(head_count):
-        part = slice(head * lanes, (head + 1) * lanes)
-        state = state_scr[head]
-        start_ref[0, head] = state
-        scores = jnp.where(linked, mm_nt(lifted[:, part], lowered[:, part]), 0.0)
-        results = mm_nn(scores.astype(BF16), values[:, part])
-        results = results + mm_nt(fresh_lifted[:, part], state.astype(BF16))
-        mixed_ref[:, part] = results * (key_scale * keep)
-        state = state * end_decay[:, part] + mm_tn(values[:, part], moved[:, part])
-        state_scr[head] = state
-        end_ref[head] = state
-
-
-def mixer_forward(pre, open_part, counts, keep, flags, head_count, key_scale):
-    tokens, all_width = pre.shape
-    width = open_part.shape[1]
-    lanes = width // head_count
-    blocks = tokens // BLOCK
-    return pl.pallas_call(
-        partial(mixer_forward_kernel, head_count, key_scale),
-        grid=(blocks,),
-        in_specs=[
-            pl.BlockSpec((BLOCK, all_width), lambda i: (i, 0)),
-            pl.BlockSpec((1, width), lambda i: (0, 0)),
-            pl.BlockSpec((BLOCK, 1), lambda i: (i, 0)),
-            pl.BlockSpec((BLOCK, 1), lambda i: (i, 0)),
-            pl.BlockSpec((1, 8, BLOCK), lambda i: (i, 0, 0)),
-        ],
-        out_specs=[
-            pl.BlockSpec((BLOCK, width), lambda i: (i, 0)),
-            pl.BlockSpec((BLOCK, width), lambda i: (i, 0)),
-            pl.BlockSpec((1, head_count, lanes, lanes), lambda i: (i, 0, 0, 0)),
-            pl.BlockSpec((1, 1, width), lambda i: (i, 0, 0)),
-            pl.BlockSpec((head_count, lanes, lanes), lambda i: (0, 0, 0)),
-            pl.BlockSpec((1, width), lambda i: (0, 0)),
-        ],
-        out_shape=[
-            jax.ShapeDtypeStruct((tokens, width), F32),
-            jax.ShapeDtypeStruct((tokens, width), BF16),
-            jax.ShapeDtypeStruct((blocks, head_count, lanes, lanes), F32),
-            jax.ShapeDtypeStruct((blocks, 1, width), F32),
-            jax.ShapeDtypeStruct((head_count, lanes, lanes), F32),
-            jax.ShapeDtypeStruct((1, width), F32),
-        ],
-        scratch_shapes=[
-            pltpu.VMEM((head_count, lanes, lanes), F32),
-            pltpu.VMEM((1, width), F32),
-        ],
-        compiler_params=pltpu.CompilerParams(
-            dimension_semantics=("arbitrary",), vmem_limit_bytes=40 << 20
-        ),
-        cost_estimate=pl.CostEstimate(
-            flops=tokens * width * BLOCK * 12,
-            bytes_accessed=tokens * width * 30,
-            transcendentals=tokens * width * 7,
-        ),
-        name="mixer_forward",
-    )(pre, open_part, counts, keep, flags)
-
-
-def gate_forward_kernel(
-    head_count,
-    key_scale,
-    local_ref,
-    lead_ref,
-    carry_ref,
-    gate_ref,
-    gain_ref,
-    keep_ref,
-    mixed_ref,
-    gated_ref,
-):
-    lanes = gain_ref.shape[1]
-    for head in range(head_count):
-        part = slice(head * lanes, (head + 1) * lanes)
-        carried = mm_nt(lead_ref[:, part], carry_ref[head])
-        mixed = local_ref[:, part] + carried * (key_scale * keep_ref[...])
-        mixed_ref[:, part] = mixed
-        inverse = lax.rsqrt(jnp.mean(mixed * mixed, axis=-1, keepdims=True) + EPSILON)
-        gate = gate_ref[:, part]
-        gated = mixed * inverse * gain_ref[...] * (gate * jax.nn.sigmoid(gate))
-        gated_ref[:, part] = gated.astype(BF16)
-
-
-def gate_forward(local, lead, carry, pre, gain, keep, key_scale):
-    tokens, width = local.shape
-    head_count, lanes = carry.shape[0], carry.shape[2]
-    rows = 2 * BLOCK
-    return pl.pallas_call(
-        partial(gate_forward_kernel, head_count, key_scale),
-        grid=(tokens // rows,),
-        in_specs=[
-            pl.BlockSpec((rows, width), lambda i: (i, 0)),
-            pl.BlockSpec((rows, width), lambda i: (i, 0)),
-            pl.BlockSpec((head_count, lanes, lanes), lambda i: (0, 0, 0)),
-            pl.BlockSpec((rows, width), lambda i: (i, 3)),
-            pl.BlockSpec((1, lanes), lambda i: (0, 0)),
-            pl.BlockSpec((rows, 1), lambda i: (i, 0)),
-        ],
-        out_specs=[
-            pl.BlockSpec((rows, width), lambda i: (i, 0)),
-            pl.BlockSpec((rows, width), lambda i: (i, 0)),
-        ],
-        out_shape=[
-            jax.ShapeDtypeStruct((tokens, width), F32),
-            jax.ShapeDtypeStruct((tokens, width), BF16),
-        ],
-        compiler_params=pltpu.CompilerParams(
-            dimension_semantics=("arbitrary",), vmem_limit_bytes=40 << 20
-        ),
-        cost_estimate=pl.CostEstimate(
-            flops=tokens * width * 300,
-            bytes_accessed=tokens * width * 16,
-            transcendentals=tokens * width,
-        ),
-        name="gate_forward",
-    )(local, lead, carry, pre, gain, keep)
 
 
 def gate_backward_kernel(
@@ -451,45 +286,12 @@
         + [jnp.zeros(wide, F32)] * 5,
         axis=1,
     )
-    return counts[:, None], keep[:, None], flags, lasts[-1]
-
-
-def from_earlier(values, axis, shift):
-    count = lax.axis_size(axis)
-    return lax.ppermute(values, axis, [(i, i + shift) for i in range(count - shift)])
+    return counts[:, None], keep[:, None], flags
 
 
 def from_later(values, axis, shift):
     count = lax.axis_size(axis)
     return lax.ppermute(values, axis, [(i + shift, i) for i in range(count - shift)])
-
-
-def state_before(state, decay, first_id, last_id, axis):
-    head_count, lanes, _ = state.shape
-    ids = jnp.stack([first_id, last_id, jnp.float32(1.0)] + [jnp.float32(0.0)] * 5)
-    message = jnp.concatenate(
-        [
-            state.reshape(head_count * lanes, lanes),
-            decay.reshape(head_count, lanes),
-            jnp.broadcast_to(ids[:, None], (8, lanes)),
-        ]
-    )
-    rows = head_count * lanes
-    total = jnp.zeros_like(state)
-    factor = jnp.ones((head_count, 1, lanes), F32)
-    follower = first_id
-    link_in = jnp.float32(0.0)
-    for shift in range(1, lax.axis_size(axis)):
-        got = from_earlier(message, axis, shift)
-        got_ids = got[rows + head_count :, 0]
-        linked = (got_ids[1] == follower).astype(F32) * got_ids[2]
-        if shift == 1:
-            link_in = linked
-        factor = factor * linked
-        total = total + factor * got[:rows].reshape(state.shape)
-        factor = factor * got[rows : rows + head_count].reshape(head_count, 1, lanes)
-        follower = got_ids[0]
-    return total, link_in
 
 
 def grad_after(back, decay, link_in, axis):
@@ -815,13 +617,17 @@
                 for half in range(2):
                     self.take(distance, half, False)
 
+    def arrive_from(self, distance):
+        if distance == 0:
+            for copy in self.loads():
+                copy.wait()
+        for half in range(2):
+            for copy in self.forward(distance, half):
+                copy.wait_recv()
+
     def arrive(self):
-        for copy in self.loads():
-            copy.wait()
         for distance in range(self.plane.chips):
-            for half in range(2):
-                for copy in self.forward(distance, half):
-                    copy.wait_recv()
+            self.arrive_from(distance)
 
     def finish(self):
         for distance in range(self.plane.chips):
@@ -846,6 +652,7 @@
 
 GROUP = 128
 TILE = 256
+WIDE = 512
 
 
 def middle_kernel(
@@ -975,7 +782,7 @@
     def hidden_tile(group, tile):
         first, second = both(normed_ref, group)
         slot = lax.rem(group, 2)
-        columns = pl.ds(pl.multiple_of(tile * TILE, TILE), TILE)
+        columns = pl.ds(pl.multiple_of(tile * WIDE, WIDE), WIDE)
         rows = jnp.concatenate([normed_ref[first], normed_ref[second]], axis=0)
         gate = mm_nn(rows, gate_w[:, columns])
         up = mm_nn(rows, up_w[:, columns])
@@ -992,14 +799,14 @@
     def model_tile(group, tile):
         first, second = both(part, group)
         slot = lax.rem(group, 2)
-        columns = pl.ds(pl.multiple_of(tile * TILE, TILE), TILE)
+        columns = pl.ds(pl.multiple_of(tile * WIDE, WIDE), WIDE)
         back = mm_nt(stage_gate[slot], gate_w[columns, :])
         back = (back + mm_nt(stage_up[slot], up_w[columns, :])).astype(BF16)
         part[first, columns] = back[:GROUP]
         part[second, columns] = back[GROUP:]
         stage_feed[slot, :, columns] = mm_nt(stage_hidden[slot], down_w[columns, :]).astype(BF16)
 
-    hidden_tiles, model_tiles = padded // TILE, model_width // TILE
+    hidden_tiles, model_tiles = padded // WIDE, model_width // WIDE
     ticks = hidden_tiles + model_tiles
     piece = -(-ticks // pace)
     save = pltpu.make_async_copy(residual, residual_hbm, save_sem.at[0])
@@ -1069,7 +876,7 @@
 def middle(mesh_axes, collective, mix, cotangent, inputs, gain, gate_w, up_w, down_w):
     tokens, model_width = mix.shape
     hidden_width = gate_w.shape[1]
-    padded = -(-hidden_width // TILE) * TILE
+    padded = -(-hidden_width // WIDE) * WIDE
     whole = pl.BlockSpec(memory_space=pltpu.VMEM)
     remote = pl.BlockSpec(memory_space=pl.ANY)
     group_rows = 2 * GROUP
@@ -1131,11 +938,16 @@
     hidden_ref,
     grad_gate_ref,
     grad_up_ref,
+    gated_ref,
+    mix_grad_ref,
     out_ref,
     grads_hbm,
+    out_grads_hbm,
     arrived,
     stage,
+    out_stage,
     stage_sem,
+    out_sem,
     *sems,
 ):
     model_width = normed_ref.shape[1]
@@ -1148,10 +960,13 @@
     barrier = pltpu.get_barrier_semaphore()
     pl.semaphore_wait(barrier, line.greet(barrier))
 
-    def stage_copy(tile):
+    def stage_copies(tile):
         rows = pl.ds(pl.multiple_of(tile * TILE, TILE), TILE)
         slot = lax.rem(tile, 2)
-        return pltpu.make_async_copy(stage.at[slot], grads_hbm.at[:, rows], stage_sem.at[slot])
+        return (
+            pltpu.make_async_copy(stage.at[slot], grads_hbm.at[:, rows], stage_sem.at[slot]),
+            pltpu.make_async_copy(out_stage.at[slot], out_grads_hbm.at[rows], out_sem.at[slot]),
+        )
 
     def weight_tile(time):
         tile = jnp.clip(time, 0, tiles - 1)
@@ -1160,7 +975,8 @@
 
         @pl.when(jnp.logical_and(time < tiles, time >= 2))
         def _():
-            stage_copy(tile - 2).wait()
+            for copy in stage_copies(tile - 2):
+                copy.wait()
 
         @pl.when(time < tiles)
         def _():
@@ -1168,31 +984,48 @@
             stage[slot, 0] = mm_tn(rows, grad_gate_ref[...]).astype(BF16)
             stage[slot, 1] = mm_tn(rows, grad_up_ref[...]).astype(BF16)
             stage[slot, 2] = mm_tn(cotangent_ref[:, columns], hidden_ref[...]).astype(BF16)
-            stage_copy(tile).start()
+            out_stage[slot] = mm_tn(mix_grad_ref[:, columns], gated_ref[...]).astype(BF16)
+            for copy in stage_copies(tile):
+                copy.start()
 
     line.run(0, line.steps, weight_tile)
     for tile in range(max(tiles - 2, 0), tiles):
-        stage_copy(tile).wait()
+        for copy in stage_copies(tile):
+            copy.wait()
     line.finish()
 
 
 def output_line(
-    mesh_axes, collective, part, residual, normed, cotangent, hidden_low, grad_gate, grad_up
+    mesh_axes,
+    collective,
+    part,
+    residual,
+    normed,
+    cotangent,
+    hidden_low,
+    grad_gate,
+    grad_up,
+    gated,
+    mix_grad,
 ):
     tokens, model_width = part.shape
+    width = gated.shape[1]
     hidden_width = hidden_low.shape[1]
     whole = pl.BlockSpec(memory_space=pltpu.VMEM)
     return pl.pallas_call(
         partial(output_kernel, mesh_axes),
-        in_specs=[whole] * 7,
-        out_specs=[whole, pl.BlockSpec(memory_space=pl.ANY)],
+        in_specs=[whole] * 9,
+        out_specs=[whole] + [pl.BlockSpec(memory_space=pl.ANY)] * 2,
         out_shape=[
             jax.ShapeDtypeStruct((tokens, model_width), BF16),
             jax.ShapeDtypeStruct((3, model_width, hidden_width), BF16),
+            jax.ShapeDtypeStruct((model_width, width), BF16),
         ],
         scratch_shapes=[
             pltpu.VMEM((tokens, model_width), BF16),
             pltpu.VMEM((2, 3, TILE, hidden_width), BF16),
+            pltpu.VMEM((2, TILE, width), BF16),
+            pltpu.SemaphoreType.DMA((2,)),
             pltpu.SemaphoreType.DMA((2,)),
         ]
         + line_sems(tokens),
@@ -1205,7 +1038,9 @@
             transcendentals=0,
         ),
         name="output_line",
-    )(part, residual, normed, cotangent, hidden_low, grad_gate, grad_up)
+    )(
+        part, residual, normed, cotangent, hidden_low, grad_gate, grad_up, gated, mix_grad
+    )
 
 
 def input_kernel(
@@ -1384,91 +1219,92 @@
     )(part, hidden, residual_grad, gain, grads)
 
 
-def front_kernel(
+def forward_kernel(
     mesh_axes,
+    head_count,
+    key_scale,
     hidden_ref,
     gain_ref,
-    query_ref,
-    forget_ref,
-    input_ref,
-    gate_ref,
+    query_hbm,
+    forget_hbm,
+    input_hbm,
+    gate_hbm,
+    out_shard_hbm,
+    open_ref,
+    count_ref,
+    keep_ref,
+    flags_ref,
+    ids_ref,
+    head_gain_ref,
     normed_hbm,
     pre_hbm,
     full_hbm,
+    out_full_hbm,
+    mixed_hbm,
+    lead_hbm,
+    start_hbm,
+    gated_hbm,
+    mix_hbm,
+    run_ref,
+    carry_ref,
+    decay_ref,
+    link_ref,
     normed,
     pre,
+    mine,
     full,
+    out_full,
+    mixed,
+    lead,
+    starts,
+    gated,
+    mix,
+    state_scr,
+    run_scr,
+    message,
+    received,
+    mine_sem,
+    full_sem,
     save_sem,
-    normed_sem,
     pre_sem,
-    send_sem,
-    recv_sem,
-    pair_send,
-    pair_recv,
+    mix_sem,
+    state_send,
+    state_recv,
+    *sems,
 ):
     plane = Plane(mesh_axes)
     chips = plane.chips
     tokens, model_width = hidden_ref.shape
-    block, width = query_ref.shape
-    part = block // 2
-    relayed = chips == 4
-
-    def partner(distance):
-        return jnp.bitwise_xor(plane.chip, distance)
-
-    def rows_of(chip, core, half):
-        return pl.ds(pl.multiple_of((2 * chip + core) * block + half * part, part), part)
-
-    def copy(rows, distance, half, chip):
-        return pltpu.make_async_remote_copy(
-            full.at[rows],
-            full.at[rows],
-            send_sem.at[distance - 1, half],
-            recv_sem.at[distance - 1, half],
-            device_id=plane.device(chip, plane.core),
-            device_id_type=MESH_ID,
+    block, width = query_hbm.shape
+    lanes = width // head_count
+    state_rows = head_count * lanes
+    context, context_size = lax.axis_index("context"), lax.axis_size("context")
+
+    mine_loads = [
+        pltpu.make_async_copy(
+            ref, mine.at[:, pl.ds(which * width, width)], mine_sem.at[which]
         )
-
-    def send(distance, half):
-        if relayed and distance == 3:
-            through, target = (2, 1) if half == 0 else (1, 2)
-            return copy(
-                rows_of(partner(through), plane.core, half), 3, half, partner(target)
-            )
-        return copy(rows_of(plane.chip, plane.core, half), distance, half, partner(distance))
-
-    def forward(distance, half):
-        rows = rows_of(partner(distance), plane.core, half)
-        return pltpu.make_async_remote_copy(
-            full.at[rows],
-            full.at[rows],
-            pair_send.at[distance, half],
-            pair_recv.at[distance, half],
-            device_id=plane.device(plane.chip, 1 - plane.core),
-            device_id_type=MESH_ID,
-        )
-
-    own = pl.ds(pl.multiple_of((2 * plane.chip + plane.core) * block, block), block)
-    for which, ref in enumerate((query_ref, forget_ref, input_ref, gate_ref)):
-        full[own, which * width : (which + 1) * width] = ref[...]
+        for which, ref in enumerate((query_hbm, forget_hbm, input_hbm, gate_hbm))
+    ]
+    for load in mine_loads:
+        load.start()
+    gather = Gather(plane, (mine,), (full,), sems[:5])
+    out_gather = Gather(plane, (out_shard_hbm,), (out_full,), sems[5:])
+
+    def later(shift):
+        places = {axis: lax.axis_index(axis) for axis in mesh_axes}
+        places["context"] = lax.rem(context + shift, context_size)
+        return tuple(places[axis] for axis in mesh_axes)
+
     barrier = pltpu.get_barrier_semaphore()
-    targets = [plane.device(plane.chip, 1 - plane.core)]
-    targets += [
-        plane.device(partner(step), plane.core)
-        for step in range(1, 3 if relayed else chips)
-    ]
-    for target in targets:
-        pl.semaphore_signal(barrier, inc=1, device_id=target, device_id_type=MESH_ID)
-    pl.semaphore_wait(barrier, len(targets))
-    if relayed:
-        for distance, half in ((1, 1), (2, 0), (1, 0), (2, 1)):
-            send(distance, half).start()
-    else:
-        for distance in range(1, chips):
-            send(distance, 0).start()
-            send(distance, 1).start()
-    for half in range(2):
-        forward(0, half).start()
+    expected = gather.greet(barrier)
+    for shift in range(1, context_size):
+        pl.semaphore_signal(barrier, inc=1, device_id=later(shift), device_id_type=MESH_ID)
+    pl.semaphore_wait(barrier, expected + context_size - 1)
+    for load in mine_loads:
+        load.wait()
+    gather.start()
+    out_gather.start()
 
     def norm(index, _):
         rows = pl.ds(pl.multiple_of(index * 128, 128), 128)
@@ -1477,16 +1313,33 @@
         return 0
 
     lax.fori_loop(0, tokens // 128, norm, 0)
-    normed_save = pltpu.make_async_copy(normed, normed_hbm, normed_sem.at[0])
-    normed_save.start()
+
+    saves = [
+        pltpu.make_async_copy(source, target, save_sem.at[which])
+        for which, (source, target) in enumerate(
+            (
+                (normed, normed_hbm),
+                (out_full, out_full_hbm),
+                (mixed, mixed_hbm),
+                (lead, lead_hbm),
+                (starts, start_hbm),
+                (gated, gated_hbm),
+            )
+        )
+    ]
+    saves[0].start()
     row_tile, column_tile = 256, 512
 
     def pre_save(index):
         rows = pl.ds(pl.multiple_of(index * row_tile, row_tile), row_tile)
         return pltpu.make_async_copy(pre.at[rows], pre_hbm.at[rows], pre_sem.at[index])
 
+    def depth_of(distance):
+        first = 2 * gather.partner(distance) * block
+        return pl.ds(pl.multiple_of(first, 2 * block), 2 * block)
+
     def product(distance):
-        depth = pl.ds(pl.multiple_of(2 * partner(distance) * block, 2 * block), 2 * block)
+        depth = depth_of(distance)
 
         def row_body(index, _):
             rows = pl.ds(pl.multiple_of(index * row_tile, row_tile), row_tile)
@@ -1508,85 +1361,242 @@
         lax.fori_loop(0, tokens // row_tile, row_body, 0)
 
     def full_save(distance):
-        depth = pl.ds(pl.multiple_of(2 * partner(distance) * block, 2 * block), 2 * block)
-        return pltpu.make_async_copy(full.at[depth], full_hbm.at[depth], save_sem.at[distance])
+        depth = depth_of(distance)
+        return pltpu.make_async_copy(full.at[depth], full_hbm.at[depth], full_sem.at[distance])
 
     def use(distance):
-        for half in range(2):
-            forward(distance, half).wait_recv()
+        gather.arrive_from(distance)
         full_save(distance).start()
         product(distance)
 
     use(0)
-    if relayed:
-        for distance, half in ((1, 1), (2, 0), (1, 0), (2, 1)):
-            send(distance, half).wait_recv()
-            if (distance, half) in ((1, 1), (2, 0)):
-                send(3, half).start()
-            forward(distance, half).start()
+    gather.stage(0)
+    gather.stage(1)
+    if gather.relayed:
         use(1)
         use(2)
-        for half in range(2):
-            send(3, half).wait_recv()
-            forward(3, half).start()
+    gather.stage(2)
+    if gather.relayed:
         use(3)
     else:
         for distance in range(1, chips):
-            for half in range(2):
-                send(distance, half).wait_recv()
-                forward(distance, half).start()
-            if distance > 1:
-                use(distance - 1)
-        use(chips - 1)
+            use(distance)
+    out_gather.stage(0)
+    out_gather.stage(1)
+
+    state_scr[...] = jnp.zeros_like(state_scr)
+    run_scr[...] = jnp.zeros_like(run_scr)
+
+    def recur(step, _):
+        rows = pl.ds(pl.multiple_of(step * BLOCK, BLOCK), BLOCK)
+        counts, keep = count_ref[rows], keep_ref[rows]
+        row_ids, col_ids, linked, fresh, tail, closing = block_masks(counts, flags_ref[step])
+        tri = (row_ids >= col_ids).astype(BF16)
+        query_pre = pre[rows, :width]
+        values = pre[rows, 2 * width : 3 * width].astype(BF16)
+        keys = open_ref[...] * jax.nn.sigmoid(-pre[rows, width : 2 * width])
+        cum = split_sum(tri, jnp.log1p(-keys))
+        ending = cum[BLOCK - 1 : BLOCK, :]
+        lifted = query_pre * jax.nn.sigmoid(query_pre) * jnp.exp(cum)
+        lowered = (keys * jnp.exp(-cum) * keep).astype(BF16)
+        moved = (keys * jnp.exp(ending - cum) * (keep * tail)).astype(BF16)
+        run = run_scr[...]
+        lead[rows] = (lifted * jnp.exp(run) * (counts == 0).astype(F32)).astype(BF16)
+        run_ref[step] = run
+        run_scr[...] = run + ending
+        fresh_lifted = (lifted * fresh).astype(BF16)
+        lifted = lifted.astype(BF16)
+        end_decay = jnp.exp(ending) * closing
+        for head in range(head_count):
+            part = slice(head * lanes, (head + 1) * lanes)
+            state = state_scr[head]
+            starts[step, head] = state
+            scores = jnp.where(linked, mm_nt(lifted[:, part], lowered[:, part]), 0.0)
+            results = mm_nn(scores.astype(BF16), values[:, part])
+            results = results + mm_nt(fresh_lifted[:, part], state.astype(BF16))
+            mixed[rows, part] = results * (key_scale * keep)
+            state_scr[head] = state * end_decay[:, part] + mm_tn(values[:, part], moved[:, part])
+        return 0
+
+    lax.fori_loop(0, tokens // BLOCK, recur, 0)
+    saves[3].start()
+    saves[4].start()
+
+    last_count = flags_ref[tokens // BLOCK - 1][2:3, 0:1]
+    for head in range(head_count):
+        part = slice(head * lanes, (head + 1) * lanes)
+        message[head * lanes : (head + 1) * lanes] = state_scr[head]
+        decay = jnp.exp(run_scr[:, part]) * (last_count == 0).astype(F32)
+        decay_ref[head] = decay
+        message[state_rows + 8 + head : state_rows + 9 + head] = decay
+    message[state_rows : state_rows + 8] = ids_ref[...]
+
+    def state_copy(shift):
+        return pltpu.make_async_remote_copy(
+            message,
+            received.at[shift - 1],
+            state_send.at[shift - 1],
+            state_recv.at[shift - 1],
+            device_id=later(shift),
+            device_id_type=MESH_ID,
+        )
+
+    for shift in range(1, context_size):
+
+        @pl.when(context + shift < context_size)
+        def _(shift=shift):
+            state_copy(shift).start()
+
+    out_gather.stage(2)
+    carry_ref[...] = jnp.zeros_like(carry_ref)
+    link_ref[...] = jnp.zeros_like(link_ref)
+    for shift in range(1, context_size):
+
+        @pl.when(context >= shift)
+        def _(shift=shift):
+            state_copy(shift).wait_recv()
+            linked = jnp.ones((1, lanes), F32)
+            follower = ids_ref[0:1]
+            factors = [jnp.ones((1, lanes), F32)] * head_count
+            for near in range(shift):
+                got = received.at[near]
+                linked = (got[state_rows + 1 : state_rows + 2] == follower).astype(F32)
+                follower = got[state_rows : state_rows + 1]
+                factors = [factor * linked for factor in factors]
+                if near < shift - 1:
+                    factors = [
+                        factor * got[state_rows + 8 + head : state_rows + 9 + head]
+                        for head, factor in enumerate(factors)
+                    ]
+            if shift == 1:
+                link_ref[0:1] = linked
+            for head in range(head_count):
+                rows = slice(head * lanes, (head + 1) * lanes)
+                carry_ref[head] += factors[head] * received[shift - 1, rows]
+
+    for shift in range(1, context_size):
+
+        @pl.when(context + shift < context_size)
+        def _(shift=shift):
+            state_copy(shift).wait_send()
+
     for distance in range(chips):
-        for half in range(2):
-            if distance > 0:
-                send(distance, half).wait_send()
-            forward(distance, half).wait_send()
+        out_gather.arrive_from(distance)
+    saves[1].start()
+
+    def mix_save(index):
+        rows = pl.ds(pl.multiple_of(index * row_tile, row_tile), row_tile)
+        return pltpu.make_async_copy(mix.at[rows], mix_hbm.at[rows], mix_sem.at[index])
+
+    def project(index, _):
+        rows = pl.ds(pl.multiple_of(index * row_tile, row_tile), row_tile)
+        for head in range(head_count):
+            part = slice(head * lanes, (head + 1) * lanes)
+            carried = mm_nt(lead[rows, part], carry_ref[head].astype(BF16))
+            value = mixed[rows, part] + carried * (key_scale * keep_ref[rows])
+            mixed[rows, part] = value
+            gate = pre[rows, 3 * width + head * lanes : 3 * width + (head + 1) * lanes]
+            unit = value * inverse_rms(value)
+            gated[rows, part] = (
+                unit * head_gain_ref[...] * (gate * jax.nn.sigmoid(gate))
+            ).astype(BF16)
+        left = gated[rows]
+
+        def column_body(column, _):
+            columns = pl.ds(pl.multiple_of(column * column_tile, column_tile), column_tile)
+            mix[rows, columns] = mm_nt(left, out_full[columns, :]).astype(BF16)
+            return 0
+
+        lax.fori_loop(0, model_width // column_tile, column_body, 0)
+        mix_save(index).start()
+        return 0
+
+    lax.fori_loop(0, tokens // row_tile, project, 0)
+    saves[2].start()
+    saves[5].start()
+    gather.finish()
+    out_gather.finish()
+    for distance in range(chips):
         full_save(distance).wait()
-    normed_save.wait()
+    for save in saves:
+        save.wait()
     for index in range(tokens // row_tile):
         pre_save(index).wait()
-
-
-def front(mesh_axes, collective, hidden, gain, shards):
+        mix_save(index).wait()
+
+
+def forward(
+    mesh_axes, collective, hidden, gain, shards, out_shard, open_part, masks, ids, head_gain
+):
+    counts, keep, flags = masks
     tokens, model_width = hidden.shape
     block, width = shards[0].shape
+    lanes = head_gain.shape[1]
+    head_count = width // lanes
     all_width = width * len(shards)
-    chips = lax.axis_size("shard") * lax.axis_size("context") // 2
+    blocks = tokens // BLOCK
+    context_size = lax.axis_size("context")
+    chips = lax.axis_size("shard") * context_size // 2
+    messages = head_count * lanes + 8 + -(-head_count // 8) * 8
     whole = pl.BlockSpec(memory_space=pltpu.VMEM)
     remote = pl.BlockSpec(memory_space=pl.ANY)
+    stored = [
+        ((tokens, model_width), BF16),
+        ((tokens, all_width), F32),
+        ((model_width, all_width), BF16),
+        ((model_width, width), BF16),
+        ((tokens, width), F32),
+        ((tokens, width), BF16),
+        ((blocks, head_count, lanes, lanes), F32),
+        ((tokens, width), BF16),
+        ((tokens, model_width), BF16),
+    ]
+    kept = [
+        ((blocks, 1, width), F32),
+        ((head_count, lanes, lanes), F32),
+        ((head_count, 1, lanes), F32),
+        ((8, lanes), F32),
+    ]
     return pl.pallas_call(
-        partial(front_kernel, mesh_axes),
-        in_specs=[whole] * 6,
-        out_specs=[remote] * 3,
-        out_shape=[
-            jax.ShapeDtypeStruct((tokens, model_width), BF16),
-            jax.ShapeDtypeStruct((tokens, all_width), F32),
-            jax.ShapeDtypeStruct((model_width, all_width), BF16),
-        ],
+        partial(forward_kernel, mesh_axes, head_count, lanes ** (-0.5)),
+        in_specs=[whole] * 2 + [remote] * 5 + [whole] * 6,
+        out_specs=[remote] * len(stored) + [whole] * len(kept),
+        out_shape=[jax.ShapeDtypeStruct(shape, kind) for shape, kind in stored + kept],
         scratch_shapes=[
             pltpu.VMEM((tokens, model_width), BF16),
             pltpu.VMEM((tokens, all_width), F32),
+            pltpu.VMEM((block, all_width), BF16),
             pltpu.VMEM((model_width, all_width), BF16),
+            pltpu.VMEM((model_width, width), BF16),
+            pltpu.VMEM((tokens, width), F32),
+            pltpu.VMEM((tokens, width), BF16),
+            pltpu.VMEM((blocks, head_count, lanes, lanes), F32),
+            pltpu.VMEM((tokens, width), BF16),
+            pltpu.VMEM((tokens, model_width), BF16),
+            pltpu.VMEM((head_count, lanes, lanes), F32),
+            pltpu.VMEM((1, width), F32),
+            pltpu.VMEM((messages, lanes), F32),
+            pltpu.VMEM((context_size - 1, messages, lanes), F32),
+            pltpu.SemaphoreType.DMA((4,)),
             pltpu.SemaphoreType.DMA((chips,)),
-            pltpu.SemaphoreType.DMA((1,)),
+            pltpu.SemaphoreType.DMA((6,)),
             pltpu.SemaphoreType.DMA((tokens // 256,)),
-            pltpu.SemaphoreType.DMA((chips - 1, 2)),
-            pltpu.SemaphoreType.DMA((chips - 1, 2)),
-            pltpu.SemaphoreType.DMA((chips, 2)),
-            pltpu.SemaphoreType.DMA((chips, 2)),
-        ],
+            pltpu.SemaphoreType.DMA((tokens // 256,)),
+            pltpu.SemaphoreType.DMA((context_size - 1,)),
+            pltpu.SemaphoreType.DMA((context_size - 1,)),
+        ]
+        + gather_sems(1)
+        + gather_sems(1),
         compiler_params=pltpu.CompilerParams(
-            collective_id=collective, has_side_effects=True, vmem_limit_bytes=48 << 20
+            collective_id=collective, has_side_effects=True, vmem_limit_bytes=56 << 20
         ),
         cost_estimate=pl.CostEstimate(
             flops=2 * tokens * model_width * all_width,
-            bytes_accessed=160_000_000,
-            transcendentals=0,
+            bytes_accessed=200_000_000,
+            transcendentals=tokens * width * 9,
         ),
-        name="front",
-    )(hidden, gain, *shards)
+        name="forward",
+    )(hidden, gain, *shards, out_shard, open_part, counts, keep, flags, ids, head_gain)
 
 
 def small_sum_kernel(
@@ -1712,24 +1722,37 @@
     both = ("shard", "context")
     gain_one, gain_two = norm1_gain.reshape(1, -1), norm2_gain.reshape(1, -1)
     hidden_rows = hidden.reshape(tokens, model_width)
-    normed_one, pre, mixer_full = front(
-        mesh_axes, 4, hidden_rows, gain_one, (w_query, w_forget, w_input, w_gate_out)
+    open_part = (1.0 - forget_floor).reshape(1, width)
+    counts, keep, flags = row_flags(segment_ids)
+    ends = segment_ids.reshape(-1).astype(F32)
+    ids = jnp.where(lax.broadcasted_iota(jnp.int32, (8, key_dim), 0) == 1, ends[-1], ends[0])
+    gain_row = head_gain.reshape(1, -1)
+    (
+        normed_one,
+        pre,
+        mixer_full,
+        out_full,
+        mixed,
+        lead,
+        starts,
+        gated_low,
+        mix_part,
+        runs,
+        carry,
+        decay,
+        link,
+    ) = forward(
+        mesh_axes,
+        4,
+        hidden_rows,
+        gain_one,
+        (w_query, w_forget, w_input, w_gate_out),
+        w_out.T,
+        open_part,
+        (counts, keep, flags),
+        ids,
+        gain_row,
     )
-    pre, w_out = lax.optimization_barrier((pre, w_out))
-    out_full = lax.all_gather(w_out, both, axis=1, tiled=True)
-    open_part = (1.0 - forget_floor).reshape(1, width)
-    counts, keep, flags, last_count = row_flags(segment_ids)
-    mixed_local, lead, starts, runs, state_end, run_end = mixer_forward(
-        pre, open_part, counts, keep, flags, head_count, key_scale
-    )
-    decay = (jnp.exp(run_end) * (last_count == 0).astype(F32)).reshape(head_count, 1, key_dim)
-    ids = segment_ids.reshape(-1).astype(F32)
-    carry, link_in = state_before(state_end, decay, ids[0], ids[-1], "context")
-    gain_row = head_gain.reshape(1, -1)
-    mixed, gated_low = gate_forward(
-        mixed_local, lead, carry.astype(BF16), pre, gain_row, keep, key_scale
-    )
-    mix_part = jnp.dot(gated_low, out_full, preferred_element_type=F32).astype(BF16)
     grad_rows = out_grad.reshape(tokens, model_width)
     (
         normed_two,
@@ -1752,7 +1775,7 @@
         w_ffn_up,
         w_ffn_down.T,
     )
-    output_rows, grads_ffn = output_line(
+    output_rows, grads_ffn, grad_out = output_line(
         mesh_axes,
         1,
         feed_part,
@@ -1762,13 +1785,14 @@
         hidden_low,
         grad_gate_low,
         grad_up_low,
+        gated_low,
+        grad_mix_low,
     )
-    grad_out = jnp.einsum("tv,td->vd", gated_low, grad_mix_low, preferred_element_type=F32)
-    grad_gated = jnp.einsum("td,vd->tv", grad_mix_low, out_full, preferred_element_type=F32)
+    grad_gated = jnp.dot(grad_mix_low, out_full, preferred_element_type=F32)
     grad_mixed, grad_gate_pre, grad_head_part, back = gate_backward(
         grad_gated, mixed, lead, pre, gain_row, keep, head_count, key_scale
     )
-    after = grad_after(back, decay, link_in, "context")
+    after = grad_after(back, decay, link[0, 0], "context")
     grad_pre, grad_floor_part = mixer_backward(
         pre,
         grad_mixed,
@@ -1816,7 +1840,7 @@
         share_mixer[:, 3 * width :],
         lax.dynamic_index_in_dim(floor_total, position, 1, False),
         own_slice(total, 2 * model_width, key_dim),
-        share(grad_out, 1),
+        share(grad_out, 0).T,
         own_slice(total, model_width, model_width),
         share_gate,
         share_up,

time: 677 us -> 684 us (1.010)
  Pallas kernels: 568 us -> 596 us
  matrix products: 41.6 us -> 30 us
  local copies, waits for them, and re-layouts: 39.9 us -> 31.6 us
    pallas_call x1, Pallas kernels: 122 us -> 145 us  [input_line(): pl.pallas_call(partial(input_kernel, mesh_axes), in_specs=[whole] * 4 + [...]
    dot_general x3 -> x1, matrix products: 17.8 us -> 4.67 us  [local(): grad_gated = jnp.dot(grad_mix_low, out_full, preferred_element_type=F32)]
    pallas_call x4 -> x2, Pallas kernels: 186 us -> 195 us  [the longest x1 121 us: output_line(): pl.pallas_call(partial(output_kernel, mesh_axes), in_specs=[whole] * 9, o...]
    unnamed x56 -> x46, local copies, waits for them, and re-layouts: 27.5 us -> 18.4 us
  transfers between devices with their start and end apart: 5 -> 3, of which waited for: 1 -> 1; matrix products, arithmetic and copies ran while one was open for 7% -> 6% of each run, Pallas kernels for 43% -> 26%
where the time goes in v8:
time: 684 us; the launch traced here: 683 us
  Pallas kernels  596 us (87%)
  local copies, waits for them, and re-layouts  31.6 us (5%)
  matrix products  30 us (4%)
  between operations  14.4 us (2%)
  other arithmetic  7.54 us (1%)
    pallas_call x1, Pallas kernels, middle(): pl.pallas_call(partial(middle_kernel, mesh_axes), in_specs=[remote, whole...  222 us
    pallas_call x1, Pallas kernels, input_line(): pl.pallas_call(partial(input_kernel, mesh_axes), in_specs=[whole] * 4 + [...  145 us
    pallas_call x1, Pallas kernels, output_line(): pl.pallas_call(partial(output_kernel, mesh_axes), in_specs=[whole] * 9, o...  121 us
    pallas_call x1, Pallas kernels, forward(): pl.pallas_call(partial(forward_kernel, mesh_axes, head_count, lanes ** (-...  74 us
    unnamed x46, local copies, waits for them, and re-layouts  18.4 us
    pallas_call x1, Pallas kernels, mixer_backward(): pl.pallas_call(partial(mixer_backward_kernel, head_count), grid=(blocks,)...  14.6 us
    dot_general x1, matrix products, local(): jnp.einsum('tk,dk->td', grad_pre, mixer_full, preferred_element_type=F32)  13.9 us
  transfers between devices with their start and end apart: 3, of which 1 were waited for; matrix products, arithmetic and copies ran while one was open for 6% of the time, Pallas kernels for 26%

profile of v8, /device:TPU:0, one launch (start us, length us, event | category | flops | bytes accessed | tf_op | source)
XLA Modules:
  0.0 683.0 jit_solution(10948237213816333113)
XLA Ops:
  7.2 0.9 compare_reduce_fusion
  8.2 0.2 select_reduce_fusion
  8.4 0.2 slice_reduce_fusion.1
  8.6 0.2 slice_reduce_fusion
  8.7 0.7 fusion
  9.4 0.7 convert_element_type.38
  10.1 1.0 copy.53.count_ref
  11.2 1.0 copy.54.keep_ref
  12.2 0.6 fusion.4
  12.8 1.3 broadcast_subtract_fusion
  14.0 1.8 copy.52
  15.8 2.2 copy.55
  18.1 1.3 compare_select_fusion
  19.6 0.7 stack.7.flags_ref
  20.3 0.7 iota.14.ids_ref
  20.9 74.0 %forward.1 = (bf16[1024,2048]{1,0:T(8,128)(2,1)}, f32[1024,2048]{1,0:T(8,128)}, bf16[2048,2048]{1,0:T(8,128)(2,1)}, bf16[2048,512]{1,0:T(8,128)(2,1)}, f32[1024,...) custom-call(bf16[1024,2048]{1,0:T(8,128)(2,1)} %bitcast.49, ...), custom_call_target="tpu_custom_call" | custom-call | flops 8589934592 | bytes 200000000 | tf_op jit(solution)/shard_map/forward/pallas_call | solution.py:1560
  94.9 222.4 %middle.1 = (bf16[1024,2048]{1,0:T(8,128)(2,1)}, bf16[1024,2048]{1,0:T(8,128)(2,1)}, f32[1,2048]{1,0:T(1,128)}, f32[512,2048]{1,0:T(8,128)}, bf16[1024,1408]{1,0...) custom-call(bf16[1024,2048]{1,0:T(8,128)(2,1)} %get-tuple-element.52, ...), custom_call_target="tpu_custom_call" | custom-call | flops 35433480192 | bytes 360000000 | tf_op jit(solution)/shard_map/middle/pallas_call | solution.py:883
  317.3 121.5 %output_line.1 = (bf16[1024,2048]{1,0:T(8,128)(2,1)}, bf16[3,2048,1408]{2,1,0:T(8,128)(2,1)}, bf16[2048,512]{1,0:T(8,128)(2,1)}) custom-call(bf16[1024,2048]{1,0:T(8,128)(2,1)} %get-tuple-element.53.part, f32[512,2048]{1,0:T(8,128)} %get-tuple-element.54.residual, bf16[1024,2048]{1,0:T(8,128)(2,1)} %get-tuple-element.55.normed_ref, ...), custom_call_target="tpu_custom_call" | custom-call | flops 17716740096 | bytes 360000000 | tf_op jit(solution)/shard_map/output_line/pallas_call | solution.py:1015
  438.9 1.2 slice.76
  440.1 4.7 fusion.5.grad_ref
  444.9 6.1 gate_backward.1
  451.0 0.7 maximum_multiply_fusion
  451.7 1.3 collective-permute-start
  453.0 2.3 collective-permute-done
  455.5 14.6 %mixer_backward.1 = (bf16[1024,2048]{1,0:T(8,128)(2,1)S(1)}, f32[1,512]{1,0:T(1,128)S(1)}) custom-call(f32[1024,2048]{1,0:T(8,128)} %get-tuple-element.62.gate_ref.pre_ref, bf16[1024,512]{1,0:T(8,128)(2,1)S(1)} %get-tuple-element.66.grad_mixed_ref, bf16[1024,512]{1,0:T(8,128)(2,1)S(1)} %get-tuple-element.67.grad_gate_ref, f32[8,4,128,128]{3,2,1,0:T(8,128)S(1)} %copy-done.2, ...), custom_call_target="tpu_custom_call" | custom-call | flops 2013265920 | bytes 18874368 | tf_op jit(solution)/shard_map/mixer_backward/pallas_call | solution.py:227
  470.1 2.0 copy-done.10
  472.1 11.4 %convolution_convert_fusion = bf16[2048,2048]{1,0:T(8,128)(2,1)} fusion(bf16[1024,2048]{1,0:T(8,128)(2,1)S(1)} %copy-done.18, bf16[1024,2048]{1,0:T(8,128)(2,1)S(1)} %get-tuple-element.74), kind=kOutput, calls=%fused_computation | convolution fusion | flops 8594128896 | bytes 16777216 | tf_op jit(solution)/shard_map/td,tk->dk/dot_general | solution.py:1809
  483.6 13.9 %convolution_convert_fusion.1.part = bf16[1024,2048]{1,0:T(8,128)(2,1)} fusion(bf16[1024,2048]{1,0:T(8,128)(2,1)} %copy-done.10, bf16[2048,2048]{1,0:T(8,128)(2,1)} %get-tuple-element.75), kind=kOutput, calls=%fused_computation.3 | convolution fusion | flops 8592031744 | bytes 16777216 | tf_op jit(solution)/shard_map/tk,dk->td/dot_general | solution.py:1810
  497.4 145.4 %input_line.1 = (bf16[1024,2048]{1,0:T(8,128)(2,1)}, f32[1,2048]{1,0:T(1,128)}, f32[256,1408]{1,0:T(8,128)}, f32[256,1408]{1,0:T(8,128)}, f32[256,1408]{1,0:T(8,128)}) custom-call(bf16[1024,2048]{1,0:T(8,128)(2,1)} %convolution_convert_fusion.1.part, bf16[1024,2048]{1,0:T(8,128)(2,1)} %bitcast.51, f32[512,2048]{1,0:T(8,128)} %get-tuple-element.76.residual_grad, ...), custom_call_target="tpu_custom_call" | custom-call | flops 16777216 | bytes 360000000 | tf_op jit(solution)/shard_map/input_line/pallas_call | solution.py:1191
  642.8 0.7 select_maximum_fusion
  643.6 0.6 reshape.143.value
  644.2 11.8 %small_sum.1 = (f32[8,640]{1,0:T(8,128)}, f32[8,640]{1,0:T(8,128)}) custom-call(f32[8,640]{1,0:T(8,128)} %reshape.143.value), custom_call_target="tpu_custom_call" | custom-call | flops 40960 | bytes 20000000 | tf_op jit(solution)/shard_map/small_sum/pallas_call | solution.py:1677
  656.0 0.8 slice.86
  656.8 0.7 slice.78
  657.5 0.8 slice.84
  658.4 2.9 copy.60
  661.3 0.5 fusion.1
  661.8 0.6 constant_dynamic-slice_fusion.2
  662.4 0.6 constant_dynamic-slice_fusion
  663.0 1.0 convert_bitcast_fusion
  664.0 1.0 copy.59
  665.0 2.8 fusion.2
  667.9 2.1 copy.65
  670.0 1.6 copy-done.12
  671.6 2.1 copy.66
  673.7 0.2 copy-done.14
  674.0 1.1 copy.67
  675.1 1.1 copy.68
  (52 shorter events, 0.7 us)
Async XLA Ops:
  7.2 655.8 %reduce-scatter.5.cloned.1.call-start = ((), (), s32[]{:S(2)}) async-start(), calls=%async_computation.3 | async-start | bytes 2359296 | tf_op jit(solution)/shard_map/reduce_scatter | solution.py:1828
  317.3 122.7 %copy-start.17 = (bf16[2048,512]{1,0:T(8,128)(2,1)S(1)}, bf16[2048,512]{1,0:T(8,128)(2,1)}, u32[]{:S(2)}) copy-start(bf16[2048,512]{1,0:T(8,128)(2,1)} %get-tuple-element.63) | copy-start | bytes 6291460
  438.8 226.2 %reduce-scatter.3.cloned.1.call-start = ((), (), s32[]{:S(2)}) async-start(), calls=%async_computation.2 | async-start | bytes 9437184 | tf_op jit(solution)/shard_map/reduce_scatter | solution.py:1828
  440.1 4.7 copy-start
  440.1 4.7 copy-start.3
  440.1 4.7 copy-start.4
  440.1 4.7 copy-start.9
  444.8 6.2 copy-start.16
  444.8 10.6 %copy-start.1 = (f32[1024,1]{1,0:T(8,128)S(1)}, f32[1024,1]{1,0:T(8,128)}, u32[]{:S(2)}) copy-start(f32[1024,1]{1,0:T(8,128)} %copy.53.count_ref) | copy-start | bytes 12292
  444.8 10.6 %copy-start.2 = (f32[8,4,128,128]{3,2,1,0:T(8,128)S(1)}, f32[8,4,128,128]{3,2,1,0:T(8,128)}, u32[]{:S(2)}) copy-start(f32[8,4,128,128]{3,2,1,0:T(8,128)} %get-tuple-element.68.start_ref) | copy-start | bytes 6291460
  444.8 10.6 %copy-start.5 = (f32[4,128,128]{2,1,0:T(8,128)S(1)}, f32[4,128,128]{2,1,0:T(8,128)}, u32[]{:S(2)}) copy-start(f32[4,128,128]{2,1,0:T(8,128)} %get-tuple-element.70.carry_ref) | copy-start | bytes 786436
  444.8 10.6 %copy-start.6 = (f32[8,8,128]{2,1,0:T(8,128)S(1)}, f32[8,8,128]{2,1,0:T(8,128)}, u32[]{:S(2)}) copy-start(f32[8,8,128]{2,1,0:T(8,128)} %stack.7.flags_ref) | copy-start | bytes 98308
  444.9 10.6 %copy-start.7 = (f32[8,1,512]{2,1,0:T(1,128)S(1)}, f32[8,1,512]{2,1,0:T(1,128)}, u32[]{:S(2)}) copy-start(f32[8,1,512]{2,1,0:T(1,128)} %get-tuple-element.69.run_ref) | copy-start | bytes 49156
  444.9 10.6 %copy-start.8 = (f32[4,128]{1,0:T(4,128)S(1)}, f32[4,128]{1,0:T(4,128)}, u32[]{:S(2)}) copy-start(f32[4,128]{1,0:T(4,128)} %broadcast_subtract_fusion) | copy-start | bytes 6148
  451.7 3.6 collective-permute-start
  455.4 16.6 %copy-start.18 = (bf16[1024,2048]{1,0:T(8,128)(2,1)S(1)}, bf16[1024,2048]{1,0:T(8,128)(2,1)}, u32[]{:S(2)}) copy-start(bf16[1024,2048]{1,0:T(8,128)(2,1)} %get-tuple-element.84) | copy-start | bytes 12582916
  470.1 2.0 copy-start.10
  497.4 145.4 %copy-start.15 = (f32[1,2048]{1,0:T(1,128)S(1)}, f32[1,2048]{1,0:T(1,128)}, u32[]{:S(2)}) copy-start(f32[1,2048]{1,0:T(1,128)} %get-tuple-element.80) | copy-start | bytes 24580
  665.0 2.9 copy-start.11
  667.9 3.7 copy-start.12
  671.6 2.4 copy-start.14
  671.6 3.5 copy-start.13
Sparse Core Ops, SparseCore 0:
  438.9 39.2 reduce-scatter.4
  483.7 147.9 reduce-scatter.2

commit v9 on v8

--- a/solution.py
+++ b/solution.py
@@ -267,28 +267,6 @@
     )(pre, grad_mixed, grad_gate, starts, runs, carry, after, open_part, counts, keep, flags)
 
 
-def row_flags(segment_ids):
-    ids = segment_ids.reshape(-1)
-    tokens = ids.shape[0]
-    starts = jnp.concatenate([jnp.zeros((1,), F32), (ids[1:] != ids[:-1]).astype(F32)])
-    positions = jnp.arange(tokens)
-    counts = jnp.sum(
-        jnp.where(positions[None, :] <= positions[:, None], starts[None, :], 0.0), axis=1
-    )
-    keep = (ids > 0).astype(F32)
-    blocks = tokens // BLOCK
-    by_block = counts.reshape(blocks, BLOCK)
-    lasts = by_block[:, -1]
-    before = jnp.concatenate([jnp.zeros((1,), F32), lasts[:-1]])
-    wide = (blocks, BLOCK)
-    flags = jnp.stack(
-        [by_block, jnp.broadcast_to(before[:, None], wide), jnp.broadcast_to(lasts[:, None], wide)]
-        + [jnp.zeros(wide, F32)] * 5,
-        axis=1,
-    )
-    return counts[:, None], keep[:, None], flags
-
-
 def from_later(values, axis, shift):
     count = lax.axis_size(axis)
     return lax.ppermute(values, axis, [(i + shift, i) for i in range(count - shift)])
@@ -1229,12 +1207,10 @@
     forget_hbm,
     input_hbm,
     gate_hbm,
-    out_shard_hbm,
-    open_ref,
-    count_ref,
-    keep_ref,
-    flags_ref,
-    ids_ref,
+    out_shard_ref,
+    down_shard_ref,
+    floor_ref,
+    segments_ref,
     head_gain_ref,
     normed_hbm,
     pre_hbm,
@@ -1245,6 +1221,11 @@
     start_hbm,
     gated_hbm,
     mix_hbm,
+    down_turned,
+    open_ref,
+    count_ref,
+    keep_ref,
+    flags_ref,
     run_ref,
     carry_ref,
     decay_ref,
@@ -1252,6 +1233,7 @@
     normed,
     pre,
     mine,
+    out_turned,
     full,
     out_full,
     mixed,
@@ -1289,13 +1271,14 @@
     for load in mine_loads:
         load.start()
     gather = Gather(plane, (mine,), (full,), sems[:5])
-    out_gather = Gather(plane, (out_shard_hbm,), (out_full,), sems[5:])
+    out_gather = Gather(plane, (out_turned,), (out_full,), sems[5:])
 
     def later(shift):
         places = {axis: lax.axis_index(axis) for axis in mesh_axes}
         places["context"] = lax.rem(context + shift, context_size)
         return tuple(places[axis] for axis in mesh_axes)
 
+    out_turned[...] = out_shard_ref[...].T
     barrier = pltpu.get_barrier_semaphore()
     expected = gather.greet(barrier)
     for shift in range(1, context_size):
@@ -1305,6 +1288,40 @@
         load.wait()
     gather.start()
     out_gather.start()
+    down_turned[...] = down_shard_ref[...].T
+    for head in range(head_count):
+        open_ref[:, head * lanes : (head + 1) * lanes] = 1.0 - floor_ref[head : head + 1]
+
+    segments = segments_ref[...]
+    blocks = segments.shape[0]
+    block_ids = lax.broadcasted_iota(jnp.int32, segments.shape, 0)
+    slot_ids = lax.broadcasted_iota(jnp.int32, segments.shape, 1)
+    before = pltpu.roll(segments, 1, 1)
+    wrapped = pltpu.roll(before, 1, 0)
+    before = jnp.where(slot_ids == 0, wrapped, before)
+    first_slot = jnp.logical_and(slot_ids == 0, block_ids == 0)
+    begins = jnp.where(jnp.logical_or(first_slot, segments == before), 0.0, 1.0)
+    wide_rows = lax.broadcasted_iota(jnp.int32, (BLOCK, BLOCK), 0)
+    wide_columns = lax.broadcasted_iota(jnp.int32, (BLOCK, BLOCK), 1)
+    within = mm_nn(begins.astype(BF16), (wide_rows <= wide_columns).astype(BF16))
+    count_rows = []
+    running = jnp.zeros((1, 1), F32)
+    flags_ref[...] = jnp.zeros_like(flags_ref)
+    for index in range(blocks):
+        row = within[index : index + 1] + running
+        flags_ref[index, 0:1] = row
+        flags_ref[index, 1:2] = jnp.broadcast_to(running, (1, BLOCK))
+        running = row[:, BLOCK - 1 : BLOCK]
+        flags_ref[index, 2:3] = jnp.broadcast_to(running, (1, BLOCK))
+        count_rows.append(row)
+    turned_counts = jnp.concatenate(count_rows, axis=0).T
+    turned_keep = (segments > 0).astype(F32).T
+    for index in range(blocks):
+        rows = slice(index * BLOCK, (index + 1) * BLOCK)
+        count_ref[rows] = turned_counts[:, index : index + 1]
+        keep_ref[rows] = turned_keep[:, index : index + 1]
+    first_id = jnp.broadcast_to(segments[0:1, 0:1], (1, lanes))
+    last_id = jnp.broadcast_to(segments[blocks - 1 : blocks, BLOCK - 1 : BLOCK], (1, lanes))
 
     def norm(index, _):
         rows = pl.ds(pl.multiple_of(index * 128, 128), 128)
@@ -1429,7 +1446,8 @@
         decay = jnp.exp(run_scr[:, part]) * (last_count == 0).astype(F32)
         decay_ref[head] = decay
         message[state_rows + 8 + head : state_rows + 9 + head] = decay
-    message[state_rows : state_rows + 8] = ids_ref[...]
+    message[state_rows : state_rows + 1] = first_id
+    message[state_rows + 1 : state_rows + 2] = last_id
 
     def state_copy(shift):
         return pltpu.make_async_remote_copy(
@@ -1456,7 +1474,7 @@
         def _(shift=shift):
             state_copy(shift).wait_recv()
             linked = jnp.ones((1, lanes), F32)
-            follower = ids_ref[0:1]
+            follower = first_id
             factors = [jnp.ones((1, lanes), F32)] * head_count
             for near in range(shift):
                 got = received.at[near]
@@ -1526,9 +1544,8 @@
 
 
 def forward(
-    mesh_axes, collective, hidden, gain, shards, out_shard, open_part, masks, ids, head_gain
+    mesh_axes, collective, hidden, gain, shards, out_shard, down_shard, floor, segments, head_gain
 ):
-    counts, keep, flags = masks
     tokens, model_width = hidden.shape
     block, width = shards[0].shape
     lanes = head_gain.shape[1]
@@ -1552,6 +1569,11 @@
         ((tokens, model_width), BF16),
     ]
     kept = [
+        (down_shard.shape[::-1], BF16),
+        ((1, width), F32),
+        ((tokens, 1), F32),
+        ((tokens, 1), F32),
+        ((blocks, 8, BLOCK), F32),
         ((blocks, 1, width), F32),
         ((head_count, lanes, lanes), F32),
         ((head_count, 1, lanes), F32),
@@ -1559,13 +1581,14 @@
     ]
     return pl.pallas_call(
         partial(forward_kernel, mesh_axes, head_count, lanes ** (-0.5)),
-        in_specs=[whole] * 2 + [remote] * 5 + [whole] * 6,
+        in_specs=[whole] * 2 + [remote] * 4 + [whole] * 5,
         out_specs=[remote] * len(stored) + [whole] * len(kept),
         out_shape=[jax.ShapeDtypeStruct(shape, kind) for shape, kind in stored + kept],
         scratch_shapes=[
             pltpu.VMEM((tokens, model_width), BF16),
             pltpu.VMEM((tokens, all_width), F32),
             pltpu.VMEM((block, all_width), BF16),
+            pltpu.VMEM((block, width), BF16),
             pltpu.VMEM((model_width, all_width), BF16),
             pltpu.VMEM((model_width, width), BF16),
             pltpu.VMEM((tokens, width), F32),
@@ -1596,7 +1619,7 @@
             transcendentals=tokens * width * 9,
         ),
         name="forward",
-    )(hidden, gain, *shards, out_shard, open_part, counts, keep, flags, ids, head_gain)
+    )(hidden, gain, *shards, out_shard, down_shard, floor, segments, head_gain)
 
 
 def small_sum_kernel(
@@ -1722,11 +1745,8 @@
     both = ("shard", "context")
     gain_one, gain_two = norm1_gain.reshape(1, -1), norm2_gain.reshape(1, -1)
     hidden_rows = hidden.reshape(tokens, model_width)
-    open_part = (1.0 - forget_floor).reshape(1, width)
-    counts, keep, flags = row_flags(segment_ids)
-    ends = segment_ids.reshape(-1).astype(F32)
-    ids = jnp.where(lax.broadcasted_iota(jnp.int32, (8, key_dim), 0) == 1, ends[-1], ends[0])
     gain_row = head_gain.reshape(1, -1)
+    segments = segment_ids.reshape(tokens // BLOCK, BLOCK).astype(F32)
     (
         normed_one,
         pre,
@@ -1737,6 +1757,11 @@
         starts,
         gated_low,
         mix_part,
+        down_turned,
+        open_part,
+        counts,
+        keep,
+        flags,
         runs,
         carry,
         decay,
@@ -1747,10 +1772,10 @@
         hidden_rows,
         gain_one,
         (w_query, w_forget, w_input, w_gate_out),
-        w_out.T,
-        open_part,
-        (counts, keep, flags),
-        ids,
+        w_out,
+        w_ffn_down,
+        forget_floor,
+        segments,
         gain_row,
     )
     grad_rows = out_grad.reshape(tokens, model_width)
@@ -1773,20 +1798,7 @@
         gain_two,
         w_ffn_gate,
         w_ffn_up,
-        w_ffn_down.T,
-    )
-    output_rows, grads_ffn, grad_out = output_line(
-        mesh_axes,
-        1,
-        feed_part,
-        residual,
-        normed_two,
-        grad_rows,
-        hidden_low,
-        grad_gate_low,
-        grad_up_low,
-        gated_low,
-        grad_mix_low,
+        down_turned,
     )
     grad_gated = jnp.dot(grad_mix_low, out_full, preferred_element_type=F32)
     grad_mixed, grad_gate_pre, grad_head_part, back = gate_backward(
@@ -1806,7 +1818,23 @@
         keep,
         flags,
     )
-    grad_mixer = jnp.einsum("td,tk->dk", normed_one, grad_pre, preferred_element_type=F32)
+    grad_mixer = jnp.einsum(
+        "td,tk->dk", normed_one, grad_pre, preferred_element_type=F32
+    ).astype(BF16)
+    feed_part, grad_mixer = lax.optimization_barrier((feed_part, grad_mixer))
+    output_rows, grads_ffn, grad_out = output_line(
+        mesh_axes,
+        1,
+        feed_part,
+        residual,
+        normed_two,
+        grad_rows,
+        hidden_low,
+        grad_gate_low,
+        grad_up_low,
+        gated_low,
+        grad_mix_low,
+    )
     back_one = jnp.einsum("tk,dk->td", grad_pre, mixer_full, preferred_element_type=F32)
     input_rows, grad_norm_one, share_gate, share_up, share_down = input_line(
         mesh_axes, 3, back_one.astype(BF16), hidden_rows, grad_residual, gain_one, grads_ffn

time: 684 us -> 659 us (0.963)
  Pallas kernels: 596 us -> 579 us
  local copies, waits for them, and re-layouts: 31.6 us -> 23.1 us
    pallas_call x1, Pallas kernels: 145 us -> 128 us  [input_line(): pl.pallas_call(partial(input_kernel, mesh_axes), in_specs=[whole] * 4 + [...]
    unnamed x46 -> x44, local copies, waits for them, and re-layouts: 18.4 us -> 14.4 us
  transfers between devices with their start and end apart: 3 -> 3, of which waited for: 1 -> 2; matrix products, arithmetic and copies ran while one was open for 6% -> 4% of each run, Pallas kernels for 26% -> 21%
where the time goes in v9:
time: 659 us; the launch traced here: 658 us
  Pallas kernels  579 us (88%)
  matrix products  30.1 us (5%)
  local copies, waits for them, and re-layouts  23.1 us (4%)
  between operations  14.4 us (2%)
    pallas_call x1, Pallas kernels, middle(): pl.pallas_call(partial(middle_kernel, mesh_axes), in_specs=[remote, whole...  222 us
    pallas_call x1, Pallas kernels, input_line(): pl.pallas_call(partial(input_kernel, mesh_axes), in_specs=[whole] * 4 + [...  128 us
    pallas_call x1, Pallas kernels, output_line(): pl.pallas_call(partial(output_kernel, mesh_axes), in_specs=[whole] * 9, o...  122 us
    pallas_call x1, Pallas kernels, forward(): pl.pallas_call(partial(forward_kernel, mesh_axes, head_count, lanes ** (-...  74.8 us
    pallas_call x1, Pallas kernels, mixer_backward(): pl.pallas_call(partial(mixer_backward_kernel, head_count), grid=(blocks,)...  14.6 us
    unnamed x44, local copies, waits for them, and re-layouts  14.4 us
    dot_general x1, matrix products, local(): jnp.einsum('tk,dk->td', grad_pre, mixer_full, preferred_element_type=F32)  14 us
  transfers between devices with their start and end apart: 3, of which 2 were waited for; matrix products, arithmetic and copies ran while one was open for 4% of the time, Pallas kernels for 21%

profile of v9, /device:TPU:0, one launch (start us, length us, event | category | flops | bytes accessed | tf_op | source)
XLA Modules:
  0.0 658.1 jit_solution(4929524706572087079)
XLA Ops:
  7.2 0.0 reduce-scatter.5.cloned.1.call-start
  7.2 1.3 convert_element_type.19
  8.5 74.8 %forward.1 = (bf16[1024,2048]{1,0:T(8,128)(2,1)}, f32[1024,2048]{1,0:T(8,128)}, bf16[2048,2048]{1,0:T(8,128)(2,1)}, bf16[2048,512]{1,0:T(8,128)(2,1)}, f32[1024,...) custom-call(bf16[1024,2048]{1,0:T(8,128)(2,1)} %bitcast.38, ...), custom_call_target="tpu_custom_call" | custom-call | flops 8589934592 | bytes 200000000 | tf_op jit(solution)/shard_map/forward/pallas_call | solution.py:1582
  83.3 1.2 slice.40
  84.5 222.4 %middle.1 = (bf16[1024,2048]{1,0:T(8,128)(2,1)}, bf16[1024,2048]{1,0:T(8,128)(2,1)}, f32[1,2048]{1,0:T(1,128)}, f32[512,2048]{1,0:T(8,128)}, bf16[1024,1408]{1,0...) custom-call(bf16[1024,2048]{1,0:T(8,128)(2,1)} %get-tuple-element.59, ...), custom_call_target="tpu_custom_call" | custom-call | flops 35433480192 | bytes 360000000 | tf_op jit(solution)/shard_map/middle/pallas_call | solution.py:861
  306.9 0.0 copy-done.17
  306.9 0.0 copy-start
  307.0 0.0 copy-start.2
  307.0 0.0 copy-start.3
  307.0 0.0 copy-start.9
  307.0 4.7 fusion.3.grad_ref
  311.8 6.1 gate_backward.1
  317.9 0.0 copy-done.16
  317.9 0.7 maximum_multiply_fusion
  318.6 1.5 collective-permute-start
  320.1 2.4 collective-permute-done
  322.6 14.6 %mixer_backward.1 = (bf16[1024,2048]{1,0:T(8,128)(2,1)S(1)}, f32[1,512]{1,0:T(1,128)S(1)}) custom-call(f32[1024,2048]{1,0:T(8,128)} %get-tuple-element.63.gate_ref.pre_ref, bf16[1024,512]{1,0:T(8,128)(2,1)S(1)} %get-tuple-element.69.grad_mixed_ref, bf16[1024,512]{1,0:T(8,128)(2,1)S(1)} %get-tuple-element.70.grad_gate_ref, f32[8,4,128,128]{3,2,1,0:T(8,128)S(1)} %copy-done.1, ...), custom_call_target="tpu_custom_call" | custom-call | flops 2013265920 | bytes 18874368 | tf_op jit(solution)/shard_map/mixer_backward/pallas_call | solution.py:227
  337.2 0.0 copy-start.10
  337.2 2.0 copy-done.10
  339.2 0.0 copy-done.18
  339.2 11.4 %convolution_convert_fusion = bf16[2048,2048]{1,0:T(8,128)(2,1)} fusion(bf16[1024,2048]{1,0:T(8,128)(2,1)S(1)} %copy-done.18, bf16[1024,2048]{1,0:T(8,128)(2,1)S(1)} %get-tuple-element.80), kind=kOutput, calls=%fused_computation | convolution fusion | flops 8594128896 | bytes 16777216 | tf_op jit(solution)/shard_map/td,tk->dk/dot_general | solution.py:1821
  350.6 121.9 %output_line.1 = (bf16[1024,2048]{1,0:T(8,128)(2,1)}, bf16[3,2048,1408]{2,1,0:T(8,128)(2,1)}, bf16[2048,512]{1,0:T(8,128)(2,1)}) custom-call(bf16[1024,2048]{1,0:T(8,128)(2,1)} %get-tuple-element.81.part, f32[512,2048]{1,0:T(8,128)} %get-tuple-element.82.residual, bf16[1024,2048]{1,0:T(8,128)(2,1)} %get-tuple-element.83.normed_ref, ...), custom_call_target="tpu_custom_call" | custom-call | flops 17716740096 | bytes 360000000 | tf_op jit(solution)/shard_map/output_line/pallas_call | solution.py:993
  472.5 0.0 reduce-scatter.5.cloned.1.call-update
  472.6 0.3 reduce-scatter.3.cloned.1.call-start
  472.9 0.4 reduce-scatter.3.cloned.1.call-update
  473.3 14.0 %convolution_convert_fusion.1.part = bf16[1024,2048]{1,0:T(8,128)(2,1)} fusion(bf16[1024,2048]{1,0:T(8,128)(2,1)} %copy-done.10, bf16[2048,2048]{1,0:T(8,128)(2,1)} %get-tuple-element.89), kind=kOutput, calls=%fused_computation.1 | convolution fusion | flops 8592031744 | bytes 16777216 | tf_op jit(solution)/shard_map/tk,dk->td/dot_general | solution.py:1838
  487.3 128.3 %input_line.1 = (bf16[1024,2048]{1,0:T(8,128)(2,1)}, f32[1,2048]{1,0:T(1,128)}, f32[256,1408]{1,0:T(8,128)}, f32[256,1408]{1,0:T(8,128)}, f32[256,1408]{1,0:T(8,128)}) custom-call(bf16[1024,2048]{1,0:T(8,128)(2,1)} %convolution_convert_fusion.1.part, bf16[1024,2048]{1,0:T(8,128)(2,1)} %bitcast.40, f32[512,2048]{1,0:T(8,128)} %get-tuple-element.90.residual_grad, ...), custom_call_target="tpu_custom_call" | custom-call | flops 16777216 | bytes 360000000 | tf_op jit(solution)/shard_map/input_line/pallas_call | solution.py:1169
  615.7 0.7 select_maximum_fusion
  616.4 0.6 reshape.103.value
  617.0 10.5 %small_sum.1 = (f32[8,640]{1,0:T(8,128)}, f32[8,640]{1,0:T(8,128)}) custom-call(f32[8,640]{1,0:T(8,128)} %reshape.103.value), custom_call_target="tpu_custom_call" | custom-call | flops 40960 | bytes 20000000 | tf_op jit(solution)/shard_map/small_sum/pallas_call | solution.py:1700
  627.5 0.8 slice.50
  628.4 0.7 slice.42
  629.1 0.8 slice.48
  630.0 2.9 copy.33
  632.9 0.5 fusion
  633.4 0.6 constant_dynamic-slice_fusion.2
  634.0 0.6 constant_dynamic-slice_fusion
  634.5 1.0 convert_bitcast_fusion
  635.5 1.0 copy.32
  636.5 3.5 reduce-scatter.3.cloned.1.call-done
  640.1 2.8 fusion.1
  642.9 0.2 copy-done.11
  643.0 2.1 copy.38
  645.1 1.6 copy-done.12
  646.7 2.1 copy.39
  648.8 0.2 copy-done.14
  649.1 1.1 copy.40
  650.2 1.1 copy.41
  (32 shorter events, 0.1 us)
Async XLA Ops:
  7.2 627.4 %reduce-scatter.5.cloned.1.call-start = ((), (), s32[]{:S(2)}) async-start(), calls=%async_computation.3 | async-start | bytes 2359296 | tf_op jit(solution)/shard_map/reduce_scatter | solution.py:1856
  84.5 222.4 %copy-start.17 = (bf16[2048,512]{1,0:T(8,128)(2,1)S(1)}, bf16[2048,512]{1,0:T(8,128)(2,1)}, u32[]{:S(2)}) copy-start(bf16[2048,512]{1,0:T(8,128)(2,1)} %get-tuple-element.65) | copy-start | bytes 6291460
  306.9 4.7 copy-start
  307.0 4.7 copy-start.2
  307.0 4.7 copy-start.3
  307.0 4.7 copy-start.9
  311.7 6.2 copy-start.16
  311.7 10.8 %copy-start.1 = (f32[8,4,128,128]{3,2,1,0:T(8,128)S(1)}, f32[8,4,128,128]{3,2,1,0:T(8,128)}, u32[]{:S(2)}) copy-start(f32[8,4,128,128]{3,2,1,0:T(8,128)} %get-tuple-element.71.start_ref) | copy-start | bytes 6291460
  311.7 10.8 %copy-start.4 = (f32[1024,1]{1,0:T(8,128)S(1)}, f32[1024,1]{1,0:T(8,128)}, u32[]{:S(2)}) copy-start(f32[1024,1]{1,0:T(8,128)} %get-tuple-element.78.count_ref) | copy-start | bytes 12292
  311.7 10.8 %copy-start.5 = (f32[4,128,128]{2,1,0:T(8,128)S(1)}, f32[4,128,128]{2,1,0:T(8,128)}, u32[]{:S(2)}) copy-start(f32[4,128,128]{2,1,0:T(8,128)} %get-tuple-element.73.carry_ref) | copy-start | bytes 786436
  311.7 10.8 %copy-start.6 = (f32[8,8,128]{2,1,0:T(8,128)S(1)}, f32[8,8,128]{2,1,0:T(8,128)}, u32[]{:S(2)}) copy-start(f32[8,8,128]{2,1,0:T(8,128)} %get-tuple-element.79.flags_ref) | copy-start | bytes 98308
  311.7 10.8 %copy-start.7 = (f32[8,1,512]{2,1,0:T(1,128)S(1)}, f32[8,1,512]{2,1,0:T(1,128)}, u32[]{:S(2)}) copy-start(f32[8,1,512]{2,1,0:T(1,128)} %get-tuple-element.72.run_ref) | copy-start | bytes 49156
  311.8 10.8 %copy-start.8 = (f32[1,512]{1,0:T(1,128)S(1)}, f32[1,512]{1,0:T(1,128)}, u32[]{:S(2)}) copy-start(f32[1,512]{1,0:T(1,128)} %get-tuple-element.77.open_ref) | copy-start | bytes 6148
  318.6 3.9 collective-permute-start
  322.6 16.6 %copy-start.18 = (bf16[1024,2048]{1,0:T(8,128)(2,1)S(1)}, bf16[1024,2048]{1,0:T(8,128)(2,1)}, u32[]{:S(2)}) copy-start(bf16[1024,2048]{1,0:T(8,128)(2,1)} %get-tuple-element.62) | copy-start | bytes 12582916
  337.2 2.0 copy-start.10
  472.6 167.5 %reduce-scatter.3.cloned.1.call-start = ((), (), s32[]{:S(2)}) async-start(), calls=%async_computation.2 | async-start | bytes 9437184 | tf_op jit(solution)/shard_map/reduce_scatter | solution.py:1856
  487.3 128.3 %copy-start.15 = (f32[1,2048]{1,0:T(1,128)S(1)}, f32[1,2048]{1,0:T(1,128)}, u32[]{:S(2)}) copy-start(f32[1,2048]{1,0:T(1,128)} %get-tuple-element.94) | copy-start | bytes 24580
  640.1 2.9 copy-start.11
  643.0 3.7 copy-start.12
  646.7 2.4 copy-start.14
  646.7 3.5 copy-start.13
Sparse Core Ops, SparseCore 0:
  472.7 81.2 reduce-scatter.4
  557.8 82.2 reduce-scatter.2

commit v10 on v9

--- a/solution.py
+++ b/solution.py
@@ -46,246 +46,6 @@
     tail = (counts == flags_row[2:3, 0:1]).astype(F32)
     closing = (flags_row[1:2, 0:1] == flags_row[2:3, 0:1]).astype(F32)
     return row_ids, col_ids, linked, fresh, tail, closing
-
-
-def gate_backward_kernel(
-    head_count,
-    key_scale,
-    grad_ref,
-    mixed_ref,
-    lead_ref,
-    gate_ref,
-    gain_ref,
-    keep_ref,
-    grad_mixed_ref,
-    grad_gate_ref,
-    grad_gain_ref,
-    back_ref,
-):
-    lanes = gain_ref.shape[1]
-
-    @pl.when(pl.program_id(0) == 0)
-    def _():
-        grad_gain_ref[...] = jnp.zeros_like(grad_gain_ref)
-        back_ref[...] = jnp.zeros_like(back_ref)
-
-    gain = gain_ref[...]
-    total = jnp.zeros_like(gain)
-    for head in range(head_count):
-        part = slice(head * lanes, (head + 1) * lanes)
-        mixed, gate, grad = mixed_ref[:, part], gate_ref[:, part], grad_ref[:, part]
-        inverse = lax.rsqrt(jnp.mean(mixed * mixed, axis=-1, keepdims=True) + EPSILON)
-        unit = mixed * inverse
-        sigma = jax.nn.sigmoid(gate)
-        scaled = grad * unit
-        total = total + jnp.sum(scaled * (gate * sigma), axis=0, keepdims=True)
-        grad_gate = scaled * gain * sigma * (1.0 + gate * (1.0 - sigma))
-        grad_gate_ref[:, part] = grad_gate.astype(BF16)
-        lifted = grad * gain * (gate * sigma)
-        mean = jnp.mean(lifted * unit, axis=-1, keepdims=True)
-        grad_mixed = inverse * (lifted - unit * mean) * (key_scale * keep_ref[...])
-        grad_mixed = grad_mixed.astype(BF16)
-        grad_mixed_ref[:, part] = grad_mixed
-        back_ref[head] += mm_tn(grad_mixed, lead_ref[:, part])
-    grad_gain_ref[...] += total
-
-
-def gate_backward(grad, mixed, lead, pre, gain, keep, head_count, key_scale):
-    tokens, width = mixed.shape
-    lanes = gain.shape[1]
-    rows = 2 * BLOCK
-    return pl.pallas_call(
-        partial(gate_backward_kernel, head_count, key_scale),
-        grid=(tokens // rows,),
-        in_specs=[
-            pl.BlockSpec((rows, width), lambda i: (i, 0)),
-            pl.BlockSpec((rows, width), lambda i: (i, 0)),
-            pl.BlockSpec((rows, width), lambda i: (i, 0)),
-            pl.BlockSpec((rows, width), lambda i: (i, 3)),
-            pl.BlockSpec((1, lanes), lambda i: (0, 0)),
-            pl.BlockSpec((rows, 1), lambda i: (i, 0)),
-        ],
-        out_specs=[
-            pl.BlockSpec((rows, width), lambda i: (i, 0)),
-            pl.BlockSpec((rows, width), lambda i: (i, 0)),
-            pl.BlockSpec((1, lanes), lambda i: (0, 0)),
-            pl.BlockSpec((head_count, lanes, lanes), lambda i: (0, 0, 0)),
-        ],
-        out_shape=[
-            jax.ShapeDtypeStruct((tokens, width), BF16),
-            jax.ShapeDtypeStruct((tokens, width), BF16),
-            jax.ShapeDtypeStruct((1, lanes), F32),
-            jax.ShapeDtypeStruct((head_count, lanes, lanes), F32),
-        ],
-        compiler_params=pltpu.CompilerParams(
-            dimension_semantics=("arbitrary",), vmem_limit_bytes=40 << 20
-        ),
-        cost_estimate=pl.CostEstimate(
-            flops=tokens * width * 300,
-            bytes_accessed=tokens * width * 18,
-            transcendentals=tokens * width,
-        ),
-        name="gate_backward",
-    )(grad, mixed, lead, pre, gain, keep)
-
-
-def mixer_backward_kernel(
-    head_count,
-    pre_ref,
-    grad_mixed_ref,
-    grad_gate_ref,
-    start_ref,
-    run_ref,
-    carry_ref,
-    after_ref,
-    open_ref,
-    count_ref,
-    keep_ref,
-    flags_ref,
-    grads_ref,
-    floor_ref,
-    grad_scr,
-    lifted_scr,
-    lowered_scr,
-    moved_scr,
-    value_scr,
-):
-    width = open_ref.shape[1]
-    lanes = width // head_count
-
-    @pl.when(pl.program_id(0) == 0)
-    def _():
-        grad_scr[...] = after_ref[...]
-        floor_ref[...] = jnp.zeros_like(floor_ref)
-
-    counts, keep = count_ref[...], keep_ref[...]
-    flags = flags_ref[0]
-    row_ids, col_ids, linked, fresh, tail, closing = block_masks(counts, flags)
-    tri = (row_ids >= col_ids).astype(BF16)
-    tri_back = (row_ids <= col_ids).astype(BF16)
-    query_pre = pre_ref[:, :width]
-    values = pre_ref[:, 2 * width : 3 * width].astype(BF16)
-    opened = open_ref[...]
-    closed = jax.nn.sigmoid(-pre_ref[:, width : 2 * width])
-    keys = opened * closed
-    cum = split_sum(tri, jnp.log1p(-keys))
-    rows = cum.shape[0]
-    ending = cum[rows - 1 : rows, :]
-    rise, fall = jnp.exp(cum), jnp.exp(-cum) * keep
-    shift = jnp.exp(ending - cum) * (keep * tail)
-    sigma_query = jax.nn.sigmoid(query_pre)
-    lifted = (query_pre * sigma_query * rise).astype(BF16)
-    lowered = (keys * fall).astype(BF16)
-    moved = (keys * shift).astype(BF16)
-    fresh_lifted = (lifted.astype(F32) * fresh).astype(BF16)
-    end_decay = jnp.exp(ending) * closing
-    lead_in = jnp.exp(run_ref[0]) * (flags[1:2, 0:1] == 0).astype(F32)
-    for head in range(head_count):
-        part = slice(head * lanes, (head + 1) * lanes)
-        grad_out, value = grad_mixed_ref[:, part], values[:, part]
-        lift, lower, move = lifted[:, part], lowered[:, part], moved[:, part]
-        scores = jnp.where(linked, mm_nt(lift, lower), 0.0).astype(BF16)
-        pulls = jnp.where(linked, mm_nt(grad_out, value), 0.0).astype(BF16)
-        state = start_ref[0, head] + lead_in[:, part] * carry_ref[head]
-        grad_state = grad_scr[head]
-        grad_low = grad_state.astype(BF16)
-        lifted_scr[:, part] = mm_nn(pulls, lower) + fresh * mm_nn(grad_out, state.astype(BF16))
-        lowered_scr[:, part] = mm_tn(pulls, lift)
-        grad_moved = mm_nn(value, grad_low)
-        moved_scr[:, part] = grad_moved
-        grads_ref[:, 2 * width + head * lanes : 2 * width + (head + 1) * lanes] = (
-            mm_tn(scores, grad_out) + mm_nt(move, grad_low)
-        ).astype(BF16)
-        value_scr[:, part] = jnp.sum(
-            grad_moved * move.astype(F32), axis=0, keepdims=True
-        ) + end_decay[:, part] * jnp.sum(state * grad_state, axis=0, keepdims=True)
-        grad_scr[head] = grad_state * end_decay[:, part] + mm_tn(grad_out, fresh_lifted[:, part])
-    grad_lifted, grad_lowered, grad_moved = lifted_scr[...], lowered_scr[...], moved_scr[...]
-    grad_cum = (
-        grad_lifted * lifted.astype(F32)
-        - grad_lowered * lowered.astype(F32)
-        - grad_moved * moved.astype(F32)
-    )
-    grad_decay = split_sum(tri_back, grad_cum) + value_scr[...]
-    key_total = grad_lowered * fall + grad_moved * shift - grad_decay / (1.0 - keys)
-    floor_ref[...] -= jnp.sum(key_total * closed, axis=0, keepdims=True)
-    grads_ref[:, :width] = (
-        grad_lifted * rise * sigma_query * (1.0 + query_pre * (1.0 - sigma_query))
-    ).astype(BF16)
-    grads_ref[:, width : 2 * width] = (-key_total * opened * closed * (1.0 - closed)).astype(BF16)
-    grads_ref[:, 3 * width :] = grad_gate_ref[...]
-
-
-def mixer_backward(
-    pre, grad_mixed, grad_gate, starts, runs, carry, after, open_part, counts, keep, flags
-):
-    tokens, all_width = pre.shape
-    width = open_part.shape[1]
-    head_count, lanes = carry.shape[0], carry.shape[2]
-    blocks = tokens // BLOCK
-    last = blocks - 1
-    return pl.pallas_call(
-        partial(mixer_backward_kernel, head_count),
-        grid=(blocks,),
-        in_specs=[
-            pl.BlockSpec((BLOCK, all_width), lambda i: (last - i, 0)),
-            pl.BlockSpec((BLOCK, width), lambda i: (last - i, 0)),
-            pl.BlockSpec((BLOCK, width), lambda i: (last - i, 0)),
-            pl.BlockSpec((1, head_count, lanes, lanes), lambda i: (last - i, 0, 0, 0)),
-            pl.BlockSpec((1, 1, width), lambda i: (last - i, 0, 0)),
-            pl.BlockSpec((head_count, lanes, lanes), lambda i: (0, 0, 0)),
-            pl.BlockSpec((head_count, lanes, lanes), lambda i: (0, 0, 0)),
-            pl.BlockSpec((1, width), lambda i: (0, 0)),
-            pl.BlockSpec((BLOCK, 1), lambda i: (last - i, 0)),
-            pl.BlockSpec((BLOCK, 1), lambda i: (last - i, 0)),
-            pl.BlockSpec((1, 8, BLOCK), lambda i: (last - i, 0, 0)),
-        ],
-        out_specs=[
-            pl.BlockSpec((BLOCK, all_width), lambda i: (last - i, 0)),
-            pl.BlockSpec((1, width), lambda i: (0, 0)),
-        ],
-        out_shape=[
-            jax.ShapeDtypeStruct((tokens, all_width), BF16),
-            jax.ShapeDtypeStruct((1, width), F32),
-        ],
-        scratch_shapes=[
-            pltpu.VMEM((head_count, lanes, lanes), F32),
-            pltpu.VMEM((BLOCK, width), F32),
-            pltpu.VMEM((BLOCK, width), F32),
-            pltpu.VMEM((BLOCK, width), F32),
-            pltpu.VMEM((1, width), F32),
-        ],
-        compiler_params=pltpu.CompilerParams(
-            dimension_semantics=("arbitrary",), vmem_limit_bytes=40 << 20
-        ),
-        cost_estimate=pl.CostEstimate(
-            flops=tokens * width * BLOCK * 30,
-            bytes_accessed=tokens * width * 36,
-            transcendentals=tokens * width * 9,
-        ),
-        name="mixer_backward",
-    )(pre, grad_mixed, grad_gate, starts, runs, carry, after, open_part, counts, keep, flags)
-
-
-def from_later(values, axis, shift):
-    count = lax.axis_size(axis)
-    return lax.ppermute(values, axis, [(i + shift, i) for i in range(count - shift)])
-
-
-def grad_after(back, decay, link_in, axis):
-    head_count, lanes, _ = back.shape
-    rows = head_count * lanes
-    message = (
-        jnp.concatenate([back.reshape(rows, lanes), decay.reshape(head_count, lanes)]) * link_in
-    )
-    message = jnp.pad(message, ((0, 8 - head_count % 8 if head_count % 8 else 0), (0, 0)))
-    total = jnp.zeros_like(back)
-    factor = jnp.ones((head_count, 1, lanes), F32)
-    for shift in range(1, lax.axis_size(axis)):
-        got = from_later(message, axis, shift)
-        total = total + factor * got[:rows].reshape(back.shape)
-        factor = factor * got[rows : rows + head_count].reshape(head_count, 1, lanes)
-    return total
 
 
 CHUNK = 32
@@ -909,106 +669,399 @@
 
 def output_kernel(
     mesh_axes,
+    head_count,
+    key_scale,
     part,
     residual,
-    normed_ref,
-    cotangent_ref,
     hidden_ref,
     grad_gate_ref,
     grad_up_ref,
     gated_ref,
     mix_grad_ref,
+    out_full,
+    mixed_ref,
+    lead_ref,
+    starts_ref,
+    run_ref,
+    carry_ref,
+    decay_ref,
+    link_ref,
+    open_ref,
+    count_ref,
+    keep_ref,
+    flags_ref,
+    gain_ref,
+    normed_two_hbm,
+    cotangent_hbm,
+    normed_one_hbm,
+    pre_hbm,
     out_ref,
+    gain_grad,
+    floor_grad,
     grads_hbm,
     out_grads_hbm,
+    mixer_grads_hbm,
+    grad_pre_hbm,
     arrived,
+    left,
+    right,
     stage,
     out_stage,
+    mixer_stage,
+    gates,
+    pre,
+    grad_mixed,
+    back_scr,
+    message,
+    received,
+    grad_scr,
+    lifted_scr,
+    lowered_scr,
+    moved_scr,
+    value_scr,
+    load_sem,
+    pre_sem,
     stage_sem,
-    out_sem,
+    save_sem,
+    grad_send,
+    grad_recv,
     *sems,
 ):
-    model_width = normed_ref.shape[1]
-    tiles = model_width // TILE
+    tokens, model_width = left.shape
+    width = gated_ref.shape[1]
+    lanes = width // head_count
+    state_rows = head_count * lanes
+    tiles, blocks = model_width // TILE, tokens // BLOCK
+    piece_rows = 2 * BLOCK
+    context, context_size = lax.axis_index("context"), lax.axis_size("context")
+
+    left_load = pltpu.make_async_copy(normed_two_hbm, left, load_sem.at[0])
+    right_load = pltpu.make_async_copy(cotangent_hbm, right, load_sem.at[1])
+    gate_load = pltpu.make_async_copy(
+        pre_hbm.at[:, pl.ds(3 * width, width)], gates, load_sem.at[2]
+    )
+    next_load = pltpu.make_async_copy(normed_one_hbm, left, load_sem.at[3])
+    for load in (left_load, right_load, gate_load):
+        load.start()
+    gain_grad[...] = jnp.zeros_like(gain_grad)
+    floor_grad[...] = jnp.zeros_like(floor_grad)
+    back_scr[...] = jnp.zeros_like(back_scr)
 
     def turn(total, rows, own):
         out_ref[rows] = (residual[own] + total).astype(BF16)
 
+    def earlier(shift):
+        places = {axis: lax.axis_index(axis) for axis in mesh_axes}
+        places["context"] = lax.rem(context + context_size - shift, context_size)
+        return tuple(places[axis] for axis in mesh_axes)
+
     line = Line(mesh_axes, part, arrived, out_ref, sems, turn)
     barrier = pltpu.get_barrier_semaphore()
-    pl.semaphore_wait(barrier, line.greet(barrier))
+    expected = line.greet(barrier)
+    for shift in range(1, context_size):
+        pl.semaphore_signal(barrier, inc=1, device_id=earlier(shift), device_id_type=MESH_ID)
+    pl.semaphore_wait(barrier, expected + context_size - 1)
+    for load in (left_load, right_load, gate_load):
+        load.wait()
+
+    def tile_columns(tile):
+        return pl.ds(pl.multiple_of(tile * TILE, TILE), TILE)
 
     def stage_copies(tile):
-        rows = pl.ds(pl.multiple_of(tile * TILE, TILE), TILE)
-        slot = lax.rem(tile, 2)
+        rows = tile_columns(tile)
         return (
-            pltpu.make_async_copy(stage.at[slot], grads_hbm.at[:, rows], stage_sem.at[slot]),
-            pltpu.make_async_copy(out_stage.at[slot], out_grads_hbm.at[rows], out_sem.at[slot]),
+            pltpu.make_async_copy(stage, grads_hbm.at[:, rows], stage_sem.at[0]),
+            pltpu.make_async_copy(out_stage, out_grads_hbm.at[rows], stage_sem.at[1]),
         )
 
-    def weight_tile(time):
-        tile = jnp.clip(time, 0, tiles - 1)
-        slot = lax.rem(tile, 2)
-        columns = pl.ds(pl.multiple_of(tile * TILE, TILE), TILE)
-
-        @pl.when(jnp.logical_and(time < tiles, time >= 2))
+    def mixer_copy(tile):
+        rows = tile_columns(tile)
+        return pltpu.make_async_copy(mixer_stage, mixer_grads_hbm.at[rows], stage_sem.at[2])
+
+    grad_save = pltpu.make_async_copy(right, grad_pre_hbm, save_sem.at[0])
+
+    def feed_tile(tile):
+        columns = tile_columns(tile)
+
+        @pl.when(tile > 0)
         def _():
-            for copy in stage_copies(tile - 2):
+            for copy in stage_copies(tile - 1):
                 copy.wait()
 
+        rows = left[:, columns]
+        stage[0] = mm_tn(rows, grad_gate_ref[...]).astype(BF16)
+        stage[1] = mm_tn(rows, grad_up_ref[...]).astype(BF16)
+        stage[2] = mm_tn(right[:, columns], hidden_ref[...]).astype(BF16)
+        out_stage[...] = mm_tn(mix_grad_ref[:, columns], gated_ref[...]).astype(BF16)
+        for copy in stage_copies(tile):
+            copy.start()
+
+    def gate_piece(index):
+        rows = pl.ds(pl.multiple_of(index * piece_rows, piece_rows), piece_rows)
+        grads = mm_nn(mix_grad_ref[rows], out_full[...])
+        gain = gain_ref[...]
+        total = jnp.zeros_like(gain)
+        for head in range(head_count):
+            part_of = slice(head * lanes, (head + 1) * lanes)
+            mixed, gate, grad = mixed_ref[rows, part_of], gates[rows, part_of], grads[:, part_of]
+            inverse = inverse_rms(mixed)
+            unit = mixed * inverse
+            sigma = jax.nn.sigmoid(gate)
+            scaled = grad * unit
+            total = total + jnp.sum(scaled * (gate * sigma), axis=0, keepdims=True)
+            grad_gate = scaled * gain * sigma * (1.0 + gate * (1.0 - sigma))
+            first = 3 * width + head * lanes
+            right[rows, first : first + lanes] = grad_gate.astype(BF16)
+            lifted = grad * gain * (gate * sigma)
+            mean = jnp.mean(lifted * unit, axis=-1, keepdims=True)
+            grad_in = inverse * (lifted - unit * mean) * (key_scale * keep_ref[rows])
+            grad_in = grad_in.astype(BF16)
+            grad_mixed[rows, part_of] = grad_in
+            back_scr[head] += mm_tn(grad_in, lead_ref[rows, part_of])
+        gain_grad[...] += total
+
+    def state_copy(shift):
+        return pltpu.make_async_remote_copy(
+            message,
+            received.at[shift - 1],
+            grad_send.at[shift - 1],
+            grad_recv.at[shift - 1],
+            device_id=earlier(shift),
+            device_id_type=MESH_ID,
+        )
+
+    def block_of(index):
+        return blocks - 1 - index
+
+    def pre_load(index):
+        rows = pl.ds(pl.multiple_of(block_of(index) * BLOCK, BLOCK), BLOCK)
+        slot = lax.rem(index, 2)
+        return pltpu.make_async_copy(
+            pre_hbm.at[rows, pl.ds(0, 3 * width)], pre.at[slot], pre_sem.at[slot]
+        )
+
+    def send_back():
+        for head in range(head_count):
+            rows = slice(head * lanes, (head + 1) * lanes)
+            message[rows] = back_scr[head] * link_ref[0:1]
+            message[state_rows + head : state_rows + head + 1] = decay_ref[head] * link_ref[0:1]
+        for shift in range(1, context_size):
+
+            @pl.when(context >= shift)
+            def _(shift=shift):
+                state_copy(shift).start()
+
+        pre_load(0).start()
+
+    def take_back():
+        grad_scr[...] = jnp.zeros_like(grad_scr)
+        for shift in range(1, context_size):
+
+            @pl.when(context + shift < context_size)
+            def _(shift=shift):
+                state_copy(shift).wait_recv()
+                for head in range(head_count):
+                    value = received[shift - 1, head * lanes : (head + 1) * lanes]
+                    for near in range(shift - 1):
+                        value = value * received[near, state_rows + head : state_rows + head + 1]
+                    grad_scr[head] += value
+
+        for shift in range(1, context_size):
+
+            @pl.when(context >= shift)
+            def _(shift=shift):
+                state_copy(shift).wait_send()
+
+    def mixer_block(index):
+        block = block_of(index)
+        slot = lax.rem(index, 2)
+        block_rows = pl.ds(pl.multiple_of(block * BLOCK, BLOCK), BLOCK)
+
+        @pl.when(index + 1 < blocks)
+        def _():
+            pre_load(index + 1).start()
+
+        pre_load(index).wait()
+        counts, keep, flags = count_ref[block_rows], keep_ref[block_rows], flags_ref[block]
+        row_ids, col_ids, linked, fresh, tail, closing = block_masks(counts, flags)
+        tri = (row_ids >= col_ids).astype(BF16)
+        tri_back = (row_ids <= col_ids).astype(BF16)
+        query_pre = pre[slot, :, :width]
+        values = pre[slot, :, 2 * width : 3 * width].astype(BF16)
+        opened = open_ref[...]
+        closed = jax.nn.sigmoid(-pre[slot, :, width : 2 * width])
+        keys = opened * closed
+        cum = split_sum(tri, jnp.log1p(-keys))
+        ending = cum[BLOCK - 1 : BLOCK, :]
+        rise, fall = jnp.exp(cum), jnp.exp(-cum) * keep
+        shift = jnp.exp(ending - cum) * (keep * tail)
+        sigma_query = jax.nn.sigmoid(query_pre)
+        lifted = (query_pre * sigma_query * rise).astype(BF16)
+        lowered = (keys * fall).astype(BF16)
+        moved = (keys * shift).astype(BF16)
+        fresh_lifted = (lifted.astype(F32) * fresh).astype(BF16)
+        end_decay = jnp.exp(ending) * closing
+        lead_in = jnp.exp(run_ref[block]) * (flags[1:2, 0:1] == 0).astype(F32)
+        for head in range(head_count):
+            part_of = slice(head * lanes, (head + 1) * lanes)
+            grad_out, value = grad_mixed[block_rows, part_of], values[:, part_of]
+            lift, lower, move = lifted[:, part_of], lowered[:, part_of], moved[:, part_of]
+            scores = jnp.where(linked, mm_nt(lift, lower), 0.0).astype(BF16)
+            pulls = jnp.where(linked, mm_nt(grad_out, value), 0.0).astype(BF16)
+            state = starts_ref[block, head] + lead_in[:, part_of] * carry_ref[head]
+            grad_state = grad_scr[head]
+            grad_low = grad_state.astype(BF16)
+            lifted_scr[:, part_of] = mm_nn(pulls, lower) + fresh * mm_nn(
+                grad_out, state.astype(BF16)
+            )
+            lowered_scr[:, part_of] = mm_tn(pulls, lift)
+            grad_moved = mm_nn(value, grad_low)
+            moved_scr[:, part_of] = grad_moved
+            first = 2 * width + head * lanes
+            right[block_rows, first : first + lanes] = (
+                mm_tn(scores, grad_out) + mm_nt(move, grad_low)
+            ).astype(BF16)
+            value_scr[:, part_of] = jnp.sum(
+                grad_moved * move.astype(F32), axis=0, keepdims=True
+            ) + end_decay[:, part_of] * jnp.sum(state * grad_state, axis=0, keepdims=True)
+            grad_scr[head] = grad_state * end_decay[:, part_of] + mm_tn(
+                grad_out, fresh_lifted[:, part_of]
+            )
+        grad_lifted, grad_lowered, grad_moved = lifted_scr[...], lowered_scr[...], moved_scr[...]
+        grad_cum = (
+            grad_lifted * lifted.astype(F32)
+            - grad_lowered * lowered.astype(F32)
+            - grad_moved * moved.astype(F32)
+        )
+        grad_decay = split_sum(tri_back, grad_cum) + value_scr[...]
+        key_total = grad_lowered * fall + grad_moved * shift - grad_decay / (1.0 - keys)
+        floor_grad[...] -= jnp.sum(key_total * closed, axis=0, keepdims=True)
+        right[block_rows, :width] = (
+            grad_lifted * rise * sigma_query * (1.0 + query_pre * (1.0 - sigma_query))
+        ).astype(BF16)
+        right[block_rows, width : 2 * width] = (
+            -key_total * opened * closed * (1.0 - closed)
+        ).astype(BF16)
+
+    def mixer_tile(tile):
+        @pl.when(tile > 0)
+        def _():
+            mixer_copy(tile - 1).wait()
+
+        rows = left[:, tile_columns(tile)]
+        for first in range(0, 4 * width, 1024):
+            columns = slice(first, min(first + 1024, 4 * width))
+            mixer_stage[:, columns] = mm_tn(rows, right[:, columns]).astype(BF16)
+        mixer_copy(tile).start()
+
+    gate_time = tiles
+    send_time = gate_time + tokens // piece_rows
+    block_time = send_time + 1
+    tile_time = block_time + blocks
+    end_time = tile_time + tiles
+
+    def beside(time):
         @pl.when(time < tiles)
         def _():
-            rows = normed_ref[:, columns]
-            stage[slot, 0] = mm_tn(rows, grad_gate_ref[...]).astype(BF16)
-            stage[slot, 1] = mm_tn(rows, grad_up_ref[...]).astype(BF16)
-            stage[slot, 2] = mm_tn(cotangent_ref[:, columns], hidden_ref[...]).astype(BF16)
-            out_stage[slot] = mm_tn(mix_grad_ref[:, columns], gated_ref[...]).astype(BF16)
-            for copy in stage_copies(tile):
-                copy.start()
-
-    line.run(0, line.steps, weight_tile)
-    for tile in range(max(tiles - 2, 0), tiles):
-        for copy in stage_copies(tile):
-            copy.wait()
+            feed_tile(time)
+
+        @pl.when(time == gate_time)
+        def _():
+            next_load.start()
+
+        @pl.when(jnp.logical_and(time >= gate_time, time < send_time))
+        def _():
+            gate_piece(time - gate_time)
+
+        @pl.when(time == send_time)
+        def _():
+            send_back()
+
+        @pl.when(time == block_time)
+        def _():
+            take_back()
+
+        @pl.when(jnp.logical_and(time >= block_time, time < tile_time))
+        def _():
+            mixer_block(time - block_time)
+
+        @pl.when(time == tile_time)
+        def _():
+            grad_save.start()
+            next_load.wait()
+
+        @pl.when(jnp.logical_and(time >= tile_time, time < end_time))
+        def _():
+            mixer_tile(time - tile_time)
+
+    steps = max(line.steps, end_time)
+
+    def body(time, _):
+        @pl.when(time < line.steps)
+        def _():
+            line.step(time)
+
+        beside(time)
+        return 0
+
+    lax.fori_loop(0, steps, body, 0)
+    for copy in stage_copies(tiles - 1):
+        copy.wait()
+    mixer_copy(tiles - 1).wait()
+    grad_save.wait()
     line.finish()
 
 
-def output_line(
-    mesh_axes,
-    collective,
-    part,
-    residual,
-    normed,
-    cotangent,
-    hidden_low,
-    grad_gate,
-    grad_up,
-    gated,
-    mix_grad,
-):
+def output_line(mesh_axes, collective, in_vmem, in_hbm, head_count):
+    part, _, hidden_low, _, _, gated = in_vmem[:6]
     tokens, model_width = part.shape
-    width = gated.shape[1]
-    hidden_width = hidden_low.shape[1]
+    hidden_width, width = hidden_low.shape[1], gated.shape[1]
+    lanes = width // head_count
+    context_size = lax.axis_size("context")
+    messages = head_count * lanes + -(-head_count // 8) * 8
     whole = pl.BlockSpec(memory_space=pltpu.VMEM)
+    remote = pl.BlockSpec(memory_space=pl.ANY)
     return pl.pallas_call(
-        partial(output_kernel, mesh_axes),
-        in_specs=[whole] * 9,
-        out_specs=[whole] + [pl.BlockSpec(memory_space=pl.ANY)] * 2,
+        partial(output_kernel, mesh_axes, head_count, lanes ** (-0.5)),
+        in_specs=[whole] * len(in_vmem) + [remote] * len(in_hbm),
+        out_specs=[whole] * 3 + [remote] * 4,
         out_shape=[
             jax.ShapeDtypeStruct((tokens, model_width), BF16),
+            jax.ShapeDtypeStruct((1, lanes), F32),
+            jax.ShapeDtypeStruct((1, width), F32),
             jax.ShapeDtypeStruct((3, model_width, hidden_width), BF16),
             jax.ShapeDtypeStruct((model_width, width), BF16),
+            jax.ShapeDtypeStruct((model_width, 4 * width), BF16),
+            jax.ShapeDtypeStruct((tokens, 4 * width), BF16),
         ],
         scratch_shapes=[
             pltpu.VMEM((tokens, model_width), BF16),
-            pltpu.VMEM((2, 3, TILE, hidden_width), BF16),
-            pltpu.VMEM((2, TILE, width), BF16),
+            pltpu.VMEM((tokens, model_width), BF16),
+            pltpu.VMEM((tokens, model_width), BF16),
+            pltpu.VMEM((3, TILE, hidden_width), BF16),
+            pltpu.VMEM((TILE, width), BF16),
+            pltpu.VMEM((TILE, 4 * width), BF16),
+            pltpu.VMEM((tokens, width), F32),
+            pltpu.VMEM((2, BLOCK, 3 * width), F32),
+            pltpu.VMEM((tokens, width), BF16),
+            pltpu.VMEM((head_count, lanes, lanes), F32),
+            pltpu.VMEM((messages, lanes), F32),
+            pltpu.VMEM((context_size - 1, messages, lanes), F32),
+            pltpu.VMEM((head_count, lanes, lanes), F32),
+            pltpu.VMEM((BLOCK, width), F32),
+            pltpu.VMEM((BLOCK, width), F32),
+            pltpu.VMEM((BLOCK, width), F32),
+            pltpu.VMEM((1, width), F32),
+            pltpu.SemaphoreType.DMA((4,)),
             pltpu.SemaphoreType.DMA((2,)),
-            pltpu.SemaphoreType.DMA((2,)),
+            pltpu.SemaphoreType.DMA((3,)),
+            pltpu.SemaphoreType.DMA((1,)),
+            pltpu.SemaphoreType.DMA((context_size - 1,)),
+            pltpu.SemaphoreType.DMA((context_size - 1,)),
         ]
         + line_sems(tokens),
         compiler_params=pltpu.CompilerParams(
-            collective_id=collective, has_side_effects=True, vmem_limit_bytes=56 << 20
+            collective_id=collective, has_side_effects=True, vmem_limit_bytes=61 << 20
         ),
         cost_estimate=pl.CostEstimate(
             flops=tokens * model_width * hidden_width * 6,
@@ -1016,9 +1069,7 @@
             transcendentals=0,
         ),
         name="output_line",
-    )(
-        part, residual, normed, cotangent, hidden_low, grad_gate, grad_up, gated, mix_grad
-    )
+    )(*in_vmem, *in_hbm)
 
 
 def input_kernel(
@@ -1800,40 +1851,41 @@
         w_ffn_up,
         down_turned,
     )
-    grad_gated = jnp.dot(grad_mix_low, out_full, preferred_element_type=F32)
-    grad_mixed, grad_gate_pre, grad_head_part, back = gate_backward(
-        grad_gated, mixed, lead, pre, gain_row, keep, head_count, key_scale
-    )
-    after = grad_after(back, decay, link[0, 0], "context")
-    grad_pre, grad_floor_part = mixer_backward(
-        pre,
-        grad_mixed,
-        grad_gate_pre,
-        starts,
-        runs,
-        carry,
-        after,
-        open_part,
-        counts,
-        keep,
-        flags,
-    )
-    grad_mixer = jnp.einsum(
-        "td,tk->dk", normed_one, grad_pre, preferred_element_type=F32
-    ).astype(BF16)
-    feed_part, grad_mixer = lax.optimization_barrier((feed_part, grad_mixer))
-    output_rows, grads_ffn, grad_out = output_line(
+    (
+        output_rows,
+        grad_head_part,
+        grad_floor_part,
+        grads_ffn,
+        grad_out,
+        grad_mixer,
+        grad_pre,
+    ) = output_line(
         mesh_axes,
         1,
-        feed_part,
-        residual,
-        normed_two,
-        grad_rows,
-        hidden_low,
-        grad_gate_low,
-        grad_up_low,
-        gated_low,
-        grad_mix_low,
+        (
+            feed_part,
+            residual,
+            hidden_low,
+            grad_gate_low,
+            grad_up_low,
+            gated_low,
+            grad_mix_low,
+            out_full,
+            mixed,
+            lead,
+            starts,
+            runs,
+            carry,
+            decay,
+            link,
+            open_part,
+            counts,
+            keep,
+            flags,
+            gain_row,
+        ),
+        (normed_two, grad_rows, normed_one, pre),
+        head_count,
     )
     back_one = jnp.einsum("tk,dk->td", grad_pre, mixer_full, preferred_element_type=F32)
     input_rows, grad_norm_one, share_gate, share_up, share_down = input_line(

time: 659 us -> 628 us (0.953)
  matrix products: 30.1 us -> 13.9 us
    dot_general x2 -> x0, matrix products: 16.1 us -> none  [the longest x1 11.4 us: local(): jnp.einsum('td,tk->dk', normed_one, grad_pre, preferred_element_type=F32)]
    pallas_call x3 -> x1, Pallas kernels: 143 us -> 136 us  [output_line(): pl.pallas_call(partial(output_kernel, mesh_axes, head_count, lanes ** (-0...]
    unnamed x44 -> x20, local copies, waits for them, and re-layouts: 14.4 us -> 12.3 us
  transfers between devices with their start and end apart: 3 -> 2, of which waited for: 2 -> 1; matrix products, arithmetic and copies ran while one was open for 4% -> 4% of each run, Pallas kernels for 21% -> 23%
where the time goes in v10:
time: 628 us; the launch traced here: 627 us
  Pallas kernels  574 us (91%)
  local copies, waits for them, and re-layouts  19.8 us (3%)
  between operations  14.2 us (2%)
  matrix products  13.9 us (2%)
    pallas_call x1, Pallas kernels, middle(): pl.pallas_call(partial(middle_kernel, mesh_axes), in_specs=[remote, whole...  222 us
    pallas_call x1, Pallas kernels, output_line(): pl.pallas_call(partial(output_kernel, mesh_axes, head_count, lanes ** (-0...  136 us
    pallas_call x1, Pallas kernels, input_line(): pl.pallas_call(partial(input_kernel, mesh_axes), in_specs=[whole] * 4 + [...  130 us
    pallas_call x1, Pallas kernels, forward(): pl.pallas_call(partial(forward_kernel, mesh_axes, head_count, lanes ** (-...  74.8 us
    dot_general x1, matrix products, local(): jnp.einsum('tk,dk->td', grad_pre, mixer_full, preferred_element_type=F32)  13.9 us
  transfers between devices with their start and end apart: 2, of which 1 were waited for; matrix products, arithmetic and copies ran while one was open for 4% of the time, Pallas kernels for 23%

profile of v10, /device:TPU:0, one launch (start us, length us, event | category | flops | bytes accessed | tf_op | source)
XLA Modules:
  0.0 627.3 jit_solution(15990023220733286924)
XLA Ops:
  7.2 0.0 reduce-scatter.5.cloned.1.call-start
  7.2 1.3 convert_element_type.14
  8.5 74.8 %forward.1 = (bf16[1024,2048]{1,0:T(8,128)(2,1)}, f32[1024,2048]{1,0:T(8,128)}, bf16[2048,2048]{1,0:T(8,128)(2,1)}, bf16[2048,512]{1,0:T(8,128)(2,1)}, f32[1024,...) custom-call(bf16[1024,2048]{1,0:T(8,128)(2,1)} %bitcast.24, ...), custom_call_target="tpu_custom_call" | custom-call | flops 8589934592 | bytes 200000000 | tf_op jit(solution)/shard_map/forward/pallas_call | solution.py:1633
  83.3 222.3 %middle.1 = (bf16[1024,2048]{1,0:T(8,128)(2,1)}, bf16[1024,2048]{1,0:T(8,128)(2,1)}, f32[1,2048]{1,0:T(1,128)}, f32[512,2048]{1,0:T(8,128)}, bf16[1024,1408]{1,0...) custom-call(bf16[1024,2048]{1,0:T(8,128)(2,1)} %get-tuple-element.55, ...), custom_call_target="tpu_custom_call" | custom-call | flops 35433480192 | bytes 360000000 | tf_op jit(solution)/shard_map/middle/pallas_call | solution.py:621
  305.6 135.9 %output_line.1 = (bf16[1024,2048]{1,0:T(8,128)(2,1)}, f32[1,128]{1,0:T(1,128)}, f32[1,512]{1,0:T(1,128)}, bf16[3,2048,1408]{2,1,0:T(8,128)(2,1)}, bf16[2048,512]...) custom-call(bf16[1024,2048]{1,0:T(8,128)(2,1)} %get-tuple-element.57.part, ...), custom_call_target="tpu_custom_call" | custom-call | flops 17716740096 | bytes 360000000 | tf_op jit(solution)/shard_map/output_line/pallas_call | solution.py:1024
  441.5 0.0 reduce-scatter.5.cloned.1.call-update
  441.5 0.0 reduce-scatter.3.cloned.1.call-start
  441.6 0.7 reduce-scatter.3.cloned.1.call-update
  442.3 13.9 %convolution_convert_fusion.part = bf16[1024,2048]{1,0:T(8,128)(2,1)} fusion(bf16[1024,2048]{1,0:T(8,128)(2,1)} %get-tuple-element.80, bf16[2048,2048]{1,0:T(8,128)(2,1)} %get-tuple-element.81), kind=kOutput, calls=%fused_computation | convolution fusion | flops 8592031744 | bytes 16777216 | tf_op jit(solution)/shard_map/tk,dk->td/dot_general | solution.py:1890
  456.2 0.0 copy-start.4
  456.2 0.0 copy-start.5
  456.2 0.0 copy-start.6
  456.2 129.6 %input_line.1 = (bf16[1024,2048]{1,0:T(8,128)(2,1)}, f32[1,2048]{1,0:T(1,128)}, f32[256,1408]{1,0:T(8,128)}, f32[256,1408]{1,0:T(8,128)}, f32[256,1408]{1,0:T(8,128)}) custom-call(bf16[1024,2048]{1,0:T(8,128)(2,1)} %convolution_convert_fusion.part, bf16[1024,2048]{1,0:T(8,128)(2,1)} %bitcast.26, f32[512,2048]{1,0:T(8,128)} %get-tuple-element.82.residual_grad, ...), custom_call_target="tpu_custom_call" | custom-call | flops 16777216 | bytes 360000000 | tf_op jit(solution)/shard_map/input_line/pallas_call | solution.py:1220
  585.8 0.0 copy-done.4
  585.8 0.0 copy-done.5
  585.8 0.0 copy-done.6
  585.8 0.7 select_maximum_fusion
  586.5 0.6 reshape.91.value
  587.2 11.8 %small_sum.1 = (f32[8,640]{1,0:T(8,128)}, f32[8,640]{1,0:T(8,128)}) custom-call(f32[8,640]{1,0:T(8,128)} %reshape.91.value), custom_call_target="tpu_custom_call" | custom-call | flops 40960 | bytes 20000000 | tf_op jit(solution)/shard_map/small_sum/pallas_call | solution.py:1751
  598.9 0.8 slice.42
  599.8 0.7 slice.34
  600.5 0.8 slice.40
  601.4 2.9 copy.33
  604.3 0.5 fusion
  604.8 0.6 constant_dynamic-slice_fusion.2
  605.4 0.6 constant_dynamic-slice_fusion
  605.9 0.0 reduce-scatter.5.cloned.1.call-done
  605.9 1.0 convert_bitcast_fusion
  607.0 1.0 copy.32
  608.0 1.3 reduce-scatter.3.cloned.1.call-done
  609.2 0.0 copy-start
  609.2 2.8 fusion.1
  612.0 0.2 copy-done
  612.1 0.0 copy-start.1
  612.1 2.1 copy.38
  614.3 1.6 copy-done.1
  615.8 0.0 copy-start.3
  615.9 0.0 copy-start.2
  615.9 2.1 copy.39
  618.0 0.2 copy-done.3
  618.2 1.1 copy.40
  619.3 0.0 copy-done.2
  619.3 1.1 copy.41
  (3 shorter events, 0.0 us)
Async XLA Ops:
  7.2 598.8 %reduce-scatter.5.cloned.1.call-start = ((), (), s32[]{:S(2)}) async-start(), calls=%async_computation.3 | async-start | bytes 2359296 | tf_op jit(solution)/shard_map/reduce_scatter | solution.py:1908
  441.5 167.7 %reduce-scatter.3.cloned.1.call-start = ((), (), s32[]{:S(2)}) async-start(), calls=%async_computation.2 | async-start | bytes 9437184 | tf_op jit(solution)/shard_map/reduce_scatter | solution.py:1908
  456.2 129.6 %copy-start.4 = (f32[1,2048]{1,0:T(1,128)S(1)}, f32[1,2048]{1,0:T(1,128)}, u32[]{:S(2)}) copy-start(f32[1,2048]{1,0:T(1,128)} %get-tuple-element.86) | copy-start | bytes 24580
  456.2 129.6 %copy-start.5 = (f32[1,512]{1,0:T(1,128)S(1)}, f32[1,512]{1,0:T(1,128)}, u32[]{:S(2)}) copy-start(f32[1,512]{1,0:T(1,128)} %get-tuple-element.88) | copy-start | bytes 6148
  456.2 129.6 %copy-start.6 = (f32[1,128]{1,0:T(1,128)S(1)}, f32[1,128]{1,0:T(1,128)}, u32[]{:S(2)}) copy-start(f32[1,128]{1,0:T(1,128)} %get-tuple-element.87) | copy-start | bytes 1540
  609.2 2.9 copy-start
  612.1 3.7 copy-start.1
  615.8 2.4 copy-start.3
  615.9 3.5 copy-start.2
Sparse Core Ops, SparseCore 0:
  441.7 81.4 reduce-scatter.4
  527.0 82.1 reduce-scatter.2

commit v11 on v10

--- a/solution.py
+++ b/solution.py
@@ -411,6 +411,7 @@
     grad_up_hbm,
     feed_hbm,
     grad_hbm,
+    grads_hbm,
     gate_w,
     up_w,
     down_w,
@@ -428,6 +429,8 @@
     save_sem,
     stage_sem,
     grad_sem,
+    back_sem,
+    tile_sem,
     *sems,
 ):
     tokens, model_width = normed_ref.shape
@@ -599,13 +602,72 @@
         return 0
 
     lax.fori_loop(0, groups, group_body, 0)
-    line.run((groups - 1) * pace, line.steps)
-    grad_save = pltpu.make_async_copy(residual, grad_hbm, grad_sem.at[0])
-    grad_save.start()
     for group in range(max(groups - 2, 0), groups):
         for copy in stage_copies(group):
             copy.wait()
     gather.finish()
+
+    token_rows, hidden_columns = pl.ds(0, tokens), pl.ds(0, hidden_width)
+    returned = [
+        pltpu.make_async_copy(
+            source, target.at[token_rows, hidden_columns], back_sem.at[which]
+        )
+        for which, (source, target) in enumerate(
+            ((grad_gate_hbm, gate_w), (grad_up_hbm, up_w), (hidden_hbm, down_w))
+        )
+    ]
+    for copy in returned:
+        copy.start()
+    tiles = model_width // TILE
+    first_time = (groups - 1) * pace + 1
+    stages = (stage_gate, stage_up, stage_hidden)
+
+    def tile_copies(tile):
+        rows = pl.ds(pl.multiple_of(tile * TILE, TILE), TILE)
+        slot = lax.rem(tile, 2)
+        return [
+            pltpu.make_async_copy(
+                stage.at[slot, pl.ds(0, TILE), hidden_columns],
+                grads_hbm.at[which, rows],
+                tile_sem.at[slot, which],
+            )
+            for which, stage in enumerate(stages)
+        ]
+
+    def weight_tile(time):
+        tile = time - first_time
+
+        @pl.when(tile == 0)
+        def _():
+            for copy in returned:
+                copy.wait()
+
+        @pl.when(jnp.logical_and(tile >= 2, tile < tiles))
+        def _():
+            for copy in tile_copies(tile - 2):
+                copy.wait()
+
+        @pl.when(jnp.logical_and(tile >= 0, tile < tiles))
+        def _():
+            slot = lax.rem(tile, 2)
+            columns = pl.ds(pl.multiple_of(tile * TILE, TILE), TILE)
+            rows = normed_ref[:, columns]
+            for source, right, stage in (
+                (rows, gate_w, stage_gate),
+                (rows, up_w, stage_up),
+                (cotangent_ref[:, columns], down_w, stage_hidden),
+            ):
+                product = mm_tn(source, right[:tokens, :hidden_width])
+                stage[slot, :TILE, :hidden_width] = product.astype(BF16)
+            for copy in tile_copies(tile):
+                copy.start()
+
+    line.run((groups - 1) * pace, line.steps, weight_tile)
+    grad_save = pltpu.make_async_copy(residual, grad_hbm, grad_sem.at[0])
+    grad_save.start()
+    for tile in range(max(tiles - 2, 0), tiles):
+        for copy in tile_copies(tile):
+            copy.wait()
     mix_line.finish(source_waits=False)
     line.finish()
     grad_save.wait()
@@ -621,7 +683,7 @@
     return pl.pallas_call(
         partial(middle_kernel, mesh_axes),
         in_specs=[remote, whole, remote, whole, remote, remote, remote],
-        out_specs=[whole, whole, whole] + [remote] * 6,
+        out_specs=[whole, whole, whole] + [remote] * 7,
         out_shape=[
             jax.ShapeDtypeStruct((tokens, model_width), BF16),
             jax.ShapeDtypeStruct((tokens, model_width), BF16),
@@ -632,6 +694,7 @@
             jax.ShapeDtypeStruct((tokens, hidden_width), BF16),
             jax.ShapeDtypeStruct((tokens, model_width), BF16),
             jax.ShapeDtypeStruct((tokens // 2, model_width), F32),
+            jax.ShapeDtypeStruct((3, model_width, hidden_width), BF16),
         ],
         scratch_shapes=[
             pltpu.VMEM((model_width, padded), BF16),
@@ -651,6 +714,8 @@
             pltpu.SemaphoreType.DMA((1,)),
             pltpu.SemaphoreType.DMA((2, 4, 2)),
             pltpu.SemaphoreType.DMA((1,)),
+            pltpu.SemaphoreType.DMA((3,)),
+            pltpu.SemaphoreType.DMA((2, 3)),
         ]
         + line_sems(tokens)
         + line_sems(tokens)
@@ -673,9 +738,6 @@
     key_scale,
     part,
     residual,
-    hidden_ref,
-    grad_gate_ref,
-    grad_up_ref,
     gated_ref,
     mix_grad_ref,
     out_full,
@@ -691,21 +753,19 @@
     keep_ref,
     flags_ref,
     gain_ref,
-    normed_two_hbm,
-    cotangent_hbm,
-    normed_one_hbm,
+    normed_hbm,
     pre_hbm,
+    full_hbm,
     out_ref,
     gain_grad,
     floor_grad,
-    grads_hbm,
+    back_ref,
     out_grads_hbm,
     mixer_grads_hbm,
-    grad_pre_hbm,
     arrived,
     left,
     right,
-    stage,
+    full,
     out_stage,
     mixer_stage,
     gates,
@@ -722,7 +782,6 @@
     load_sem,
     pre_sem,
     stage_sem,
-    save_sem,
     grad_send,
     grad_recv,
     *sems,
@@ -735,13 +794,12 @@
     piece_rows = 2 * BLOCK
     context, context_size = lax.axis_index("context"), lax.axis_size("context")
 
-    left_load = pltpu.make_async_copy(normed_two_hbm, left, load_sem.at[0])
-    right_load = pltpu.make_async_copy(cotangent_hbm, right, load_sem.at[1])
+    left_load = pltpu.make_async_copy(normed_hbm, left, load_sem.at[0])
+    full_load = pltpu.make_async_copy(full_hbm, full, load_sem.at[1])
     gate_load = pltpu.make_async_copy(
         pre_hbm.at[:, pl.ds(3 * width, width)], gates, load_sem.at[2]
     )
-    next_load = pltpu.make_async_copy(normed_one_hbm, left, load_sem.at[3])
-    for load in (left_load, right_load, gate_load):
+    for load in (gate_load, left_load, full_load):
         load.start()
     gain_grad[...] = jnp.zeros_like(gain_grad)
     floor_grad[...] = jnp.zeros_like(floor_grad)
@@ -761,8 +819,7 @@
     for shift in range(1, context_size):
         pl.semaphore_signal(barrier, inc=1, device_id=earlier(shift), device_id_type=MESH_ID)
     pl.semaphore_wait(barrier, expected + context_size - 1)
-    for load in (left_load, right_load, gate_load):
-        load.wait()
+    gate_load.wait()
 
     def tile_columns(tile):
         return pl.ds(pl.multiple_of(tile * TILE, TILE), TILE)
@@ -770,31 +827,9 @@
     def stage_copies(tile):
         rows = tile_columns(tile)
         return (
-            pltpu.make_async_copy(stage, grads_hbm.at[:, rows], stage_sem.at[0]),
-            pltpu.make_async_copy(out_stage, out_grads_hbm.at[rows], stage_sem.at[1]),
+            pltpu.make_async_copy(out_stage, out_grads_hbm.at[rows], stage_sem.at[0]),
+            pltpu.make_async_copy(mixer_stage, mixer_grads_hbm.at[rows], stage_sem.at[1]),
         )
-
-    def mixer_copy(tile):
-        rows = tile_columns(tile)
-        return pltpu.make_async_copy(mixer_stage, mixer_grads_hbm.at[rows], stage_sem.at[2])
-
-    grad_save = pltpu.make_async_copy(right, grad_pre_hbm, save_sem.at[0])
-
-    def feed_tile(tile):
-        columns = tile_columns(tile)
-
-        @pl.when(tile > 0)
-        def _():
-            for copy in stage_copies(tile - 1):
-                copy.wait()
-
-        rows = left[:, columns]
-        stage[0] = mm_tn(rows, grad_gate_ref[...]).astype(BF16)
-        stage[1] = mm_tn(rows, grad_up_ref[...]).astype(BF16)
-        stage[2] = mm_tn(right[:, columns], hidden_ref[...]).astype(BF16)
-        out_stage[...] = mm_tn(mix_grad_ref[:, columns], gated_ref[...]).astype(BF16)
-        for copy in stage_copies(tile):
-            copy.start()
 
     def gate_piece(index):
         rows = pl.ds(pl.multiple_of(index * piece_rows, piece_rows), piece_rows)
@@ -943,35 +978,35 @@
             -key_total * opened * closed * (1.0 - closed)
         ).astype(BF16)
 
+    def back_tile(tile):
+        columns = tile_columns(tile)
+        back_ref[:, columns] = mm_nt(right[...], full[columns, :]).astype(BF16)
+
     def mixer_tile(tile):
         @pl.when(tile > 0)
         def _():
-            mixer_copy(tile - 1).wait()
-
-        rows = left[:, tile_columns(tile)]
+            for copy in stage_copies(tile - 1):
+                copy.wait()
+
+        columns = tile_columns(tile)
+        rows = left[:, columns]
         for first in range(0, 4 * width, 1024):
-            columns = slice(first, min(first + 1024, 4 * width))
-            mixer_stage[:, columns] = mm_tn(rows, right[:, columns]).astype(BF16)
-        mixer_copy(tile).start()
-
-    gate_time = tiles
-    send_time = gate_time + tokens // piece_rows
+            some = slice(first, min(first + 1024, 4 * width))
+            mixer_stage[:, some] = mm_tn(rows, right[:, some]).astype(BF16)
+        out_stage[...] = mm_tn(mix_grad_ref[:, columns], gated_ref[...]).astype(BF16)
+        for copy in stage_copies(tile):
+            copy.start()
+
+    send_time = tokens // piece_rows
     block_time = send_time + 1
-    tile_time = block_time + blocks
+    back_time = block_time + blocks
+    tile_time = back_time + tiles
     end_time = tile_time + tiles
 
     def beside(time):
-        @pl.when(time < tiles)
+        @pl.when(time < send_time)
         def _():
-            feed_tile(time)
-
-        @pl.when(time == gate_time)
-        def _():
-            next_load.start()
-
-        @pl.when(jnp.logical_and(time >= gate_time, time < send_time))
-        def _():
-            gate_piece(time - gate_time)
+            gate_piece(time)
 
         @pl.when(time == send_time)
         def _():
@@ -981,14 +1016,21 @@
         def _():
             take_back()
 
-        @pl.when(jnp.logical_and(time >= block_time, time < tile_time))
+        @pl.when(jnp.logical_and(time >= block_time, time < back_time))
         def _():
             mixer_block(time - block_time)
 
+        @pl.when(time == back_time)
+        def _():
+            full_load.wait()
+
+        @pl.when(jnp.logical_and(time >= back_time, time < tile_time))
+        def _():
+            back_tile(time - back_time)
+
         @pl.when(time == tile_time)
         def _():
-            grad_save.start()
-            next_load.wait()
+            left_load.wait()
 
         @pl.when(jnp.logical_and(time >= tile_time, time < end_time))
         def _():
@@ -1007,15 +1049,13 @@
     lax.fori_loop(0, steps, body, 0)
     for copy in stage_copies(tiles - 1):
         copy.wait()
-    mixer_copy(tiles - 1).wait()
-    grad_save.wait()
     line.finish()
 
 
 def output_line(mesh_axes, collective, in_vmem, in_hbm, head_count):
-    part, _, hidden_low, _, _, gated = in_vmem[:6]
+    part, _, gated = in_vmem[:3]
     tokens, model_width = part.shape
-    hidden_width, width = hidden_low.shape[1], gated.shape[1]
+    width = gated.shape[1]
     lanes = width // head_count
     context_size = lax.axis_size("context")
     messages = head_count * lanes + -(-head_count // 8) * 8
@@ -1024,21 +1064,20 @@
     return pl.pallas_call(
         partial(output_kernel, mesh_axes, head_count, lanes ** (-0.5)),
         in_specs=[whole] * len(in_vmem) + [remote] * len(in_hbm),
-        out_specs=[whole] * 3 + [remote] * 4,
+        out_specs=[whole] * 4 + [remote] * 2,
         out_shape=[
             jax.ShapeDtypeStruct((tokens, model_width), BF16),
             jax.ShapeDtypeStruct((1, lanes), F32),
             jax.ShapeDtypeStruct((1, width), F32),
-            jax.ShapeDtypeStruct((3, model_width, hidden_width), BF16),
+            jax.ShapeDtypeStruct((tokens, model_width), BF16),
             jax.ShapeDtypeStruct((model_width, width), BF16),
             jax.ShapeDtypeStruct((model_width, 4 * width), BF16),
-            jax.ShapeDtypeStruct((tokens, 4 * width), BF16),
         ],
         scratch_shapes=[
             pltpu.VMEM((tokens, model_width), BF16),
             pltpu.VMEM((tokens, model_width), BF16),
-            pltpu.VMEM((tokens, model_width), BF16),
-            pltpu.VMEM((3, TILE, hidden_width), BF16),
+            pltpu.VMEM((tokens, 4 * width), BF16),
+            pltpu.VMEM((model_width, 4 * width), BF16),
             pltpu.VMEM((TILE, width), BF16),
             pltpu.VMEM((TILE, 4 * width), BF16),
             pltpu.VMEM((tokens, width), F32),
@@ -1052,10 +1091,9 @@
             pltpu.VMEM((BLOCK, width), F32),
             pltpu.VMEM((BLOCK, width), F32),
             pltpu.VMEM((1, width), F32),
-            pltpu.SemaphoreType.DMA((4,)),
+            pltpu.SemaphoreType.DMA((3,)),
             pltpu.SemaphoreType.DMA((2,)),
-            pltpu.SemaphoreType.DMA((3,)),
-            pltpu.SemaphoreType.DMA((1,)),
+            pltpu.SemaphoreType.DMA((2,)),
             pltpu.SemaphoreType.DMA((context_size - 1,)),
             pltpu.SemaphoreType.DMA((context_size - 1,)),
         ]
@@ -1064,9 +1102,9 @@
             collective_id=collective, has_side_effects=True, vmem_limit_bytes=61 << 20
         ),
         cost_estimate=pl.CostEstimate(
-            flops=tokens * model_width * hidden_width * 6,
+            flops=tokens * model_width * width * 24,
             bytes_accessed=360_000_000,
-            transcendentals=0,
+            transcendentals=tokens * width * 12,
         ),
         name="output_line",
     )(*in_vmem, *in_hbm)
@@ -1831,15 +1869,16 @@
     )
     grad_rows = out_grad.reshape(tokens, model_width)
     (
-        normed_two,
+        _,
         grad_mix_low,
         grad_norm_two,
         residual,
-        hidden_low,
-        grad_gate_low,
-        grad_up_low,
+        _,
+        _,
+        _,
         feed_part,
         grad_residual,
+        grads_ffn,
     ) = middle(
         mesh_axes,
         2,
@@ -1855,19 +1894,15 @@
         output_rows,
         grad_head_part,
         grad_floor_part,
-        grads_ffn,
+        back_one,
         grad_out,
         grad_mixer,
-        grad_pre,
     ) = output_line(
         mesh_axes,
         1,
         (
             feed_part,
             residual,
-            hidden_low,
-            grad_gate_low,
-            grad_up_low,
             gated_low,
             grad_mix_low,
             out_full,
@@ -1884,12 +1919,11 @@
             flags,
             gain_row,
         ),
-        (normed_two, grad_rows, normed_one, pre),
+        (normed_one, pre, mixer_full),
         head_count,
     )
-    back_one = jnp.einsum("tk,dk->td", grad_pre, mixer_full, preferred_element_type=F32)
     input_rows, grad_norm_one, share_gate, share_up, share_down = input_line(
-        mesh_axes, 3, back_one.astype(BF16), hidden_rows, grad_residual, gain_one, grads_ffn
+        mesh_axes, 3, back_one, hidden_rows, grad_residual, gain_one, grads_ffn
     )
     near, total = small_sum(
         mesh_axes, 5, (grad_norm_one, grad_norm_two, grad_head_part, grad_floor_part)

time: 628 us -> 644 us (1.025)
  waiting for transfers between devices: 1.99 us -> 46.6 us
  Pallas kernels: 574 us -> 560 us
  matrix products: 13.9 us -> 0 us
    reduce_scatter x2, waiting for transfers between devices: 1.27 us -> 45.9 us  [share(): lax.psum_scatter(values.astype(BF16), both, scatter_dimension=dim, tiled=...]
    dot_general x1 -> x0, matrix products: 13.9 us -> none  [local(): jnp.einsum('tk,dk->td', grad_pre, mixer_full, preferred_element_type=F32)]
    pallas_call x1, Pallas kernels: 136 us -> 127 us  [output_line(): pl.pallas_call(partial(output_kernel, mesh_axes, head_count, lanes ** (-0...]
  transfers between devices with their start and end apart: 2 -> 2, of which waited for: 1 -> 1; matrix products, arithmetic and copies ran while one was open for 4% -> 2% of each run, Pallas kernels for 23% -> 21%
where the time goes in v11:
time: 644 us
  Pallas kernels  560 us (87%)
  waiting for transfers between devices  46.6 us (7%)
  local copies, waits for them, and re-layouts  19.8 us (3%)
  between operations  14.2 us (2%)
    pallas_call x1, Pallas kernels, middle(): pl.pallas_call(partial(middle_kernel, mesh_axes), in_specs=[remote, whole...  222 us
    pallas_call x1, Pallas kernels, output_line(): pl.pallas_call(partial(output_kernel, mesh_axes, head_count, lanes ** (-0...  127 us
    pallas_call x1, Pallas kernels, input_line(): pl.pallas_call(partial(input_kernel, mesh_axes), in_specs=[whole] * 4 + [...  124 us
    pallas_call x1, Pallas kernels, forward(): pl.pallas_call(partial(forward_kernel, mesh_axes, head_count, lanes ** (-...  74.7 us
    reduce_scatter x2, waiting for transfers between devices, share(): lax.psum_scatter(values.astype(BF16), both, scatter_dimension=dim, tiled=...  45.9 us
  transfers between devices with their start and end apart: 2, of which 1 were waited for; matrix products, arithmetic and copies ran while one was open for 2% of the time, Pallas kernels for 21%

profile of v11, /device:TPU:0, one launch (start us, length us, event | category | flops | bytes accessed | tf_op | source)
XLA Modules:
  0.0 643.6 jit_solution(12063009983843099672)
XLA Ops:
  7.2 0.0 reduce-scatter.5.cloned.1.call-start
  7.2 1.3 convert_element_type.11
  8.5 74.7 %forward.1 = (bf16[1024,2048]{1,0:T(8,128)(2,1)}, f32[1024,2048]{1,0:T(8,128)}, bf16[2048,2048]{1,0:T(8,128)(2,1)}, bf16[2048,512]{1,0:T(8,128)(2,1)}, f32[1024,...) custom-call(bf16[1024,2048]{1,0:T(8,128)(2,1)} %bitcast.22, ...), custom_call_target="tpu_custom_call" | custom-call | flops 8589934592 | bytes 200000000 | tf_op jit(solution)/shard_map/forward/pallas_call | solution.py:1671
  83.2 222.5 %middle.1 = (bf16[1024,2048]{1,0:T(8,128)(2,1)}, bf16[1024,2048]{1,0:T(8,128)(2,1)}, f32[1,2048]{1,0:T(1,128)}, f32[512,2048]{1,0:T(8,128)}, bf16[1024,1408]{1,0...) custom-call(bf16[1024,2048]{1,0:T(8,128)(2,1)} %get-tuple-element.51, ...), custom_call_target="tpu_custom_call" | custom-call | flops 35433480192 | bytes 360000000 | tf_op jit(solution)/shard_map/middle/pallas_call | solution.py:683
  305.6 127.1 %output_line.1 = (bf16[1024,2048]{1,0:T(8,128)(2,1)}, f32[1,128]{1,0:T(1,128)}, f32[1,512]{1,0:T(1,128)}, bf16[1024,2048]{1,0:T(8,128)(2,1)}, bf16[2048,512]{1,0:T(8,128)(2,1)}, /*index=5*/bf16[2048,2048]{1,0:T(8,128)(2,1)}) custom-call(bf16[1024,2048]{1,0:T(8,128)(2,1)} %get-tuple-element.53.part, f32[512,2048]{1,0:T(8,128)} %get-tuple-element.54.residual, ...), custom_call_target="tpu_custom_call" | custom-call | flops 25769803776 | bytes 360000000 | tf_op jit(solution)/shard_map/output_line/pallas_call | solution.py:1064
  432.8 0.0 reduce-scatter.5.cloned.1.call-update
  432.8 0.0 reduce-scatter.3.cloned.1.call-start
  432.9 0.7 reduce-scatter.3.cloned.1.call-update
  433.6 0.0 copy-start.4
  433.6 0.0 copy-start.5
  433.6 0.0 copy-start.6
  433.6 124.2 %input_line.1 = (bf16[1024,2048]{1,0:T(8,128)(2,1)}, f32[1,2048]{1,0:T(1,128)}, f32[256,1408]{1,0:T(8,128)}, f32[256,1408]{1,0:T(8,128)}, f32[256,1408]{1,0:T(8,128)}) custom-call(bf16[1024,2048]{1,0:T(8,128)(2,1)} %get-tuple-element.73.part, bf16[1024,2048]{1,0:T(8,128)(2,1)} %bitcast.24, f32[512,2048]{1,0:T(8,128)} %get-tuple-element.74.residual_grad, ...), custom_call_target="tpu_custom_call" | custom-call | flops 16777216 | bytes 360000000 | tf_op jit(solution)/shard_map/input_line/pallas_call | solution.py:1258
  557.8 0.0 copy-done.4
  557.8 0.0 copy-done.5
  557.8 0.0 copy-done.6
  557.9 0.7 select_maximum_fusion
  558.6 0.6 reshape.91.value
  559.2 11.5 %small_sum.1 = (f32[8,640]{1,0:T(8,128)}, f32[8,640]{1,0:T(8,128)}) custom-call(f32[8,640]{1,0:T(8,128)} %reshape.91.value), custom_call_target="tpu_custom_call" | custom-call | flops 40960 | bytes 20000000 | tf_op jit(solution)/shard_map/small_sum/pallas_call | solution.py:1789
  570.7 0.8 slice.42
  571.5 0.7 slice.34
  572.2 0.8 slice.40
  573.1 2.9 copy.33
  576.0 0.5 fusion
  576.5 0.6 constant_dynamic-slice_fusion.2
  577.1 0.6 constant_dynamic-slice_fusion
  577.7 0.0 reduce-scatter.5.cloned.1.call-done
  577.7 1.0 convert_bitcast_fusion
  578.7 1.0 copy.32
  579.7 45.9 %reduce-scatter.3.cloned.1.call-done = bf16[256,2048]{1,0:T(8,128)(2,1)} async-done(((bf16[2048,2048]{1,0:T(8,128)(2,1)}), bf16[256,2048]{1,0:T(8,128)(2,1)}) %reduce-scatter.3.cloned.1.call-update) | async-done | bytes 1048592 | tf_op jit(solution)/shard_map/reduce_scatter | solution.py:1942
  625.5 0.0 copy-start
  625.5 2.8 fusion.1
  628.3 0.2 copy-done
  628.5 0.0 copy-start.1
  628.5 2.1 copy.38
  630.6 1.6 copy-done.1
  632.2 0.0 copy-start.3
  632.2 0.0 copy-start.2
  632.2 2.1 copy.39
  634.3 0.2 copy-done.3
  634.5 1.1 copy.40
  635.6 0.0 copy-done.2
  635.6 1.1 copy.41
  (3 shorter events, 0.0 us)
Async XLA Ops:
  7.2 570.5 %reduce-scatter.5.cloned.1.call-start = ((), (), s32[]{:S(2)}) async-start(), calls=%async_computation.3 | async-start | bytes 2359296 | tf_op jit(solution)/shard_map/reduce_scatter | solution.py:1942
  432.8 192.7 %reduce-scatter.3.cloned.1.call-start = ((), (), s32[]{:S(2)}) async-start(), calls=%async_computation.2 | async-start | bytes 9437184 | tf_op jit(solution)/shard_map/reduce_scatter | solution.py:1942
  433.6 124.2 %copy-start.4 = (f32[1,2048]{1,0:T(1,128)S(1)}, f32[1,2048]{1,0:T(1,128)}, u32[]{:S(2)}) copy-start(f32[1,2048]{1,0:T(1,128)} %get-tuple-element.78) | copy-start | bytes 24580
  433.6 124.2 %copy-start.5 = (f32[1,512]{1,0:T(1,128)S(1)}, f32[1,512]{1,0:T(1,128)}, u32[]{:S(2)}) copy-start(f32[1,512]{1,0:T(1,128)} %get-tuple-element.80) | copy-start | bytes 6148
  433.6 124.2 %copy-start.6 = (f32[1,128]{1,0:T(1,128)S(1)}, f32[1,128]{1,0:T(1,128)}, u32[]{:S(2)}) copy-start(f32[1,128]{1,0:T(1,128)} %get-tuple-element.79) | copy-start | bytes 1540
  625.5 2.9 copy-start
  628.5 3.7 copy-start.1
  632.2 2.4 copy-start.3
  632.2 3.5 copy-start.2
Sparse Core Ops, SparseCore 0:
  432.9 85.2 reduce-scatter.4
  522.1 103.3 reduce-scatter.2

commit v12 on v11

--- a/solution.py
+++ b/solution.py
@@ -628,7 +628,7 @@
         return [
             pltpu.make_async_copy(
                 stage.at[slot, pl.ds(0, TILE), hidden_columns],
-                grads_hbm.at[which, rows],
+                grads_hbm.at[rows, pl.ds(which * hidden_width, hidden_width)],
                 tile_sem.at[slot, which],
             )
             for which, stage in enumerate(stages)
@@ -694,7 +694,7 @@
             jax.ShapeDtypeStruct((tokens, hidden_width), BF16),
             jax.ShapeDtypeStruct((tokens, model_width), BF16),
             jax.ShapeDtypeStruct((tokens // 2, model_width), F32),
-            jax.ShapeDtypeStruct((3, model_width, hidden_width), BF16),
+            jax.ShapeDtypeStruct((model_width, 3 * hidden_width), BF16),
         ],
         scratch_shapes=[
             pltpu.VMEM((model_width, padded), BF16),
@@ -760,13 +760,11 @@
     gain_grad,
     floor_grad,
     back_ref,
-    out_grads_hbm,
     mixer_grads_hbm,
     arrived,
     left,
     right,
     full,
-    out_stage,
     mixer_stage,
     gates,
     pre,
@@ -824,12 +822,9 @@
     def tile_columns(tile):
         return pl.ds(pl.multiple_of(tile * TILE, TILE), TILE)
 
-    def stage_copies(tile):
+    def stage_copy(tile):
         rows = tile_columns(tile)
-        return (
-            pltpu.make_async_copy(out_stage, out_grads_hbm.at[rows], stage_sem.at[0]),
-            pltpu.make_async_copy(mixer_stage, mixer_grads_hbm.at[rows], stage_sem.at[1]),
-        )
+        return pltpu.make_async_copy(mixer_stage, mixer_grads_hbm.at[rows], stage_sem.at[0])
 
     def gate_piece(index):
         rows = pl.ds(pl.multiple_of(index * piece_rows, piece_rows), piece_rows)
@@ -985,17 +980,16 @@
     def mixer_tile(tile):
         @pl.when(tile > 0)
         def _():
-            for copy in stage_copies(tile - 1):
-                copy.wait()
+            stage_copy(tile - 1).wait()
 
         columns = tile_columns(tile)
         rows = left[:, columns]
         for first in range(0, 4 * width, 1024):
             some = slice(first, min(first + 1024, 4 * width))
             mixer_stage[:, some] = mm_tn(rows, right[:, some]).astype(BF16)
-        out_stage[...] = mm_tn(mix_grad_ref[:, columns], gated_ref[...]).astype(BF16)
-        for copy in stage_copies(tile):
-            copy.start()
+        product = mm_tn(mix_grad_ref[:, columns], gated_ref[...])
+        mixer_stage[:, 4 * width :] = product.astype(BF16)
+        stage_copy(tile).start()
 
     send_time = tokens // piece_rows
     block_time = send_time + 1
@@ -1047,8 +1041,7 @@
         return 0
 
     lax.fori_loop(0, steps, body, 0)
-    for copy in stage_copies(tiles - 1):
-        copy.wait()
+    stage_copy(tiles - 1).wait()
     line.finish()
 
 
@@ -1064,22 +1057,20 @@
     return pl.pallas_call(
         partial(output_kernel, mesh_axes, head_count, lanes ** (-0.5)),
         in_specs=[whole] * len(in_vmem) + [remote] * len(in_hbm),
-        out_specs=[whole] * 4 + [remote] * 2,
+        out_specs=[whole] * 4 + [remote],
         out_shape=[
             jax.ShapeDtypeStruct((tokens, model_width), BF16),
             jax.ShapeDtypeStruct((1, lanes), F32),
             jax.ShapeDtypeStruct((1, width), F32),
             jax.ShapeDtypeStruct((tokens, model_width), BF16),
-            jax.ShapeDtypeStruct((model_width, width), BF16),
-            jax.ShapeDtypeStruct((model_width, 4 * width), BF16),
+            jax.ShapeDtypeStruct((model_width, 5 * width), BF16),
         ],
         scratch_shapes=[
             pltpu.VMEM((tokens, model_width), BF16),
             pltpu.VMEM((tokens, model_width), BF16),
             pltpu.VMEM((tokens, 4 * width), BF16),
             pltpu.VMEM((model_width, 4 * width), BF16),
-            pltpu.VMEM((TILE, width), BF16),
-            pltpu.VMEM((TILE, 4 * width), BF16),
+            pltpu.VMEM((TILE, 5 * width), BF16),
             pltpu.VMEM((tokens, width), F32),
             pltpu.VMEM((2, BLOCK, 3 * width), F32),
             pltpu.VMEM((tokens, width), BF16),
@@ -1093,7 +1084,7 @@
             pltpu.VMEM((1, width), F32),
             pltpu.SemaphoreType.DMA((3,)),
             pltpu.SemaphoreType.DMA((2,)),
-            pltpu.SemaphoreType.DMA((2,)),
+            pltpu.SemaphoreType.DMA((1,)),
             pltpu.SemaphoreType.DMA((context_size - 1,)),
             pltpu.SemaphoreType.DMA((context_size - 1,)),
         ]
@@ -1119,9 +1110,11 @@
     grads_hbm,
     out_ref,
     gain_grad,
+    share_query,
+    share_forget,
+    share_input,
     share_gate,
-    share_up,
-    share_down,
+    share_out,
     arrived,
     own,
     other,
@@ -1135,7 +1128,7 @@
 ):
     plane = Plane(mesh_axes)
     chips = plane.chips
-    block = own.shape[2]
+    block = own.shape[1]
     gain_grad[...] = jnp.zeros_like(gain_grad)
 
     def turn(total, rows, own_rows):
@@ -1158,12 +1151,12 @@
 
     def load(slot):
         return pltpu.make_async_copy(
-            grads_hbm.at[:, rows_of(slot, plane.core)], own.at[slot], load_sem.at[slot]
+            grads_hbm.at[rows_of(slot, plane.core)], own.at[slot], load_sem.at[slot]
         )
 
     def pair_copy(slot):
         return pltpu.make_async_remote_copy(
-            grads_hbm.at[:, rows_of(slot, 1 - plane.core)],
+            grads_hbm.at[rows_of(slot, 1 - plane.core)],
             other.at[slot],
             pair_send.at[slot],
             pair_recv.at[slot],
@@ -1200,9 +1193,8 @@
 
             def add(index, _):
                 rows = pl.ds(pl.multiple_of(index * strip, strip), strip)
-                for which in range(3):
-                    total = own[slot, which, rows].astype(F32) + other[slot, which, rows].astype(F32)
-                    own[slot, which, rows] = total.astype(BF16)
+                total = own[slot, rows].astype(F32) + other[slot, rows].astype(F32)
+                own[slot, rows] = total.astype(BF16)
                 return 0
 
             lax.fori_loop(0, block // strip, add, 0)
@@ -1222,15 +1214,15 @@
     def total(index, _):
         rows = pl.ds(pl.multiple_of(index * strip, strip), strip)
 
-        def whole(which):
-            def add(slot, value):
-                return value + remote[slot, which, rows].astype(F32)
-
-            return lax.fori_loop(0, chips - 1, add, own[0, which, rows].astype(F32))
-
-        share_gate[rows] = whole(0)
-        share_up[rows] = whole(1)
-        share_down[rows] = whole(2)
+        for which, share in enumerate(
+            (share_query, share_forget, share_input, share_gate, share_out)
+        ):
+            columns = pl.ds(which * share.shape[1], share.shape[1])
+
+            def add(slot, value, columns=columns):
+                return value + remote[slot, rows, columns].astype(F32)
+
+            share[rows] = lax.fori_loop(0, chips - 1, add, own[0, rows, columns].astype(F32))
         return 0
 
     lax.fori_loop(0, block // strip, total, 0)
@@ -1251,24 +1243,24 @@
 
 def input_line(mesh_axes, collective, part, hidden, residual_grad, gain, grads):
     tokens, model_width = part.shape
-    hidden_width = grads.shape[2]
+    all_width = grads.shape[1]
     chips = lax.axis_size("shard") * lax.axis_size("context") // 2
     block = model_width // (2 * chips)
     whole = pl.BlockSpec(memory_space=pltpu.VMEM)
     return pl.pallas_call(
         partial(input_kernel, mesh_axes),
         in_specs=[whole] * 4 + [pl.BlockSpec(memory_space=pl.ANY)],
-        out_specs=[whole] * 5,
+        out_specs=[whole] * 7,
         out_shape=[
             jax.ShapeDtypeStruct((tokens, model_width), BF16),
             jax.ShapeDtypeStruct((1, model_width), F32),
         ]
-        + [jax.ShapeDtypeStruct((block, hidden_width), F32)] * 3,
+        + [jax.ShapeDtypeStruct((block, all_width // 5), F32)] * 5,
         scratch_shapes=[
             pltpu.VMEM((tokens, model_width), BF16),
-            pltpu.VMEM((chips, 3, block, hidden_width), BF16),
-            pltpu.VMEM((chips, 3, block, hidden_width), BF16),
-            pltpu.VMEM((chips - 1, 3, block, hidden_width), BF16),
+            pltpu.VMEM((chips, block, all_width), BF16),
+            pltpu.VMEM((chips, block, all_width), BF16),
+            pltpu.VMEM((chips - 1, block, all_width), BF16),
             pltpu.SemaphoreType.DMA((chips,)),
             pltpu.SemaphoreType.DMA((chips,)),
             pltpu.SemaphoreType.DMA((chips,)),
@@ -1895,8 +1887,7 @@
         grad_head_part,
         grad_floor_part,
         back_one,
-        grad_out,
-        grad_mixer,
+        grads_mixer,
     ) = output_line(
         mesh_axes,
         1,
@@ -1922,8 +1913,14 @@
         (normed_one, pre, mixer_full),
         head_count,
     )
-    input_rows, grad_norm_one, share_gate, share_up, share_down = input_line(
-        mesh_axes, 3, back_one, hidden_rows, grad_residual, gain_one, grads_ffn
+    share_ffn = lax.psum_scatter(grads_ffn, both, scatter_dimension=0, tiled=True)
+    hidden_width = w_ffn_gate.shape[1]
+
+    def ffn_share(which):
+        return share_ffn[:, which * hidden_width : (which + 1) * hidden_width].astype(F32)
+
+    input_rows, grad_norm_one, *mixer_shares, share_out = input_line(
+        mesh_axes, 3, back_one, hidden_rows, grad_residual, gain_one, grads_mixer
     )
     near, total = small_sum(
         mesh_axes, 5, (grad_norm_one, grad_norm_two, grad_head_part, grad_floor_part)
@@ -1938,27 +1935,18 @@
     floor_total = near[2 * model_width + key_dim : 2 * model_width + key_dim + width]
     floor_total = floor_total.reshape(head_count, shares, key_dim // shares)
 
-    def share(values, dim):
-        return lax.psum_scatter(
-            values.astype(BF16), both, scatter_dimension=dim, tiled=True
-        ).astype(F32)
-
-    share_mixer = share(grad_mixer, 0)
     return (
         output_rows.reshape(hidden.shape),
         input_rows.reshape(hidden.shape),
         own_slice(total, 0, model_width),
-        share_mixer[:, :width],
-        share_mixer[:, width : 2 * width],
-        share_mixer[:, 2 * width : 3 * width],
-        share_mixer[:, 3 * width :],
+        *mixer_shares,
         lax.dynamic_index_in_dim(floor_total, position, 1, False),
         own_slice(total, 2 * model_width, key_dim),
-        share(grad_out, 0).T,
+        share_out.T,
         own_slice(total, model_width, model_width),
-        share_gate,
-        share_up,
-        share_down.T,
+        ffn_share(0),
+        ffn_share(1),
+        ffn_share(2).T,
     )
 
 

time: 644 us -> 596 us (0.925)
  waiting for transfers between devices: 46.6 us -> 0.02 us
    reduce_scatter x2 -> x1, waiting for transfers between devices: 45.9 us -> 0.01 us  [local(): lax.psum_scatter(grads_ffn, both, scatter_dimension=0, tiled=True)]
    unnamed x20 -> x24, local copies, waits for them, and re-layouts: 12.3 us -> 13.8 us
  transfers between devices with their start and end apart: 2 -> 1, of which waited for: 1 -> 0; matrix products, arithmetic and copies ran while one was open for 2% -> 1% of each run, Pallas kernels for 21% -> 44%
where the time goes in v12:
time: 596 us; the launch traced here: 595 us
  Pallas kernels  557 us (93%)
  local copies, waits for them, and re-layouts  18.5 us (3%)
  between operations  14.2 us (2%)
    pallas_call x1, Pallas kernels, middle(): pl.pallas_call(partial(middle_kernel, mesh_axes), in_specs=[remote, whole...  223 us
    pallas_call x1, Pallas kernels, output_line(): pl.pallas_call(partial(output_kernel, mesh_axes, head_count, lanes ** (-0...  128 us
    pallas_call x1, Pallas kernels, input_line(): pl.pallas_call(partial(input_kernel, mesh_axes), in_specs=[whole] * 4 + [...  121 us
    pallas_call x1, Pallas kernels, forward(): pl.pallas_call(partial(forward_kernel, mesh_axes, head_count, lanes ** (-...  74.9 us
    unnamed x24, local copies, waits for them, and re-layouts  13.8 us
  transfers between devices with their start and end apart: 1, of which 0 were waited for; matrix products, arithmetic and copies ran while one was open for 1% of the time, Pallas kernels for 44%

profile of v12, /device:TPU:0, one launch (start us, length us, event | category | flops | bytes accessed | tf_op | source)
XLA Modules:
  0.0 595.3 jit_solution(14743505408556178813)
XLA Ops:
  7.2 0.0 reduce-scatter.2.cloned.1.call-start
  7.2 1.3 convert_element_type.14
  8.5 74.9 %forward.1 = (bf16[1024,2048]{1,0:T(8,128)(2,1)}, f32[1024,2048]{1,0:T(8,128)}, bf16[2048,2048]{1,0:T(8,128)(2,1)}, bf16[2048,512]{1,0:T(8,128)(2,1)}, f32[1024,...) custom-call(bf16[1024,2048]{1,0:T(8,128)(2,1)} %bitcast.22, ...), custom_call_target="tpu_custom_call" | custom-call | flops 8589934592 | bytes 200000000 | tf_op jit(solution)/shard_map/forward/pallas_call | solution.py:1663
  83.4 222.7 %middle.1 = (bf16[1024,2048]{1,0:T(8,128)(2,1)}, bf16[1024,2048]{1,0:T(8,128)(2,1)}, f32[1,2048]{1,0:T(1,128)}, f32[512,2048]{1,0:T(8,128)}, bf16[1024,1408]{1,0...) custom-call(bf16[1024,2048]{1,0:T(8,128)(2,1)} %get-tuple-element.52, ...), custom_call_target="tpu_custom_call" | custom-call | flops 35433480192 | bytes 360000000 | tf_op jit(solution)/shard_map/middle/pallas_call | solution.py:683
  306.0 0.0 reduce-scatter.2.cloned.1.call-update
  306.1 128.3 %output_line.1 = (bf16[1024,2048]{1,0:T(8,128)(2,1)}, f32[1,128]{1,0:T(1,128)}, f32[1,512]{1,0:T(1,128)}, bf16[1024,2048]{1,0:T(8,128)(2,1)}, bf16[2048,2560]{1,0:T(8,128)(2,1)}) custom-call(bf16[1024,2048]{1,0:T(8,128)(2,1)} %get-tuple-element.54.part, f32[512,2048]{1,0:T(8,128)} %get-tuple-element.55.residual, ...), custom_call_target="tpu_custom_call" | custom-call | flops 25769803776 | bytes 360000000 | tf_op jit(solution)/shard_map/output_line/pallas_call | solution.py:1057
  434.3 0.0 copy-start.5
  434.4 0.0 copy-start.6
  434.4 0.0 copy-start.7
  434.4 121.3 %input_line.1 = (bf16[1024,2048]{1,0:T(8,128)(2,1)}, f32[1,2048]{1,0:T(1,128)}, f32[256,512]{1,0:T(8,128)}, f32[256,512]{1,0:T(8,128)}, f32[256,512]{1,0:T(8,128...) custom-call(bf16[1024,2048]{1,0:T(8,128)(2,1)} %get-tuple-element.74.part, bf16[1024,2048]{1,0:T(8,128)(2,1)} %bitcast.24, ...), custom_call_target="tpu_custom_call" | custom-call | flops 16777216 | bytes 360000000 | tf_op jit(solution)/shard_map/input_line/pallas_call | solution.py:1250
  555.6 0.0 copy-done.5
  555.7 0.0 copy-done.6
  555.7 0.0 copy-done.7
  555.7 0.7 select_maximum_fusion
  556.4 0.6 reshape.91.value
  557.0 10.1 %small_sum.1 = (f32[8,640]{1,0:T(8,128)}, f32[8,640]{1,0:T(8,128)}) custom-call(f32[8,640]{1,0:T(8,128)} %reshape.91.value), custom_call_target="tpu_custom_call" | custom-call | flops 40960 | bytes 20000000 | tf_op jit(solution)/shard_map/small_sum/pallas_call | solution.py:1781
  567.1 0.8 slice.35
  567.9 0.7 slice.31
  568.7 0.8 slice.33
  569.5 2.0 copy.32
  571.6 0.5 fusion
  572.1 0.6 constant_dynamic-slice_fusion.2
  572.7 0.6 constant_dynamic-slice_fusion
  573.2 0.0 reduce-scatter.2.cloned.1.call-done
  573.2 3.4 convert_bitcast_fusion
  576.7 1.5 copy.33
  578.2 0.0 copy-start
  578.2 4.9 copy.40
  583.1 0.0 copy-done
  583.1 0.0 copy-start.4
  583.1 0.0 copy-start.3
  583.1 0.0 copy-start.2
  583.1 0.0 copy-start.1
  583.2 2.1 copy.41
  585.3 0.0 copy-done.4
  585.3 0.8 copy.42
  586.1 0.0 copy-done.3
  586.1 0.8 copy.43
  586.9 0.0 copy-done.2
  586.9 0.8 copy.44
  587.7 0.0 copy-done.1
  587.7 0.8 copy.45
  (3 shorter events, 0.0 us)
Async XLA Ops:
  7.2 566.1 %reduce-scatter.2.cloned.1.call-start = ((), (), s32[]{:S(2)}) async-start(), calls=%async_computation.1 | async-start | bytes 19464192 | tf_op jit(solution)/shard_map/reduce_scatter | solution.py:1916
  434.3 121.3 %copy-start.5 = (f32[1,2048]{1,0:T(1,128)S(1)}, f32[1,2048]{1,0:T(1,128)}, u32[]{:S(2)}) copy-start(f32[1,2048]{1,0:T(1,128)} %get-tuple-element.79) | copy-start | bytes 24580
  434.4 121.3 %copy-start.6 = (f32[1,512]{1,0:T(1,128)S(1)}, f32[1,512]{1,0:T(1,128)}, u32[]{:S(2)}) copy-start(f32[1,512]{1,0:T(1,128)} %get-tuple-element.81) | copy-start | bytes 6148
  434.4 121.3 %copy-start.7 = (f32[1,128]{1,0:T(1,128)S(1)}, f32[1,128]{1,0:T(1,128)}, u32[]{:S(2)}) copy-start(f32[1,128]{1,0:T(1,128)} %get-tuple-element.80) | copy-start | bytes 1540
  578.2 4.9 copy-start
  583.1 2.1 copy-start.4
  583.1 2.9 copy-start.3
  583.1 3.7 copy-start.2
  583.1 4.5 copy-start.1
Sparse Core Ops, SparseCore 0:
  306.2 118.1 reduce-scatter.1

commit v13 on v12

--- a/solution.py
+++ b/solution.py
@@ -54,17 +54,22 @@
 
 
 class Line:
-    def __init__(self, mesh_axes, part, arrived, out, sems, transform):
+    def __init__(self, mesh_axes, part, arrived, out, sems, transform, sums=True, backs=True):
         self.mesh_axes = mesh_axes
+        self.sums, self.backs = sums, backs
         self.part, self.arrived, self.out = part, arrived, out
-        self.sum_send, self.sum_recv, self.back_send, self.back_recv = sems
+        if sums:
+            self.sum_send, self.sum_recv = sems[:2]
+        if backs:
+            self.back_send, self.back_recv = sems[-2:]
         self.transform = transform
-        self.half = part.shape[0] // 2
+        self.half = (part if sums else out).shape[0] // 2
         self.chunks = self.half // CHUNK
         self.size = lax.axis_size("tensor")
         self.place = lax.axis_index("tensor")
         self.lines = ((self.size - 1 - self.place, -1), (self.place, 1))
-        self.steps = self.chunks + 2 * LAG * (self.size - 1)
+        self.offset = LAG * (self.size - 1) if sums else 0
+        self.steps = self.chunks + self.offset + (LAG * (self.size - 1) if backs else 0)
 
     def device(self, position):
         return tuple(
@@ -113,47 +118,64 @@
     def step(self, time):
         for side in (0, 1):
             hops = self.lines[side][0]
-            index = time - LAG * hops
-            valid = jnp.logical_and(index >= 0, index < self.chunks)
             at_source, at_owner = hops == 0, hops == self.size - 1
-            index = jnp.clip(index, 0, self.chunks - 1)
-            rows = self.rows_of(side, index)
-
-            @pl.when(jnp.logical_and(valid, at_source))
-            def _(side=side, index=index):
-                self.sum_copy(side, index, self.part).start()
-
-            @pl.when(jnp.logical_and(valid, jnp.logical_not(at_source)))
-            def _(side=side, index=index):
-                self.sum_copy(side, index, self.arrived).wait_recv()
-
-            between = jnp.logical_and(jnp.logical_not(at_source), jnp.logical_not(at_owner))
-
-            @pl.when(jnp.logical_and(valid, between))
-            def _(side=side, index=index, rows=rows):
-                total = self.part[rows].astype(F32) + self.arrived[rows].astype(F32)
-                self.arrived[rows] = total.astype(BF16)
-                self.sum_copy(side, index, self.arrived).start()
-
-            @pl.when(jnp.logical_and(valid, at_owner))
-            def _(side=side, index=index, rows=rows):
-                total = self.part[rows].astype(F32) + self.arrived[rows].astype(F32)
-                own = pl.ds(pl.multiple_of(index * CHUNK, CHUNK), CHUNK)
-                self.transform(total, rows, own)
-                self.back_copy(side, index).start()
-
-            away = self.size - 1 - hops
-            index = time - LAG * (self.size - 1 + away)
-            valid = jnp.logical_and(jnp.logical_and(index >= 0, index < self.chunks), away > 0)
-            index = jnp.clip(index, 0, self.chunks - 1)
-
-            @pl.when(valid)
-            def _(side=side, index=index):
-                self.back_copy(side, index).wait_recv()
-
-            @pl.when(jnp.logical_and(valid, away < self.size - 1))
-            def _(side=side, index=index):
-                self.back_copy(side, index).start()
+            if self.sums:
+                self.sum_step(time, side, hops, at_source, at_owner)
+            if self.backs:
+                self.back_step(time, side, hops, at_owner)
+
+    def sum_step(self, time, side, hops, at_source, at_owner):
+        index = time - LAG * hops
+        valid = jnp.logical_and(index >= 0, index < self.chunks)
+        index = jnp.clip(index, 0, self.chunks - 1)
+        rows = self.rows_of(side, index)
+
+        @pl.when(jnp.logical_and(valid, at_source))
+        def _():
+            self.sum_copy(side, index, self.part).start()
+
+        @pl.when(jnp.logical_and(valid, jnp.logical_not(at_source)))
+        def _():
+            self.sum_copy(side, index, self.arrived).wait_recv()
+
+        between = jnp.logical_and(jnp.logical_not(at_source), jnp.logical_not(at_owner))
+
+        @pl.when(jnp.logical_and(valid, between))
+        def _():
+            total = self.part[rows].astype(F32) + self.arrived[rows].astype(F32)
+            self.arrived[rows] = total.astype(BF16)
+            self.sum_copy(side, index, self.arrived).start()
+
+        @pl.when(jnp.logical_and(valid, at_owner))
+        def _():
+            total = self.part[rows].astype(F32) + self.arrived[rows].astype(F32)
+            self.turn(total, side, index)
+
+    def turn(self, total, side, index):
+        own = pl.ds(pl.multiple_of(index * CHUNK, CHUNK), CHUNK)
+        self.transform(total, self.rows_of(side, index), own)
+        if self.backs:
+            self.back_copy(side, index).start()
+
+    def back_step(self, time, side, hops, at_owner):
+        if not self.sums:
+
+            @pl.when(jnp.logical_and(at_owner, time < self.chunks))
+            def _():
+                self.turn(None, side, jnp.clip(time, 0, self.chunks - 1))
+
+        away = self.size - 1 - hops
+        index = time - self.offset - LAG * away
+        valid = jnp.logical_and(jnp.logical_and(index >= 0, index < self.chunks), away > 0)
+        index = jnp.clip(index, 0, self.chunks - 1)
+
+        @pl.when(valid)
+        def _():
+            self.back_copy(side, index).wait_recv()
+
+        @pl.when(jnp.logical_and(valid, away < self.size - 1))
+        def _():
+            self.back_copy(side, index).start()
 
     def run(self, first, last, beside=None):
         def body(time, _):
@@ -184,21 +206,25 @@
                 if not source_waits:
                     passed = jnp.logical_and(passed, hops > 0)
 
-                @pl.when(passed)
-                def _(side=side):
-                    self.sum_copy(side, index, self.arrived).wait_send()
-
-                @pl.when(hops > 0)
-                def _(side=side):
-                    self.back_copy(side, index).wait_send()
+                if self.sums:
+
+                    @pl.when(passed)
+                    def _(side=side):
+                        self.sum_copy(side, index, self.arrived).wait_send()
+
+                if self.backs:
+
+                    @pl.when(hops > 0)
+                    def _(side=side):
+                        self.back_copy(side, index).wait_send()
 
             return 0
 
         lax.fori_loop(0, self.chunks, body, 0)
 
 
-def line_sems(tokens):
-    return [pltpu.SemaphoreType.DMA((2, tokens // 2 // CHUNK))] * 4
+def line_sems(tokens, count=4):
+    return [pltpu.SemaphoreType.DMA((2, tokens // 2 // CHUNK))] * count
 
 
 def inverse_rms(values):
@@ -741,7 +767,6 @@
     gated_ref,
     mix_grad_ref,
     out_full,
-    mixed_ref,
     lead_ref,
     starts_ref,
     run_ref,
@@ -756,17 +781,20 @@
     normed_hbm,
     pre_hbm,
     full_hbm,
+    mixed_hbm,
     out_ref,
     gain_grad,
     floor_grad,
-    back_ref,
+    total_ref,
     mixer_grads_hbm,
     arrived,
+    back,
+    back_arrived,
     left,
     right,
     full,
     mixer_stage,
-    gates,
+    piece_rows_scr,
     pre,
     grad_mixed,
     back_scr,
@@ -778,6 +806,8 @@
     moved_scr,
     value_scr,
     load_sem,
+    piece_sem,
+    full_sem,
     pre_sem,
     stage_sem,
     grad_send,
@@ -793,11 +823,23 @@
     context, context_size = lax.axis_index("context"), lax.axis_size("context")
 
     left_load = pltpu.make_async_copy(normed_hbm, left, load_sem.at[0])
-    full_load = pltpu.make_async_copy(full_hbm, full, load_sem.at[1])
-    gate_load = pltpu.make_async_copy(
-        pre_hbm.at[:, pl.ds(3 * width, width)], gates, load_sem.at[2]
-    )
-    for load in (gate_load, left_load, full_load):
+    left_load.start()
+
+    def piece_loads(index):
+        rows = pl.ds(pl.multiple_of(index * piece_rows, piece_rows), piece_rows)
+        slot = lax.rem(index, 2)
+        return (
+            pltpu.make_async_copy(
+                pre_hbm.at[rows, pl.ds(3 * width, width)],
+                piece_rows_scr.at[slot, 0],
+                piece_sem.at[slot, 0],
+            ),
+            pltpu.make_async_copy(
+                mixed_hbm.at[rows], piece_rows_scr.at[slot, 1], piece_sem.at[slot, 1]
+            ),
+        )
+
+    for load in piece_loads(0):
         load.start()
     gain_grad[...] = jnp.zeros_like(gain_grad)
     floor_grad[...] = jnp.zeros_like(floor_grad)
@@ -811,13 +853,16 @@
         places["context"] = lax.rem(context + context_size - shift, context_size)
         return tuple(places[axis] for axis in mesh_axes)
 
-    line = Line(mesh_axes, part, arrived, out_ref, sems, turn)
+    def keep_total(total, rows, own):
+        total_ref[own] = total
+
+    line = Line(mesh_axes, part, arrived, out_ref, sems[:4], turn)
+    back_line = Line(mesh_axes, back, back_arrived, None, sems[4:], keep_total, backs=False)
     barrier = pltpu.get_barrier_semaphore()
     expected = line.greet(barrier)
     for shift in range(1, context_size):
         pl.semaphore_signal(barrier, inc=1, device_id=earlier(shift), device_id_type=MESH_ID)
     pl.semaphore_wait(barrier, expected + context_size - 1)
-    gate_load.wait()
 
     def tile_columns(tile):
         return pl.ds(pl.multiple_of(tile * TILE, TILE), TILE)
@@ -828,12 +873,22 @@
 
     def gate_piece(index):
         rows = pl.ds(pl.multiple_of(index * piece_rows, piece_rows), piece_rows)
+        slot = lax.rem(index, 2)
+
+        @pl.when(index + 1 < tokens // piece_rows)
+        def _():
+            for load in piece_loads(index + 1):
+                load.start()
+
+        for load in piece_loads(index):
+            load.wait()
         grads = mm_nn(mix_grad_ref[rows], out_full[...])
         gain = gain_ref[...]
         total = jnp.zeros_like(gain)
         for head in range(head_count):
             part_of = slice(head * lanes, (head + 1) * lanes)
-            mixed, gate, grad = mixed_ref[rows, part_of], gates[rows, part_of], grads[:, part_of]
+            gate, mixed = piece_rows_scr[slot, 0, :, part_of], piece_rows_scr[slot, 1, :, part_of]
+            grad = grads[:, part_of]
             inverse = inverse_rms(mixed)
             unit = mixed * inverse
             sigma = jax.nn.sigmoid(gate)
@@ -973,9 +1028,20 @@
             -key_total * opened * closed * (1.0 - closed)
         ).astype(BF16)
 
+    def full_load(tile):
+        slot = lax.rem(tile, 2)
+        return pltpu.make_async_copy(
+            full_hbm.at[tile_columns(tile)], full.at[slot], full_sem.at[slot]
+        )
+
     def back_tile(tile):
-        columns = tile_columns(tile)
-        back_ref[:, columns] = mm_nt(right[...], full[columns, :]).astype(BF16)
+        @pl.when(tile + 1 < tiles)
+        def _():
+            full_load(tile + 1).start()
+
+        full_load(tile).wait()
+        product = mm_nt(right[...], full[lax.rem(tile, 2)])
+        back[:, tile_columns(tile)] = product.astype(BF16)
 
     def mixer_tile(tile):
         @pl.when(tile > 0)
@@ -992,12 +1058,12 @@
         stage_copy(tile).start()
 
     send_time = tokens // piece_rows
-    block_time = send_time + 1
+    block_time = send_time + 2
     back_time = block_time + blocks
     tile_time = back_time + tiles
     end_time = tile_time + tiles
 
-    def beside(time):
+    def piece(time):
         @pl.when(time < send_time)
         def _():
             gate_piece(time)
@@ -1014,9 +1080,9 @@
         def _():
             mixer_block(time - block_time)
 
-        @pl.when(time == back_time)
-        def _():
-            full_load.wait()
+        @pl.when(time == back_time - 1)
+        def _():
+            full_load(0).start()
 
         @pl.when(jnp.logical_and(time >= back_time, time < tile_time))
         def _():
@@ -1030,19 +1096,29 @@
         def _():
             mixer_tile(time - tile_time)
 
-    steps = max(line.steps, end_time)
+    begin = -(-tile_time // 2)
+    steps = max(line.steps, begin + back_line.steps, -(-end_time // 2))
 
     def body(time, _):
         @pl.when(time < line.steps)
         def _():
             line.step(time)
 
-        beside(time)
+        @pl.when(time >= begin)
+        def _():
+            back_line.step(time - begin)
+
+        def pieces(offset, _):
+            piece(2 * time + offset)
+            return 0
+
+        lax.fori_loop(0, 2, pieces, 0)
         return 0
 
     lax.fori_loop(0, steps, body, 0)
     stage_copy(tiles - 1).wait()
     line.finish()
+    back_line.finish()
 
 
 def output_line(mesh_axes, collective, in_vmem, in_hbm, head_count):
@@ -1062,16 +1138,18 @@
             jax.ShapeDtypeStruct((tokens, model_width), BF16),
             jax.ShapeDtypeStruct((1, lanes), F32),
             jax.ShapeDtypeStruct((1, width), F32),
-            jax.ShapeDtypeStruct((tokens, model_width), BF16),
+            jax.ShapeDtypeStruct((tokens // 2, model_width), F32),
             jax.ShapeDtypeStruct((model_width, 5 * width), BF16),
         ],
         scratch_shapes=[
             pltpu.VMEM((tokens, model_width), BF16),
             pltpu.VMEM((tokens, model_width), BF16),
+            pltpu.VMEM((tokens, model_width), BF16),
+            pltpu.VMEM((tokens, model_width), BF16),
             pltpu.VMEM((tokens, 4 * width), BF16),
-            pltpu.VMEM((model_width, 4 * width), BF16),
+            pltpu.VMEM((2, TILE, 4 * width), BF16),
             pltpu.VMEM((TILE, 5 * width), BF16),
-            pltpu.VMEM((tokens, width), F32),
+            pltpu.VMEM((2, 2, 2 * BLOCK, width), F32),
             pltpu.VMEM((2, BLOCK, 3 * width), F32),
             pltpu.VMEM((tokens, width), BF16),
             pltpu.VMEM((head_count, lanes, lanes), F32),
@@ -1082,13 +1160,16 @@
             pltpu.VMEM((BLOCK, width), F32),
             pltpu.VMEM((BLOCK, width), F32),
             pltpu.VMEM((1, width), F32),
-            pltpu.SemaphoreType.DMA((3,)),
+            pltpu.SemaphoreType.DMA((1,)),
+            pltpu.SemaphoreType.DMA((2, 2)),
+            pltpu.SemaphoreType.DMA((2,)),
             pltpu.SemaphoreType.DMA((2,)),
             pltpu.SemaphoreType.DMA((1,)),
             pltpu.SemaphoreType.DMA((context_size - 1,)),
             pltpu.SemaphoreType.DMA((context_size - 1,)),
         ]
-        + line_sems(tokens),
+        + line_sems(tokens)
+        + line_sems(tokens, 2),
         compiler_params=pltpu.CompilerParams(
             collective_id=collective, has_side_effects=True, vmem_limit_bytes=61 << 20
         ),
@@ -1103,7 +1184,7 @@
 
 def input_kernel(
     mesh_axes,
-    part,
+    total_ref,
     hidden_ref,
     residual_grad,
     gain_ref,
@@ -1115,7 +1196,6 @@
     share_input,
     share_gate,
     share_out,
-    arrived,
     own,
     other,
     remote,
@@ -1132,6 +1212,7 @@
     gain_grad[...] = jnp.zeros_like(gain_grad)
 
     def turn(total, rows, own_rows):
+        total = total_ref[own_rows]
         values = hidden_ref[rows].astype(F32)
         inverse = inverse_rms(values)
         unit = values * inverse
@@ -1141,7 +1222,7 @@
         grad = residual_grad[own_rows] + inverse * (lifted - unit * mean)
         out_ref[rows] = grad.astype(BF16)
 
-    line = Line(mesh_axes, part, arrived, out_ref, sems, turn)
+    line = Line(mesh_axes, None, None, out_ref, sems, turn, sums=False)
     barrier = pltpu.get_barrier_semaphore()
     expected = line.greet(barrier) + plane.greet(barrier)
     pl.semaphore_wait(barrier, expected)
@@ -1241,8 +1322,8 @@
     line.finish()
 
 
-def input_line(mesh_axes, collective, part, hidden, residual_grad, gain, grads):
-    tokens, model_width = part.shape
+def input_line(mesh_axes, collective, total, hidden, residual_grad, gain, grads):
+    tokens, model_width = hidden.shape
     all_width = grads.shape[1]
     chips = lax.axis_size("shard") * lax.axis_size("context") // 2
     block = model_width // (2 * chips)
@@ -1257,7 +1338,6 @@
         ]
         + [jax.ShapeDtypeStruct((block, all_width // 5), F32)] * 5,
         scratch_shapes=[
-            pltpu.VMEM((tokens, model_width), BF16),
             pltpu.VMEM((chips, block, all_width), BF16),
             pltpu.VMEM((chips, block, all_width), BF16),
             pltpu.VMEM((chips - 1, block, all_width), BF16),
@@ -1267,7 +1347,7 @@
             pltpu.SemaphoreType.DMA((chips - 1,)),
             pltpu.SemaphoreType.DMA((chips - 1,)),
         ]
-        + line_sems(tokens),
+        + line_sems(tokens, 2),
         compiler_params=pltpu.CompilerParams(
             collective_id=collective, has_side_effects=True, vmem_limit_bytes=58 << 20
         ),
@@ -1275,7 +1355,7 @@
             flops=tokens * model_width * 8, bytes_accessed=360_000_000, transcendentals=0
         ),
         name="input_line",
-    )(part, hidden, residual_grad, gain, grads)
+    )(total, hidden, residual_grad, gain, grads)
 
 
 def forward_kernel(
@@ -1897,7 +1977,6 @@
             gated_low,
             grad_mix_low,
             out_full,
-            mixed,
             lead,
             starts,
             runs,
@@ -1910,7 +1989,7 @@
             flags,
             gain_row,
         ),
-        (normed_one, pre, mixer_full),
+        (normed_one, pre, mixer_full, mixed),
         head_count,
     )
     share_ffn = lax.psum_scatter(grads_ffn, both, scatter_dimension=0, tiled=True)

time: 596 us -> 599 us (level)
    pallas_call x1, Pallas kernels: 128 us -> 180 us  [output_line(): pl.pallas_call(partial(output_kernel, mesh_axes, head_count, lanes ** (-0...]
    pallas_call x1, Pallas kernels: 121 us -> 72 us  [input_line(): pl.pallas_call(partial(input_kernel, mesh_axes), in_specs=[whole] * 4 + [...]
where the time goes in v13:
time: 599 us
  Pallas kernels  561 us (94%)
  local copies, waits for them, and re-layouts  18.5 us (3%)
  between operations  14.2 us (2%)
    pallas_call x1, Pallas kernels, middle(): pl.pallas_call(partial(middle_kernel, mesh_axes), in_specs=[remote, whole...  223 us
    pallas_call x1, Pallas kernels, output_line(): pl.pallas_call(partial(output_kernel, mesh_axes, head_count, lanes ** (-0...  180 us
    pallas_call x1, Pallas kernels, forward(): pl.pallas_call(partial(forward_kernel, mesh_axes, head_count, lanes ** (-...  74.9 us
    pallas_call x1, Pallas kernels, input_line(): pl.pallas_call(partial(input_kernel, mesh_axes), in_specs=[whole] * 4 + [...  72 us
    unnamed x24, local copies, waits for them, and re-layouts  13.8 us
  transfers between devices with their start and end apart: 1, of which 0 were waited for; matrix products, arithmetic and copies ran while one was open for 1% of the time, Pallas kernels for 44%

profile of v13, /device:TPU:0, one launch (start us, length us, event | category | flops | bytes accessed | tf_op | source)
XLA Modules:
  0.0 598.7 jit_solution(10691514398675650503)
XLA Ops:
  7.2 0.0 reduce-scatter.2.cloned.1.call-start
  7.2 1.3 convert_element_type.14
  8.5 74.9 %forward.1 = (bf16[1024,2048]{1,0:T(8,128)(2,1)}, f32[1024,2048]{1,0:T(8,128)}, bf16[2048,2048]{1,0:T(8,128)(2,1)}, bf16[2048,512]{1,0:T(8,128)(2,1)}, f32[1024,...) custom-call(bf16[1024,2048]{1,0:T(8,128)(2,1)} %bitcast.22, ...), custom_call_target="tpu_custom_call" | custom-call | flops 8589934592 | bytes 200000000 | tf_op jit(solution)/shard_map/forward/pallas_call | solution.py:1743
  83.4 222.6 %middle.1 = (bf16[1024,2048]{1,0:T(8,128)(2,1)}, bf16[1024,2048]{1,0:T(8,128)(2,1)}, f32[1,2048]{1,0:T(1,128)}, f32[512,2048]{1,0:T(8,128)}, bf16[1024,1408]{1,0...) custom-call(bf16[1024,2048]{1,0:T(8,128)(2,1)} %get-tuple-element.52, ...), custom_call_target="tpu_custom_call" | custom-call | flops 35433480192 | bytes 360000000 | tf_op jit(solution)/shard_map/middle/pallas_call | solution.py:709
  306.0 0.0 reduce-scatter.2.cloned.1.call-update
  306.0 179.8 %output_line.1 = (bf16[1024,2048]{1,0:T(8,128)(2,1)}, f32[1,128]{1,0:T(1,128)}, f32[1,512]{1,0:T(1,128)}, f32[512,2048]{1,0:T(8,128)}, bf16[2048,2560]{1,0:T(8,128)(2,1)}) custom-call(bf16[1024,2048]{1,0:T(8,128)(2,1)} %get-tuple-element.54.part, f32[512,2048]{1,0:T(8,128)} %get-tuple-element.55.residual, bf16[1024,512]{1,0:T(8,128)(2,1)} %get-tuple-element.56.gated_ref, ...), custom_call_target="tpu_custom_call" | custom-call | flops 25769803776 | bytes 360000000 | tf_op jit(solution)/shard_map/output_line/pallas_call | solution.py:1133
  485.8 0.0 copy-start.5
  485.8 0.0 copy-start.6
  485.8 0.0 copy-start.7
  485.9 72.0 %input_line.1 = (bf16[1024,2048]{1,0:T(8,128)(2,1)}, f32[1,2048]{1,0:T(1,128)}, f32[256,512]{1,0:T(8,128)}, f32[256,512]{1,0:T(8,128)}, f32[256,512]{1,0:T(8,128...) custom-call(f32[512,2048]{1,0:T(8,128)} %get-tuple-element.74.total_ref, bf16[1024,2048]{1,0:T(8,128)(2,1)} %bitcast.24, ...), custom_call_target="tpu_custom_call" | custom-call | flops 16777216 | bytes 360000000 | tf_op jit(solution)/shard_map/input_line/pallas_call | solution.py:1331
  557.9 0.0 copy-done.5
  557.9 0.0 copy-done.6
  557.9 0.0 copy-done.7
  557.9 0.7 select_maximum_fusion
  558.6 0.6 reshape.91.value
  559.3 11.2 %small_sum.1 = (f32[8,640]{1,0:T(8,128)}, f32[8,640]{1,0:T(8,128)}) custom-call(f32[8,640]{1,0:T(8,128)} %reshape.91.value), custom_call_target="tpu_custom_call" | custom-call | flops 40960 | bytes 20000000 | tf_op jit(solution)/shard_map/small_sum/pallas_call | solution.py:1861
  570.5 0.8 slice.35
  571.3 0.7 slice.31
  572.0 0.8 slice.33
  572.9 2.0 copy.32
  574.9 0.5 fusion
  575.5 0.6 constant_dynamic-slice_fusion.2
  576.0 0.6 constant_dynamic-slice_fusion
  576.6 0.0 reduce-scatter.2.cloned.1.call-done
  576.6 3.4 convert_bitcast_fusion
  580.0 1.5 copy.33
  581.6 0.0 copy-start
  581.6 4.9 copy.40
  586.5 0.0 copy-done
  586.5 0.0 copy-start.4
  586.5 0.0 copy-start.3
  586.5 0.0 copy-start.2
  586.5 0.0 copy-start.1
  586.5 2.1 copy.41
  588.7 0.0 copy-done.4
  588.7 0.8 copy.42
  589.4 0.0 copy-done.3
  589.5 0.8 copy.43
  590.2 0.0 copy-done.2
  590.2 0.8 copy.44
  591.0 0.0 copy-done.1
  591.0 0.8 copy.45
  (3 shorter events, 0.0 us)
Async XLA Ops:
  7.2 569.4 %reduce-scatter.2.cloned.1.call-start = ((), (), s32[]{:S(2)}) async-start(), calls=%async_computation.1 | async-start | bytes 19464192 | tf_op jit(solution)/shard_map/reduce_scatter | solution.py:1995
  485.8 72.1 %copy-start.5 = (f32[1,2048]{1,0:T(1,128)S(1)}, f32[1,2048]{1,0:T(1,128)}, u32[]{:S(2)}) copy-start(f32[1,2048]{1,0:T(1,128)} %get-tuple-element.79) | copy-start | bytes 24580
  485.8 72.1 %copy-start.6 = (f32[1,512]{1,0:T(1,128)S(1)}, f32[1,512]{1,0:T(1,128)}, u32[]{:S(2)}) copy-start(f32[1,512]{1,0:T(1,128)} %get-tuple-element.81) | copy-start | bytes 6148
  485.8 72.1 %copy-start.7 = (f32[1,128]{1,0:T(1,128)S(1)}, f32[1,128]{1,0:T(1,128)}, u32[]{:S(2)}) copy-start(f32[1,128]{1,0:T(1,128)} %get-tuple-element.80) | copy-start | bytes 1540
  581.6 4.9 copy-start
  586.5 2.1 copy-start.4
  586.5 2.9 copy-start.3
  586.5 3.7 copy-start.2
  586.5 4.5 copy-start.1
Sparse Core Ops, SparseCore 0:
  306.1 118.0 reduce-scatter.1

commit v14 on v13

--- a/solution.py
+++ b/solution.py
@@ -49,6 +49,7 @@
 
 
 CHUNK = 32
+QUIET, MANY = 6, 2
 LAG = 2
 MESH_ID = pl.DeviceIdType.MESH
 
@@ -422,13 +423,12 @@
 def middle_kernel(
     mesh_axes,
     mix_hbm,
-    cotangent_ref,
+    cotangent_hbm,
     input_hbm,
     gain_ref,
     gate_hbm,
     up_hbm,
     down_hbm,
-    normed_ref,
     out_ref,
     gain_grad,
     residual_hbm,
@@ -438,6 +438,8 @@
     feed_hbm,
     grad_hbm,
     grads_hbm,
+    normed_ref,
+    cotangent_ref,
     gate_w,
     up_w,
     down_w,
@@ -470,6 +472,8 @@
     part_load.start()
     input_load = pltpu.make_async_copy(input_hbm.at[own_half], inputs, input_sem.at[0])
     input_load.start()
+    cotangent_load = pltpu.make_async_copy(cotangent_hbm, cotangent_ref, input_sem.at[1])
+    cotangent_load.start()
     if padded > hidden_width:
         spare = slice(hidden_width, padded)
         gate_w[:, spare] = jnp.zeros((model_width, padded - hidden_width), BF16)
@@ -513,6 +517,7 @@
     mix_line.run(begin - 4, begin)
     gather.stage(2)
     gather.arrive()
+    cotangent_load.wait()
 
     def both(ref, group):
         first = pl.ds(pl.multiple_of(group * GROUP, GROUP), GROUP)
@@ -708,10 +713,9 @@
     group_rows = 2 * GROUP
     return pl.pallas_call(
         partial(middle_kernel, mesh_axes),
-        in_specs=[remote, whole, remote, whole, remote, remote, remote],
-        out_specs=[whole, whole, whole] + [remote] * 7,
+        in_specs=[remote, remote, remote, whole, remote, remote, remote],
+        out_specs=[whole, whole] + [remote] * 7,
         out_shape=[
-            jax.ShapeDtypeStruct((tokens, model_width), BF16),
             jax.ShapeDtypeStruct((tokens, model_width), BF16),
             jax.ShapeDtypeStruct((1, model_width), F32),
             jax.ShapeDtypeStruct((tokens // 2, model_width), F32),
@@ -723,6 +727,8 @@
             jax.ShapeDtypeStruct((model_width, 3 * hidden_width), BF16),
         ],
         scratch_shapes=[
+            pltpu.VMEM((tokens, model_width), BF16),
+            pltpu.VMEM((tokens, model_width), BF16),
             pltpu.VMEM((model_width, padded), BF16),
             pltpu.VMEM((model_width, padded), BF16),
             pltpu.VMEM((model_width, padded), BF16),
@@ -736,7 +742,7 @@
             pltpu.VMEM((2, group_rows, padded), BF16),
             pltpu.VMEM((2, group_rows, model_width), BF16),
             pltpu.SemaphoreType.DMA((1,)),
-            pltpu.SemaphoreType.DMA((1,)),
+            pltpu.SemaphoreType.DMA((2,)),
             pltpu.SemaphoreType.DMA((1,)),
             pltpu.SemaphoreType.DMA((2, 4, 2)),
             pltpu.SemaphoreType.DMA((1,)),
@@ -762,13 +768,6 @@
     mesh_axes,
     head_count,
     key_scale,
-    part,
-    residual,
-    gated_ref,
-    mix_grad_ref,
-    out_full,
-    lead_ref,
-    starts_ref,
     run_ref,
     carry_ref,
     decay_ref,
@@ -778,6 +777,13 @@
     keep_ref,
     flags_ref,
     gain_ref,
+    part_hbm,
+    residual_hbm,
+    gated_hbm,
+    mix_grad_hbm,
+    out_full_hbm,
+    lead_hbm,
+    starts_hbm,
     normed_hbm,
     pre_hbm,
     full_hbm,
@@ -787,6 +793,13 @@
     floor_grad,
     total_ref,
     mixer_grads_hbm,
+    part,
+    residual,
+    gated_ref,
+    mix_grad_ref,
+    out_full,
+    lead_ref,
+    starts_ref,
     arrived,
     back,
     back_arrived,
@@ -815,15 +828,32 @@
     *sems,
 ):
     tokens, model_width = left.shape
-    width = gated_ref.shape[1]
+    width = gated_hbm.shape[1]
     lanes = width // head_count
     state_rows = head_count * lanes
     tiles, blocks = model_width // TILE, tokens // BLOCK
     piece_rows = 2 * BLOCK
     context, context_size = lax.axis_index("context"), lax.axis_size("context")
 
-    left_load = pltpu.make_async_copy(normed_hbm, left, load_sem.at[0])
-    left_load.start()
+    loads = [
+        pltpu.make_async_copy(source, target, load_sem.at[which])
+        for which, (source, target) in enumerate(
+            (
+                (part_hbm, part),
+                (out_full_hbm, out_full),
+                (mix_grad_hbm, mix_grad_ref),
+                (lead_hbm, lead_ref),
+                (residual_hbm, residual),
+                (starts_hbm, starts_ref),
+                (gated_hbm, gated_ref),
+                (normed_hbm, left),
+            )
+        )
+    ]
+    part_load, *gate_loads = loads[:5]
+    starts_load, *tile_loads = loads[5:]
+    for load in loads:
+        load.start()
 
     def piece_loads(index):
         rows = pl.ds(pl.multiple_of(index * piece_rows, piece_rows), piece_rows)
@@ -1064,6 +1094,11 @@
     end_time = tile_time + tiles
 
     def piece(time):
+        @pl.when(time == 0)
+        def _():
+            for load in gate_loads:
+                load.wait()
+
         @pl.when(time < send_time)
         def _():
             gate_piece(time)
@@ -1074,6 +1109,7 @@
 
         @pl.when(time == block_time)
         def _():
+            starts_load.wait()
             take_back()
 
         @pl.when(jnp.logical_and(time >= block_time, time < back_time))
@@ -1090,14 +1126,17 @@
 
         @pl.when(time == tile_time)
         def _():
-            left_load.wait()
+            for load in tile_loads:
+                load.wait()
 
         @pl.when(jnp.logical_and(time >= tile_time, time < end_time))
         def _():
             mixer_tile(time - tile_time)
 
-    begin = -(-tile_time // 2)
-    steps = max(line.steps, begin + back_line.steps, -(-end_time // 2))
+    slow = QUIET
+    part_load.wait()
+    begin = slow + -(-(tile_time - slow) // MANY)
+    steps = max(line.steps, begin + back_line.steps, slow + -(-(end_time - slow) // MANY))
 
     def body(time, _):
         @pl.when(time < line.steps)
@@ -1108,11 +1147,12 @@
         def _():
             back_line.step(time - begin)
 
-        def pieces(offset, _):
-            piece(2 * time + offset)
+        def pieces(index, _):
+            piece(index)
             return 0
 
-        lax.fori_loop(0, 2, pieces, 0)
+        first = jnp.where(time < slow, time, slow + MANY * (time - slow))
+        lax.fori_loop(first, first + jnp.where(time < slow, 1, MANY), pieces, 0)
         return 0
 
     lax.fori_loop(0, steps, body, 0)
@@ -1122,7 +1162,7 @@
 
 
 def output_line(mesh_axes, collective, in_vmem, in_hbm, head_count):
-    part, _, gated = in_vmem[:3]
+    part, residual, gated, mix_grad, out_full, lead, starts = in_hbm[:7]
     tokens, model_width = part.shape
     width = gated.shape[1]
     lanes = width // head_count
@@ -1142,6 +1182,10 @@
             jax.ShapeDtypeStruct((model_width, 5 * width), BF16),
         ],
         scratch_shapes=[
+            pltpu.VMEM(array.shape, array.dtype)
+            for array in (part, residual, gated, mix_grad, out_full, lead, starts)
+        ]
+        + [
             pltpu.VMEM((tokens, model_width), BF16),
             pltpu.VMEM((tokens, model_width), BF16),
             pltpu.VMEM((tokens, model_width), BF16),
@@ -1160,7 +1204,7 @@
             pltpu.VMEM((BLOCK, width), F32),
             pltpu.VMEM((BLOCK, width), F32),
             pltpu.VMEM((1, width), F32),
-            pltpu.SemaphoreType.DMA((1,)),
+            pltpu.SemaphoreType.DMA((8,)),
             pltpu.SemaphoreType.DMA((2, 2)),
             pltpu.SemaphoreType.DMA((2,)),
             pltpu.SemaphoreType.DMA((2,)),
@@ -1184,10 +1228,10 @@
 
 def input_kernel(
     mesh_axes,
-    total_ref,
-    hidden_ref,
-    residual_grad,
     gain_ref,
+    total_hbm,
+    hidden_hbm,
+    residual_hbm,
     grads_hbm,
     out_ref,
     gain_grad,
@@ -1196,9 +1240,13 @@
     share_input,
     share_gate,
     share_out,
+    total_ref,
+    hidden_ref,
+    residual_grad,
     own,
     other,
     remote,
+    quarter_sem,
     load_sem,
     pair_send,
     pair_recv,
@@ -1210,10 +1258,36 @@
     chips = plane.chips
     block = own.shape[1]
     gain_grad[...] = jnp.zeros_like(gain_grad)
+    half, line_size = total_ref.shape[0], lax.axis_size("tensor")
+    place = lax.axis_index("tensor")
+    at_end = jnp.logical_or(place == 0, place == line_size - 1)
+    first_row = jnp.where(place == 0, 0, half)
+    quarters = 4
+    length = half // quarters
+
+    def quarter_loads(index):
+        rows = pl.ds(pl.multiple_of(index * length, length), length)
+        inputs = pl.ds(pl.multiple_of(first_row + index * length, length), length)
+        return [
+            pltpu.make_async_copy(source, target.at[rows], quarter_sem.at[which, index])
+            for which, (source, target) in enumerate(
+                (
+                    (total_hbm.at[rows], total_ref),
+                    (hidden_hbm.at[inputs], hidden_ref),
+                    (residual_hbm.at[rows], residual_grad),
+                )
+            )
+        ]
+
+    @pl.when(at_end)
+    def _():
+        for index in range(quarters):
+            for load in quarter_loads(index):
+                load.start()
 
     def turn(total, rows, own_rows):
         total = total_ref[own_rows]
-        values = hidden_ref[rows].astype(F32)
+        values = hidden_ref[own_rows].astype(F32)
         inverse = inverse_rms(values)
         unit = values * inverse
         gain_grad[...] += jnp.sum(total * unit, axis=0, keepdims=True)
@@ -1284,7 +1358,20 @@
         def _():
             chip_copy(slot).start()
 
-    line.run(0, line.steps, combine)
+    def step(time, _):
+        index = time * CHUNK // length
+        fresh = jnp.logical_and(lax.rem(time * CHUNK, length) == 0, index < quarters)
+
+        @pl.when(jnp.logical_and(at_end, fresh))
+        def _():
+            for load in quarter_loads(index):
+                load.wait()
+
+        line.step(time)
+        combine(time)
+        return 0
+
+    lax.fori_loop(0, line.steps, step, 0)
 
     def arrive(index, _):
         chip_copy(index).wait_recv()
@@ -1330,7 +1417,7 @@
     whole = pl.BlockSpec(memory_space=pltpu.VMEM)
     return pl.pallas_call(
         partial(input_kernel, mesh_axes),
-        in_specs=[whole] * 4 + [pl.BlockSpec(memory_space=pl.ANY)],
+        in_specs=[whole] + [pl.BlockSpec(memory_space=pl.ANY)] * 4,
         out_specs=[whole] * 7,
         out_shape=[
             jax.ShapeDtypeStruct((tokens, model_width), BF16),
@@ -1338,9 +1425,13 @@
         ]
         + [jax.ShapeDtypeStruct((block, all_width // 5), F32)] * 5,
         scratch_shapes=[
+            pltpu.VMEM((tokens // 2, model_width), F32),
+            pltpu.VMEM((tokens // 2, model_width), BF16),
+            pltpu.VMEM((tokens // 2, model_width), F32),
             pltpu.VMEM((chips, block, all_width), BF16),
             pltpu.VMEM((chips, block, all_width), BF16),
             pltpu.VMEM((chips - 1, block, all_width), BF16),
+            pltpu.SemaphoreType.DMA((3, 4)),
             pltpu.SemaphoreType.DMA((chips,)),
             pltpu.SemaphoreType.DMA((chips,)),
             pltpu.SemaphoreType.DMA((chips,)),
@@ -1355,7 +1446,7 @@
             flops=tokens * model_width * 8, bytes_accessed=360_000_000, transcendentals=0
         ),
         name="input_line",
-    )(total, hidden, residual_grad, gain, grads)
+    )(gain, total, hidden, residual_grad, grads)
 
 
 def forward_kernel(
@@ -1941,7 +2032,6 @@
     )
     grad_rows = out_grad.reshape(tokens, model_width)
     (
-        _,
         grad_mix_low,
         grad_norm_two,
         residual,
@@ -1972,13 +2062,6 @@
         mesh_axes,
         1,
         (
-            feed_part,
-            residual,
-            gated_low,
-            grad_mix_low,
-            out_full,
-            lead,
-            starts,
             runs,
             carry,
             decay,
@@ -1989,7 +2072,19 @@
             flags,
             gain_row,
         ),
-        (normed_one, pre, mixer_full, mixed),
+        (
+            feed_part,
+            residual,
+            gated_low,
+            grad_mix_low,
+            out_full,
+            lead,
+            starts,
+            normed_one,
+            pre,
+            mixer_full,
+            mixed,
+        ),
         head_count,
     )
     share_ffn = lax.psum_scatter(grads_ffn, both, scatter_dimension=0, tiled=True)

time: 599 us -> 588 us (0.982)
  Pallas kernels: 561 us -> 549 us
    pallas_call x1, Pallas kernels: 180 us -> 173 us  [output_line(): pl.pallas_call(partial(output_kernel, mesh_axes, head_count, lanes ** (-0...]
  transfers between devices with their start and end apart: 1 -> 1, of which waited for: 0 -> 0; matrix products, arithmetic and copies ran while one was open for 1% -> 1% of each run, Pallas kernels for 44% -> 43%
where the time goes in v14:
time: 588 us
  Pallas kernels  549 us (93%)
  local copies, waits for them, and re-layouts  18.5 us (3%)
  between operations  14.2 us (2%)
    pallas_call x1, Pallas kernels, middle(): pl.pallas_call(partial(middle_kernel, mesh_axes), in_specs=[remote, remot...  220 us
    pallas_call x1, Pallas kernels, output_line(): pl.pallas_call(partial(output_kernel, mesh_axes, head_count, lanes ** (-0...  173 us
    pallas_call x1, Pallas kernels, forward(): pl.pallas_call(partial(forward_kernel, mesh_axes, head_count, lanes ** (-...  74.9 us
    pallas_call x1, Pallas kernels, input_line(): pl.pallas_call(partial(input_kernel, mesh_axes), in_specs=[whole] + [pl.B...  71.4 us
    unnamed x24, local copies, waits for them, and re-layouts  13.8 us
  transfers between devices with their start and end apart: 1, of which 0 were waited for; matrix products, arithmetic and copies ran while one was open for 1% of the time, Pallas kernels for 43%

profile of v14, /device:TPU:0, one launch (start us, length us, event | category | flops | bytes accessed | tf_op | source)
XLA Modules:
  0.0 587.7 jit_solution(11634323689051994269)
XLA Ops:
  7.2 0.0 reduce-scatter.2.cloned.1.call-start
  7.2 1.3 convert_element_type.14
  8.5 74.9 %forward.1 = (bf16[1024,2048]{1,0:T(8,128)(2,1)}, f32[1024,2048]{1,0:T(8,128)}, bf16[2048,2048]{1,0:T(8,128)(2,1)}, bf16[2048,512]{1,0:T(8,128)(2,1)}, f32[1024,...) custom-call(bf16[1024,2048]{1,0:T(8,128)(2,1)} %bitcast.22, ...), custom_call_target="tpu_custom_call" | custom-call | flops 8589934592 | bytes 200000000 | tf_op jit(solution)/shard_map/forward/pallas_call | solution.py:1834
  83.4 219.6 %middle.1 = (bf16[1024,2048]{1,0:T(8,128)(2,1)}, f32[1,2048]{1,0:T(1,128)}, f32[512,2048]{1,0:T(8,128)}, bf16[1024,1408]{1,0:T(8,128)(2,1)}, bf16[1024,1408]{1,0...) custom-call(bf16[1024,2048]{1,0:T(8,128)(2,1)} %get-tuple-element.60, ...), custom_call_target="tpu_custom_call" | custom-call | flops 35433480192 | bytes 360000000 | tf_op jit(solution)/shard_map/middle/pallas_call | solution.py:714
  303.1 0.0 reduce-scatter.2.cloned.1.call-update
  303.1 172.9 %output_line.1 = (bf16[1024,2048]{1,0:T(8,128)(2,1)}, f32[1,128]{1,0:T(1,128)}, f32[1,512]{1,0:T(1,128)}, f32[512,2048]{1,0:T(8,128)}, bf16[2048,2560]{1,0:T(8,128)(2,1)}) custom-call(f32[8,1,512]{2,1,0:T(1,128)} %get-tuple-element.52.run_ref, f32[4,128,128]{2,1,0:T(8,128)} %get-tuple-element.53.carry_ref, f32[4,1,128]{2,1,0:T(1,128)} %get-tuple-element.54.decay_ref, ...), custom_call_target="tpu_custom_call" | custom-call | flops 25769803776 | bytes 360000000 | tf_op jit(solution)/shard_map/output_line/pallas_call | solution.py:1173
  476.0 0.0 copy-start.5
  476.0 0.0 copy-start.6
  476.0 0.0 copy-start.7
  476.0 71.4 %input_line.1 = (bf16[1024,2048]{1,0:T(8,128)(2,1)}, f32[1,2048]{1,0:T(1,128)}, f32[256,512]{1,0:T(8,128)}, f32[256,512]{1,0:T(8,128)}, f32[256,512]{1,0:T(8,128...) custom-call(f32[1,2048]{1,0:T(1,128)} %bitcast.27, f32[512,2048]{1,0:T(8,128)} %get-tuple-element.74.total_hbm, ...), custom_call_target="tpu_custom_call" | custom-call | flops 16777216 | bytes 360000000 | tf_op jit(solution)/shard_map/input_line/pallas_call | solution.py:1418
  547.4 0.0 copy-done.5
  547.4 0.0 copy-done.6
  547.4 0.0 copy-done.7
  547.5 0.7 select_maximum_fusion
  548.2 0.6 reshape.91.value
  548.8 10.7 %small_sum.1 = (f32[8,640]{1,0:T(8,128)}, f32[8,640]{1,0:T(8,128)}) custom-call(f32[8,640]{1,0:T(8,128)} %reshape.91.value), custom_call_target="tpu_custom_call" | custom-call | flops 40960 | bytes 20000000 | tf_op jit(solution)/shard_map/small_sum/pallas_call | solution.py:1952
  559.5 0.8 slice.35
  560.3 0.7 slice.31
  561.0 0.8 slice.33
  561.9 2.0 copy.32
  563.9 0.5 fusion
  564.4 0.6 constant_dynamic-slice_fusion.2
  565.0 0.6 constant_dynamic-slice_fusion
  565.6 0.0 reduce-scatter.2.cloned.1.call-done
  565.6 3.4 convert_bitcast_fusion
  569.0 1.5 copy.33
  570.5 0.0 copy-start
  570.6 4.9 copy.40
  575.5 0.0 copy-done
  575.5 0.0 copy-start.4
  575.5 0.0 copy-start.3
  575.5 0.0 copy-start.2
  575.5 0.0 copy-start.1
  575.5 2.1 copy.41
  577.6 0.0 copy-done.4
  577.6 0.8 copy.42
  578.4 0.0 copy-done.3
  578.4 0.8 copy.43
  579.2 0.0 copy-done.2
  579.2 0.8 copy.44
  580.0 0.0 copy-done.1
  580.0 0.8 copy.45
  (3 shorter events, 0.0 us)
Async XLA Ops:
  7.2 558.4 %reduce-scatter.2.cloned.1.call-start = ((), (), s32[]{:S(2)}) async-start(), calls=%async_computation.1 | async-start | bytes 19464192 | tf_op jit(solution)/shard_map/reduce_scatter | solution.py:2090
  476.0 71.4 %copy-start.5 = (f32[1,2048]{1,0:T(1,128)S(1)}, f32[1,2048]{1,0:T(1,128)}, u32[]{:S(2)}) copy-start(f32[1,2048]{1,0:T(1,128)} %get-tuple-element.79) | copy-start | bytes 24580
  476.0 71.4 %copy-start.6 = (f32[1,512]{1,0:T(1,128)S(1)}, f32[1,512]{1,0:T(1,128)}, u32[]{:S(2)}) copy-start(f32[1,512]{1,0:T(1,128)} %get-tuple-element.81) | copy-start | bytes 6148
  476.0 71.4 %copy-start.7 = (f32[1,128]{1,0:T(1,128)S(1)}, f32[1,128]{1,0:T(1,128)}, u32[]{:S(2)}) copy-start(f32[1,128]{1,0:T(1,128)} %get-tuple-element.80) | copy-start | bytes 1540
  570.5 4.9 copy-start
  575.5 2.1 copy-start.4
  575.5 2.9 copy-start.3
  575.5 3.7 copy-start.2
  575.5 4.5 copy-start.1
Sparse Core Ops, SparseCore 0:
  303.2 118.1 reduce-scatter.1

commit v15 on v14

--- a/solution.py
+++ b/solution.py
@@ -509,7 +509,7 @@
     part_load.wait()
     input_load.wait()
     pace = GROUP // CHUNK
-    begin = pace + 2 * LAG * (line_size - 1) + 4
+    begin = pace + 2 * LAG * (line_size - 1) + 2
     mix_line.run(0, begin - 10)
     gather.stage(0)
     mix_line.run(begin - 10, begin - 4)
@@ -1226,15 +1226,96 @@
     )(*in_vmem, *in_hbm)
 
 
+class SmallSum:
+    def __init__(self, mesh_axes, value, local, total, near, far, sems):
+        self.mesh_axes = mesh_axes
+        self.value, self.local, self.total, self.near, self.far = value, local, total, near, far
+        self.near_send, self.near_recv, self.far_send, self.far_recv = sems
+        self.context_size = lax.axis_size("context")
+        self.group = lax.axis_size("shard") * self.context_size
+        self.line_size = lax.axis_size("tensor")
+        self.place = lax.axis_index("shard") * self.context_size + lax.axis_index("context")
+        self.line_place = lax.axis_index("tensor")
+
+    def device(self, position, line_position):
+        places = {
+            "shard": position // self.context_size,
+            "context": lax.rem(position, self.context_size),
+            "tensor": line_position,
+        }
+        return tuple(places[axis] for axis in self.mesh_axes)
+
+    def near_target(self, step):
+        return self.device(lax.rem(self.place + step, self.group), self.line_place)
+
+    def far_target(self, step):
+        return self.device(self.place, lax.rem(self.line_place + step, self.line_size))
+
+    def near_copy(self, step):
+        return pltpu.make_async_remote_copy(
+            self.value,
+            self.near.at[step - 1],
+            self.near_send.at[step - 1],
+            self.near_recv.at[step - 1],
+            device_id=self.near_target(step),
+            device_id_type=MESH_ID,
+        )
+
+    def far_copy(self, step):
+        return pltpu.make_async_remote_copy(
+            self.local,
+            self.far.at[step - 1],
+            self.far_send.at[step - 1],
+            self.far_recv.at[step - 1],
+            device_id=self.far_target(step),
+            device_id_type=MESH_ID,
+        )
+
+    def greet(self, barrier):
+        targets = [self.near_target(step) for step in range(1, self.group)]
+        targets += [self.far_target(step) for step in range(1, self.line_size)]
+        for target in targets:
+            pl.semaphore_signal(barrier, inc=1, device_id=target, device_id_type=MESH_ID)
+        return len(targets)
+
+    def start(self):
+        for step in range(1, self.group):
+            self.near_copy(step).start()
+
+    def pass_on(self):
+        total = self.value[...]
+        for step in range(1, self.group):
+            self.near_copy(step).wait_recv()
+            total = total + self.near[step - 1]
+        self.local[...] = total
+        for step in range(1, self.line_size):
+            self.far_copy(step).start()
+
+    def finish(self):
+        total = self.local[...]
+        for step in range(1, self.line_size):
+            self.far_copy(step).wait_recv()
+            total = total + self.far[step - 1]
+        self.total[...] = total
+        for step in range(1, self.group):
+            self.near_copy(step).wait_send()
+        for step in range(1, self.line_size):
+            self.far_copy(step).wait_send()
+
+
 def input_kernel(
     mesh_axes,
     gain_ref,
+    norm_two_ref,
+    head_ref,
+    floor_ref,
     total_hbm,
     hidden_hbm,
     residual_hbm,
     grads_hbm,
     out_ref,
-    gain_grad,
+    small_local,
+    small_total,
     share_query,
     share_forget,
     share_input,
@@ -1246,6 +1327,10 @@
     own,
     other,
     remote,
+    gain_grad,
+    small,
+    small_near,
+    small_far,
     quarter_sem,
     load_sem,
     pair_send,
@@ -1296,9 +1381,12 @@
         grad = residual_grad[own_rows] + inverse * (lifted - unit * mean)
         out_ref[rows] = grad.astype(BF16)
 
-    line = Line(mesh_axes, None, None, out_ref, sems, turn, sums=False)
+    line = Line(mesh_axes, None, None, out_ref, sems[:2], turn, sums=False)
+    small_sum = SmallSum(
+        mesh_axes, small, small_local, small_total, small_near, small_far, sems[2:]
+    )
     barrier = pltpu.get_barrier_semaphore()
-    expected = line.greet(barrier) + plane.greet(barrier)
+    expected = line.greet(barrier) + plane.greet(barrier) + small_sum.greet(barrier)
     pl.semaphore_wait(barrier, expected)
 
     def rows_of(slot, core):
@@ -1372,6 +1460,13 @@
         return 0
 
     lax.fori_loop(0, line.steps, step, 0)
+    small[...] = jnp.zeros_like(small)
+    row = 0
+    for ref in (gain_grad, norm_two_ref, head_ref, floor_ref):
+        for first in range(0, ref.shape[1], 128):
+            small[row : row + 1] = ref[:, first : first + 128]
+            row += 1
+    small_sum.start()
 
     def arrive(index, _):
         chip_copy(index).wait_recv()
@@ -1393,7 +1488,9 @@
             share[rows] = lax.fori_loop(0, chips - 1, add, own[0, rows, columns].astype(F32))
         return 0
 
+    small_sum.pass_on()
     lax.fori_loop(0, block // strip, total, 0)
+    small_sum.finish()
 
     def sent(index, _):
         pair_copy(index).wait_send()
@@ -1409,19 +1506,23 @@
     line.finish()
 
 
-def input_line(mesh_axes, collective, total, hidden, residual_grad, gain, grads):
+def input_line(mesh_axes, collective, total, hidden, residual_grad, gain, grads, small):
     tokens, model_width = hidden.shape
     all_width = grads.shape[1]
     chips = lax.axis_size("shard") * lax.axis_size("context") // 2
     block = model_width // (2 * chips)
+    values = model_width + sum(value.shape[1] for value in small)
+    small_shape = (-(-values // 1024) * 8, 128)
+    group, line_size = 2 * chips, lax.axis_size("tensor")
     whole = pl.BlockSpec(memory_space=pltpu.VMEM)
     return pl.pallas_call(
         partial(input_kernel, mesh_axes),
-        in_specs=[whole] + [pl.BlockSpec(memory_space=pl.ANY)] * 4,
-        out_specs=[whole] * 7,
+        in_specs=[whole] * 4 + [pl.BlockSpec(memory_space=pl.ANY)] * 4,
+        out_specs=[whole] * 8,
         out_shape=[
             jax.ShapeDtypeStruct((tokens, model_width), BF16),
-            jax.ShapeDtypeStruct((1, model_width), F32),
+            jax.ShapeDtypeStruct(small_shape, F32),
+            jax.ShapeDtypeStruct(small_shape, F32),
         ]
         + [jax.ShapeDtypeStruct((block, all_width // 5), F32)] * 5,
         scratch_shapes=[
@@ -1431,6 +1532,10 @@
             pltpu.VMEM((chips, block, all_width), BF16),
             pltpu.VMEM((chips, block, all_width), BF16),
             pltpu.VMEM((chips - 1, block, all_width), BF16),
+            pltpu.VMEM((1, model_width), F32),
+            pltpu.VMEM(small_shape, F32),
+            pltpu.VMEM((group - 1, *small_shape), F32),
+            pltpu.VMEM((line_size - 1, *small_shape), F32),
             pltpu.SemaphoreType.DMA((3, 4)),
             pltpu.SemaphoreType.DMA((chips,)),
             pltpu.SemaphoreType.DMA((chips,)),
@@ -1438,7 +1543,13 @@
             pltpu.SemaphoreType.DMA((chips - 1,)),
             pltpu.SemaphoreType.DMA((chips - 1,)),
         ]
-        + line_sems(tokens, 2),
+        + line_sems(tokens, 2)
+        + [
+            pltpu.SemaphoreType.DMA((group - 1,)),
+            pltpu.SemaphoreType.DMA((group - 1,)),
+            pltpu.SemaphoreType.DMA((line_size - 1,)),
+            pltpu.SemaphoreType.DMA((line_size - 1,)),
+        ],
         compiler_params=pltpu.CompilerParams(
             collective_id=collective, has_side_effects=True, vmem_limit_bytes=58 << 20
         ),
@@ -1446,7 +1557,7 @@
             flops=tokens * model_width * 8, bytes_accessed=360_000_000, transcendentals=0
         ),
         name="input_line",
-    )(gain, total, hidden, residual_grad, grads)
+    )(gain, *small, total, hidden, residual_grad, grads)
 
 
 def forward_kernel(
@@ -1872,103 +1983,6 @@
         ),
         name="forward",
     )(hidden, gain, *shards, out_shard, down_shard, floor, segments, head_gain)
-
-
-def small_sum_kernel(
-    mesh_axes, value, local_ref, total_ref, near, far, near_send, near_recv, far_send, far_recv
-):
-    shard_size, context_size = lax.axis_size("shard"), lax.axis_size("context")
-    line_size = lax.axis_size("tensor")
-    group = shard_size * context_size
-    place = lax.axis_index("shard") * context_size + lax.axis_index("context")
-    line_place = lax.axis_index("tensor")
-
-    def device(position, line_position):
-        places = {
-            "shard": position // context_size,
-            "context": lax.rem(position, context_size),
-            "tensor": line_position,
-        }
-        return tuple(places[axis] for axis in mesh_axes)
-
-    def near_target(step):
-        return device(lax.rem(place + step, group), line_place)
-
-    def far_target(step):
-        return device(place, lax.rem(line_place + step, line_size))
-
-    def near_copy(step):
-        return pltpu.make_async_remote_copy(
-            value,
-            near.at[step - 1],
-            near_send.at[step - 1],
-            near_recv.at[step - 1],
-            device_id=near_target(step),
-            device_id_type=MESH_ID,
-        )
-
-    def far_copy(step):
-        return pltpu.make_async_remote_copy(
-            local_ref,
-            far.at[step - 1],
-            far_send.at[step - 1],
-            far_recv.at[step - 1],
-            device_id=far_target(step),
-            device_id_type=MESH_ID,
-        )
-
-    barrier = pltpu.get_barrier_semaphore()
-    for step in range(1, group):
-        pl.semaphore_signal(barrier, inc=1, device_id=near_target(step), device_id_type=MESH_ID)
-    for step in range(1, line_size):
-        pl.semaphore_signal(barrier, inc=1, device_id=far_target(step), device_id_type=MESH_ID)
-    pl.semaphore_wait(barrier, group + line_size - 2)
-    for step in range(1, group):
-        near_copy(step).start()
-    total = value[...]
-    for step in range(1, group):
-        near_copy(step).wait_recv()
-        total = total + near[step - 1]
-    local_ref[...] = total
-    for step in range(1, line_size):
-        far_copy(step).start()
-    for step in range(1, line_size):
-        far_copy(step).wait_recv()
-        total = total + far[step - 1]
-    total_ref[...] = total
-    for step in range(1, group):
-        near_copy(step).wait_send()
-    for step in range(1, line_size):
-        far_copy(step).wait_send()
-
-
-def small_sum(mesh_axes, collective, values):
-    flat = jnp.concatenate([value.reshape(-1) for value in values])
-    lanes = -(-flat.shape[0] // 1024) * 128
-    flat = jnp.pad(flat, (0, 8 * lanes - flat.shape[0])).reshape(8, lanes)
-    group = lax.axis_size("shard") * lax.axis_size("context")
-    line_size = lax.axis_size("tensor")
-    whole = pl.BlockSpec(memory_space=pltpu.VMEM)
-    local, total = pl.pallas_call(
-        partial(small_sum_kernel, mesh_axes),
-        in_specs=[whole],
-        out_specs=[whole] * 2,
-        out_shape=[jax.ShapeDtypeStruct((8, lanes), F32)] * 2,
-        scratch_shapes=[
-            pltpu.VMEM((group - 1, 8, lanes), F32),
-            pltpu.VMEM((line_size - 1, 8, lanes), F32),
-            pltpu.SemaphoreType.DMA((group - 1,)),
-            pltpu.SemaphoreType.DMA((group - 1,)),
-            pltpu.SemaphoreType.DMA((line_size - 1,)),
-            pltpu.SemaphoreType.DMA((line_size - 1,)),
-        ],
-        compiler_params=pltpu.CompilerParams(collective_id=collective, has_side_effects=True),
-        cost_estimate=pl.CostEstimate(
-            flops=8 * lanes * group, bytes_accessed=20_000_000, transcendentals=0
-        ),
-        name="small_sum",
-    )(flat)
-    return local.reshape(-1), total.reshape(-1)
 
 
 def local(
@@ -2093,31 +2107,37 @@
     def ffn_share(which):
         return share_ffn[:, which * hidden_width : (which + 1) * hidden_width].astype(F32)
 
-    input_rows, grad_norm_one, *mixer_shares, share_out = input_line(
-        mesh_axes, 3, back_one, hidden_rows, grad_residual, gain_one, grads_mixer
+    input_rows, near, total, *mixer_shares, share_out = input_line(
+        mesh_axes,
+        3,
+        back_one,
+        hidden_rows,
+        grad_residual,
+        gain_one,
+        grads_mixer,
+        (grad_norm_two, grad_head_part, grad_floor_part),
     )
-    near, total = small_sum(
-        mesh_axes, 5, (grad_norm_one, grad_norm_two, grad_head_part, grad_floor_part)
-    )
+    near, total = near.reshape(-1), total.reshape(-1)
     shares = lax.axis_size("shard") * lax.axis_size("context")
     position = lax.axis_index("shard") * lax.axis_size("context") + lax.axis_index("context")
 
-    def own_slice(values, first, length):
-        values = values[first : first + length].reshape(shares, length // shares)
-        return lax.dynamic_index_in_dim(values, position, 0, False)
-
-    floor_total = near[2 * model_width + key_dim : 2 * model_width + key_dim + width]
-    floor_total = floor_total.reshape(head_count, shares, key_dim // shares)
+    def own_slice(first, length):
+        length = length // shares
+        return lax.dynamic_slice_in_dim(total, first + position * length, length, 0)
+
+    first = 2 * model_width + key_dim
+    floor_total = near[first : first + width].reshape(head_count, key_dim)
+    floor_part = key_dim // shares
 
     return (
         output_rows.reshape(hidden.shape),
         input_rows.reshape(hidden.shape),
-        own_slice(total, 0, model_width),
+        own_slice(0, model_width),
         *mixer_shares,
-        lax.dynamic_index_in_dim(floor_total, position, 1, False),
-        own_slice(total, 2 * model_width, key_dim),
+        lax.dynamic_slice_in_dim(floor_total, position * floor_part, floor_part, 1),
+        own_slice(2 * model_width, key_dim),
         share_out.T,
-        own_slice(total, model_width, model_width),
+        own_slice(model_width, model_width),
         ffn_share(0),
         ffn_share(1),
         ffn_share(2).T,

time: 588 us -> 576 us (0.980)
  Pallas kernels: 549 us -> 539 us
    pallas_call x2 -> x1, Pallas kernels: 82.1 us -> 80.8 us  [input_line(): pl.pallas_call(partial(input_kernel, mesh_axes), in_specs=[whole] * 4 + [...]
    unnamed x24 -> x18, local copies, waits for them, and re-layouts: 13.8 us -> 13.8 us
where the time goes in v15:
time: 576 us; the launch traced here: 575 us
  Pallas kernels  539 us (94%)
  local copies, waits for them, and re-layouts  17.7 us (3%)
  between operations  14.1 us (2%)
    pallas_call x1, Pallas kernels, middle(): pl.pallas_call(partial(middle_kernel, mesh_axes), in_specs=[remote, remot...  216 us
    pallas_call x1, Pallas kernels, output_line(): pl.pallas_call(partial(output_kernel, mesh_axes, head_count, lanes ** (-0...  167 us
    pallas_call x1, Pallas kernels, input_line(): pl.pallas_call(partial(input_kernel, mesh_axes), in_specs=[whole] * 4 + [...  80.8 us
    pallas_call x1, Pallas kernels, forward(): pl.pallas_call(partial(forward_kernel, mesh_axes, head_count, lanes ** (-...  74.8 us
    unnamed x18, local copies, waits for them, and re-layouts  13.8 us
  transfers between devices with their start and end apart: 1, of which 0 were waited for; matrix products, arithmetic and copies ran while one was open for 1% of the time, Pallas kernels for 43%

profile of v15, /device:TPU:0, one launch (start us, length us, event | category | flops | bytes accessed | tf_op | source)
XLA Modules:
  0.0 575.4 jit_solution(16588275249412873785)
XLA Ops:
  7.2 0.0 reduce-scatter.2.cloned.1.call-start
  7.2 1.3 convert_element_type.12
  8.5 74.8 %forward.1 = (bf16[1024,2048]{1,0:T(8,128)(2,1)}, f32[1024,2048]{1,0:T(8,128)}, bf16[2048,2048]{1,0:T(8,128)(2,1)}, bf16[2048,512]{1,0:T(8,128)(2,1)}, f32[1024,...) custom-call(bf16[1024,2048]{1,0:T(8,128)(2,1)} %bitcast.14, ...), custom_call_target="tpu_custom_call" | custom-call | flops 8589934592 | bytes 200000000 | tf_op jit(solution)/shard_map/forward/pallas_call | solution.py:1945
  83.3 216.0 %middle.1 = (bf16[1024,2048]{1,0:T(8,128)(2,1)}, f32[1,2048]{1,0:T(1,128)}, f32[512,2048]{1,0:T(8,128)}, bf16[1024,1408]{1,0:T(8,128)(2,1)}, bf16[1024,1408]{1,0...) custom-call(bf16[1024,2048]{1,0:T(8,128)(2,1)} %get-tuple-element.59, ...), custom_call_target="tpu_custom_call" | custom-call | flops 35433480192 | bytes 360000000 | tf_op jit(solution)/shard_map/middle/pallas_call | solution.py:714
  299.3 0.0 reduce-scatter.2.cloned.1.call-update
  299.3 167.3 %output_line.1 = (bf16[1024,2048]{1,0:T(8,128)(2,1)}, f32[1,128]{1,0:T(1,128)}, f32[1,512]{1,0:T(1,128)}, f32[512,2048]{1,0:T(8,128)}, bf16[2048,2560]{1,0:T(8,128)(2,1)}) custom-call(f32[8,1,512]{2,1,0:T(1,128)} %get-tuple-element.51.run_ref, f32[4,128,128]{2,1,0:T(8,128)} %get-tuple-element.52.carry_ref, f32[4,1,128]{2,1,0:T(1,128)} %get-tuple-element.53.decay_ref, ...), custom_call_target="tpu_custom_call" | custom-call | flops 25769803776 | bytes 360000000 | tf_op jit(solution)/shard_map/output_line/pallas_call | solution.py:1173
  466.6 80.8 %input_line.1 = (bf16[1024,2048]{1,0:T(8,128)(2,1)}, f32[40,128]{1,0:T(8,128)}, f32[40,128]{1,0:T(8,128)}, f32[256,512]{1,0:T(8,128)}, f32[256,512]{1,0:T(8,128)...) custom-call(f32[1,2048]{1,0:T(1,128)} %bitcast.19, f32[1,2048]{1,0:T(1,128)} %get-tuple-element.73.norm_two_ref, ...), custom_call_target="tpu_custom_call" | custom-call | flops 16777216 | bytes 360000000 | tf_op jit(solution)/shard_map/input_line/pallas_call | solution.py:1518
  547.4 2.0 copy.29
  549.5 0.7 slice.13
  550.1 1.3 dynamic_slice.14
  551.4 1.3 fusion
  552.7 0.6 constant_dynamic-slice_fusion
  553.4 0.0 reduce-scatter.2.cloned.1.call-done
  553.4 3.4 convert_bitcast_fusion
  556.8 1.5 copy.30
  558.3 0.0 copy-start
  558.3 4.9 copy.37
  563.3 0.0 copy-done
  563.3 0.0 copy-start.4
  563.3 0.0 copy-start.3
  563.3 0.0 copy-start.2
  563.3 0.0 copy-start.1
  563.3 2.1 copy.38
  565.4 0.0 copy-done.4
  565.4 0.8 copy.39
  566.2 0.0 copy-done.3
  566.2 0.8 copy.40
  567.0 0.0 copy-done.2
  567.0 0.8 copy.41
  567.8 0.0 copy-done.1
  567.8 0.8 copy.42
Async XLA Ops:
  7.2 546.2 %reduce-scatter.2.cloned.1.call-start = ((), (), s32[]{:S(2)}) async-start(), calls=%async_computation.1 | async-start | bytes 19464192 | tf_op jit(solution)/shard_map/reduce_scatter | solution.py:2104
  558.3 4.9 copy-start
  563.3 2.1 copy-start.4
  563.3 2.9 copy-start.3
  563.3 3.7 copy-start.2
  563.3 4.5 copy-start.1
Sparse Core Ops, SparseCore 0:
  299.5 121.4 reduce-scatter.1

commit v16 on v15

--- a/solution.py
+++ b/solution.py
@@ -1983,6 +1983,61 @@
         ),
         name="forward",
     )(hidden, gain, *shards, out_shard, down_shard, floor, segments, head_gain)
+
+
+def closing_kernel(
+    count,
+    ffn_ref,
+    out_share_ref,
+    *refs,
+):
+    moved_in, refs = refs[:count], refs[count:]
+    gate_ref, up_ref, down_ref, out_ref = refs[:4]
+    moved_out, sem = refs[4 : 4 + count], refs[4 + count]
+    pieces = 4
+    copies = []
+    for which, (source, target) in enumerate(zip(moved_in, moved_out)):
+        length = source.shape[0] // pieces
+        for index in range(pieces):
+            rows = pl.ds(index * length, length)
+            copies.append(
+                pltpu.make_async_copy(source.at[rows], target.at[rows], sem.at[which, index])
+            )
+    for copy in copies:
+        copy.start()
+    hidden_width = gate_ref.shape[1]
+    gate_ref[...] = ffn_ref[:, :hidden_width].astype(F32)
+    up_ref[...] = ffn_ref[:, hidden_width : 2 * hidden_width].astype(F32)
+    for first in range(0, hidden_width, 128):
+        columns = slice(2 * hidden_width + first, 2 * hidden_width + first + 128)
+        down_ref[first : first + 128] = ffn_ref[:, columns].astype(F32).T
+    for first in range(0, out_share_ref.shape[1], 128):
+        out_ref[first : first + 128] = out_share_ref[:, first : first + 128].T
+    for copy in copies:
+        copy.wait()
+
+
+def closing(share_ffn, share_out, moved):
+    block, all_width = share_ffn.shape
+    hidden_width = all_width // 3
+    whole = pl.BlockSpec(memory_space=pltpu.VMEM)
+    remote = pl.BlockSpec(memory_space=pl.ANY)
+    return pl.pallas_call(
+        partial(closing_kernel, len(moved)),
+        in_specs=[whole] * 2 + [remote] * len(moved),
+        out_specs=[whole] * 4 + [remote] * len(moved),
+        out_shape=[
+            jax.ShapeDtypeStruct((block, hidden_width), F32),
+            jax.ShapeDtypeStruct((block, hidden_width), F32),
+            jax.ShapeDtypeStruct((hidden_width, block), F32),
+            jax.ShapeDtypeStruct(share_out.shape[::-1], F32),
+        ]
+        + [jax.ShapeDtypeStruct(value.shape, value.dtype) for value in moved],
+        scratch_shapes=[pltpu.SemaphoreType.DMA((len(moved), 4))],
+        compiler_params=pltpu.CompilerParams(vmem_limit_bytes=40 << 20),
+        cost_estimate=pl.CostEstimate(flops=0, bytes_accessed=30_000_000, transcendentals=0),
+        name="closing",
+    )(share_ffn, share_out, *moved)
 
 
 def local(
@@ -2102,11 +2157,6 @@
         head_count,
     )
     share_ffn = lax.psum_scatter(grads_ffn, both, scatter_dimension=0, tiled=True)
-    hidden_width = w_ffn_gate.shape[1]
-
-    def ffn_share(which):
-        return share_ffn[:, which * hidden_width : (which + 1) * hidden_width].astype(F32)
-
     input_rows, near, total, *mixer_shares, share_out = input_line(
         mesh_axes,
         3,
@@ -2129,6 +2179,9 @@
     floor_total = near[first : first + width].reshape(head_count, key_dim)
     floor_part = key_dim // shares
 
+    share_gate, share_up, share_down, share_out, output_rows, input_rows, *mixer_shares = closing(
+        share_ffn, share_out, (output_rows, input_rows, *mixer_shares)
+    )
     return (
         output_rows.reshape(hidden.shape),
         input_rows.reshape(hidden.shape),
@@ -2136,11 +2189,11 @@
         *mixer_shares,
         lax.dynamic_slice_in_dim(floor_total, position * floor_part, floor_part, 1),
         own_slice(2 * model_width, key_dim),
-        share_out.T,
+        share_out,
         own_slice(model_width, model_width),
-        ffn_share(0),
-        ffn_share(1),
-        ffn_share(2).T,
+        share_gate,
+        share_up,
+        share_down,
     )
 
 

time: 576 us -> 577 us (level)
  Pallas kernels: 539 us -> 545 us
    pallas_call x0 -> x1, Pallas kernels: none -> 6.32 us  [closing(): pl.pallas_call(partial(closing_kernel, len(moved)), in_specs=[whole] * 2...]
    unnamed x18 -> x16, local copies, waits for them, and re-layouts: 13.8 us -> 11.2 us
where the time goes in v16:
time: 577 us; the launch traced here: 576 us
  Pallas kernels  545 us (94%)
  local copies, waits for them, and re-layouts  15.1 us (3%)
  between operations  14.1 us (2%)
    pallas_call x1, Pallas kernels, middle(): pl.pallas_call(partial(middle_kernel, mesh_axes), in_specs=[remote, remot...  216 us
    pallas_call x1, Pallas kernels, output_line(): pl.pallas_call(partial(output_kernel, mesh_axes, head_count, lanes ** (-0...  167 us
    pallas_call x1, Pallas kernels, input_line(): pl.pallas_call(partial(input_kernel, mesh_axes), in_specs=[whole] * 4 + [...  80.8 us
    pallas_call x1, Pallas kernels, forward(): pl.pallas_call(partial(forward_kernel, mesh_axes, head_count, lanes ** (-...  74.9 us
  transfers between devices with their start and end apart: 1, of which 0 were waited for; matrix products, arithmetic and copies ran while one was open for 1% of the time, Pallas kernels for 43%

profile of v16, /device:TPU:0, one launch (start us, length us, event | category | flops | bytes accessed | tf_op | source)
XLA Modules:
  0.0 575.8 jit_solution(15915081939023647330)
XLA Ops:
  7.2 0.0 reduce-scatter.2.cloned.1.call-start
  7.2 1.3 convert_element_type.5
  8.5 74.9 %forward.1 = (bf16[1024,2048]{1,0:T(8,128)(2,1)}, f32[1024,2048]{1,0:T(8,128)}, bf16[2048,2048]{1,0:T(8,128)(2,1)}, bf16[2048,512]{1,0:T(8,128)(2,1)}, f32[1024,...) custom-call(bf16[1024,2048]{1,0:T(8,128)(2,1)} %bitcast.9, ...), custom_call_target="tpu_custom_call" | custom-call | flops 8589934592 | bytes 200000000 | tf_op jit(solution)/shard_map/forward/pallas_call | solution.py:1945
  83.4 216.0 %middle.1 = (bf16[1024,2048]{1,0:T(8,128)(2,1)}, f32[1,2048]{1,0:T(1,128)}, f32[512,2048]{1,0:T(8,128)}, bf16[1024,1408]{1,0:T(8,128)(2,1)}, bf16[1024,1408]{1,0...) custom-call(bf16[1024,2048]{1,0:T(8,128)(2,1)} %get-tuple-element.61, ...), custom_call_target="tpu_custom_call" | custom-call | flops 35433480192 | bytes 360000000 | tf_op jit(solution)/shard_map/middle/pallas_call | solution.py:714
  299.4 0.0 reduce-scatter.2.cloned.1.call-update
  299.4 167.2 %output_line.1 = (bf16[1024,2048]{1,0:T(8,128)(2,1)}, f32[1,128]{1,0:T(1,128)}, f32[1,512]{1,0:T(1,128)}, f32[512,2048]{1,0:T(8,128)}, bf16[2048,2560]{1,0:T(8,128)(2,1)}) custom-call(f32[8,1,512]{2,1,0:T(1,128)} %get-tuple-element.65.run_ref, f32[4,128,128]{2,1,0:T(8,128)} %get-tuple-element.66.carry_ref, f32[4,1,128]{2,1,0:T(1,128)} %get-tuple-element.67.decay_ref, ...), custom_call_target="tpu_custom_call" | custom-call | flops 25769803776 | bytes 360000000 | tf_op jit(solution)/shard_map/output_line/pallas_call | solution.py:1173
  466.7 80.8 %input_line.1 = (bf16[1024,2048]{1,0:T(8,128)(2,1)}, f32[40,128]{1,0:T(8,128)}, f32[40,128]{1,0:T(8,128)}, f32[256,512]{1,0:T(8,128)}, f32[256,512]{1,0:T(8,128)...) custom-call(f32[1,2048]{1,0:T(1,128)} %bitcast.13, f32[1,2048]{1,0:T(1,128)} %get-tuple-element.64.norm_two_ref, ...), custom_call_target="tpu_custom_call" | custom-call | flops 16777216 | bytes 360000000 | tf_op jit(solution)/shard_map/input_line/pallas_call | solution.py:1518
  547.5 0.7 slice.4
  548.2 1.3 dynamic_slice.14
  549.5 1.3 fusion
  550.8 0.6 constant_dynamic-slice_fusion
  551.4 0.0 reduce-scatter.2.cloned.1.call-done.ffn_ref
  551.4 0.0 copy-start
  551.4 2.2 copy-done
  553.6 0.0 copy-start.1
  553.6 2.2 copy-done.1
  555.8 0.0 copy-start.2
  555.8 1.6 copy-done.2
  557.4 0.0 copy-start.3
  557.4 1.0 copy-done.3
  558.5 0.0 copy-start.4
  558.5 1.0 copy-done.4
  559.5 0.0 copy-start.5
  559.5 1.0 copy-done.5
  560.5 0.0 copy-start.6
  560.6 1.0 copy-done.6
  561.6 0.0 copy-start.7
  561.6 1.0 copy-done.7
  562.6 6.3 %closing.1 = (f32[256,1408]{1,0:T(8,128)}, f32[256,1408]{1,0:T(8,128)}, f32[1408,256]{1,0:T(8,128)}, f32[512,256]{1,0:T(8,128)}, bf16[1024,2048]{1,0:T(8,128)(2,...) custom-call(bf16[256,4224]{1,0:T(8,128)(2,1)S(1)} %copy-done.2, ...), custom_call_target="tpu_custom_call" | custom-call | bytes 30000000 | tf_op jit(solution)/shard_map/closing/pallas_call | solution.py:2025
Async XLA Ops:
  7.2 544.3 %reduce-scatter.2.cloned.1.call-start = ((), (), s32[]{:S(2)}) async-start(), calls=%async_computation.1 | async-start | bytes 19464192 | tf_op jit(solution)/shard_map/reduce_scatter | solution.py:2159
  551.4 2.2 copy-start
  553.6 2.2 copy-start.1
  555.8 1.6 copy-start.2
  557.4 1.0 copy-start.3
  558.5 1.0 copy-start.4
  559.5 1.0 copy-start.5
  560.5 1.0 copy-start.6
  561.6 1.0 copy-start.7
Sparse Core Ops, SparseCore 0:
  299.6 121.3 reduce-scatter.1

commit v17 on v16

--- a/solution.py
+++ b/solution.py
@@ -2034,7 +2034,7 @@
         ]
         + [jax.ShapeDtypeStruct(value.shape, value.dtype) for value in moved],
         scratch_shapes=[pltpu.SemaphoreType.DMA((len(moved), 4))],
-        compiler_params=pltpu.CompilerParams(vmem_limit_bytes=40 << 20),
+        compiler_params=pltpu.CompilerParams(vmem_limit_bytes=61 << 20),
         cost_estimate=pl.CostEstimate(flops=0, bytes_accessed=30_000_000, transcendentals=0),
         name="closing",
     )(share_ffn, share_out, *moved)

time: 577 us -> 882 us (1.53)
  Pallas kernels: 545 us -> 862 us
  local copies, waits for them, and re-layouts: 15.1 us -> 3.91 us
    pallas_call x1, Pallas kernels: 6.32 us -> 323 us  [closing(): pl.pallas_call(partial(closing_kernel, len(moved)), in_specs=[whole] * 2...]
    unnamed x16 -> x0, local copies, waits for them, and re-layouts: 11.2 us -> none
  transfers between devices with their start and end apart: 1 -> 1, of which waited for: 0 -> 0; matrix products, arithmetic and copies ran while one was open for 1% -> 0% of each run, Pallas kernels for 43% -> 28%
where the time goes in v17:
time: 882 us; the launch traced here: 881 us
  Pallas kernels  862 us (98%)
  between operations  14.1 us (2%)
    pallas_call x1, Pallas kernels, closing(): pl.pallas_call(partial(closing_kernel, len(moved)), in_specs=[whole] * 2...  323 us
    pallas_call x1, Pallas kernels, middle(): pl.pallas_call(partial(middle_kernel, mesh_axes), in_specs=[remote, remot...  216 us
    pallas_call x1, Pallas kernels, output_line(): pl.pallas_call(partial(output_kernel, mesh_axes, head_count, lanes ** (-0...  167 us
    pallas_call x1, Pallas kernels, input_line(): pl.pallas_call(partial(input_kernel, mesh_axes), in_specs=[whole] * 4 + [...  80.8 us
    pallas_call x1, Pallas kernels, forward(): pl.pallas_call(partial(forward_kernel, mesh_axes, head_count, lanes ** (-...  74.8 us
  transfers between devices with their start and end apart: 1, of which 0 were waited for; matrix products, arithmetic and copies ran while one was open for 0% of the time, Pallas kernels for 28%

profile of v17, /device:TPU:0, one launch (start us, length us, event | category | flops | bytes accessed | tf_op | source)
XLA Modules:
  0.0 881.0 jit_solution(14416317592935768036)
XLA Ops:
  7.2 0.0 reduce-scatter.2.cloned.1.call-start
  7.2 1.3 convert_element_type.5
  8.5 74.8 %forward.1 = (bf16[1024,2048]{1,0:T(8,128)(2,1)}, f32[1024,2048]{1,0:T(8,128)}, bf16[2048,2048]{1,0:T(8,128)(2,1)}, bf16[2048,512]{1,0:T(8,128)(2,1)}, f32[1024,...) custom-call(bf16[1024,2048]{1,0:T(8,128)(2,1)} %bitcast.9, ...), custom_call_target="tpu_custom_call" | custom-call | flops 8589934592 | bytes 200000000 | tf_op jit(solution)/shard_map/forward/pallas_call | solution.py:1945
  83.3 216.0 %middle.1 = (bf16[1024,2048]{1,0:T(8,128)(2,1)}, f32[1,2048]{1,0:T(1,128)}, f32[512,2048]{1,0:T(8,128)}, bf16[1024,1408]{1,0:T(8,128)(2,1)}, bf16[1024,1408]{1,0...) custom-call(bf16[1024,2048]{1,0:T(8,128)(2,1)} %get-tuple-element.61, ...), custom_call_target="tpu_custom_call" | custom-call | flops 35433480192 | bytes 360000000 | tf_op jit(solution)/shard_map/middle/pallas_call | solution.py:714
  299.3 0.0 reduce-scatter.2.cloned.1.call-update
  299.3 167.3 %output_line.1 = (bf16[1024,2048]{1,0:T(8,128)(2,1)}, f32[1,128]{1,0:T(1,128)}, f32[1,512]{1,0:T(1,128)}, f32[512,2048]{1,0:T(8,128)}, bf16[2048,2560]{1,0:T(8,128)(2,1)}) custom-call(f32[8,1,512]{2,1,0:T(1,128)} %get-tuple-element.65.run_ref, f32[4,128,128]{2,1,0:T(8,128)} %get-tuple-element.66.carry_ref, f32[4,1,128]{2,1,0:T(1,128)} %get-tuple-element.67.decay_ref, ...), custom_call_target="tpu_custom_call" | custom-call | flops 25769803776 | bytes 360000000 | tf_op jit(solution)/shard_map/output_line/pallas_call | solution.py:1173
  466.6 80.8 %input_line.1 = (bf16[1024,2048]{1,0:T(8,128)(2,1)}, f32[40,128]{1,0:T(8,128)}, f32[40,128]{1,0:T(8,128)}, f32[256,512]{1,0:T(8,128)}, f32[256,512]{1,0:T(8,128)...) custom-call(f32[1,2048]{1,0:T(1,128)} %bitcast.13, f32[1,2048]{1,0:T(1,128)} %get-tuple-element.64.norm_two_ref, ...), custom_call_target="tpu_custom_call" | custom-call | flops 16777216 | bytes 360000000 | tf_op jit(solution)/shard_map/input_line/pallas_call | solution.py:1518
  547.4 0.7 slice.4
  548.1 1.3 dynamic_slice.14
  549.3 1.3 fusion
  550.7 0.6 constant_dynamic-slice_fusion
  551.3 0.0 reduce-scatter.2.cloned.1.call-done.ffn_ref
  551.3 322.9 %closing.1 = (f32[256,1408]{1,0:T(8,128)}, f32[256,1408]{1,0:T(8,128)}, f32[1408,256]{1,0:T(8,128)}, f32[512,256]{1,0:T(8,128)}, bf16[1024,2048]{1,0:T(8,128)(2,...) custom-call(bf16[256,4224]{1,0:T(8,128)(2,1)} %reduce-scatter.2.clon, ...), custom_call_target="tpu_custom_call" | custom-call | bytes 30000000 | tf_op jit(solution)/shard_map/closing/pallas_call | solution.py:2025
Async XLA Ops:
  7.2 544.1 %reduce-scatter.2.cloned.1.call-start = ((), (), s32[]{:S(2)}) async-start(), calls=%async_computation.1 | async-start | bytes 19464192 | tf_op jit(solution)/shard_map/reduce_scatter | solution.py:2159
Sparse Core Ops, SparseCore 0:
  299.4 121.4 reduce-scatter.1

commit v18 on v17

--- a/solution.py
+++ b/solution.py
@@ -1993,19 +1993,27 @@
 ):
     moved_in, refs = refs[:count], refs[count:]
     gate_ref, up_ref, down_ref, out_ref = refs[:4]
-    moved_out, sem = refs[4 : 4 + count], refs[4 + count]
+    moved_out, held = refs[4 : 4 + count], refs[4 + count : 4 + 2 * count]
+    load_sem, store_sem = refs[4 + 2 * count :]
     pieces = 4
-    copies = []
-    for which, (source, target) in enumerate(zip(moved_in, moved_out)):
+    loads, stores = [], []
+    for which, (source, middle_ref, target) in enumerate(zip(moved_in, held, moved_out)):
         length = source.shape[0] // pieces
         for index in range(pieces):
             rows = pl.ds(index * length, length)
-            copies.append(
-                pltpu.make_async_copy(source.at[rows], target.at[rows], sem.at[which, index])
+            inside = middle_ref.at[rows]
+            loads.append(
+                pltpu.make_async_copy(source.at[rows], inside, load_sem.at[which, index])
             )
-    for copy in copies:
-        copy.start()
+            stores.append(
+                pltpu.make_async_copy(inside, target.at[rows], store_sem.at[which, index])
+            )
+    for load in loads:
+        load.start()
     hidden_width = gate_ref.shape[1]
+    for load, store in zip(loads, stores):
+        load.wait()
+        store.start()
     gate_ref[...] = ffn_ref[:, :hidden_width].astype(F32)
     up_ref[...] = ffn_ref[:, hidden_width : 2 * hidden_width].astype(F32)
     for first in range(0, hidden_width, 128):
@@ -2013,8 +2021,8 @@
         down_ref[first : first + 128] = ffn_ref[:, columns].astype(F32).T
     for first in range(0, out_share_ref.shape[1], 128):
         out_ref[first : first + 128] = out_share_ref[:, first : first + 128].T
-    for copy in copies:
-        copy.wait()
+    for store in stores:
+        store.wait()
 
 
 def closing(share_ffn, share_out, moved):
@@ -2033,7 +2041,8 @@
             jax.ShapeDtypeStruct(share_out.shape[::-1], F32),
         ]
         + [jax.ShapeDtypeStruct(value.shape, value.dtype) for value in moved],
-        scratch_shapes=[pltpu.SemaphoreType.DMA((len(moved), 4))],
+        scratch_shapes=[pltpu.VMEM(value.shape, value.dtype) for value in moved]
+        + [pltpu.SemaphoreType.DMA((len(moved), 4))] * 2,
         compiler_params=pltpu.CompilerParams(vmem_limit_bytes=61 << 20),
         cost_estimate=pl.CostEstimate(flops=0, bytes_accessed=30_000_000, transcendentals=0),
         name="closing",

time: 882 us -> 571 us (0.65)
  Pallas kernels: 862 us -> 551 us
    pallas_call x1, Pallas kernels: 323 us -> 12 us  [closing(): pl.pallas_call(partial(closing_kernel, len(moved)), in_specs=[whole] * 2...]
  transfers between devices with their start and end apart: 1 -> 1, of which waited for: 0 -> 0; matrix products, arithmetic and copies ran while one was open for 0% -> 1% of each run, Pallas kernels for 28% -> 44%
where the time goes in v18:
time: 571 us; the launch traced here: 570 us
  Pallas kernels  551 us (96%)
  between operations  14.1 us (2%)
    pallas_call x1, Pallas kernels, middle(): pl.pallas_call(partial(middle_kernel, mesh_axes), in_specs=[remote, remot...  216 us
    pallas_call x1, Pallas kernels, output_line(): pl.pallas_call(partial(output_kernel, mesh_axes, head_count, lanes ** (-0...  167 us
    pallas_call x1, Pallas kernels, input_line(): pl.pallas_call(partial(input_kernel, mesh_axes), in_specs=[whole] * 4 + [...  80.8 us
    pallas_call x1, Pallas kernels, forward(): pl.pallas_call(partial(forward_kernel, mesh_axes, head_count, lanes ** (-...  74.8 us
    pallas_call x1, Pallas kernels, closing(): pl.pallas_call(partial(closing_kernel, len(moved)), in_specs=[whole] * 2...  12 us
  transfers between devices with their start and end apart: 1, of which 0 were waited for; matrix products, arithmetic and copies ran while one was open for 1% of the time, Pallas kernels for 44%

profile of v18, /device:TPU:0, one launch (start us, length us, event | category | flops | bytes accessed | tf_op | source)
XLA Modules:
  0.0 570.1 jit_solution(2223978295118948904)
XLA Ops:
  7.2 0.0 reduce-scatter.2.cloned.1.call-start
  7.2 1.3 convert_element_type.5
  8.5 74.8 %forward.1 = (bf16[1024,2048]{1,0:T(8,128)(2,1)}, f32[1024,2048]{1,0:T(8,128)}, bf16[2048,2048]{1,0:T(8,128)(2,1)}, bf16[2048,512]{1,0:T(8,128)(2,1)}, f32[1024,...) custom-call(bf16[1024,2048]{1,0:T(8,128)(2,1)} %bitcast.9, ...), custom_call_target="tpu_custom_call" | custom-call | flops 8589934592 | bytes 200000000 | tf_op jit(solution)/shard_map/forward/pallas_call | solution.py:1945
  83.3 216.0 %middle.1 = (bf16[1024,2048]{1,0:T(8,128)(2,1)}, f32[1,2048]{1,0:T(1,128)}, f32[512,2048]{1,0:T(8,128)}, bf16[1024,1408]{1,0:T(8,128)(2,1)}, bf16[1024,1408]{1,0...) custom-call(bf16[1024,2048]{1,0:T(8,128)(2,1)} %get-tuple-element.61, ...), custom_call_target="tpu_custom_call" | custom-call | flops 35433480192 | bytes 360000000 | tf_op jit(solution)/shard_map/middle/pallas_call | solution.py:714
  299.3 0.0 reduce-scatter.2.cloned.1.call-update
  299.3 167.3 %output_line.1 = (bf16[1024,2048]{1,0:T(8,128)(2,1)}, f32[1,128]{1,0:T(1,128)}, f32[1,512]{1,0:T(1,128)}, f32[512,2048]{1,0:T(8,128)}, bf16[2048,2560]{1,0:T(8,128)(2,1)}) custom-call(f32[8,1,512]{2,1,0:T(1,128)} %get-tuple-element.65.run_ref, f32[4,128,128]{2,1,0:T(8,128)} %get-tuple-element.66.carry_ref, f32[4,1,128]{2,1,0:T(1,128)} %get-tuple-element.67.decay_ref, ...), custom_call_target="tpu_custom_call" | custom-call | flops 25769803776 | bytes 360000000 | tf_op jit(solution)/shard_map/output_line/pallas_call | solution.py:1173
  466.6 80.8 %input_line.1 = (bf16[1024,2048]{1,0:T(8,128)(2,1)}, f32[40,128]{1,0:T(8,128)}, f32[40,128]{1,0:T(8,128)}, f32[256,512]{1,0:T(8,128)}, f32[256,512]{1,0:T(8,128)...) custom-call(f32[1,2048]{1,0:T(1,128)} %bitcast.13, f32[1,2048]{1,0:T(1,128)} %get-tuple-element.64.norm_two_ref, ...), custom_call_target="tpu_custom_call" | custom-call | flops 16777216 | bytes 360000000 | tf_op jit(solution)/shard_map/input_line/pallas_call | solution.py:1518
  547.4 0.7 slice.4
  548.1 1.3 dynamic_slice.14
  549.3 1.3 fusion
  550.7 0.6 constant_dynamic-slice_fusion
  551.3 0.0 reduce-scatter.2.cloned.1.call-done.ffn_ref
  551.3 12.0 %closing.1 = (f32[256,1408]{1,0:T(8,128)}, f32[256,1408]{1,0:T(8,128)}, f32[1408,256]{1,0:T(8,128)}, f32[512,256]{1,0:T(8,128)}, bf16[1024,2048]{1,0:T(8,128)(2,...) custom-call(bf16[256,4224]{1,0:T(8,128)(2,1)} %reduce-scatter.2.clon, ...), custom_call_target="tpu_custom_call" | custom-call | bytes 30000000 | tf_op jit(solution)/shard_map/closing/pallas_call | solution.py:2033
Async XLA Ops:
  7.2 544.1 %reduce-scatter.2.cloned.1.call-start = ((), (), s32[]{:S(2)}) async-start(), calls=%async_computation.1 | async-start | bytes 19464192 | tf_op jit(solution)/shard_map/reduce_scatter | solution.py:2168
Sparse Core Ops, SparseCore 0:
  299.4 121.4 reduce-scatter.1
